TPU v7x, 256 devices: a whole 4x4x8 slice. The times are simulated.
256 devices in a mesh: dom: 64 (over y, z, core), rep: 4 (over x).
Axes of the slice: x: 4, y: 4, z: 8, core: 2. Of those that a mesh axis runs over, the one named last changes fastest.
Arguments:
- feats: bfloat16 [256, 262144], P('rep', 'dom'), may hold values from -6 to 6
- w_self: bfloat16 [256, 256], P(None, 'rep'), may hold values from -0.375 to 0.375
- w_neigh: bfloat16 [256, 256], P(None, 'rep'), may hold values from -3 to 3
- local_cols: int32 [2048, 2], P('dom'), may hold values from 0 to 31
- local_tiles: bfloat16 [2048, 2, 128, 128], P('dom'), may hold values from 0 to 3, as said below
- send_list: int32 [64, 64, 2], P('dom'), may hold values from 0 to 31
- remote_rows: int32 [64, 64, 2], P('dom'), may hold values from 0 to 31
- remote_tiles: bfloat16 [64, 64, 2, 128, 128], P('dom'), may hold values from 0 to 3, as said below
- cotangent: bfloat16 [256, 262144], P('rep', 'dom'), may hold values from -6 to 6
Outputs:
- output: bfloat16 [256, 262144], P('rep', 'dom')
- grad_feats: bfloat16 [256, 262144], P('rep', 'dom')
- grad_w_self: float32 [256, 256], P(None, 'rep')
- grad_w_neigh: float32 [256, 256], P(None, 'rep')
Inputs may be any that keep to these rules, and one draw needn't show every extreme that they name: `local_tiles`: edge weights: zero where a tile has no edge, positive otherwise. `remote_tiles`: edge weights: zero where a tile has no edge, positive otherwise.
All inputs are finite; a program needn't handle non-finite values.
Results may differ from a plain program's by a relative error of at most 0.0055.
Values may be sent and summed in bfloat16 or wider, within the bound.
No kernel may reach another device: no remote copies, remote signals or barrier semaphores. Data moves between devices by JAX's collectives and lax.ppermute only.
A program may use at most 128 MiB of HBM per device.

v0:
```python
import jax
import jax.numpy as jnp
from jax import lax
from jax.sharding import PartitionSpec as P


def local(
    feats, w_self, w_neigh, local_cols, local_tiles, send_list, remote_rows, remote_tiles, cotangent
):
    highest = lax.Precision.HIGHEST
    feat_width, node_count = feats.shape
    blocks, local_links, tile_side, _ = local_tiles.shape
    block_ids = jnp.arange(blocks, dtype=jnp.int32)
    blocked = feats.reshape(feat_width, blocks, tile_side)
    outgoing = blocked[:, send_list[0]]
    incoming = lax.all_to_all(outgoing, "dom", split_axis=1, concat_axis=1, tiled=True)
    full_feats = lax.all_gather(feats, "rep", axis=0, tiled=True)
    gathered = blocked[:, local_cols]
    summed = jnp.einsum("fblj,blij->fbi", gathered, local_tiles, preferred_element_type=jnp.float32)
    weight_rows = jnp.sum(local_tiles, axis=(1, 3), dtype=jnp.float32)
    far_tiles = remote_tiles[0]
    far_rows = remote_rows[0]
    placing = (far_rows[:, :, None] == block_ids).astype(jnp.float32)
    far_sums = jnp.sum(far_tiles, axis=3, dtype=jnp.float32)
    divisor = 1.0 + weight_rows + jnp.einsum("ski,skb->bi", far_sums, placing, precision=highest)
    far_terms = jnp.einsum(
        "fskj,skij->fski", incoming, far_tiles, preferred_element_type=jnp.float32
    )
    summed = summed + jnp.einsum("fski,skb->fbi", far_terms, placing, precision=highest)
    aggregate = (summed / divisor).astype(jnp.bfloat16).reshape(feat_width, node_count)
    full_agg = lax.all_gather(aggregate, "rep", axis=0, tiled=True)
    preact = jnp.einsum("ab,an->bn", w_self, full_feats, preferred_element_type=jnp.float32)
    preact = preact + jnp.einsum("ab,an->bn", w_neigh, full_agg, preferred_element_type=jnp.float32)
    sigmoid_val = jax.nn.sigmoid(preact)
    output = (preact * sigmoid_val).astype(jnp.bfloat16)
    slope = sigmoid_val * (1.0 + preact * (1.0 - sigmoid_val))
    grad_pre = (cotangent.astype(jnp.float32) * slope).astype(jnp.bfloat16)
    wg_self = jnp.einsum("an,bn->ab", full_feats, grad_pre, preferred_element_type=jnp.float32)
    wg_neigh = jnp.einsum("an,bn->ab", full_agg, grad_pre, preferred_element_type=jnp.float32)
    wg_self, wg_neigh = lax.psum((wg_self, wg_neigh), "dom")
    term_self = jnp.dot(w_self, grad_pre, preferred_element_type=jnp.float32)
    term_neigh = jnp.dot(w_neigh, grad_pre, preferred_element_type=jnp.float32)
    stacked = lax.psum_scatter(
        jnp.concatenate([term_self, term_neigh], axis=1), "rep", scatter_dimension=0, tiled=True
    )
    back_self = stacked[:, :node_count]
    back_agg = stacked[:, node_count:]
    scaled = (back_agg.reshape(feat_width, blocks, tile_side) / divisor).astype(jnp.bfloat16)
    picked = scaled[:, far_rows]
    far_back = jnp.einsum("fski,skij->fskj", picked, far_tiles, preferred_element_type=jnp.float32)
    returned = lax.all_to_all(far_back, "dom", split_axis=1, concat_axis=1, tiled=True)
    near_back = jnp.einsum(
        "fbi,blij->fblj", scaled, local_tiles, preferred_element_type=jnp.float32
    )
    landing = (local_cols[:, :, None] == block_ids).astype(jnp.float32)
    collected = jnp.einsum("fblj,blc->fcj", near_back, landing, precision=highest)
    homing = (send_list[0][:, :, None] == block_ids).astype(jnp.float32)
    collected = collected + jnp.einsum("fdkj,dkc->fcj", returned, homing, precision=highest)
    grad_feats = (back_self + collected.reshape(feat_width, node_count)).astype(jnp.bfloat16)
    return (output, grad_feats, wg_self, wg_neigh)


def solution(mesh):
    placed = (
        P("rep", "dom"),
        P(None, "rep"),
        P(None, "rep"),
        P("dom", None),
        P("dom", None, None, None),
        P("dom", None, None),
        P("dom", None, None),
        P("dom", None, None, None, None),
        P("rep", "dom"),
    )
    return jax.shard_map(
        local,
        mesh=mesh,
        in_specs=placed,
        out_specs=(P("rep", "dom"), P("rep", "dom"), P(None, "rep"), P(None, "rep")),
        check_vma=False,
    )
```

profile of v0, /device:TPU:1, one launch (start us, length us, event | category | flops | bytes accessed | tf_op | source)
XLA Modules:
  0.0 480.7 jit_solution(3183939513342969295)
XLA Ops:
  9.3 2.1 gather_fusion.1
  11.5 13.3 %all-to-all-start = ((bf16[64,64,2,128]{3,0,2,1:T(8,128)(2,1)}), bf16[64,64,2,128]{3,0,2,1:T(8,128)(2,1)S(1)}, u32[]{:S(2)}, u32[]{:S(2)}) async-start(bf16[64,64,2,128]{3,0,2,1:T(8,128)(2,1)} %bitcast.123), calls=%async_computation | async-start | bytes 4194304 | tf_op jit(solution)/shard_map/all_to_all | solution.py:16
  26.7 2.2 convert_reduce_fusion.1
  28.9 3.4 convert_reduce_fusion
  32.5 43.5 %all-to-all-done = bf16[64,64,2,128]{3,0,2,1:T(8,128)(2,1)S(1)} async-done(((bf16[64,64,2,128]{3,0,2,1:T(8,128)(2,1)}), bf16[64,64,2,128]{3,0,2,1:T(8,128)(2,1)S(1)}, u32[]{:S(2)}, u32[]{:S(2)}) %all-to-all-start) | async-done | bytes 2097184 | tf_op jit(solution)/shard_map/all_to_all | solution.py:16
  76.0 5.1 %fusion.8 = f32[64,64,2,128]{3,0,2,1:T(8,128)S(1)} fusion(bf16[64,64,2,128]{3,0,2,1:T(8,128)(2,1)S(1)} %all-to-all-done, bf16[1,64,2,128,128]{4,3,2,1,0:T(8,128)(2,1)} %param.16), kind=kOutput, calls=%fused_computation.18 | convolution fusion | flops 268435456 | bytes 10485760 | tf_op jit(solution)/shard_map/fskj,skij->fski/dot_general | solution.py:26
  81.2 4.0 fusion.20
  88.2 29.0 %all-gather.5.cloned.1.call-done = bf16[256,4096]{1,0:T(8,128)(2,1)} async-done(((bf16[64,4096]{1,0:T(8,128)(2,1)}), bf16[256,4096]{1,0:T(8,128)(2,1)}) %all-gather.5.cloned.1.call-update) | async-done | bytes 2097168 | tf_op jit(solution)/shard_map/all_gather | solution.py:31
  117.2 2.1 convolution_bitcast_fusion.2
  119.2 33.2 %all-gather.3.cloned.1.call-done = bf16[256,4096]{1,0:T(8,128)(2,1)} async-done(((bf16[64,4096]{1,0:T(8,128)(2,1)}), bf16[256,4096]{1,0:T(8,128)(2,1)}) %all-gather.3.cloned.1.call-update) | async-done | bytes 2097168 | tf_op jit(solution)/shard_map/all_gather | solution.py:17
  152.4 3.2 multiply_convert_fusion
  157.1 3.8 pad_maximum_fusion
  160.9 8.9 %copy.60 = f32[256,8192]{1,0:T(8,128)} copy(f32[256,8192]{0,1:T(8,128)} %pad_maximum_fusion) | data formatting | bytes 16777216
  170.1 83.0 %reduce-scatter.4.cloned.1.call-done = f32[64,8192]{1,0:T(8,128)} async-done(((f32[256,8192]{1,0:T(8,128)}), f32[64,8192]{1,0:T(8,128)}) %reduce-scatter.4.cloned.1.call-update) | async-done | bytes 2097168
  253.1 3.1 fusion.49
  256.2 1.8 copy.63
  261.9 5.4 %fusion.11 = f32[64,64,2,128]{3,0,2,1:T(8,128)} fusion(bf16[64,64,2,128]{3,0,2,1:T(8,128)(2,1)S(1)} %bitcast.121, bf16[1,64,2,128,128]{4,3,2,1,0:T(8,128)(2,1)} %param.16), kind=kOutput, calls=%fused_computation.19 | convolution fusion | flops 268435456 | bytes 10485760 | tf_op jit(solution)/shard_map/fski,skij->fskj/dot_general | solution.py:50
  267.3 11.0 %all-to-all-start.1 = ((f32[64,64,2,128]{3,0,2,1:T(8,128)}), f32[64,64,2,128]{3,0,2,1:T(8,128)}, u32[]{:S(2)}, u32[]{:S(2)}) async-start(f32[64,64,2,128]{3,0,2,1:T(8,128)} %fusion.11), calls=%async_computation.1 | async-start | bytes 8388608 | tf_op jit(solution)/shard_map/all_to_all | solution.py:51
  281.6 3.4 copy.62
  285.4 2.1 fusion.17
  287.5 87.6 %all-to-all-done.1 = f32[64,64,2,128]{3,0,2,1:T(8,128)} async-done(((f32[64,64,2,128]{3,0,2,1:T(8,128)}), f32[64,64,2,128]{3,0,2,1:T(8,128)}, u32[]{:S(2)}, u32[]{:S(2)}) %all-to-all-start.1) | async-done | bytes 4194336 | tf_op jit(solution)/shard_map/all_to_all | solution.py:51
  375.1 5.9 %fusion.31 = f32[64,32,128]{2,1,0:T(8,128)S(1)} fusion(f32[32,64,128]{2,0,1:T(8,128)S(1)} %fusion.17, f32[64,64,2,128]{3,0,2,1:T(8,128)} %all-to-all-done.1, s32[64,2]{0,1:T(2,128)S(1)} %bitcast.128), kind=kOutput, calls=%fused_computation.32 | convolution fusion | flops 402919424 | bytes 6291968 | tf_op jit(solution)/shard_map/fdkj,dkc->fcj/dot_general | solution.py:58
  381.0 2.0 copy.59
  386.0 85.2 %all-reduce.3.cloned.1.call-done = (f32[256,64]{0,1:T(8,128)}, f32[256,64]{0,1:T(8,128)}) async-done(((f32[256,64]{0,1:T(8,128)}, f32[256,64]{0,1:T(8,128)}), (f32[256,64]{0,1:T(8,128)}, f32[256,64]{0,1:T(8,128)})) %all-reduce.3.cloned.1.call-update) | async-done | bytes 131088 | tf_op jit(solution)/shard_map/psum | solution.py:40
  (63 shorter events, 22.4 us)
Async XLA Ops:
  7.2 145.3 %copy-start = (bf16[256,64]{0,1:T(8,128)(2,1)S(1)}, bf16[256,64]{0,1:T(8,128)(2,1)}, u32[]{:S(2)}) copy-start(bf16[256,64]{0,1:T(8,128)(2,1)} %param.10) | copy-start | bytes 98308
  11.5 13.3 %copy-start.10 = (s32[32,2]{0,1:T(2,128)S(1)}, s32[32,2]{0,1:T(2,128)}, u32[]{:S(2)}) copy-start(s32[32,2]{0,1:T(2,128)} %param.12) | copy-start | bytes 772
  11.5 64.5 %all-to-all-start = ((bf16[64,64,2,128]{3,0,2,1:T(8,128)(2,1)}), bf16[64,64,2,128]{3,0,2,1:T(8,128)(2,1)S(1)}, u32[]{:S(2)}, u32[]{:S(2)}) async-start(bf16[64,64,2,128]{3,0,2,1:T(8,128)(2,1)} %bitcast.123), calls=%async_computation | async-start | bytes 4194304 | tf_op jit(solution)/shard_map/all_to_all | solution.py:16
  24.8 92.4 %all-gather.5.cloned.1.call-start = ((), (), s32[]{:S(2)}) async-start(), calls=%async_computation.4 | async-start | bytes 2621440 | tf_op jit(solution)/shard_map/all_gather | solution.py:31
  28.9 3.4 copy-start.9
  81.1 4.0 copy-start.2
  81.1 4.0 copy-start.7
  86.3 30.9 %copy-start.8 = (bf16[256,64]{0,1:T(8,128)(2,1)S(1)}, bf16[256,64]{0,1:T(8,128)(2,1)}, u32[]{:S(2)}) copy-start(bf16[256,64]{0,1:T(8,128)(2,1)} %param.11) | copy-start | bytes 98308
  87.2 65.3 %copy-start.12 = (bf16[64,4096]{1,0:T(8,128)(2,1)S(1)}, bf16[64,4096]{1,0:T(8,128)(2,1)}, u32[]{:S(2)}) copy-start(bf16[64,4096]{1,0:T(8,128)(2,1)} %param.17) | copy-start | bytes 1572868
  87.2 65.3 %all-gather.3.cloned.1.call-start = ((), (), s32[]{:S(2)}) async-start(), calls=%async_computation.3 | async-start | bytes 2621440 | tf_op jit(solution)/shard_map/all_gather | solution.py:17
  87.9 165.2 %reduce-scatter.4.cloned.1.call-start = ((), (), s32[]{:S(2)}) async-start(), calls=%async_computation.5 | async-start | bytes 10485760
  267.3 11.2 %copy-start.4 = (bf16[256,4096]{1,0:T(8,128)(2,1)S(1)}, bf16[256,4096]{1,0:T(8,128)(2,1)}, u32[]{:S(2)}) copy-start(bf16[256,4096]{1,0:T(8,128)(2,1)} %all-gather.5.cloned.1.call-done) | copy-start | bytes 6291460
  267.3 107.7 %all-to-all-start.1 = ((f32[64,64,2,128]{3,0,2,1:T(8,128)}), f32[64,64,2,128]{3,0,2,1:T(8,128)}, u32[]{:S(2)}, u32[]{:S(2)}) async-start(f32[64,64,2,128]{3,0,2,1:T(8,128)} %fusion.11), calls=%async_computation.1 | async-start | bytes 8388608 | tf_op jit(solution)/shard_map/all_to_all | solution.py:51
  278.3 192.9 %all-reduce.3.cloned.1.call-start = ((), (), s32[]{:S(2)}) async-start(), calls=%async_computation.6 | async-start | bytes 262144 | tf_op jit(solution)/shard_map/psum | solution.py:40
  278.6 1.6 copy-start.6
  281.6 3.4 copy-start.3
  285.4 89.6 %copy-start.11 = (s32[1,64,2]{1,2,0:T(2,128)S(1)}, s32[1,64,2]{1,2,0:T(2,128)}, u32[]{:S(2)}) copy-start(s32[1,64,2]{1,2,0:T(2,128)} %param.14) | copy-start | bytes 1540
  381.0 2.0 copy-start.5
  383.0 91.1 %copy-start.1 = (bf16[256,64]{0,1:T(8,128)(2,1)S(1)}, bf16[256,64]{0,1:T(8,128)(2,1)}, u32[]{:S(2)}) copy-start(bf16[256,64]{0,1:T(8,128)(2,1)} %param.10) | copy-start | bytes 98308
Sparse Core Ops, SparseCore 0:
  87.3 29.8 all-gather.4
  119.0 33.4 all-gather.2
  169.9 83.1 reduce-scatter.3
  283.0 188.1 all-reduce.2
where the time goes:
time: 482 us; the launch traced here: 481 us
  waiting for transfers between devices  362 us (75%)
  matrix products  33.7 us (7%)
  local copies, waits for them, and re-layouts  32.6 us (7%)
  starting transfers between devices  24.8 us (5%)
  between operations  14 us (3%)
  other arithmetic  13.2 us (3%)
    all_to_all x1, waiting for transfers between devices, local(): lax.all_to_all(far_back, 'dom', split_axis=1, concat_axis=1, tiled=True)  87.6 us
    psum x1, waiting for transfers between devices, local(): wg_self, wg_neigh = lax.psum((wg_self, wg_neigh), 'dom')  85.2 us
    unnamed x5, waiting for transfers between devices  83.8 us
    all_to_all x1, waiting for transfers between devices, local(): lax.all_to_all(outgoing, 'dom', split_axis=1, concat_axis=1, tiled=True)  43.5 us
    all_gather x1, waiting for transfers between devices, local(): full_feats = lax.all_gather(feats, 'rep', axis=0, tiled=True)  33.2 us
    all_gather x1, waiting for transfers between devices, local(): full_agg = lax.all_gather(aggregate, 'rep', axis=0, tiled=True)  29 us
    unnamed x32, local copies, waits for them, and re-layouts  18.5 us
    all_to_all x1, starting transfers between devices, local(): lax.all_to_all(outgoing, 'dom', split_axis=1, concat_axis=1, tiled=True)  13.3 us
  transfers between devices with their start and end apart: 6, of which 6 were waited for; matrix products, arithmetic and copies ran while one was open for 6% of the time, Pallas kernels for 0%

commit v1 on v0

v1 whole, which is shorter than its diff:
```python
import jax
import jax.numpy as jnp
from jax import lax
from jax.experimental import pallas as pl
from jax.experimental.pallas import tpu as pltpu
from jax.sharding import PartitionSpec as P

TILE = 128
STEP = 8
VMEM_BYTES = 40 * 1024 * 1024
F32 = jnp.float32
BF16 = jnp.bfloat16


def whole(shape):
    return pl.BlockSpec(shape, lambda *_: (0,) * len(shape))


def lanes(index, width):
    return pl.ds(pl.multiple_of(index * width, width), width)


def params():
    return pltpu.CompilerParams(vmem_limit_bytes=VMEM_BYTES)


def cost(flops, nbytes):
    return pl.CostEstimate(flops=flops, bytes_accessed=nbytes, transcendentals=0)


def call(body, args, prefetch, grid, in_specs, out_shape, out_specs, scratch=(), aliases=None, flops=0, nbytes=1 << 20):
    return pl.pallas_call(
        body,
        grid_spec=pltpu.PrefetchScalarGridSpec(
            num_scalar_prefetch=prefetch, grid=grid, in_specs=in_specs, out_specs=out_specs, scratch_shapes=scratch
        ),
        out_shape=out_shape,
        input_output_aliases=aliases or {},
        compiler_params=params(),
        cost_estimate=cost(flops, nbytes),
    )(*args)


def shape(dims, kind):
    return jax.ShapeDtypeStruct(dims, kind)


def dot(left, right, left_dim, right_dim):
    return lax.dot_general(left, right, (((left_dim,), (right_dim,)), ((), ())), preferred_element_type=F32)


def pick_body(send_ref, feats_ref, out_ref):
    step = pl.program_id(0)
    chans = feats_ref.shape[0]
    for item in range(STEP):
        for slot in range(2):
            block = send_ref[step * STEP + item, slot]
            out_ref[item, slot * chans : (slot + 1) * chans, :] = feats_ref[:, lanes(block, TILE)]


def chunk_body(rep_ref, feats_ref, cot_ref, *outs):
    reps = len(outs) // 2
    width = outs[0].shape[1]
    for k in range(reps):
        chunk = lax.rem(rep_ref[0] + k, reps)
        outs[k][...] = feats_ref[:, lanes(chunk, width)]
        outs[reps + k][...] = cot_ref[:, lanes(chunk, width)]


def near_body(cols_ref, rows_ref, feats_ref, near_ref, far_ref, acc_ref, div_ref):
    step = pl.program_id(0)
    ones = jnp.ones((8, TILE), BF16)
    near_blocks = near_ref.shape[0]

    @pl.when(step == 0)
    def _():
        div_ref[...] = jnp.ones_like(div_ref)

    for item in range(near_blocks):
        row = step * near_blocks + item
        total = None
        sums = None
        for link in range(2):
            tile = near_ref[item, link]
            block = feats_ref[:, lanes(cols_ref[row, link], TILE)]
            term = dot(block, tile, 1, 1)
            part = dot(ones, tile, 1, 1)
            total = term if total is None else total + term
            sums = part if sums is None else sums + part
        acc_ref[:, lanes(row, TILE)] = total
        div_ref[:, lanes(row, TILE)] += sums
    for item in range(STEP):
        for slot in range(2):
            row = rows_ref[step * STEP + item, slot]
            div_ref[:, lanes(row, TILE)] += dot(ones, far_ref[item, slot], 1, 1)


def far_body(rep_ref, rows_ref, got_ref, far_ref, near_acc_ref, div_ref, *rest):
    outs, acc_ref = rest[:-1], rest[-1]
    step = pl.program_id(0)
    reps = len(outs)
    chans = acc_ref.shape[0]
    width = outs[0].shape[1]

    @pl.when(step == 0)
    def _():
        acc_ref[...] = near_acc_ref[...]

    for item in range(STEP):
        for slot in range(2):
            row = rows_ref[step * STEP + item, slot]
            block = got_ref[item, slot * chans : (slot + 1) * chans, :]
            acc_ref[:, lanes(row, TILE)] += dot(block, far_ref[item, slot], 1, 1)

    @pl.when(step == pl.num_programs(0) - 1)
    def _():
        for k in range(reps):
            chunk = lax.rem(rep_ref[0] + k, reps)
            where = lanes(chunk, width)
            outs[k][...] = (acc_ref[:, where] / div_ref[0:1, where]).astype(BF16)


def gather_rows(ref, pieces, rep):
    reps = len(pieces)
    rows = pieces[0].shape[0]
    for k in range(reps):
        source = lax.rem(rep + reps - k, reps)
        ref[lanes(source, rows), :] = pieces[k][...]


def dense_body(rep_ref, *refs):
    agg, feats, cot, wts = refs[0:4], refs[4:8], refs[8:12], refs[12:16]
    div_ref = refs[16]
    scaled_out, out_out = refs[17:21], refs[21:25]
    grad_ref, back_ref, full_feats, full_agg = refs[25:29]
    rep = rep_ref[0]
    reps = 4
    rows, width = agg[0].shape
    gather_rows(full_feats, feats, rep)
    gather_rows(full_agg, agg, rep)
    for k in range(reps):
        preact = dot(wts[k][0], full_feats[...], 1, 0) + dot(wts[k][1], full_agg[...], 1, 0)
        gate = jax.nn.sigmoid(preact)
        out_out[k][...] = (preact * gate).astype(BF16)
        slope = gate * (1.0 + preact * (1.0 - gate))
        grad_ref[k * rows : (k + 1) * rows, :] = (cot[k][...].astype(F32) * slope).astype(BF16)
    w_neigh = jnp.concatenate([wts[k][1] for k in range(reps)], axis=0)
    back_ref[...] = dot(w_neigh, grad_ref[...], 0, 0)
    div = div_ref[0:1, lanes(rep, width)]
    for k in range(reps):
        target = lax.rem(rep + k, reps)
        scaled_out[k][...] = (back_ref[lanes(target, rows), :] / div).astype(BF16)


def weight_body(rep_ref, *refs):
    agg, feats, wts = refs[0:4], refs[4:8], refs[8:12]
    grad_ref = refs[12]
    back_out = refs[13:17]
    slices_ref, back_ref, full, prod_ref = refs[17:21]
    rep = rep_ref[0]
    reps = 4
    rows = agg[0].shape[0]
    for which, pieces in ((0, feats), (1, agg)):
        gather_rows(full, pieces, rep)
        prod_ref[...] = dot(grad_ref[...], full[...], 1, 1)
        for group in range(rows // 4):
            for half in range(2):
                index = which * 32 + group * 2 + half
                for k in range(reps):
                    start = k * rows + group * 4
                    slices_ref[index, 4 * k : 4 * k + 4, :] = prod_ref[
                        start : start + 4, half * TILE : (half + 1) * TILE
                    ].astype(BF16)
    w_self = jnp.concatenate([wts[k][0] for k in range(reps)], axis=0)
    back_ref[...] = dot(w_self, grad_ref[...], 0, 0)
    for k in range(reps):
        target = lax.rem(rep + k, reps)
        back_out[k][...] = back_ref[lanes(target, rows), :]


def slice_sum_body(got_ref, *outs):
    total = jnp.sum(got_ref[...].astype(F32), axis=0)
    for k in range(len(outs)):
        outs[k][...] = total[4 * k : 4 * k + 4, :]


def slice_send_body(*refs):
    parts, out_ref = refs[:4], refs[-1]
    total = parts[0][...] + parts[1][...] + parts[2][...] + parts[3][...]
    high = total.astype(BF16)
    low = (total - high.astype(F32)).astype(BF16)
    both = jnp.concatenate([high.astype(F32), low.astype(F32)], axis=0).astype(BF16)
    out_ref[...] = jnp.broadcast_to(both[None], out_ref.shape)


def gather_lanes(ref, pieces, rep):
    reps = len(pieces)
    width = pieces[0].shape[1]
    for k in range(reps):
        source = lax.rem(rep + reps - k, reps)
        ref[:, lanes(source, width)] = pieces[k][...]


def far_back_body(rep_ref, rows_ref, s0, s1, s2, s3, far_ref, out_ref, full_ref):
    step = pl.program_id(0)
    chans = full_ref.shape[0]

    @pl.when(step == 0)
    def _():
        gather_lanes(full_ref, (s0, s1, s2, s3), rep_ref[0])

    for item in range(STEP):
        for slot in range(2):
            row = rows_ref[step * STEP + item, slot]
            term = dot(full_ref[:, lanes(row, TILE)], far_ref[item, slot], 1, 0)
            out_ref[item, slot * chans : (slot + 1) * chans, :] = term.astype(BF16)


def near_back_body(rep_ref, cols_ref, *refs):
    scaled, back, outs = refs[0:4], refs[4:8], refs[8:12]
    near_ref, acc_ref, output_ref, full_ref = refs[12:16]
    rep = rep_ref[0]
    reps = 4
    width = scaled[0].shape[1]
    gather_lanes(full_ref, scaled, rep)
    gather_lanes(acc_ref, back, rep)
    for k in range(reps):
        output_ref[:, lanes(lax.rem(rep + k, reps), width)] = outs[k][...]
    for row in range(near_ref.shape[0]):
        for link in range(2):
            term = dot(full_ref[:, row * TILE : (row + 1) * TILE], near_ref[row, link], 1, 0)
            acc_ref[:, lanes(cols_ref[row, link], TILE)] += term


def home_body(send_ref, got_ref, near_acc_ref, grad_ref, weight_ref, acc_ref):
    step = pl.program_id(0)
    chans = acc_ref.shape[0]

    @pl.when(step == 0)
    def _():
        acc_ref[...] = near_acc_ref[...]

    for item in range(STEP):
        for slot in range(2):
            block = send_ref[step * STEP + item, slot]
            acc_ref[:, lanes(block, TILE)] += got_ref[item, slot * chans : (slot + 1) * chans, :].astype(F32)
        both = got_ref[item, 2 * chans : 2 * chans + 8, :].astype(F32)
        group, half = item // 2, item % 2
        weight_ref[4 * group : 4 * group + 4, half * TILE : (half + 1) * TILE] = both[0:4] + both[4:8]

    @pl.when(step == pl.num_programs(0) - 1)
    def _():
        grad_ref[...] = acc_ref[...].astype(BF16)


def local(feats, w_self, w_neigh, local_cols, local_tiles, send_list, remote_rows, remote_tiles, cotangent):
    chans, nodes = feats.shape
    full = w_self.shape[0]
    reps = full // chans
    width = nodes // reps
    parts = remote_tiles.shape[1]
    blocks = local_tiles.shape[0]
    steps = parts // STEP
    far_tiles = remote_tiles[0]
    far_rows = remote_rows[0]
    sends = send_list[0]
    rep = lax.axis_index("rep").astype(jnp.int32).reshape(1)
    piece = shape((chans, width), BF16)
    piece32 = shape((chans, width), F32)
    piece_spec = whole((chans, width))
    wide_spec = whole((chans, nodes))
    tile_spec = pl.BlockSpec((STEP, 2, TILE, TILE), lambda i, *_: (i, 0, 0, 0))
    far_flops = 2 * parts * 2 * chans * TILE * TILE
    far_bytes = far_tiles.size * 2

    def shift(value, by):
        return lax.ppermute(value, "rep", [(i, (i + by) % reps) for i in range(reps)])

    def exchange(pieces, sign=1):
        return [pieces[0]] + [shift(pieces[k], (sign * k) % reps) for k in range(1, reps)]

    with jax.named_scope("pick"):
        outgoing = call(
            pick_body, (sends, feats), 1, (steps,), [wide_spec],
            shape((parts, 2 * chans, TILE), BF16), pl.BlockSpec((STEP, 2 * chans, TILE), lambda i, *_: (i, 0, 0)),
            nbytes=3 << 20,
        )
    incoming = lax.all_to_all(outgoing, "dom", split_axis=0, concat_axis=0, tiled=True)

    with jax.named_scope("chunks"):
        pieces = call(
            chunk_body, (rep, feats, cotangent), 1, (1,), [wide_spec, wide_spec],
            [piece] * (2 * reps), [piece_spec] * (2 * reps), nbytes=2 << 20,
        )
    feats_in = exchange(pieces[:reps])
    cot_in = exchange(pieces[reps:])
    weights = jnp.stack([w_self.T, w_neigh.T])
    weights_in = exchange([weights] * reps)
    weight_spec = whole(weights.shape)

    with jax.named_scope("near"):
        near_acc, div = call(
            near_body, (local_cols, far_rows, feats, local_tiles, far_tiles), 2, (steps,),
            [wide_spec, pl.BlockSpec((blocks // steps, 2, TILE, TILE), lambda i, *_: (i, 0, 0, 0)), tile_spec],
            [shape((chans, nodes), F32), shape((8, nodes), F32)], [wide_spec, whole((8, nodes))],
            flops=far_flops, nbytes=far_bytes * 2,
        )
    with jax.named_scope("far"):
        agg = call(
            far_body, (rep, far_rows, incoming, far_tiles, near_acc, div), 2, (steps,),
            [pl.BlockSpec((STEP, 2 * chans, TILE), lambda i, *_: (i, 0, 0)), tile_spec, wide_spec, whole((8, nodes))],
            [piece] * reps, [piece_spec] * reps, [pltpu.VMEM((chans, nodes), F32)],
            flops=far_flops, nbytes=far_bytes * 2,
        )
    agg_in = exchange(agg)

    with jax.named_scope("dense"):
        dense = call(
            dense_body, (rep, *agg_in, *feats_in, *cot_in, *weights_in, div), 1, (1,),
            [piece_spec] * (3 * reps) + [weight_spec] * reps + [whole((8, nodes))],
            [piece] * (2 * reps) + [shape((full, width), BF16)],
            [piece_spec] * (2 * reps) + [whole((full, width))],
            [pltpu.VMEM((full, width), F32), pltpu.VMEM((full, width), BF16), pltpu.VMEM((full, width), BF16)],
            flops=6 * full * full * width, nbytes=3 << 20,
        )
    scaled, out_pieces, grad_pre = dense[:reps], dense[reps : 2 * reps], dense[2 * reps]
    scaled_in = exchange(scaled)

    with jax.named_scope("weights"):
        weight_out = call(
            weight_body, (rep, *agg_in, *feats_in, *weights_in, grad_pre), 1, (1,),
            [piece_spec] * (2 * reps) + [weight_spec] * reps + [whole((full, width))],
            [piece32] * reps + [shape((parts, 4 * reps, TILE), BF16)],
            [piece_spec] * reps + [whole((parts, 4 * reps, TILE))],
            [pltpu.VMEM((full, width), F32), pltpu.VMEM((full, width), BF16), pltpu.VMEM((full, full), F32)],
            flops=6 * full * full * width, nbytes=3 << 20,
        )
    back_self, slices = weight_out[:reps], weight_out[reps]
    slices_in = lax.all_to_all(slices, "dom", split_axis=0, concat_axis=0, tiled=True)
    with jax.named_scope("slice_sum"):
        sums = call(
            slice_sum_body, (slices_in,), 0, (1,), [whole(slices.shape)],
            [shape((4, TILE), F32)] * reps, [whole((4, TILE))] * reps,
        )
    sums_in = exchange(sums, -1)

    with jax.named_scope("far_back"):
        far_back = call(
            far_back_body, (rep, far_rows, *scaled_in, far_tiles), 2, (steps,),
            [piece_spec] * reps + [tile_spec],
            shape((parts, 2 * chans + 8, TILE), BF16),
            pl.BlockSpec((STEP, 2 * chans + 8, TILE), lambda i, *_: (i, 0, 0)),
            [pltpu.VMEM((chans, nodes), BF16)],
            flops=far_flops, nbytes=far_bytes * 2,
        )
    with jax.named_scope("slice_send"):
        sending = call(
            slice_send_body, (*sums_in, far_back), 0, (1,),
            [whole((4, TILE))] * reps + [pl.BlockSpec(memory_space=pl.ANY)],
            shape(far_back.shape, BF16),
            pl.BlockSpec((parts, 8, TILE), lambda i: (0, 2 * chans // 8, 0)),
            aliases={reps: 0},
        )
    returned = lax.all_to_all(sending, "dom", split_axis=0, concat_axis=0, tiled=True)

    back_in = exchange(back_self)
    out_in = exchange(out_pieces, -1)
    with jax.named_scope("near_back"):
        near_back, output = call(
            near_back_body, (rep, local_cols, *scaled_in, *back_in, *out_in, local_tiles), 2, (1,),
            [piece_spec] * (3 * reps) + [whole(local_tiles.shape)],
            [shape((chans, nodes), F32), shape((chans, nodes), BF16)], [wide_spec, wide_spec],
            [pltpu.VMEM((chans, nodes), BF16)],
            flops=far_flops // 2, nbytes=far_bytes,
        )
    with jax.named_scope("home"):
        grad_feats, weight_grads = call(
            home_body, (sends, returned, near_back), 1, (steps,),
            [pl.BlockSpec((STEP, 2 * chans + 8, TILE), lambda i, *_: (i, 0, 0)), wide_spec],
            [shape((chans, nodes), BF16), shape((2 * chans, full), F32)],
            [wide_spec, pl.BlockSpec((2 * STEP, full), lambda i, *_: (i, 0))],
            [pltpu.VMEM((chans, nodes), F32)],
            nbytes=4 << 20,
        )
    return output, grad_feats, weight_grads[:chans].T, weight_grads[chans:].T


def solution(mesh):
    placed = (
        P("rep", "dom"),
        P(None, "rep"),
        P(None, "rep"),
        P("dom", None),
        P("dom", None, None, None),
        P("dom", None, None),
        P("dom", None, None),
        P("dom", None, None, None, None),
        P("rep", "dom"),
    )
    return jax.shard_map(
        local,
        mesh=mesh,
        in_specs=placed,
        out_specs=(P("rep", "dom"), P("rep", "dom"), P(None, "rep"), P(None, "rep")),
        check_vma=False,
    )
```

time: 482 us -> 202 us (0.42)
  waiting for transfers between devices: 362 us -> 83.4 us
  matrix products: 33.7 us -> 0 us
  Pallas kernels: 0 us -> 33 us
  starting transfers between devices: 24.8 us -> 57.8 us
  other arithmetic: 13.2 us -> 0.01 us
  between operations: 14 us -> 0.93 us
  local copies, waits for them, and re-layouts: 32.6 us -> 25.6 us
    psum x1 -> x0, waiting for transfers between devices: 85.2 us -> none  [local(): wg_self, wg_neigh = lax.psum((wg_self, wg_neigh), 'dom')]
    unnamed x5 -> x0, waiting for transfers between devices: 83.8 us -> none
    all_to_all x2 -> x3, waiting for transfers between devices: 131 us -> 61 us  [the longest x1 29.2 us: local(): lax.all_to_all(outgoing, 'dom', split_axis=0, concat_axis=0, tiled=True)]
    all_gather x2 -> x0, waiting for transfers between devices: 62.2 us -> none  [the longest x1 33.2 us: local(): full_feats = lax.all_gather(feats, 'rep', axis=0, tiled=True)]
    dot_general x14 -> x0, matrix products: 33.7 us -> none  [the longest x1 5.89 us: local(): jnp.einsum('fdkj,dkc->fcj', returned, homing, precision=highest)]
    pallas_call x0 -> x11, Pallas kernels: none -> 33 us  [call(): pl.pallas_call(body, grid_spec=pltpu.PrefetchScalarGridSpec(num_scalar_pr...]
    ppermute x0 -> x24, starting transfers between devices: none -> 30.9 us  [shift(): lax.ppermute(value, 'rep', [(i, (i + by) % reps) for i in range(reps)])]
    ppermute x0 -> x24, waiting for transfers between devices: none -> 22.3 us  [shift(): lax.ppermute(value, 'rep', [(i, (i + by) % reps) for i in range(reps)])]
  transfers between devices with their start and end apart: 6 -> 27, of which waited for: 6 -> 9; matrix products, arithmetic and copies ran while one was open for 6% -> 0% of each run, Pallas kernels for 0% -> 11%
where the time goes in v1:
time: 202 us; the launch traced here: 201 us
  waiting for transfers between devices  83.4 us (41%)
  starting transfers between devices  57.8 us (29%)
  Pallas kernels  33 us (16%)
  local copies, waits for them, and re-layouts  25.6 us (13%)
    pallas_call x11, Pallas kernels, call(): pl.pallas_call(body, grid_spec=pltpu.PrefetchScalarGridSpec(num_scalar_pr...  33 us
    ppermute x24, starting transfers between devices, shift(): lax.ppermute(value, 'rep', [(i, (i + by) % reps) for i in range(reps)])  30.9 us
    all_to_all x1, waiting for transfers between devices, local(): lax.all_to_all(outgoing, 'dom', split_axis=0, concat_axis=0, tiled=True)  29.2 us
    unnamed x89, local copies, waits for them, and re-layouts  24.1 us
    all_to_all x1, waiting for transfers between devices, local(): lax.all_to_all(sending, 'dom', split_axis=0, concat_axis=0, tiled=True)  23.7 us
    ppermute x24, waiting for transfers between devices, shift(): lax.ppermute(value, 'rep', [(i, (i + by) % reps) for i in range(reps)])  22.3 us
    all_to_all x1, starting transfers between devices, local(): lax.all_to_all(outgoing, 'dom', split_axis=0, concat_axis=0, tiled=True)  13.6 us
    all_to_all x1, waiting for transfers between devices, local(): lax.all_to_all(slices, 'dom', split_axis=0, concat_axis=0, tiled=True)  8.13 us
  transfers between devices with their start and end apart: 27, of which 9 were waited for; matrix products, arithmetic and copies ran while one was open for 0% of the time, Pallas kernels for 11%

profile of v1, /device:TPU:1, one launch (start us, length us, event | category | flops | bytes accessed | tf_op | source)
XLA Modules:
  0.0 200.7 jit_solution(4749844344448753380)
XLA Ops:
  6.2 13.6 %all-to-all-start = ((bf16[64,128,128]{2,1,0:T(8,128)(2,1)}), bf16[64,128,128]{2,1,0:T(8,128)(2,1)}, u32[]{:S(2)}, u32[]{:S(2)}) async-start(bf16[64,128,128]{2,1,0:T(8,128)(2,1)} %copy-done.5), calls=%async_computation | async-start | bytes 4194304 | tf_op jit(solution)/shard_map/all_to_all | solution.py:288
  21.2 2.5 %collective-permute-start.10 = (bf16[2,64,256]{2,1,0:T(8,128)(2,1)S(1)}, bf16[2,64,256]{2,1,0:T(8,128)(2,1)S(1)}, u32[]{:S(2)}, u32[]{:S(2)}) collective-permute-start(bf16[2,64,256]{2,1,0:T(8,128)(2,1)S(1)} %pad_maximum_fusion.refs_12_.refs_8_), channel_id=1, source_target_pairs={{0,2},{1,3},{2,0},{3,1},{4,6},{5,7},{6,4},{7,5},{8,10},{9,11},{10,... | collective-permute-start | bytes 196616 | tf_op jit(solution)/shard_map/ppermute | solution.py:277
  26.4 2.3 %collective-permute-start.4 = (bf16[64,1024]{1,0:T(8,128)(2,1)}, bf16[64,1024]{1,0:T(8,128)(2,1)S(1)}, u32[]{:S(2)}, u32[]{:S(2)}) collective-permute-start(bf16[64,1024]{1,0:T(8,128)(2,1)} %get-tuple-element.48), channel_id=1, source_target_pairs={{0,2},{1,3},{2,0},{3,1},{4,6},{5,7},{6,4},{7,5},{8,10},{9,11},{10,... | collective-permute-start | bytes 393224 | tf_op jit(solution)/shard_map/ppermute | solution.py:277
  34.2 6.6 %near.1 = (f32[64,4096]{1,0:T(8,128)S(1)}, f32[8,4096]{1,0:T(8,128)S(1)}) custom-call(s32[32,2]{1,0:T(8,128)S(1)} %copy.18.cols_ref, s32[64,2]{1,0:T(8,128)S(1)} %copy.17.rows_ref, bf16[64,4096]{1,0:T(8,128)(2,1)S(1)} %copy-done.7, bf16[32,2,128,128]{3,2,1,0:T(8,128)(2,1)S(1)} %copy-done.3, bf16[64,2,128,128]{3,2,1,0:T(8,128)(2,1)S(1)} %bitcast.14), custom_call_target="tpu_custom_call" | custom-call | flops 268435456 | bytes 8388608 | tf_op jit(solution)/shard_map/near/pallas_call | solution.py:32
  41.9 29.2 %all-to-all-done.got_ref = bf16[64,128,128]{2,1,0:T(8,128)(2,1)} async-done(((bf16[64,128,128]{2,1,0:T(8,128)(2,1)}), bf16[64,128,128]{2,1,0:T(8,128)(2,1)}, u32[]{:S(2)}, u32[]{:S(2)}) %all-to-all-start) | async-done | bytes 2097184 | tf_op jit(solution)/shard_map/all_to_all | solution.py:288
  74.4 7.5 %far.1 = (bf16[64,1024]{1,0:T(8,128)(2,1)S(1)}, bf16[64,1024]{1,0:T(8,128)(2,1)S(1)}, bf16[64,1024]{1,0:T(8,128)(2,1)S(1)}, bf16[64,1024]{1,0:T(8,128)(2,1)S(1)}) custom-call(s32[1]{0:T(128)} %bitcast.rep_ref, s32[64,2]{1,0:T(8,128)S(1)} %copy.17.rows_ref, bf16[64,128,128]{2,1,0:T(8,128)(2,1)} %all-to-all-done.got_ref, ...), custom_call_target="tpu_custom_call" | custom-call | flops 268435456 | bytes 8388608 | tf_op jit(solution)/shard_map/far/pallas_call | solution.py:32
  81.9 2.8 %collective-permute-start.7 = (bf16[64,1024]{1,0:T(8,128)(2,1)S(1)}, bf16[64,1024]{1,0:T(8,128)(2,1)S(1)}, u32[]{:S(2)}, u32[]{:S(2)}) collective-permute-start(bf16[64,1024]{1,0:T(8,128)(2,1)S(1)} %copy-done.39), channel_id=1, source_target_pairs={{0,2},{1,3},{2,0},{3,1},{4,6},{5,7},{6,4},{7,5},{8,10},{9,11},{10,... | collective-permute-start | bytes 393224 | tf_op jit(solution)/shard_map/ppermute | solution.py:277
  91.4 2.5 %collective-permute-done.1.refs_2_ = bf16[64,1024]{1,0:T(8,128)(2,1)S(1)} collective-permute-done((bf16[64,1024]{1,0:T(8,128)(2,1)S(1)}, bf16[64,1024]{1,0:T(8,128)(2,1)S(1)}, u32[]{:S(2)}, u32[]{:S(2)}) %collective-permute-start.1) | collective-permute-done | bytes 131104 | tf_op jit(solution)/shard_map/ppermute | solution.py:277
  93.9 2.9 %collective-permute-done.2.refs_3_ = bf16[64,1024]{1,0:T(8,128)(2,1)S(1)} collective-permute-done((bf16[64,1024]{1,0:T(8,128)(2,1)S(1)}, bf16[64,1024]{1,0:T(8,128)(2,1)S(1)}, u32[]{:S(2)}, u32[]{:S(2)}) %collective-permute-start.2) | collective-permute-done | bytes 131104 | tf_op jit(solution)/shard_map/ppermute | solution.py:277
  96.8 2.4 %dense.1 = (bf16[64,1024]{1,0:T(8,128)(2,1)S(1)}, bf16[64,1024]{1,0:T(8,128)(2,1)S(1)}, bf16[64,1024]{1,0:T(8,128)(2,1)S(1)}, bf16[64,1024]{1,0:T(8,128)(2,1)S(1...) custom-call(s32[1]{0:T(128)} %bitcast.rep_ref, ...), custom_call_target="tpu_custom_call" | custom-call | flops 402653184 | bytes 3145728 | tf_op jit(solution)/shard_map/dense/pallas_call | solution.py:32
  101.1 2.3 %weights.1 = (f32[64,1024]{1,0:T(8,128)S(1)}, f32[64,1024]{1,0:T(8,128)S(1)}, f32[64,1024]{1,0:T(8,128)S(1)}, f32[64,1024]{1,0:T(8,128)S(1)}, bf16[64,16,128]{2,1,0:T(8,128)(2,1)}) custom-call(s32[1]{0:T(128)} %bitcast.rep_ref, bf16[64,1024]{1,0:T(8,128)(2,1)S(1)} %get-tuple-element.42.refs_0_, bf16[64,1024]{1,0:T(8,128)(2,1)S(1)} %collective-permute-done.refs_1_, ...), custom_call_target="tpu_custom_call" | custom-call | flops 402653184 | bytes 3145728 | tf_op jit(solution)/shard_map/weights/pallas_call | solution.py:32
  105.5 6.5 %all-to-all-start.1 = ((bf16[64,16,128]{2,1,0:T(8,128)(2,1)}), bf16[64,16,128]{2,1,0:T(8,128)(2,1)S(1)}, u32[]{:S(2)}, u32[]{:S(2)}) async-start(bf16[64,16,128]{2,1,0:T(8,128)(2,1)} %get-tuple-element.68), calls=%async_computation.1 | async-start | bytes 524288 | tf_op jit(solution)/shard_map/all_to_all | solution.py:339
  113.1 2.5 %collective-permute-start.13 = (bf16[64,1024]{1,0:T(8,128)(2,1)S(1)}, bf16[64,1024]{1,0:T(8,128)(2,1)S(1)}, u32[]{:S(2)}, u32[]{:S(2)}) collective-permute-start(bf16[64,1024]{1,0:T(8,128)(2,1)S(1)} %get-tuple-element.56), channel_id=1, source_target_pairs={{0,2},{1,3},{2,0},{3,1},{4,6},{5,7},{6,4},{7,5},{8,10},{9,11},{10,... | collective-permute-start | bytes 393224 | tf_op jit(solution)/shard_map/ppermute | solution.py:277
  115.9 8.1 %all-to-all-done.1.got_ref = bf16[64,16,128]{2,1,0:T(8,128)(2,1)S(1)} async-done(((bf16[64,16,128]{2,1,0:T(8,128)(2,1)}), bf16[64,16,128]{2,1,0:T(8,128)(2,1)S(1)}, u32[]{:S(2)}, u32[]{:S(2)}) %all-to-all-start.1) | async-done | bytes 262176 | tf_op jit(solution)/shard_map/all_to_all | solution.py:339
  124.1 2.4 %collective-permute-start.21 = (f32[4,128]{1,0:T(4,128)S(1)}, f32[4,128]{1,0:T(4,128)S(1)}, u32[]{:S(2)}, u32[]{:S(2)}) collective-permute-start(f32[4,128]{1,0:T(4,128)S(1)} %get-tuple-element.70), channel_id=1, source_target_pairs={{0,3},{1,0},{2,1},{3,2},{4,7},{5,4},{6,5},{7,6},{8,11},{9,8},{10,9... | collective-permute-start | bytes 6152 | tf_op jit(solution)/shard_map/ppermute | solution.py:277
  127.2 2.3 %copy-done.2 = bf16[1,64,2,128,128]{4,3,2,1,0:T(8,128)(2,1)S(1)} copy-done((bf16[1,64,2,128,128]{4,3,2,1,0:T(8,128)(2,1)S(1)}, bf16[1,64,2,128,128]{4,3,2,1,0:T(8,128)(2,1)}, u32[]{:S(2)}) %copy-start.2) | copy-done | bytes 4194328
  129.5 5.4 %far_back.1.refs_4_ = bf16[64,136,128]{2,1,0:T(8,128)(2,1)} custom-call(s32[1]{0:T(128)} %bitcast.rep_ref, s32[64,2]{1,0:T(8,128)S(1)} %copy.17.rows_ref, bf16[64,1024]{1,0:T(8,128)(2,1)S(1)} %get-tuple-element.54.refs_0_.s0, bf16[64,1024]{1,0:T(8,128)(2,1)S(1)} %collective-permute-done.12.refs_1_.s1, ...), custom_call_target="tpu_custom_call" | custom-call | flops 268435456 | bytes 8388608 | tf_op jit(solution)/shard_map/far_back/pallas_call | solution.py:32
  135.6 6.7 %all-to-all-start.2 = ((bf16[64,136,128]{2,1,0:T(8,128)(2,1)}), bf16[64,136,128]{2,1,0:T(8,128)(2,1)S(1)}, u32[]{:S(2)}, u32[]{:S(2)}) async-start(bf16[64,136,128]{2,1,0:T(8,128)(2,1)} %slice_send.1), calls=%async_computation.2 | async-start | bytes 4456448 | tf_op jit(solution)/shard_map/all_to_all | solution.py:364
  142.4 2.9 %collective-permute-start.18 = (bf16[64,1024]{1,0:T(8,128)(2,1)}, bf16[64,1024]{1,0:T(8,128)(2,1)S(1)}, u32[]{:S(2)}, u32[]{:S(2)}) collective-permute-start(bf16[64,1024]{1,0:T(8,128)(2,1)} %copy-done.35), channel_id=1, source_target_pairs={{0,3},{1,0},{2,1},{3,2},{4,7},{5,4},{6,5},{7,6},{8,11},{9,8},{10,9... | collective-permute-start | bytes 393224 | tf_op jit(solution)/shard_map/ppermute | solution.py:277
  150.3 10.6 %collective-permute-done.19.refs_10_ = bf16[64,1024]{1,0:T(8,128)(2,1)S(1)} collective-permute-done((bf16[64,1024]{1,0:T(8,128)(2,1)S(1)}, bf16[64,1024]{1,0:T(8,128)(2,1)S(1)}, u32[]{:S(2)}, u32[]{:S(2)}) %collective-permute-start.19) | collective-permute-done | bytes 131104 | tf_op jit(solution)/shard_map/ppermute | solution.py:277
  160.9 3.8 %collective-permute-done.20.refs_11_ = bf16[64,1024]{1,0:T(8,128)(2,1)S(1)} collective-permute-done((bf16[64,1024]{1,0:T(8,128)(2,1)S(1)}, bf16[64,1024]{1,0:T(8,128)(2,1)S(1)}, u32[]{:S(2)}, u32[]{:S(2)}) %collective-permute-start.20) | collective-permute-done | bytes 131104 | tf_op jit(solution)/shard_map/ppermute | solution.py:277
  170.1 2.4 %near_back.1 = (f32[64,4096]{1,0:T(8,128)S(1)}, bf16[64,4096]{1,0:T(8,128)(2,1)}) custom-call(s32[1]{0:T(128)} %bitcast.rep_ref, s32[32,2]{1,0:T(8,128)S(1)} %copy.18.cols_ref, bf16[64,1024]{1,0:T(8,128)(2,1)S(1)} %get-tuple-element.54.refs_0_.s0, bf16[64,1024]{1,0:T(8,128)(2,1)S(1)} %collective-permute-done.12.refs_1_.s1, bf16[64,1024]{1,0:T(8,128)(2,1)S(1)} %copy-done.11, ...), custom_call_target="tpu_custom_call" | custom-call | flops 134217728 | bytes 4194304 | tf_op jit(solution)/shard_map/near_back/pallas_call | solution.py:32
  172.5 23.7 %all-to-all-done.2.got_ref = bf16[64,136,128]{2,1,0:T(8,128)(2,1)S(1)} async-done(((bf16[64,136,128]{2,1,0:T(8,128)(2,1)}), bf16[64,136,128]{2,1,0:T(8,128)(2,1)S(1)}, u32[]{:S(2)}, u32[]{:S(2)}) %all-to-all-start.2) | async-done | bytes 2228256 | tf_op jit(solution)/shard_map/all_to_all | solution.py:364
  197.0 3.1 %home.1 = (bf16[64,4096]{1,0:T(8,128)(2,1)}, f32[128,256]{1,0:T(8,128)S(1)}) custom-call(s32[64,2]{1,0:T(8,128)S(1)} %copy-done.16, bf16[64,136,128]{2,1,0:T(8,128)(2,1)S(1)} %all-to-all-done.2.got_ref, f32[64,4096]{1,0:T(8,128)S(1)} %get-tuple-element.73.near_acc_ref), custom_call_target="tpu_custom_call" | custom-call | bytes 4194304 | tf_op jit(solution)/shard_map/home/pallas_call | solution.py:32
  (134 shorter events, 44.8 us)
Async XLA Ops:
  6.2 64.8 %all-to-all-start = ((bf16[64,128,128]{2,1,0:T(8,128)(2,1)}), bf16[64,128,128]{2,1,0:T(8,128)(2,1)}, u32[]{:S(2)}, u32[]{:S(2)}) async-start(bf16[64,128,128]{2,1,0:T(8,128)(2,1)} %copy-done.5), calls=%async_computation | async-start | bytes 4194304 | tf_op jit(solution)/shard_map/all_to_all | solution.py:288
  19.9 9.2 %collective-permute-start.9 = (bf16[2,64,256]{2,1,0:T(8,128)(2,1)S(1)}, bf16[2,64,256]{2,1,0:T(8,128)(2,1)S(1)}, u32[]{:S(2)}, u32[]{:S(2)}) collective-permute-start(bf16[2,64,256]{2,1,0:T(8,128)(2,1)S(1)} %pad_maximum_fusion.refs_12_.refs_8_), channel_id=1, source_target_pairs={{0,1},{1,2},{2,3},{3,0},{4,5},{5,6},{6,7},{7,4},{8,9},{9,10},{10,1... | collective-permute-start | bytes 196616 | tf_op jit(solution)/shard_map/ppermute | solution.py:277
  21.2 9.1 %collective-permute-start.10 = (bf16[2,64,256]{2,1,0:T(8,128)(2,1)S(1)}, bf16[2,64,256]{2,1,0:T(8,128)(2,1)S(1)}, u32[]{:S(2)}, u32[]{:S(2)}) collective-permute-start(bf16[2,64,256]{2,1,0:T(8,128)(2,1)S(1)} %pad_maximum_fusion.refs_12_.refs_8_), channel_id=1, source_target_pairs={{0,2},{1,3},{2,0},{3,1},{4,6},{5,7},{6,4},{7,5},{8,10},{9,11},{10,... | collective-permute-start | bytes 196616 | tf_op jit(solution)/shard_map/ppermute | solution.py:277
  26.4 58.3 %collective-permute-start.3 = (bf16[64,1024]{1,0:T(8,128)(2,1)}, bf16[64,1024]{1,0:T(8,128)(2,1)S(1)}, u32[]{:S(2)}, u32[]{:S(2)}) collective-permute-start(bf16[64,1024]{1,0:T(8,128)(2,1)} %get-tuple-element.47), channel_id=1, source_target_pairs={{0,1},{1,2},{2,3},{3,0},{4,5},{5,6},{6,7},{7,4},{8,9},{9,10},{10,1... | collective-permute-start | bytes 393224 | tf_op jit(solution)/shard_map/ppermute | solution.py:277
  26.4 59.2 %collective-permute-start.4 = (bf16[64,1024]{1,0:T(8,128)(2,1)}, bf16[64,1024]{1,0:T(8,128)(2,1)S(1)}, u32[]{:S(2)}, u32[]{:S(2)}) collective-permute-start(bf16[64,1024]{1,0:T(8,128)(2,1)} %get-tuple-element.48), channel_id=1, source_target_pairs={{0,2},{1,3},{2,0},{3,1},{4,6},{5,7},{6,4},{7,5},{8,10},{9,11},{10,... | collective-permute-start | bytes 393224 | tf_op jit(solution)/shard_map/ppermute | solution.py:277
  28.8 57.5 %collective-permute-start.5 = (bf16[64,1024]{1,0:T(8,128)(2,1)}, bf16[64,1024]{1,0:T(8,128)(2,1)S(1)}, u32[]{:S(2)}, u32[]{:S(2)}) collective-permute-start(bf16[64,1024]{1,0:T(8,128)(2,1)} %get-tuple-element.49), channel_id=1, source_target_pairs={{0,3},{1,0},{2,1},{3,2},{4,7},{5,4},{6,5},{7,6},{8,11},{9,8},{10,9... | collective-permute-start | bytes 393224 | tf_op jit(solution)/shard_map/ppermute | solution.py:277
  29.1 57.9 %collective-permute-start.6 = (bf16[64,1024]{1,0:T(8,128)(2,1)}, bf16[64,1024]{1,0:T(8,128)(2,1)}, u32[]{:S(2)}, u32[]{:S(2)}) collective-permute-start(bf16[64,1024]{1,0:T(8,128)(2,1)} %get-tuple-element.51), channel_id=1, source_target_pairs={{0,1},{1,2},{2,3},{3,0},{4,5},{5,6},{6,7},{7,4},{8,9},{9,10},{10,1... | collective-permute-start | bytes 393224 | tf_op jit(solution)/shard_map/ppermute | solution.py:277
  30.2 51.7 %collective-permute-start.11 = (bf16[2,64,256]{2,1,0:T(8,128)(2,1)S(1)}, bf16[2,64,256]{2,1,0:T(8,128)(2,1)}, u32[]{:S(2)}, u32[]{:S(2)}) collective-permute-start(bf16[2,64,256]{2,1,0:T(8,128)(2,1)S(1)} %pad_maximum_fusion.refs_12_.refs_8_), channel_id=1, source_target_pairs={{0,3},{1,0},{2,1},{3,2},{4,7},{5,4},{6,5},{7,6},{8,11},{9,8},{10,9... | collective-permute-start | bytes 196616 | tf_op jit(solution)/shard_map/ppermute | solution.py:277
  86.2 7.6 %collective-permute-start.1 = (bf16[64,1024]{1,0:T(8,128)(2,1)S(1)}, bf16[64,1024]{1,0:T(8,128)(2,1)S(1)}, u32[]{:S(2)}, u32[]{:S(2)}) collective-permute-start(bf16[64,1024]{1,0:T(8,128)(2,1)S(1)} %get-tuple-element.44), channel_id=1, source_target_pairs={{0,2},{1,3},{2,0},{3,1},{4,6},{5,7},{6,4},{7,5},{8,10},{9,11},{10,... | collective-permute-start | bytes 393224 | tf_op jit(solution)/shard_map/ppermute | solution.py:277
  87.0 9.8 %collective-permute-start.2 = (bf16[64,1024]{1,0:T(8,128)(2,1)S(1)}, bf16[64,1024]{1,0:T(8,128)(2,1)S(1)}, u32[]{:S(2)}, u32[]{:S(2)}) collective-permute-start(bf16[64,1024]{1,0:T(8,128)(2,1)S(1)} %get-tuple-element.45), channel_id=1, source_target_pairs={{0,3},{1,0},{2,1},{3,2},{4,7},{5,4},{6,5},{7,6},{8,11},{9,8},{10,9... | collective-permute-start | bytes 393224 | tf_op jit(solution)/shard_map/ppermute | solution.py:277
  105.5 18.5 %all-to-all-start.1 = ((bf16[64,16,128]{2,1,0:T(8,128)(2,1)}), bf16[64,16,128]{2,1,0:T(8,128)(2,1)S(1)}, u32[]{:S(2)}, u32[]{:S(2)}) async-start(bf16[64,16,128]{2,1,0:T(8,128)(2,1)} %get-tuple-element.68), calls=%async_computation.1 | async-start | bytes 524288 | tf_op jit(solution)/shard_map/all_to_all | solution.py:339
  112.0 15.0 %collective-permute-start.12 = (bf16[64,1024]{1,0:T(8,128)(2,1)S(1)}, bf16[64,1024]{1,0:T(8,128)(2,1)S(1)}, u32[]{:S(2)}, u32[]{:S(2)}) collective-permute-start(bf16[64,1024]{1,0:T(8,128)(2,1)S(1)} %get-tuple-element.55), channel_id=1, source_target_pairs={{0,1},{1,2},{2,3},{3,0},{4,5},{5,6},{6,7},{7,4},{8,9},{9,10},{10,1... | collective-permute-start | bytes 393224 | tf_op jit(solution)/shard_map/ppermute | solution.py:277
  113.1 14.0 %collective-permute-start.13 = (bf16[64,1024]{1,0:T(8,128)(2,1)S(1)}, bf16[64,1024]{1,0:T(8,128)(2,1)S(1)}, u32[]{:S(2)}, u32[]{:S(2)}) collective-permute-start(bf16[64,1024]{1,0:T(8,128)(2,1)S(1)} %get-tuple-element.56), channel_id=1, source_target_pairs={{0,2},{1,3},{2,0},{3,1},{4,6},{5,7},{6,4},{7,5},{8,10},{9,11},{10,... | collective-permute-start | bytes 393224 | tf_op jit(solution)/shard_map/ppermute | solution.py:277
  115.6 11.6 %collective-permute-start.14 = (bf16[64,1024]{1,0:T(8,128)(2,1)S(1)}, bf16[64,1024]{1,0:T(8,128)(2,1)S(1)}, u32[]{:S(2)}, u32[]{:S(2)}) collective-permute-start(bf16[64,1024]{1,0:T(8,128)(2,1)S(1)} %get-tuple-element.57), channel_id=1, source_target_pairs={{0,3},{1,0},{2,1},{3,2},{4,7},{5,4},{6,5},{7,6},{8,11},{9,8},{10,9... | collective-permute-start | bytes 393224 | tf_op jit(solution)/shard_map/ppermute | solution.py:277
  124.1 10.8 %collective-permute-start.21 = (f32[4,128]{1,0:T(4,128)S(1)}, f32[4,128]{1,0:T(4,128)S(1)}, u32[]{:S(2)}, u32[]{:S(2)}) collective-permute-start(f32[4,128]{1,0:T(4,128)S(1)} %get-tuple-element.70), channel_id=1, source_target_pairs={{0,3},{1,0},{2,1},{3,2},{4,7},{5,4},{6,5},{7,6},{8,11},{9,8},{10,9... | collective-permute-start | bytes 6152 | tf_op jit(solution)/shard_map/ppermute | solution.py:277
  126.5 8.4 %collective-permute-start.22 = (f32[4,128]{1,0:T(4,128)S(1)}, f32[4,128]{1,0:T(4,128)S(1)}, u32[]{:S(2)}, u32[]{:S(2)}) collective-permute-start(f32[4,128]{1,0:T(4,128)S(1)} %get-tuple-element.71), channel_id=1, source_target_pairs={{0,2},{1,3},{2,0},{3,1},{4,6},{5,7},{6,4},{7,5},{8,10},{9,11},{10,... | collective-permute-start | bytes 6152 | tf_op jit(solution)/shard_map/ppermute | solution.py:277
  127.0 7.9 %collective-permute-start.23 = (f32[4,128]{1,0:T(4,128)S(1)}, f32[4,128]{1,0:T(4,128)S(1)}, u32[]{:S(2)}, u32[]{:S(2)}) collective-permute-start(f32[4,128]{1,0:T(4,128)S(1)} %get-tuple-element.72), channel_id=1, source_target_pairs={{0,1},{1,2},{2,3},{3,0},{4,5},{5,6},{6,7},{7,4},{8,9},{9,10},{10,1... | collective-permute-start | bytes 6152 | tf_op jit(solution)/shard_map/ppermute | solution.py:277
  135.6 60.6 %all-to-all-start.2 = ((bf16[64,136,128]{2,1,0:T(8,128)(2,1)}), bf16[64,136,128]{2,1,0:T(8,128)(2,1)S(1)}, u32[]{:S(2)}, u32[]{:S(2)}) async-start(bf16[64,136,128]{2,1,0:T(8,128)(2,1)} %slice_send.1), calls=%async_computation.2 | async-start | bytes 4456448 | tf_op jit(solution)/shard_map/all_to_all | solution.py:364
  142.4 7.9 %collective-permute-start.18 = (bf16[64,1024]{1,0:T(8,128)(2,1)}, bf16[64,1024]{1,0:T(8,128)(2,1)S(1)}, u32[]{:S(2)}, u32[]{:S(2)}) collective-permute-start(bf16[64,1024]{1,0:T(8,128)(2,1)} %copy-done.35), channel_id=1, source_target_pairs={{0,3},{1,0},{2,1},{3,2},{4,7},{5,4},{6,5},{7,6},{8,11},{9,8},{10,9... | collective-permute-start | bytes 393224 | tf_op jit(solution)/shard_map/ppermute | solution.py:277
  145.2 19.6 %collective-permute-start.15 = (f32[64,1024]{1,0:T(8,128)S(1)}, f32[64,1024]{1,0:T(8,128)S(1)}, u32[]{:S(2)}, u32[]{:S(2)}) collective-permute-start(f32[64,1024]{1,0:T(8,128)S(1)} %copy-done.30), channel_id=1, source_target_pairs={{0,1},{1,2},{2,3},{3,0},{4,5},{5,6},{6,7},{7,4},{8,9},{9,10},{10,1... | collective-permute-start | bytes 786440 | tf_op jit(solution)/shard_map/ppermute | solution.py:277
  145.2 19.5 %collective-permute-start.16 = (f32[64,1024]{1,0:T(8,128)S(1)}, f32[64,1024]{1,0:T(8,128)S(1)}, u32[]{:S(2)}, u32[]{:S(2)}) collective-permute-start(f32[64,1024]{1,0:T(8,128)S(1)} %copy-done.28), channel_id=1, source_target_pairs={{0,2},{1,3},{2,0},{3,1},{4,6},{5,7},{6,4},{7,5},{8,10},{9,11},{10,... | collective-permute-start | bytes 786440 | tf_op jit(solution)/shard_map/ppermute | solution.py:277
  146.6 18.2 %collective-permute-start.17 = (f32[64,1024]{1,0:T(8,128)S(1)}, f32[64,1024]{1,0:T(8,128)S(1)}, u32[]{:S(2)}, u32[]{:S(2)}) collective-permute-start(f32[64,1024]{1,0:T(8,128)S(1)} %get-tuple-element.62), channel_id=1, source_target_pairs={{0,3},{1,0},{2,1},{3,2},{4,7},{5,4},{6,5},{7,6},{8,11},{9,8},{10,9... | collective-permute-start | bytes 786440 | tf_op jit(solution)/shard_map/ppermute | solution.py:277
  148.6 12.4 %collective-permute-start.19 = (bf16[64,1024]{1,0:T(8,128)(2,1)S(1)}, bf16[64,1024]{1,0:T(8,128)(2,1)S(1)}, u32[]{:S(2)}, u32[]{:S(2)}) collective-permute-start(bf16[64,1024]{1,0:T(8,128)(2,1)S(1)} %copy-done.34), channel_id=1, source_target_pairs={{0,2},{1,3},{2,0},{3,1},{4,6},{5,7},{6,4},{7,5},{8,10},{9,11},{10,... | collective-permute-start | bytes 393224 | tf_op jit(solution)/shard_map/ppermute | solution.py:277
  150.3 14.5 %collective-permute-start.20 = (bf16[64,1024]{1,0:T(8,128)(2,1)S(1)}, bf16[64,1024]{1,0:T(8,128)(2,1)S(1)}, u32[]{:S(2)}, u32[]{:S(2)}) collective-permute-start(bf16[64,1024]{1,0:T(8,128)(2,1)S(1)} %copy-done.32), channel_id=1, source_target_pairs={{0,1},{1,2},{2,3},{3,0},{4,5},{5,6},{6,7},{7,4},{8,9},{9,10},{10,1... | collective-permute-start | bytes 393224 | tf_op jit(solution)/shard_map/ppermute | solution.py:277
  (47 other events, 354.1 us)

commit v2 on v1

v2 whole, which is shorter than its diff:
```python
import jax
import jax.numpy as jnp
from jax import lax
from jax.experimental import pallas as pl
from jax.experimental.pallas import tpu as pltpu
from jax.sharding import PartitionSpec as P

TILE = 128
STEP = 8
VMEM_BYTES = 12 * 1024 * 1024
F32 = jnp.float32
BF16 = jnp.bfloat16
IN_VMEM = pl.BlockSpec(memory_space=pltpu.VMEM)
IN_SMEM = pl.BlockSpec(memory_space=pltpu.SMEM)
IN_HBM = pl.BlockSpec(memory_space=pltpu.HBM)


def lanes(index, width):
    return pl.ds(pl.multiple_of(index * width, width), width)


def call(body, scalars, args, out_shape, scratch=(), micros=1.0, hbm=(), hbm_out=()):
    many = isinstance(out_shape, list)
    out_specs = [IN_HBM if i in hbm_out else IN_VMEM for i in range(len(out_shape) if many else 1)]
    out_specs = out_specs if many else out_specs[0]
    args = [pinned(arg) if i in hbm else arg for i, arg in enumerate(args)]
    return pl.pallas_call(
        body,
        in_specs=[IN_SMEM] * len(scalars) + [IN_HBM if i in hbm else IN_VMEM for i in range(len(args))],
        out_shape=out_shape,
        out_specs=out_specs,
        scratch_shapes=scratch,
        compiler_params=pltpu.CompilerParams(vmem_limit_bytes=VMEM_BYTES),
        cost_estimate=pl.CostEstimate(flops=int(micros * 1.1e9), bytes_accessed=1 << 16, transcendentals=0),
    )(*scalars, *args)


def shape(dims, kind):
    return jax.ShapeDtypeStruct(dims, kind)


def in_hbm(dims, kind):
    return pltpu.HBM(dims, kind)


def pinned(value):
    return pltpu.with_memory_space_constraint(value, pltpu.HBM)


def dot(left, right, left_dim, right_dim):
    return lax.dot_general(left, right, (((left_dim,), (right_dim,)), ((), ())), preferred_element_type=F32)


def pick_body(send_ref, feats_hbm, out_ref, feats_ref, buf_ref, sems, feats_sem):
    chans = feats_ref.shape[0]
    load = pltpu.make_async_copy(feats_hbm, feats_ref, feats_sem)
    load.start()
    load.wait()
    parts = buf_ref.shape[0]
    for step in range(parts // STEP):
        for item in range(step * STEP, (step + 1) * STEP):
            for slot in range(2):
                block = send_ref[slot, item]
                buf_ref[item, slot * chans : (slot + 1) * chans, :] = feats_ref[:, lanes(block, TILE)]
        rows = pl.ds(step * STEP, STEP)
        pltpu.make_async_copy(buf_ref.at[rows], out_ref.at[rows], sems.at[step]).start()
    for step in range(parts // STEP):
        rows = pl.ds(step * STEP, STEP)
        pltpu.make_async_copy(buf_ref.at[rows], out_ref.at[rows], sems.at[step]).wait()


def tile_copy(far_hbm, far_ref, sems, step):
    rows = pl.ds(step * STEP, STEP)
    return pltpu.make_async_copy(far_hbm.at[rows], far_ref.at[rows], sems.at[step])


def chunk_body(rep_ref, feats_ref, cot_ref, *outs):
    reps = len(outs) // 2
    width = outs[0].shape[1]
    for k in range(reps):
        chunk = lax.rem(rep_ref[0] + k, reps)
        outs[k][...] = feats_ref[:, lanes(chunk, width)]
        outs[reps + k][...] = cot_ref[:, lanes(chunk, width)]


def near_body(cols_ref, rows_ref, feats_ref, near_ref, far_ref, acc_ref, div_ref):
    ones = jnp.ones((8, TILE), BF16)
    div_ref[...] = jnp.ones_like(div_ref)

    @pl.loop(0, near_ref.shape[0] // 4)
    def _(step):
        for item in range(4):
            row = step * 4 + item
            total = None
            sums = None
            for link in range(2):
                tile = near_ref[row, link]
                term = dot(feats_ref[:, lanes(cols_ref[link, row], TILE)], tile, 1, 1)
                part = dot(ones, tile, 1, 1)
                total = term if total is None else total + term
                sums = part if sums is None else sums + part
            acc_ref[:, lanes(row, TILE)] = total
            div_ref[:, lanes(row, TILE)] += sums

    @pl.loop(0, far_ref.shape[0] // STEP)
    def _(step):
        for item in range(STEP):
            for slot in range(2):
                part = step * STEP + item
                row = rows_ref[slot, part]
                div_ref[:, lanes(row, TILE)] += dot(ones, far_ref[part, slot], 1, 1)


def far_body(rep_ref, rows_ref, got_ref, far_hbm, near_acc_hbm, div_hbm, *rest):
    outs = rest[:4]
    acc_ref, far_ref, div_ref, sems, acc_sem, div_sem = rest[4:]
    reps = len(outs)
    chans = acc_ref.shape[0]
    width = outs[0].shape[1]
    load_acc = pltpu.make_async_copy(near_acc_hbm, acc_ref, acc_sem)
    load_div = pltpu.make_async_copy(div_hbm, div_ref, div_sem)
    load_acc.start()
    for step in range(far_ref.shape[0] // STEP):
        tile_copy(far_hbm, far_ref, sems, step).start()
    load_div.start()
    load_acc.wait()

    @pl.loop(0, far_ref.shape[0] // STEP)
    def _(step):
        tile_copy(far_hbm, far_ref, sems, step).wait()
        for item in range(STEP):
            for slot in range(2):
                part = step * STEP + item
                row = rows_ref[slot, part]
                block = got_ref[part, slot * chans : (slot + 1) * chans, :]
                acc_ref[:, lanes(row, TILE)] += dot(block, far_ref[part, slot], 1, 1)

    load_div.wait()
    for k in range(reps):
        where = lanes(lax.rem(rep_ref[0] + k, reps), width)
        outs[k][...] = (acc_ref[:, where] / div_ref[0:1, where]).astype(BF16)


def gather_rows(ref, pieces, rep):
    reps = len(pieces)
    rows = pieces[0].shape[0]
    for k in range(reps):
        source = lax.rem(rep + reps - k, reps)
        ref[lanes(source, rows), :] = pieces[k][...]


def dense_body(rep_ref, *refs):
    agg, feats, cot, wts = refs[0:4], refs[4:8], refs[8:12], refs[12:16]
    div_ref = refs[16]
    scaled_out, out_out, grad_hbm, slices_hbm = refs[17:21], refs[21:25], refs[25], refs[26]
    back_ref, full_feats, full_agg, grad_ref, out_buf, prod_ref, slices_ref = refs[27:34]
    out_sems, grad_sem, slices_sem = refs[34:37]
    rep = rep_ref[0]
    reps = 4
    rows, width = agg[0].shape
    gather_rows(full_feats, feats, rep)
    gather_rows(full_agg, agg, rep)
    copies = []

    def leave(source, target, sem):
        copies.append(pltpu.make_async_copy(source, target, sem))
        copies[-1].start()

    for k in range(reps):
        preact = dot(wts[k][0], full_feats[...], 1, 0) + dot(wts[k][1], full_agg[...], 1, 0)
        gate = jax.nn.sigmoid(preact)
        slope = gate * (1.0 + preact * (1.0 - gate))
        grad_ref[k * rows : (k + 1) * rows, :] = (cot[k][...].astype(F32) * slope).astype(BF16)
        out_buf[k] = (preact * gate).astype(BF16)
        leave(out_buf.at[k], out_out[k], out_sems.at[k])
    leave(grad_ref, grad_hbm, grad_sem)
    for which, full in ((0, full_feats), (1, full_agg)):
        prod_ref[...] = dot(grad_ref[...], full[...], 1, 1)
        for group in range(rows // 4):
            for half in range(2):
                index = which * 32 + group * 2 + half
                for k in range(reps):
                    start = k * rows + group * 4
                    slices_ref[index, 4 * k : 4 * k + 4, :] = prod_ref[
                        start : start + 4, half * TILE : (half + 1) * TILE
                    ].astype(BF16)
    leave(slices_ref, slices_hbm, slices_sem)
    w_neigh = jnp.concatenate([wts[k][1] for k in range(reps)], axis=0)
    back_ref[...] = dot(w_neigh, grad_ref[...], 0, 0)
    div = div_ref[0:1, lanes(rep, width)]
    for k in range(reps):
        target = lax.rem(rep + k, reps)
        scaled_out[k][...] = (back_ref[lanes(target, rows), :] / div).astype(BF16)
    for copy in copies:
        copy.wait()


def back_body(rep_ref, *refs):
    wts, grad_ref, back_out, back_ref = refs[0:4], refs[4], refs[5:9], refs[9]
    rep = rep_ref[0]
    reps = 4
    rows = back_out[0].shape[0]
    w_self = jnp.concatenate([wts[k][0] for k in range(reps)], axis=0)
    back_ref[...] = dot(w_self, grad_ref[...], 0, 0)
    for k in range(reps):
        target = lax.rem(rep + k, reps)
        back_out[k][...] = back_ref[lanes(target, rows), :]


def slice_sum_body(got_ref, *outs):
    total = jnp.sum(got_ref[...].astype(F32), axis=0)
    for k in range(len(outs)):
        outs[k][...] = total[4 * k : 4 * k + 4, :]


def slice_send_body(*refs):
    parts, out_ref = refs[:4], refs[-1]
    total = parts[0][...] + parts[1][...] + parts[2][...] + parts[3][...]
    high = total.astype(BF16)
    low = (total - high.astype(F32)).astype(BF16)
    both = jnp.concatenate([high.astype(F32), low.astype(F32)], axis=0).astype(BF16)
    out_ref[...] = jnp.broadcast_to(both[None], out_ref.shape)


def gather_lanes(ref, pieces, rep):
    reps = len(pieces)
    width = pieces[0].shape[1]
    for k in range(reps):
        source = lax.rem(rep + reps - k, reps)
        ref[:, lanes(source, width)] = pieces[k][...]


def far_back_body(rep_ref, rows_ref, s0, s1, s2, s3, far_hbm, out_ref, full_ref, buf_ref, far_ref, sems, out_sems):
    chans = full_ref.shape[0]
    parts = far_ref.shape[0]
    for step in range(parts // STEP):
        tile_copy(far_hbm, far_ref, sems, step).start()
    gather_lanes(full_ref, (s0, s1, s2, s3), rep_ref[0])

    def copy(step):
        rows = pl.ds(step * STEP, STEP)
        return pltpu.make_async_copy(
            buf_ref.at[rows], out_ref.at[rows, pl.ds(0, 2 * chans)], out_sems.at[step]
        )

    @pl.loop(0, parts // STEP)
    def _(step):
        tile_copy(far_hbm, far_ref, sems, step).wait()
        for item in range(STEP):
            for slot in range(2):
                part = step * STEP + item
                row = rows_ref[slot, part]
                term = dot(full_ref[:, lanes(row, TILE)], far_ref[part, slot], 1, 0)
                buf_ref[part, slot * chans : (slot + 1) * chans, :] = term.astype(BF16)
        copy(step).start()

    for step in range(parts // STEP):
        copy(step).wait()


def near_back_body(rep_ref, cols_ref, *refs):
    scaled, back, outs = refs[0:4], refs[4:8], refs[8:12]
    near_ref, acc_ref, output_ref, full_ref = refs[12:16]
    rep = rep_ref[0]
    reps = 4
    width = scaled[0].shape[1]
    gather_lanes(full_ref, scaled, rep)
    gather_lanes(acc_ref, back, rep)
    for k in range(reps):
        output_ref[:, lanes(lax.rem(rep + k, reps), width)] = outs[k][...]

    @pl.loop(0, near_ref.shape[0] // 4)
    def _(step):
        for item in range(4):
            row = step * 4 + item
            for link in range(2):
                term = dot(full_ref[:, lanes(row, TILE)], near_ref[row, link], 1, 0)
                acc_ref[:, lanes(cols_ref[link, row], TILE)] += term


def home_body(send_ref, got_ref, near_acc_hbm, grad_ref, w_self_ref, w_neigh_ref, acc_ref, near_acc_ref, sem):
    chans = acc_ref.shape[0]
    parts = got_ref.shape[0]
    load = pltpu.make_async_copy(near_acc_hbm, near_acc_ref, sem)
    load.start()
    acc_ref[...] = jnp.zeros_like(acc_ref)
    for item in range(parts):
        for slot in range(2):
            block = send_ref[slot, item]
            acc_ref[:, lanes(block, TILE)] += got_ref[item, slot * chans : (slot + 1) * chans, :].astype(F32)
        both = got_ref[item, 2 * chans : 2 * chans + 8, :].astype(F32)
        weight_ref = (w_self_ref, w_neigh_ref)[item // (parts // 2)]
        group, half = item % (parts // 2) // 2, item % 2
        weight_ref[4 * group : 4 * group + 4, half * TILE : (half + 1) * TILE] = both[0:4] + both[4:8]
    load.wait()
    grad_ref[...] = (near_acc_ref[...] + acc_ref[...]).astype(BF16)


def local(feats, w_self, w_neigh, local_cols, local_tiles, send_list, remote_rows, remote_tiles, cotangent):
    chans, nodes = feats.shape
    full = w_self.shape[0]
    reps = full // chans
    width = nodes // reps
    parts = remote_tiles.shape[1]
    far_tiles = remote_tiles[0]
    rows = remote_rows[0].T
    sends = send_list[0].T
    cols = local_cols.T
    rep = lax.axis_index("rep").astype(jnp.int32).reshape(1)
    piece = shape((chans, width), BF16)
    piece32 = shape((chans, width), F32)
    sems = pltpu.SemaphoreType.DMA((parts // STEP,))
    sem = pltpu.SemaphoreType.DMA(())
    tile_buf = pltpu.VMEM(far_tiles.shape, BF16)
    wide32 = pltpu.VMEM((chans, nodes), F32)

    def shift(value, by):
        return lax.ppermute(value, "rep", [(i, (i + by) % reps) for i in range(reps)])

    def exchange(pieces, sign=1):
        return [pieces[0]] + [shift(pieces[k], (sign * k) % reps) for k in range(1, reps)]

    with jax.named_scope("pick"):
        outgoing = call(
            pick_body, (sends,), (feats,), in_hbm((parts, 2 * chans, TILE), BF16),
            [pltpu.VMEM((chans, nodes), BF16), pltpu.VMEM((parts, 2 * chans, TILE), BF16), sems, sem], 2.0, (0,), (0,),
        )
    incoming = lax.all_to_all(outgoing, "dom", split_axis=0, concat_axis=0, tiled=True)

    with jax.named_scope("chunks"):
        pieces = call(chunk_body, (rep,), (feats, cotangent), [piece] * (2 * reps))
    feats_in = exchange(pieces[:reps])
    cot_in = exchange(pieces[reps:])
    weights_in = exchange([jnp.stack([w_self.T, w_neigh.T])] * reps)
    with jax.named_scope("near"):
        near_acc, div = call(
            near_body, (cols, rows), (feats, local_tiles, far_tiles),
            [shape((chans, nodes), F32), shape((8, nodes), F32)], (), 6.0,
        )
    incoming, feats_in, cot_in, weights_in, near_acc, div = lax.optimization_barrier(
        (incoming, feats_in, cot_in, weights_in, near_acc, div)
    )
    with jax.named_scope("far"):
        agg = call(
            far_body, (rep, rows), (incoming, far_tiles, near_acc, div), [piece] * reps,
            [wide32, tile_buf, pltpu.VMEM((8, nodes), F32), sems, sem, sem], 6.0, (1, 2, 3),
        )
    agg_in = exchange(agg)

    with jax.named_scope("dense"):
        dense = call(
            dense_body, (rep,), (*agg_in, *feats_in, *cot_in, *weights_in, div),
            [piece] * reps
            + [in_hbm((chans, width), BF16)] * reps
            + [in_hbm((full, width), BF16), in_hbm((parts, 4 * reps, TILE), BF16)],
            [
                pltpu.VMEM((full, width), F32), pltpu.VMEM((full, width), BF16), pltpu.VMEM((full, width), BF16),
                pltpu.VMEM((full, width), BF16), pltpu.VMEM((reps, chans, width), BF16), pltpu.VMEM((full, full), F32),
                pltpu.VMEM((parts, 4 * reps, TILE), BF16), pltpu.SemaphoreType.DMA((reps,)), sem, sem,
            ],
            3.0, (), range(reps, 2 * reps + 2),
        )
    scaled, out_pieces, grad_pre, slices = dense[:reps], dense[reps : 2 * reps], dense[2 * reps], dense[2 * reps + 1]
    scaled_in = exchange(scaled)
    slices_in = lax.all_to_all(slices, "dom", split_axis=0, concat_axis=0, tiled=True)
    with jax.named_scope("far_back"):
        far_back = call(
            far_back_body, (rep, rows), (*scaled_in, far_tiles), in_hbm((parts, 2 * chans + 8, TILE), BF16),
            [
                pltpu.VMEM((chans, nodes), BF16), pltpu.VMEM((parts, 2 * chans, TILE), BF16), tile_buf, sems, sems,
            ],
            5.0, (reps,), (0,),
        )
    with jax.named_scope("slice_sum"):
        sums = call(slice_sum_body, (), (slices_in,), [shape((4, TILE), F32)] * reps)
    sums_in = exchange(sums, -1)
    with jax.named_scope("slice_send"):
        sending = pl.pallas_call(
            slice_send_body,
            grid=(1,),
            in_specs=[IN_VMEM] * reps + [IN_HBM],
            out_shape=in_hbm(far_back.shape, BF16),
            out_specs=pl.BlockSpec((parts, 8, TILE), lambda i: (0, 2 * chans // 8, 0)),
            input_output_aliases={reps: 0},
            compiler_params=pltpu.CompilerParams(vmem_limit_bytes=VMEM_BYTES),
        )(*sums_in, pinned(far_back))
    returned = lax.all_to_all(sending, "dom", split_axis=0, concat_axis=0, tiled=True)

    with jax.named_scope("back"):
        back_self = call(
            back_body, (rep,), (*weights_in, grad_pre), [piece32] * reps, [pltpu.VMEM((full, width), F32)], 1.0
        )
    back_in = exchange(back_self)
    out_in = exchange(out_pieces, -1)
    with jax.named_scope("near_back"):
        near_back, output = call(
            near_back_body, (rep, cols), (*scaled_in, *back_in, *out_in, local_tiles),
            [shape((chans, nodes), F32), shape((chans, nodes), BF16)], [pltpu.VMEM((chans, nodes), BF16)], 2.0,
        )
    with jax.named_scope("home"):
        grad_feats, wg_self, wg_neigh = call(
            home_body, (sends,), (returned, near_back),
            [shape((chans, nodes), BF16), shape((chans, full), F32), shape((chans, full), F32)],
            [wide32, wide32, sem], 3.0, (1,),
        )
    return output, grad_feats, wg_self.T, wg_neigh.T


def solution(mesh):
    placed = (
        P("rep", "dom"),
        P(None, "rep"),
        P(None, "rep"),
        P("dom", None),
        P("dom", None, None, None),
        P("dom", None, None),
        P("dom", None, None),
        P("dom", None, None, None, None),
        P("rep", "dom"),
    )
    return jax.shard_map(
        local,
        mesh=mesh,
        in_specs=placed,
        out_specs=(P("rep", "dom"), P("rep", "dom"), P(None, "rep"), P(None, "rep")),
        check_vma=False,
    )
```

time: 202 us -> 180 us (0.89)
  local copies, waits for them, and re-layouts: 25.6 us -> 7.95 us
  waiting for transfers between devices: 83.4 us -> 80.7 us
  Pallas kernels: 33 us -> 30.7 us
    unnamed x89 -> x68, local copies, waits for them, and re-layouts: 24.1 us -> 7.95 us
    all_to_all x1, waiting for transfers between devices: 29.2 us -> 26.5 us  [local(): lax.all_to_all(outgoing, 'dom', split_axis=0, concat_axis=0, tiled=True)]
    all_to_all x1, waiting for transfers between devices: 23.7 us -> 26 us  [local(): lax.all_to_all(sending, 'dom', split_axis=0, concat_axis=0, tiled=True)]
    pallas_call x11, Pallas kernels: 33 us -> 30.7 us  [the longest x10 30 us: call(): pl.pallas_call(body, in_specs=[IN_SMEM] * len(scalars) + [IN_HBM if i in...]
  transfers between devices with their start and end apart: 27 -> 27, of which waited for: 9 -> 9; matrix products, arithmetic and copies ran while one was open for 0% -> 0% of each run, Pallas kernels for 11% -> 9%
where the time goes in v2:
time: 180 us; the launch traced here: 179 us
  waiting for transfers between devices  80.7 us (45%)
  starting transfers between devices  58.4 us (32%)
  Pallas kernels  30.7 us (17%)
  local copies, waits for them, and re-layouts  7.95 us (4%)
    ppermute x24, starting transfers between devices, shift(): lax.ppermute(value, 'rep', [(i, (i + by) % reps) for i in range(reps)])  31.6 us
    pallas_call x10, Pallas kernels, call(): pl.pallas_call(body, in_specs=[IN_SMEM] * len(scalars) + [IN_HBM if i in...  30 us
    all_to_all x1, waiting for transfers between devices, local(): lax.all_to_all(outgoing, 'dom', split_axis=0, concat_axis=0, tiled=True)  26.5 us
    all_to_all x1, waiting for transfers between devices, local(): lax.all_to_all(sending, 'dom', split_axis=0, concat_axis=0, tiled=True)  26 us
    ppermute x24, waiting for transfers between devices, shift(): lax.ppermute(value, 'rep', [(i, (i + by) % reps) for i in range(reps)])  20.8 us
    all_to_all x1, starting transfers between devices, local(): lax.all_to_all(outgoing, 'dom', split_axis=0, concat_axis=0, tiled=True)  13.3 us
    unnamed x68, local copies, waits for them, and re-layouts  7.95 us
    all_to_all x1, waiting for transfers between devices, local(): lax.all_to_all(slices, 'dom', split_axis=0, concat_axis=0, tiled=True)  7.4 us
  transfers between devices with their start and end apart: 27, of which 9 were waited for; matrix products, arithmetic and copies ran while one was open for 0% of the time, Pallas kernels for 9%

profile of v2, /device:TPU:1, one launch (start us, length us, event | category | flops | bytes accessed | tf_op | source)
XLA Modules:
  0.0 179.0 jit_solution(7418319678046402375)
XLA Ops:
  1.3 3.1 %pick.1 = bf16[64,128,128]{2,1,0:T(8,128)(2,1)} custom-call(s32[2,64]{1,0:T(2,128)S(1)} %bitcast.25, bf16[64,4096]{1,0:T(8,128)(2,1)} %feats_ref.3), custom_call_target="tpu_custom_call" | custom-call | flops 2200000000 | bytes 65536 | tf_op jit(solution)/shard_map/pick/pallas_call | solution.py:27
  4.4 13.3 %all-to-all-start = ((bf16[64,128,128]{2,1,0:T(8,128)(2,1)}), bf16[64,128,128]{2,1,0:T(8,128)(2,1)S(1)}, u32[]{:S(2)}, u32[]{:S(2)}) async-start(bf16[64,128,128]{2,1,0:T(8,128)(2,1)} %pick.1), calls=%async_computation | async-start | bytes 4194304 | tf_op jit(solution)/shard_map/all_to_all | solution.py:328
  22.5 1.9 %collective-permute-start.8 = (bf16[2,64,256]{2,1,0:T(8,128)(2,1)S(1)}, bf16[2,64,256]{2,1,0:T(8,128)(2,1)S(1)}, u32[]{:S(2)}, u32[]{:S(2)}) collective-permute-start(bf16[2,64,256]{2,1,0:T(8,128)(2,1)S(1)} %pad_maximum_fusion.refs_12_.refs_0_), channel_id=1, source_target_pairs={{0,3},{1,0},{2,1},{3,2},{4,7},{5,4},{6,5},{7,6},{8,11},{9,8},{10,9... | collective-permute-start | bytes 196616 | tf_op jit(solution)/shard_map/ppermute | solution.py:318
  30.1 2.3 %collective-permute-start.5 = (bf16[64,1024]{1,0:T(8,128)(2,1)S(1)}, bf16[64,1024]{1,0:T(8,128)(2,1)S(1)}, u32[]{:S(2)}, u32[]{:S(2)}) collective-permute-start(bf16[64,1024]{1,0:T(8,128)(2,1)S(1)} %get-tuple-element.63), channel_id=1, source_target_pairs={{0,3},{1,0},{2,1},{3,2},{4,7},{5,4},{6,5},{7,6},{8,11},{9,8},{10,9... | collective-permute-start | bytes 393224 | tf_op jit(solution)/shard_map/ppermute | solution.py:318
  34.0 6.8 %near.1 = (f32[64,4096]{1,0:T(8,128)S(1)}, f32[8,4096]{1,0:T(8,128)S(1)}) custom-call(s32[2,32]{1,0:T(2,128)S(1)} %bitcast.23, s32[2,64]{1,0:T(2,128)S(1)} %bitcast.20, bf16[64,4096]{1,0:T(8,128)(2,1)S(1)} %copy-done.4, bf16[32,2,128,128]{3,2,1,0:T(8,128)(2,1)S(1)} %copy-done.1, bf16[64,2,128,128]{3,2,1,0:T(8,128)(2,1)S(1)} %bitcast.19), custom_call_target="tpu_custom_call" | custom-call | flops 6600000000 | bytes 65536 | tf_op jit(solution)/shard_map/near/pallas_call | solution.py:27
  42.5 26.5 %all-to-all-done.got_ref = bf16[64,128,128]{2,1,0:T(8,128)(2,1)S(1)} async-done(((bf16[64,128,128]{2,1,0:T(8,128)(2,1)}), bf16[64,128,128]{2,1,0:T(8,128)(2,1)S(1)}, u32[]{:S(2)}, u32[]{:S(2)}) %all-to-all-start) | async-done | bytes 2097184 | tf_op jit(solution)/shard_map/all_to_all | solution.py:328
  69.0 6.8 %far.1 = (bf16[64,1024]{1,0:T(8,128)(2,1)S(1)}, bf16[64,1024]{1,0:T(8,128)(2,1)S(1)}, bf16[64,1024]{1,0:T(8,128)(2,1)S(1)}, bf16[64,1024]{1,0:T(8,128)(2,1)S(1)}) custom-call(s32[1]{0:T(128)} %bitcast.rep_ref, s32[2,64]{1,0:T(2,128)S(1)} %bitcast.21, bf16[64,128,128]{2,1,0:T(8,128)(2,1)S(1)} %all-to-all-done.got_ref, bf16[64,2,128,128]{3,2,1,0:T(8,128)(2,1)} %bitcast.17, ...), custom_call_target="tpu_custom_call" | custom-call | flops 6600000000 | bytes 65536 | tf_op jit(solution)/shard_map/far/pallas_call | solution.py:27
  77.1 2.5 %collective-permute-start.10 = (bf16[64,1024]{1,0:T(8,128)(2,1)S(1)}, bf16[64,1024]{1,0:T(8,128)(2,1)S(1)}, u32[]{:S(2)}, u32[]{:S(2)}) collective-permute-start(bf16[64,1024]{1,0:T(8,128)(2,1)S(1)} %get-tuple-element.71), channel_id=1, source_target_pairs={{0,2},{1,3},{2,0},{3,1},{4,6},{5,7},{6,4},{7,5},{8,10},{9,11},{10,... | collective-permute-start | bytes 393224 | tf_op jit(solution)/shard_map/ppermute | solution.py:318
  81.8 3.8 %collective-permute-done.10.refs_2_ = bf16[64,1024]{1,0:T(8,128)(2,1)S(1)} collective-permute-done((bf16[64,1024]{1,0:T(8,128)(2,1)S(1)}, bf16[64,1024]{1,0:T(8,128)(2,1)S(1)}, u32[]{:S(2)}, u32[]{:S(2)}) %collective-permute-start.10) | collective-permute-done | bytes 131104 | tf_op jit(solution)/shard_map/ppermute | solution.py:318
  85.6 2.2 %dense.1 = (bf16[64,1024]{1,0:T(8,128)(2,1)S(1)}, bf16[64,1024]{1,0:T(8,128)(2,1)S(1)}, bf16[64,1024]{1,0:T(8,128)(2,1)S(1)}, bf16[64,1024]{1,0:T(8,128)(2,1)S(1...) custom-call(s32[1]{0:T(128)} %bitcast.rep_ref, ...), custom_call_target="tpu_custom_call" | custom-call | flops 3300000000 | bytes 65536 | tf_op jit(solution)/shard_map/dense/pallas_call | solution.py:27
  87.8 6.5 %all-to-all-start.1 = ((bf16[64,16,128]{2,1,0:T(8,128)(2,1)}), bf16[64,16,128]{2,1,0:T(8,128)(2,1)S(1)}, u32[]{:S(2)}, u32[]{:S(2)}) async-start(bf16[64,16,128]{2,1,0:T(8,128)(2,1)} %get-tuple-element.99), calls=%async_computation.1 | async-start | bytes 524288 | tf_op jit(solution)/shard_map/all_to_all | solution.py:365
  95.6 2.1 %collective-permute-start.13 = (bf16[64,1024]{1,0:T(8,128)(2,1)S(1)}, bf16[64,1024]{1,0:T(8,128)(2,1)S(1)}, u32[]{:S(2)}, u32[]{:S(2)}) collective-permute-start(bf16[64,1024]{1,0:T(8,128)(2,1)S(1)} %get-tuple-element.87), channel_id=1, source_target_pairs={{0,2},{1,3},{2,0},{3,1},{4,6},{5,7},{6,4},{7,5},{8,10},{9,11},{10,... | collective-permute-start | bytes 393224 | tf_op jit(solution)/shard_map/ppermute | solution.py:318
  98.9 7.4 %all-to-all-done.1.got_ref = bf16[64,16,128]{2,1,0:T(8,128)(2,1)S(1)} async-done(((bf16[64,16,128]{2,1,0:T(8,128)(2,1)}), bf16[64,16,128]{2,1,0:T(8,128)(2,1)S(1)}, u32[]{:S(2)}, u32[]{:S(2)}) %all-to-all-start.1) | async-done | bytes 262176 | tf_op jit(solution)/shard_map/all_to_all | solution.py:365
  106.4 2.2 %collective-permute-start.21 = (f32[4,128]{1,0:T(4,128)S(1)}, f32[4,128]{1,0:T(4,128)S(1)}, u32[]{:S(2)}, u32[]{:S(2)}) collective-permute-start(f32[4,128]{1,0:T(4,128)S(1)} %get-tuple-element.101), channel_id=1, source_target_pairs={{0,3},{1,0},{2,1},{3,2},{4,7},{5,4},{6,5},{7,6},{8,11},{9,8},{10,9... | collective-permute-start | bytes 6152 | tf_op jit(solution)/shard_map/ppermute | solution.py:318
  109.8 4.7 %far_back.1.refs_4_ = bf16[64,136,128]{2,1,0:T(8,128)(2,1)} custom-call(s32[1]{0:T(128)} %bitcast.rep_ref, s32[2,64]{1,0:T(2,128)S(1)} %bitcast.22, bf16[64,1024]{1,0:T(8,128)(2,1)S(1)} %get-tuple-element.85.refs_0_.s0, bf16[64,1024]{1,0:T(8,128)(2,1)S(1)} %collective-permute-done.12.refs_1_.s1, bf16[64,1024]{1,0:T(8,128)(2,1)S(1)} %collective-permute-done.13.refs_2_.s2, ...), custom_call_target="tpu_custom_call" | custom-call | flops 5500000256 | bytes 65536 | tf_op jit(solution)/shard_map/far_back/pallas_call | solution.py:27
  115.3 7.0 %all-to-all-start.2 = ((bf16[64,136,128]{2,1,0:T(8,128)(2,1)}), bf16[64,136,128]{2,1,0:T(8,128)(2,1)S(1)}, u32[]{:S(2)}, u32[]{:S(2)}) async-start(bf16[64,136,128]{2,1,0:T(8,128)(2,1)} %slice_send.1), calls=%async_computation.2 | async-start | bytes 4456448 | tf_op jit(solution)/shard_map/all_to_all | solution.py:387
  122.3 2.4 %collective-permute-start.18 = (bf16[64,1024]{1,0:T(8,128)(2,1)S(1)}, bf16[64,1024]{1,0:T(8,128)(2,1)S(1)}, u32[]{:S(2)}, u32[]{:S(2)}) collective-permute-start(bf16[64,1024]{1,0:T(8,128)(2,1)S(1)} %copy-done.33), channel_id=1, source_target_pairs={{0,3},{1,0},{2,1},{3,2},{4,7},{5,4},{6,5},{7,6},{8,11},{9,8},{10,9... | collective-permute-start | bytes 393224 | tf_op jit(solution)/shard_map/ppermute | solution.py:318
  127.6 1.6 collective-permute-start.17
  129.2 2.1 %collective-permute-start.19 = (bf16[64,1024]{1,0:T(8,128)(2,1)S(1)}, bf16[64,1024]{1,0:T(8,128)(2,1)S(1)}, u32[]{:S(2)}, u32[]{:S(2)}) collective-permute-start(bf16[64,1024]{1,0:T(8,128)(2,1)S(1)} %copy-done.32), channel_id=1, source_target_pairs={{0,2},{1,3},{2,0},{3,1},{4,6},{5,7},{6,4},{7,5},{8,10},{9,11},{10,... | collective-permute-start | bytes 393224 | tf_op jit(solution)/shard_map/ppermute | solution.py:318
  131.4 10.7 %collective-permute-done.19.refs_10_ = bf16[64,1024]{1,0:T(8,128)(2,1)S(1)} collective-permute-done((bf16[64,1024]{1,0:T(8,128)(2,1)S(1)}, bf16[64,1024]{1,0:T(8,128)(2,1)S(1)}, u32[]{:S(2)}, u32[]{:S(2)}) %collective-permute-start.19) | collective-permute-done | bytes 131104 | tf_op jit(solution)/shard_map/ppermute | solution.py:318
  142.1 3.8 %collective-permute-done.20.refs_11_ = bf16[64,1024]{1,0:T(8,128)(2,1)S(1)} collective-permute-done((bf16[64,1024]{1,0:T(8,128)(2,1)S(1)}, bf16[64,1024]{1,0:T(8,128)(2,1)S(1)}, u32[]{:S(2)}, u32[]{:S(2)}) %collective-permute-start.20) | collective-permute-done | bytes 131104 | tf_op jit(solution)/shard_map/ppermute | solution.py:318
  145.9 3.2 %near_back.1 = (f32[64,4096]{1,0:T(8,128)S(1)}, bf16[64,4096]{1,0:T(8,128)(2,1)}) custom-call(s32[1]{0:T(128)} %bitcast.rep_ref, s32[2,32]{1,0:T(2,128)S(1)} %bitcast.24, bf16[64,1024]{1,0:T(8,128)(2,1)S(1)} %copy-done.24, bf16[64,1024]{1,0:T(8,128)(2,1)S(1)} %collective-permute-done.12.refs_1_.s1, bf16[64,1024]{1,0:T(8,128)(2,1)S(1)} %collective-permute-done.13.refs_2_.s2, ...), custom_call_target="tpu_custom_call" | custom-call | flops 2200000000 | bytes 65536 | tf_op jit(solution)/shard_map/near_back/pallas_call | solution.py:27
  150.1 26.0 %all-to-all-done.2.got_ref = bf16[64,136,128]{2,1,0:T(8,128)(2,1)S(1)} async-done(((bf16[64,136,128]{2,1,0:T(8,128)(2,1)}), bf16[64,136,128]{2,1,0:T(8,128)(2,1)S(1)}, u32[]{:S(2)}, u32[]{:S(2)}) %all-to-all-start.2) | async-done | bytes 2228256 | tf_op jit(solution)/shard_map/all_to_all | solution.py:387
  176.1 2.7 %home.1 = (bf16[64,4096]{1,0:T(8,128)(2,1)}, f32[64,256]{1,0:T(8,128)}, f32[64,256]{1,0:T(8,128)}) custom-call(s32[2,64]{1,0:T(2,128)S(1)} %bitcast.26, bf16[64,136,128]{2,1,0:T(8,128)(2,1)S(1)} %all-to-all-done.2.got_ref, f32[64,4096]{1,0:T(8,128)} %copy-done.17), custom_call_target="tpu_custom_call" | custom-call | flops 3300000000 | bytes 65536 | tf_op jit(solution)/shard_map/home/pallas_call | solution.py:27
  (110 shorter events, 26.3 us)
Async XLA Ops:
  4.4 64.6 %all-to-all-start = ((bf16[64,128,128]{2,1,0:T(8,128)(2,1)}), bf16[64,128,128]{2,1,0:T(8,128)(2,1)S(1)}, u32[]{:S(2)}, u32[]{:S(2)}) async-start(bf16[64,128,128]{2,1,0:T(8,128)(2,1)} %pick.1), calls=%async_computation | async-start | bytes 4194304 | tf_op jit(solution)/shard_map/all_to_all | solution.py:328
  18.5 11.5 %collective-permute-start = (bf16[64,1024]{1,0:T(8,128)(2,1)S(1)}, bf16[64,1024]{1,0:T(8,128)(2,1)S(1)}, u32[]{:S(2)}, u32[]{:S(2)}) collective-permute-start(bf16[64,1024]{1,0:T(8,128)(2,1)S(1)} %get-tuple-element.57), channel_id=1, source_target_pairs={{0,1},{1,2},{2,3},{3,0},{4,5},{5,6},{6,7},{7,4},{8,9},{9,10},{10,1... | collective-permute-start | bytes 393224 | tf_op jit(solution)/shard_map/ppermute | solution.py:318
  19.8 6.0 %collective-permute-start.6 = (bf16[2,64,256]{2,1,0:T(8,128)(2,1)S(1)}, bf16[2,64,256]{2,1,0:T(8,128)(2,1)S(1)}, u32[]{:S(2)}, u32[]{:S(2)}) collective-permute-start(bf16[2,64,256]{2,1,0:T(8,128)(2,1)S(1)} %pad_maximum_fusion.refs_12_.refs_0_), channel_id=1, source_target_pairs={{0,1},{1,2},{2,3},{3,0},{4,5},{5,6},{6,7},{7,4},{8,9},{9,10},{10,1... | collective-permute-start | bytes 196616 | tf_op jit(solution)/shard_map/ppermute | solution.py:318
  21.0 7.1 %collective-permute-start.7 = (bf16[2,64,256]{2,1,0:T(8,128)(2,1)S(1)}, bf16[2,64,256]{2,1,0:T(8,128)(2,1)S(1)}, u32[]{:S(2)}, u32[]{:S(2)}) collective-permute-start(bf16[2,64,256]{2,1,0:T(8,128)(2,1)S(1)} %pad_maximum_fusion.refs_12_.refs_0_), channel_id=1, source_target_pairs={{0,2},{1,3},{2,0},{3,1},{4,6},{5,7},{6,4},{7,5},{8,10},{9,11},{10,... | collective-permute-start | bytes 196616 | tf_op jit(solution)/shard_map/ppermute | solution.py:318
  24.4 18.1 %collective-permute-start.1 = (bf16[64,1024]{1,0:T(8,128)(2,1)S(1)}, bf16[64,1024]{1,0:T(8,128)(2,1)S(1)}, u32[]{:S(2)}, u32[]{:S(2)}) collective-permute-start(bf16[64,1024]{1,0:T(8,128)(2,1)S(1)} %get-tuple-element.58), channel_id=1, source_target_pairs={{0,2},{1,3},{2,0},{3,1},{4,6},{5,7},{6,4},{7,5},{8,10},{9,11},{10,... | collective-permute-start | bytes 393224 | tf_op jit(solution)/shard_map/ppermute | solution.py:318
  26.4 16.1 %collective-permute-start.2 = (bf16[64,1024]{1,0:T(8,128)(2,1)S(1)}, bf16[64,1024]{1,0:T(8,128)(2,1)S(1)}, u32[]{:S(2)}, u32[]{:S(2)}) collective-permute-start(bf16[64,1024]{1,0:T(8,128)(2,1)S(1)} %get-tuple-element.59), channel_id=1, source_target_pairs={{0,3},{1,0},{2,1},{3,2},{4,7},{5,4},{6,5},{7,6},{8,11},{9,8},{10,9... | collective-permute-start | bytes 393224 | tf_op jit(solution)/shard_map/ppermute | solution.py:318
  28.2 14.3 %collective-permute-start.3 = (bf16[64,1024]{1,0:T(8,128)(2,1)S(1)}, bf16[64,1024]{1,0:T(8,128)(2,1)S(1)}, u32[]{:S(2)}, u32[]{:S(2)}) collective-permute-start(bf16[64,1024]{1,0:T(8,128)(2,1)S(1)} %get-tuple-element.61), channel_id=1, source_target_pairs={{0,1},{1,2},{2,3},{3,0},{4,5},{5,6},{6,7},{7,4},{8,9},{9,10},{10,1... | collective-permute-start | bytes 393224 | tf_op jit(solution)/shard_map/ppermute | solution.py:318
  28.8 13.7 %collective-permute-start.4 = (bf16[64,1024]{1,0:T(8,128)(2,1)S(1)}, bf16[64,1024]{1,0:T(8,128)(2,1)S(1)}, u32[]{:S(2)}, u32[]{:S(2)}) collective-permute-start(bf16[64,1024]{1,0:T(8,128)(2,1)S(1)} %get-tuple-element.62), channel_id=1, source_target_pairs={{0,2},{1,3},{2,0},{3,1},{4,6},{5,7},{6,4},{7,5},{8,10},{9,11},{10,... | collective-permute-start | bytes 393224 | tf_op jit(solution)/shard_map/ppermute | solution.py:318
  30.1 12.4 %collective-permute-start.5 = (bf16[64,1024]{1,0:T(8,128)(2,1)S(1)}, bf16[64,1024]{1,0:T(8,128)(2,1)S(1)}, u32[]{:S(2)}, u32[]{:S(2)}) collective-permute-start(bf16[64,1024]{1,0:T(8,128)(2,1)S(1)} %get-tuple-element.63), channel_id=1, source_target_pairs={{0,3},{1,0},{2,1},{3,2},{4,7},{5,4},{6,5},{7,6},{8,11},{9,8},{10,9... | collective-permute-start | bytes 393224 | tf_op jit(solution)/shard_map/ppermute | solution.py:318
  77.1 8.5 %collective-permute-start.10 = (bf16[64,1024]{1,0:T(8,128)(2,1)S(1)}, bf16[64,1024]{1,0:T(8,128)(2,1)S(1)}, u32[]{:S(2)}, u32[]{:S(2)}) collective-permute-start(bf16[64,1024]{1,0:T(8,128)(2,1)S(1)} %get-tuple-element.71), channel_id=1, source_target_pairs={{0,2},{1,3},{2,0},{3,1},{4,6},{5,7},{6,4},{7,5},{8,10},{9,11},{10,... | collective-permute-start | bytes 393224 | tf_op jit(solution)/shard_map/ppermute | solution.py:318
  79.6 6.0 %collective-permute-start.11 = (bf16[64,1024]{1,0:T(8,128)(2,1)S(1)}, bf16[64,1024]{1,0:T(8,128)(2,1)S(1)}, u32[]{:S(2)}, u32[]{:S(2)}) collective-permute-start(bf16[64,1024]{1,0:T(8,128)(2,1)S(1)} %get-tuple-element.72), channel_id=1, source_target_pairs={{0,3},{1,0},{2,1},{3,2},{4,7},{5,4},{6,5},{7,6},{8,11},{9,8},{10,9... | collective-permute-start | bytes 393224 | tf_op jit(solution)/shard_map/ppermute | solution.py:318
  87.8 18.5 %all-to-all-start.1 = ((bf16[64,16,128]{2,1,0:T(8,128)(2,1)}), bf16[64,16,128]{2,1,0:T(8,128)(2,1)S(1)}, u32[]{:S(2)}, u32[]{:S(2)}) async-start(bf16[64,16,128]{2,1,0:T(8,128)(2,1)} %get-tuple-element.99), calls=%async_computation.1 | async-start | bytes 524288 | tf_op jit(solution)/shard_map/all_to_all | solution.py:365
  94.3 15.2 %collective-permute-start.12 = (bf16[64,1024]{1,0:T(8,128)(2,1)S(1)}, bf16[64,1024]{1,0:T(8,128)(2,1)S(1)}, u32[]{:S(2)}, u32[]{:S(2)}) collective-permute-start(bf16[64,1024]{1,0:T(8,128)(2,1)S(1)} %get-tuple-element.86), channel_id=1, source_target_pairs={{0,1},{1,2},{2,3},{3,0},{4,5},{5,6},{6,7},{7,4},{8,9},{9,10},{10,1... | collective-permute-start | bytes 393224 | tf_op jit(solution)/shard_map/ppermute | solution.py:318
  95.6 14.2 %collective-permute-start.13 = (bf16[64,1024]{1,0:T(8,128)(2,1)S(1)}, bf16[64,1024]{1,0:T(8,128)(2,1)S(1)}, u32[]{:S(2)}, u32[]{:S(2)}) collective-permute-start(bf16[64,1024]{1,0:T(8,128)(2,1)S(1)} %get-tuple-element.87), channel_id=1, source_target_pairs={{0,2},{1,3},{2,0},{3,1},{4,6},{5,7},{6,4},{7,5},{8,10},{9,11},{10,... | collective-permute-start | bytes 393224 | tf_op jit(solution)/shard_map/ppermute | solution.py:318
  97.7 12.1 %collective-permute-start.14 = (bf16[64,1024]{1,0:T(8,128)(2,1)S(1)}, bf16[64,1024]{1,0:T(8,128)(2,1)S(1)}, u32[]{:S(2)}, u32[]{:S(2)}) collective-permute-start(bf16[64,1024]{1,0:T(8,128)(2,1)S(1)} %get-tuple-element.88), channel_id=1, source_target_pairs={{0,3},{1,0},{2,1},{3,2},{4,7},{5,4},{6,5},{7,6},{8,11},{9,8},{10,9... | collective-permute-start | bytes 393224 | tf_op jit(solution)/shard_map/ppermute | solution.py:318
  106.4 8.1 %collective-permute-start.21 = (f32[4,128]{1,0:T(4,128)S(1)}, f32[4,128]{1,0:T(4,128)S(1)}, u32[]{:S(2)}, u32[]{:S(2)}) collective-permute-start(f32[4,128]{1,0:T(4,128)S(1)} %get-tuple-element.101), channel_id=1, source_target_pairs={{0,3},{1,0},{2,1},{3,2},{4,7},{5,4},{6,5},{7,6},{8,11},{9,8},{10,9... | collective-permute-start | bytes 6152 | tf_op jit(solution)/shard_map/ppermute | solution.py:318
  108.6 6.0 %collective-permute-start.22 = (f32[4,128]{1,0:T(4,128)S(1)}, f32[4,128]{1,0:T(4,128)S(1)}, u32[]{:S(2)}, u32[]{:S(2)}) collective-permute-start(f32[4,128]{1,0:T(4,128)S(1)} %get-tuple-element.102), channel_id=1, source_target_pairs={{0,2},{1,3},{2,0},{3,1},{4,6},{5,7},{6,4},{7,5},{8,10},{9,11},{10,... | collective-permute-start | bytes 6152 | tf_op jit(solution)/shard_map/ppermute | solution.py:318
  115.3 60.8 %all-to-all-start.2 = ((bf16[64,136,128]{2,1,0:T(8,128)(2,1)}), bf16[64,136,128]{2,1,0:T(8,128)(2,1)S(1)}, u32[]{:S(2)}, u32[]{:S(2)}) async-start(bf16[64,136,128]{2,1,0:T(8,128)(2,1)} %slice_send.1), calls=%async_computation.2 | async-start | bytes 4456448 | tf_op jit(solution)/shard_map/all_to_all | solution.py:387
  122.3 9.0 %collective-permute-start.18 = (bf16[64,1024]{1,0:T(8,128)(2,1)S(1)}, bf16[64,1024]{1,0:T(8,128)(2,1)S(1)}, u32[]{:S(2)}, u32[]{:S(2)}) collective-permute-start(bf16[64,1024]{1,0:T(8,128)(2,1)S(1)} %copy-done.33), channel_id=1, source_target_pairs={{0,3},{1,0},{2,1},{3,2},{4,7},{5,4},{6,5},{7,6},{8,11},{9,8},{10,9... | collective-permute-start | bytes 393224 | tf_op jit(solution)/shard_map/ppermute | solution.py:318
  126.2 19.6 %collective-permute-start.15 = (f32[64,1024]{1,0:T(8,128)S(1)}, f32[64,1024]{1,0:T(8,128)S(1)}, u32[]{:S(2)}, u32[]{:S(2)}) collective-permute-start(f32[64,1024]{1,0:T(8,128)S(1)} %get-tuple-element.91), channel_id=1, source_target_pairs={{0,1},{1,2},{2,3},{3,0},{4,5},{5,6},{6,7},{7,4},{8,9},{9,10},{10,1... | collective-permute-start | bytes 786440 | tf_op jit(solution)/shard_map/ppermute | solution.py:318
  126.3 19.5 %collective-permute-start.16 = (f32[64,1024]{1,0:T(8,128)S(1)}, f32[64,1024]{1,0:T(8,128)S(1)}, u32[]{:S(2)}, u32[]{:S(2)}) collective-permute-start(f32[64,1024]{1,0:T(8,128)S(1)} %get-tuple-element.92), channel_id=1, source_target_pairs={{0,2},{1,3},{2,0},{3,1},{4,6},{5,7},{6,4},{7,5},{8,10},{9,11},{10,... | collective-permute-start | bytes 786440 | tf_op jit(solution)/shard_map/ppermute | solution.py:318
  127.6 18.2 %collective-permute-start.17 = (f32[64,1024]{1,0:T(8,128)S(1)}, f32[64,1024]{1,0:T(8,128)S(1)}, u32[]{:S(2)}, u32[]{:S(2)}) collective-permute-start(f32[64,1024]{1,0:T(8,128)S(1)} %get-tuple-element.93), channel_id=1, source_target_pairs={{0,3},{1,0},{2,1},{3,2},{4,7},{5,4},{6,5},{7,6},{8,11},{9,8},{10,9... | collective-permute-start | bytes 786440 | tf_op jit(solution)/shard_map/ppermute | solution.py:318
  129.2 12.8 %collective-permute-start.19 = (bf16[64,1024]{1,0:T(8,128)(2,1)S(1)}, bf16[64,1024]{1,0:T(8,128)(2,1)S(1)}, u32[]{:S(2)}, u32[]{:S(2)}) collective-permute-start(bf16[64,1024]{1,0:T(8,128)(2,1)S(1)} %copy-done.32), channel_id=1, source_target_pairs={{0,2},{1,3},{2,0},{3,1},{4,6},{5,7},{6,4},{7,5},{8,10},{9,11},{10,... | collective-permute-start | bytes 393224 | tf_op jit(solution)/shard_map/ppermute | solution.py:318
  131.4 14.5 %collective-permute-start.20 = (bf16[64,1024]{1,0:T(8,128)(2,1)S(1)}, bf16[64,1024]{1,0:T(8,128)(2,1)S(1)}, u32[]{:S(2)}, u32[]{:S(2)}) collective-permute-start(bf16[64,1024]{1,0:T(8,128)(2,1)S(1)} %copy-done.31), channel_id=1, source_target_pairs={{0,1},{1,2},{2,3},{3,0},{4,5},{5,6},{6,7},{7,4},{8,9},{9,10},{10,1... | collective-permute-start | bytes 393224 | tf_op jit(solution)/shard_map/ppermute | solution.py:318
  (37 other events, 432.0 us)

commit v3 on v2

--- a/solution.py
+++ b/solution.py
@@ -83,7 +83,7 @@
         outs[reps + k][...] = cot_ref[:, lanes(chunk, width)]
 
 
-def near_body(cols_ref, rows_ref, feats_ref, near_ref, far_ref, acc_ref, div_ref):
+def near_body(cols_ref, rows_ref, feats_ref, near_ref, far_ref, acc_ref, div_ref, turned_hbm, turned_ref, sems):
     ones = jnp.ones((8, TILE), BF16)
     div_ref[...] = jnp.ones_like(div_ref)
 
@@ -108,22 +108,28 @@
             for slot in range(2):
                 part = step * STEP + item
                 row = rows_ref[slot, part]
-                div_ref[:, lanes(row, TILE)] += dot(ones, far_ref[part, slot], 1, 1)
+                turned = far_ref[part, slot].T
+                turned_ref[part, slot] = turned
+                div_ref[:, lanes(row, TILE)] += dot(ones, turned, 1, 0)
+        tile_copy(turned_ref, turned_hbm, sems, step).start()
+
+    for step in range(far_ref.shape[0] // STEP):
+        tile_copy(turned_ref, turned_hbm, sems, step).wait()
 
 
 def far_body(rep_ref, rows_ref, got_ref, far_hbm, near_acc_hbm, div_hbm, *rest):
     outs = rest[:4]
-    acc_ref, far_ref, div_ref, sems, acc_sem, div_sem = rest[4:]
+    acc_ref, near_acc_ref, far_ref, div_ref, sems, acc_sem, div_sem = rest[4:]
     reps = len(outs)
     chans = acc_ref.shape[0]
     width = outs[0].shape[1]
-    load_acc = pltpu.make_async_copy(near_acc_hbm, acc_ref, acc_sem)
+    load_acc = pltpu.make_async_copy(near_acc_hbm, near_acc_ref, acc_sem)
     load_div = pltpu.make_async_copy(div_hbm, div_ref, div_sem)
-    load_acc.start()
     for step in range(far_ref.shape[0] // STEP):
         tile_copy(far_hbm, far_ref, sems, step).start()
+    load_acc.start()
     load_div.start()
-    load_acc.wait()
+    acc_ref[...] = jnp.zeros_like(acc_ref)
 
     @pl.loop(0, far_ref.shape[0] // STEP)
     def _(step):
@@ -133,12 +139,13 @@
                 part = step * STEP + item
                 row = rows_ref[slot, part]
                 block = got_ref[part, slot * chans : (slot + 1) * chans, :]
-                acc_ref[:, lanes(row, TILE)] += dot(block, far_ref[part, slot], 1, 1)
-
+                acc_ref[:, lanes(row, TILE)] += dot(block, far_ref[part, slot], 1, 0)
+
+    load_acc.wait()
     load_div.wait()
     for k in range(reps):
         where = lanes(lax.rem(rep_ref[0] + k, reps), width)
-        outs[k][...] = (acc_ref[:, where] / div_ref[0:1, where]).astype(BF16)
+        outs[k][...] = ((near_acc_ref[:, where] + acc_ref[:, where]) / div_ref[0:1, where]).astype(BF16)
 
 
 def gather_rows(ref, pieces, rep):
@@ -333,17 +340,18 @@
     cot_in = exchange(pieces[reps:])
     weights_in = exchange([jnp.stack([w_self.T, w_neigh.T])] * reps)
     with jax.named_scope("near"):
-        near_acc, div = call(
+        near_acc, div, turned = call(
             near_body, (cols, rows), (feats, local_tiles, far_tiles),
-            [shape((chans, nodes), F32), shape((8, nodes), F32)], (), 6.0,
-        )
-    incoming, feats_in, cot_in, weights_in, near_acc, div = lax.optimization_barrier(
-        (incoming, feats_in, cot_in, weights_in, near_acc, div)
+            [shape((chans, nodes), F32), shape((8, nodes), F32), in_hbm(far_tiles.shape, BF16)],
+            [tile_buf, sems], 8.0, (), (2,),
+        )
+    incoming, feats_in, cot_in, weights_in, near_acc, div, turned = lax.optimization_barrier(
+        (incoming, feats_in, cot_in, weights_in, near_acc, div, turned)
     )
     with jax.named_scope("far"):
         agg = call(
-            far_body, (rep, rows), (incoming, far_tiles, near_acc, div), [piece] * reps,
-            [wide32, tile_buf, pltpu.VMEM((8, nodes), F32), sems, sem, sem], 6.0, (1, 2, 3),
+            far_body, (rep, rows), (incoming, turned, near_acc, div), [piece] * reps,
+            [wide32, wide32, tile_buf, pltpu.VMEM((8, nodes), F32), sems, sem, sem], 6.0, (1, 2, 3),
         )
     agg_in = exchange(agg)
 
@@ -369,8 +377,9 @@
             [
                 pltpu.VMEM((chans, nodes), BF16), pltpu.VMEM((parts, 2 * chans, TILE), BF16), tile_buf, sems, sems,
             ],
-            5.0, (reps,), (0,),
-        )
+            2.0, (reps,), (0,),
+        )
+    slices_in, far_back = lax.optimization_barrier((slices_in, far_back))
     with jax.named_scope("slice_sum"):
         sums = call(slice_sum_body, (), (slices_in,), [shape((4, TILE), F32)] * reps)
     sums_in = exchange(sums, -1)

time: 180 us -> 184 us (1.022)
  waiting for transfers between devices: 80.7 us -> 84.5 us
  starting transfers between devices: 58.4 us -> 61.3 us
  Pallas kernels: 30.7 us -> 28.2 us
    ppermute x24, waiting for transfers between devices: 20.8 us -> 29.1 us  [shift(): lax.ppermute(value, 'rep', [(i, (i + by) % reps) for i in range(reps)])]
    all_to_all x1, waiting for transfers between devices: 7.4 us -> 0.01 us  [local(): lax.all_to_all(slices, 'dom', split_axis=0, concat_axis=0, tiled=True)]
    all_to_all x1, starting transfers between devices: 7 us -> 12.7 us  [local(): lax.all_to_all(sending, 'dom', split_axis=0, concat_axis=0, tiled=True)]
    ppermute x24, starting transfers between devices: 31.6 us -> 28.8 us  [shift(): lax.ppermute(value, 'rep', [(i, (i + by) % reps) for i in range(reps)])]
    pallas_call x10, Pallas kernels: 30 us -> 27.5 us  [call(): pl.pallas_call(body, in_specs=[IN_SMEM] * len(scalars) + [IN_HBM if i in...]
    all_to_all x1, waiting for transfers between devices: 26 us -> 27.9 us  [local(): lax.all_to_all(sending, 'dom', split_axis=0, concat_axis=0, tiled=True)]
  transfers between devices with their start and end apart: 27 -> 27, of which waited for: 9 -> 11; matrix products, arithmetic and copies ran while one was open for 0% -> 0% of each run, Pallas kernels for 9% -> 8%
where the time goes in v3:
time: 184 us; the launch traced here: 183 us
  waiting for transfers between devices  84.5 us (46%)
  starting transfers between devices  61.3 us (33%)
  Pallas kernels  28.2 us (15%)
  local copies, waits for them, and re-layouts  8.07 us (4%)
    ppermute x24, waiting for transfers between devices, shift(): lax.ppermute(value, 'rep', [(i, (i + by) % reps) for i in range(reps)])  29.1 us
    ppermute x24, starting transfers between devices, shift(): lax.ppermute(value, 'rep', [(i, (i + by) % reps) for i in range(reps)])  28.8 us
    all_to_all x1, waiting for transfers between devices, local(): lax.all_to_all(sending, 'dom', split_axis=0, concat_axis=0, tiled=True)  27.9 us
    all_to_all x1, waiting for transfers between devices, local(): lax.all_to_all(outgoing, 'dom', split_axis=0, concat_axis=0, tiled=True)  27.5 us
    pallas_call x10, Pallas kernels, call(): pl.pallas_call(body, in_specs=[IN_SMEM] * len(scalars) + [IN_HBM if i in...  27.5 us
    all_to_all x1, starting transfers between devices, local(): lax.all_to_all(outgoing, 'dom', split_axis=0, concat_axis=0, tiled=True)  13.3 us
    all_to_all x1, starting transfers between devices, local(): lax.all_to_all(sending, 'dom', split_axis=0, concat_axis=0, tiled=True)  12.7 us
    unnamed x68, local copies, waits for them, and re-layouts  8.07 us
  transfers between devices with their start and end apart: 27, of which 11 were waited for; matrix products, arithmetic and copies ran while one was open for 0% of the time, Pallas kernels for 8%

profile of v3, /device:TPU:1, one launch (start us, length us, event | category | flops | bytes accessed | tf_op | source)
XLA Modules:
  0.0 183.2 jit_solution(13621917625922689699)
XLA Ops:
  1.3 3.1 %pick.1 = bf16[64,128,128]{2,1,0:T(8,128)(2,1)} custom-call(s32[2,64]{1,0:T(2,128)S(1)} %bitcast.24, bf16[64,4096]{1,0:T(8,128)(2,1)} %feats_ref.3), custom_call_target="tpu_custom_call" | custom-call | flops 2200000000 | bytes 65536 | tf_op jit(solution)/shard_map/pick/pallas_call | solution.py:27
  4.4 13.3 %all-to-all-start = ((bf16[64,128,128]{2,1,0:T(8,128)(2,1)}), bf16[64,128,128]{2,1,0:T(8,128)(2,1)S(1)}, u32[]{:S(2)}, u32[]{:S(2)}) async-start(bf16[64,128,128]{2,1,0:T(8,128)(2,1)} %pick.1), calls=%async_computation | async-start | bytes 4194304 | tf_op jit(solution)/shard_map/all_to_all | solution.py:335
  23.2 1.7 collective-permute-start.1
  29.4 1.9 %collective-permute-start.5 = (bf16[64,1024]{1,0:T(8,128)(2,1)S(1)}, bf16[64,1024]{1,0:T(8,128)(2,1)S(1)}, u32[]{:S(2)}, u32[]{:S(2)}) collective-permute-start(bf16[64,1024]{1,0:T(8,128)(2,1)S(1)} %get-tuple-element.67), channel_id=1, source_target_pairs={{0,3},{1,0},{2,1},{3,2},{4,7},{5,4},{6,5},{7,6},{8,11},{9,8},{10,9... | collective-permute-start | bytes 393224 | tf_op jit(solution)/shard_map/ppermute | solution.py:325
  31.3 1.6 copy-done.1
  32.8 7.0 %near.1 = (f32[64,4096]{1,0:T(8,128)S(1)}, f32[8,4096]{1,0:T(8,128)S(1)}, bf16[64,2,128,128]{3,2,1,0:T(8,128)(2,1)}) custom-call(s32[2,32]{1,0:T(2,128)S(1)} %bitcast.22, s32[2,64]{1,0:T(2,128)S(1)} %bitcast.19, bf16[64,4096]{1,0:T(8,128)(2,1)S(1)} %copy-done.4, bf16[32,2,128,128]{3,2,1,0:T(8,128)(2,1)S(1)} %copy-done.1, bf16[64,2,128,128]{3,2,1,0:T(8,128)(2,1)S(1)} %bitcast.18), custom_call_target="tpu_custom_call" | custom-call | flops 8800000000 | bytes 65536 | tf_op jit(solution)/shard_map/near/pallas_call | solution.py:27
  41.5 27.5 %all-to-all-done.got_ref = bf16[64,128,128]{2,1,0:T(8,128)(2,1)S(1)} async-done(((bf16[64,128,128]{2,1,0:T(8,128)(2,1)}), bf16[64,128,128]{2,1,0:T(8,128)(2,1)S(1)}, u32[]{:S(2)}, u32[]{:S(2)}) %all-to-all-start) | async-done | bytes 2097184 | tf_op jit(solution)/shard_map/all_to_all | solution.py:335
  69.0 4.1 %far.1 = (bf16[64,1024]{1,0:T(8,128)(2,1)S(1)}, bf16[64,1024]{1,0:T(8,128)(2,1)S(1)}, bf16[64,1024]{1,0:T(8,128)(2,1)S(1)}, bf16[64,1024]{1,0:T(8,128)(2,1)S(1)}) custom-call(s32[1]{0:T(128)} %bitcast.rep_ref, s32[2,64]{1,0:T(2,128)S(1)} %bitcast.20, bf16[64,128,128]{2,1,0:T(8,128)(2,1)S(1)} %all-to-all-done.got_ref, ...), custom_call_target="tpu_custom_call" | custom-call | flops 6600000000 | bytes 65536 | tf_op jit(solution)/shard_map/far/pallas_call | solution.py:27
  74.4 2.4 %collective-permute-start.10 = (bf16[64,1024]{1,0:T(8,128)(2,1)S(1)}, bf16[64,1024]{1,0:T(8,128)(2,1)S(1)}, u32[]{:S(2)}, u32[]{:S(2)}) collective-permute-start(bf16[64,1024]{1,0:T(8,128)(2,1)S(1)} %get-tuple-element.77), channel_id=1, source_target_pairs={{0,2},{1,3},{2,0},{3,1},{4,6},{5,7},{6,4},{7,5},{8,10},{9,11},{10,... | collective-permute-start | bytes 393224 | tf_op jit(solution)/shard_map/ppermute | solution.py:325
  79.1 3.8 %collective-permute-done.10.refs_2_ = bf16[64,1024]{1,0:T(8,128)(2,1)S(1)} collective-permute-done((bf16[64,1024]{1,0:T(8,128)(2,1)S(1)}, bf16[64,1024]{1,0:T(8,128)(2,1)S(1)}, u32[]{:S(2)}, u32[]{:S(2)}) %collective-permute-start.10) | collective-permute-done | bytes 131104 | tf_op jit(solution)/shard_map/ppermute | solution.py:325
  82.9 2.2 %dense.1 = (bf16[64,1024]{1,0:T(8,128)(2,1)S(1)}, bf16[64,1024]{1,0:T(8,128)(2,1)S(1)}, bf16[64,1024]{1,0:T(8,128)(2,1)S(1)}, bf16[64,1024]{1,0:T(8,128)(2,1)S(1...) custom-call(s32[1]{0:T(128)} %bitcast.rep_ref, ...), custom_call_target="tpu_custom_call" | custom-call | flops 3300000000 | bytes 65536 | tf_op jit(solution)/shard_map/dense/pallas_call | solution.py:27
  85.1 6.5 %all-to-all-start.1 = ((bf16[64,16,128]{2,1,0:T(8,128)(2,1)}), bf16[64,16,128]{2,1,0:T(8,128)(2,1)S(1)}, u32[]{:S(2)}, u32[]{:S(2)}) async-start(bf16[64,16,128]{2,1,0:T(8,128)(2,1)} %get-tuple-element.105), calls=%async_computation.1 | async-start | bytes 524288 | tf_op jit(solution)/shard_map/all_to_all | solution.py:373
  92.9 2.0 %collective-permute-start.13 = (bf16[64,1024]{1,0:T(8,128)(2,1)S(1)}, bf16[64,1024]{1,0:T(8,128)(2,1)S(1)}, u32[]{:S(2)}, u32[]{:S(2)}) collective-permute-start(bf16[64,1024]{1,0:T(8,128)(2,1)S(1)} %get-tuple-element.93), channel_id=1, source_target_pairs={{0,2},{1,3},{2,0},{3,1},{4,6},{5,7},{6,4},{7,5},{8,10},{9,11},{10,... | collective-permute-start | bytes 393224 | tf_op jit(solution)/shard_map/ppermute | solution.py:325
  97.5 3.4 %collective-permute-done.13.refs_2_.s2 = bf16[64,1024]{1,0:T(8,128)(2,1)S(1)} collective-permute-done((bf16[64,1024]{1,0:T(8,128)(2,1)S(1)}, bf16[64,1024]{1,0:T(8,128)(2,1)S(1)}, u32[]{:S(2)}, u32[]{:S(2)}) %collective-permute-start.13) | collective-permute-done | bytes 131104 | tf_op jit(solution)/shard_map/ppermute | solution.py:325
  100.9 4.7 %far_back.1.refs_4_ = bf16[64,136,128]{2,1,0:T(8,128)(2,1)} custom-call(s32[1]{0:T(128)} %bitcast.rep_ref, s32[2,64]{1,0:T(2,128)S(1)} %bitcast.21, bf16[64,1024]{1,0:T(8,128)(2,1)S(1)} %get-tuple-element.91.refs_0_.s0, bf16[64,1024]{1,0:T(8,128)(2,1)S(1)} %collective-permute-done.12.refs_1_.s1, bf16[64,1024]{1,0:T(8,128)(2,1)S(1)} %collective-permute-done.13.refs_2_.s2, ...), custom_call_target="tpu_custom_call" | custom-call | flops 2200000000 | bytes 65536 | tf_op jit(solution)/shard_map/far_back/pallas_call | solution.py:27
  105.8 2.6 %collective-permute-start.21 = (f32[4,128]{1,0:T(4,128)S(1)}, f32[4,128]{1,0:T(4,128)S(1)}, u32[]{:S(2)}, u32[]{:S(2)}) collective-permute-start(f32[4,128]{1,0:T(4,128)S(1)} %get-tuple-element.108), channel_id=1, source_target_pairs={{0,3},{1,0},{2,1},{3,2},{4,7},{5,4},{6,5},{7,6},{8,11},{9,8},{10,9... | collective-permute-start | bytes 6152 | tf_op jit(solution)/shard_map/ppermute | solution.py:325
  109.5 2.8 %collective-permute-done.22.refs_2_ = f32[4,128]{1,0:T(4,128)S(1)} collective-permute-done((f32[4,128]{1,0:T(4,128)S(1)}, f32[4,128]{1,0:T(4,128)S(1)}, u32[]{:S(2)}, u32[]{:S(2)}) %collective-permute-start.22) | collective-permute-done | bytes 2080 | tf_op jit(solution)/shard_map/ppermute | solution.py:325
  113.8 12.7 %all-to-all-start.2 = ((bf16[64,136,128]{2,1,0:T(8,128)(2,1)}), bf16[64,136,128]{2,1,0:T(8,128)(2,1)S(1)}, u32[]{:S(2)}, u32[]{:S(2)}) async-start(bf16[64,136,128]{2,1,0:T(8,128)(2,1)} %slice_send.1), calls=%async_computation.2 | async-start | bytes 4456448 | tf_op jit(solution)/shard_map/all_to_all | solution.py:396
  130.6 1.6 collective-permute-start.17
  133.5 11.2 %collective-permute-done.19.refs_10_ = bf16[64,1024]{1,0:T(8,128)(2,1)S(1)} collective-permute-done((bf16[64,1024]{1,0:T(8,128)(2,1)S(1)}, bf16[64,1024]{1,0:T(8,128)(2,1)S(1)}, u32[]{:S(2)}, u32[]{:S(2)}) %collective-permute-start.19) | collective-permute-done | bytes 131104 | tf_op jit(solution)/shard_map/ppermute | solution.py:325
  144.7 3.6 %collective-permute-done.20.refs_11_ = bf16[64,1024]{1,0:T(8,128)(2,1)S(1)} collective-permute-done((bf16[64,1024]{1,0:T(8,128)(2,1)S(1)}, bf16[64,1024]{1,0:T(8,128)(2,1)S(1)}, u32[]{:S(2)}, u32[]{:S(2)}) %collective-permute-start.20) | collective-permute-done | bytes 131104 | tf_op jit(solution)/shard_map/ppermute | solution.py:325
  148.3 3.2 %near_back.1 = (f32[64,4096]{1,0:T(8,128)S(1)}, bf16[64,4096]{1,0:T(8,128)(2,1)}) custom-call(s32[1]{0:T(128)} %bitcast.rep_ref, s32[2,32]{1,0:T(2,128)S(1)} %bitcast.23, bf16[64,1024]{1,0:T(8,128)(2,1)S(1)} %copy-done.18, bf16[64,1024]{1,0:T(8,128)(2,1)S(1)} %collective-permute-done.12.refs_1_.s1, bf16[64,1024]{1,0:T(8,128)(2,1)S(1)} %collective-permute-done.13.refs_2_.s2, ...), custom_call_target="tpu_custom_call" | custom-call | flops 2200000000 | bytes 65536 | tf_op jit(solution)/shard_map/near_back/pallas_call | solution.py:27
  152.5 27.9 %all-to-all-done.2.got_ref = bf16[64,136,128]{2,1,0:T(8,128)(2,1)S(1)} async-done(((bf16[64,136,128]{2,1,0:T(8,128)(2,1)}), bf16[64,136,128]{2,1,0:T(8,128)(2,1)S(1)}, u32[]{:S(2)}, u32[]{:S(2)}) %all-to-all-start.2) | async-done | bytes 2228256 | tf_op jit(solution)/shard_map/all_to_all | solution.py:396
  180.4 2.7 %home.1 = (bf16[64,4096]{1,0:T(8,128)(2,1)}, f32[64,256]{1,0:T(8,128)}, f32[64,256]{1,0:T(8,128)}) custom-call(s32[2,64]{1,0:T(2,128)S(1)} %bitcast.25, bf16[64,136,128]{2,1,0:T(8,128)(2,1)S(1)} %all-to-all-done.2.got_ref, f32[64,4096]{1,0:T(8,128)} %copy-done.19), custom_call_target="tpu_custom_call" | custom-call | flops 3300000000 | bytes 65536 | tf_op jit(solution)/shard_map/home/pallas_call | solution.py:27
  (110 shorter events, 28.6 us)
Async XLA Ops:
  4.4 64.6 %all-to-all-start = ((bf16[64,128,128]{2,1,0:T(8,128)(2,1)}), bf16[64,128,128]{2,1,0:T(8,128)(2,1)S(1)}, u32[]{:S(2)}, u32[]{:S(2)}) async-start(bf16[64,128,128]{2,1,0:T(8,128)(2,1)} %pick.1), calls=%async_computation | async-start | bytes 4194304 | tf_op jit(solution)/shard_map/all_to_all | solution.py:335
  18.6 10.8 %collective-permute-start = (bf16[64,1024]{1,0:T(8,128)(2,1)S(1)}, bf16[64,1024]{1,0:T(8,128)(2,1)S(1)}, u32[]{:S(2)}, u32[]{:S(2)}) collective-permute-start(bf16[64,1024]{1,0:T(8,128)(2,1)S(1)} %get-tuple-element.61), channel_id=1, source_target_pairs={{0,1},{1,2},{2,3},{3,0},{4,5},{5,6},{6,7},{7,4},{8,9},{9,10},{10,1... | collective-permute-start | bytes 393224 | tf_op jit(solution)/shard_map/ppermute | solution.py:325
  19.8 5.1 %collective-permute-start.8 = (bf16[2,64,256]{2,1,0:T(8,128)(2,1)S(1)}, bf16[2,64,256]{2,1,0:T(8,128)(2,1)S(1)}, u32[]{:S(2)}, u32[]{:S(2)}) collective-permute-start(bf16[2,64,256]{2,1,0:T(8,128)(2,1)S(1)} %pad_maximum_fusion.refs_12_.refs_0_), channel_id=1, source_target_pairs={{0,3},{1,0},{2,1},{3,2},{4,7},{5,4},{6,5},{7,6},{8,11},{9,8},{10,9... | collective-permute-start | bytes 196616 | tf_op jit(solution)/shard_map/ppermute | solution.py:325
  21.3 5.7 %collective-permute-start.7 = (bf16[2,64,256]{2,1,0:T(8,128)(2,1)S(1)}, bf16[2,64,256]{2,1,0:T(8,128)(2,1)S(1)}, u32[]{:S(2)}, u32[]{:S(2)}) collective-permute-start(bf16[2,64,256]{2,1,0:T(8,128)(2,1)S(1)} %pad_maximum_fusion.refs_12_.refs_0_), channel_id=1, source_target_pairs={{0,2},{1,3},{2,0},{3,1},{4,6},{5,7},{6,4},{7,5},{8,10},{9,11},{10,... | collective-permute-start | bytes 196616 | tf_op jit(solution)/shard_map/ppermute | solution.py:325
  22.9 5.2 %collective-permute-start.6 = (bf16[2,64,256]{2,1,0:T(8,128)(2,1)S(1)}, bf16[2,64,256]{2,1,0:T(8,128)(2,1)S(1)}, u32[]{:S(2)}, u32[]{:S(2)}) collective-permute-start(bf16[2,64,256]{2,1,0:T(8,128)(2,1)S(1)} %pad_maximum_fusion.refs_12_.refs_0_), channel_id=1, source_target_pairs={{0,1},{1,2},{2,3},{3,0},{4,5},{5,6},{6,7},{7,4},{8,9},{9,10},{10,1... | collective-permute-start | bytes 196616 | tf_op jit(solution)/shard_map/ppermute | solution.py:325
  23.2 18.3 %collective-permute-start.1 = (bf16[64,1024]{1,0:T(8,128)(2,1)S(1)}, bf16[64,1024]{1,0:T(8,128)(2,1)S(1)}, u32[]{:S(2)}, u32[]{:S(2)}) collective-permute-start(bf16[64,1024]{1,0:T(8,128)(2,1)S(1)} %get-tuple-element.62), channel_id=1, source_target_pairs={{0,2},{1,3},{2,0},{3,1},{4,6},{5,7},{6,4},{7,5},{8,10},{9,11},{10,... | collective-permute-start | bytes 393224 | tf_op jit(solution)/shard_map/ppermute | solution.py:325
  25.5 16.0 %collective-permute-start.2 = (bf16[64,1024]{1,0:T(8,128)(2,1)S(1)}, bf16[64,1024]{1,0:T(8,128)(2,1)S(1)}, u32[]{:S(2)}, u32[]{:S(2)}) collective-permute-start(bf16[64,1024]{1,0:T(8,128)(2,1)S(1)} %get-tuple-element.63), channel_id=1, source_target_pairs={{0,3},{1,0},{2,1},{3,2},{4,7},{5,4},{6,5},{7,6},{8,11},{9,8},{10,9... | collective-permute-start | bytes 393224 | tf_op jit(solution)/shard_map/ppermute | solution.py:325
  27.0 14.5 %collective-permute-start.3 = (bf16[64,1024]{1,0:T(8,128)(2,1)S(1)}, bf16[64,1024]{1,0:T(8,128)(2,1)S(1)}, u32[]{:S(2)}, u32[]{:S(2)}) collective-permute-start(bf16[64,1024]{1,0:T(8,128)(2,1)S(1)} %get-tuple-element.65), channel_id=1, source_target_pairs={{0,1},{1,2},{2,3},{3,0},{4,5},{5,6},{6,7},{7,4},{8,9},{9,10},{10,1... | collective-permute-start | bytes 393224 | tf_op jit(solution)/shard_map/ppermute | solution.py:325
  28.7 12.8 %collective-permute-start.4 = (bf16[64,1024]{1,0:T(8,128)(2,1)S(1)}, bf16[64,1024]{1,0:T(8,128)(2,1)S(1)}, u32[]{:S(2)}, u32[]{:S(2)}) collective-permute-start(bf16[64,1024]{1,0:T(8,128)(2,1)S(1)} %get-tuple-element.66), channel_id=1, source_target_pairs={{0,2},{1,3},{2,0},{3,1},{4,6},{5,7},{6,4},{7,5},{8,10},{9,11},{10,... | collective-permute-start | bytes 393224 | tf_op jit(solution)/shard_map/ppermute | solution.py:325
  29.4 12.1 %collective-permute-start.5 = (bf16[64,1024]{1,0:T(8,128)(2,1)S(1)}, bf16[64,1024]{1,0:T(8,128)(2,1)S(1)}, u32[]{:S(2)}, u32[]{:S(2)}) collective-permute-start(bf16[64,1024]{1,0:T(8,128)(2,1)S(1)} %get-tuple-element.67), channel_id=1, source_target_pairs={{0,3},{1,0},{2,1},{3,2},{4,7},{5,4},{6,5},{7,6},{8,11},{9,8},{10,9... | collective-permute-start | bytes 393224 | tf_op jit(solution)/shard_map/ppermute | solution.py:325
  73.1 6.0 %collective-permute-start.9 = (bf16[64,1024]{1,0:T(8,128)(2,1)S(1)}, bf16[64,1024]{1,0:T(8,128)(2,1)S(1)}, u32[]{:S(2)}, u32[]{:S(2)}) collective-permute-start(bf16[64,1024]{1,0:T(8,128)(2,1)S(1)} %get-tuple-element.76), channel_id=1, source_target_pairs={{0,1},{1,2},{2,3},{3,0},{4,5},{5,6},{6,7},{7,4},{8,9},{9,10},{10,1... | collective-permute-start | bytes 393224 | tf_op jit(solution)/shard_map/ppermute | solution.py:325
  74.4 8.5 %collective-permute-start.10 = (bf16[64,1024]{1,0:T(8,128)(2,1)S(1)}, bf16[64,1024]{1,0:T(8,128)(2,1)S(1)}, u32[]{:S(2)}, u32[]{:S(2)}) collective-permute-start(bf16[64,1024]{1,0:T(8,128)(2,1)S(1)} %get-tuple-element.77), channel_id=1, source_target_pairs={{0,2},{1,3},{2,0},{3,1},{4,6},{5,7},{6,4},{7,5},{8,10},{9,11},{10,... | collective-permute-start | bytes 393224 | tf_op jit(solution)/shard_map/ppermute | solution.py:325
  76.9 6.0 %collective-permute-start.11 = (bf16[64,1024]{1,0:T(8,128)(2,1)S(1)}, bf16[64,1024]{1,0:T(8,128)(2,1)S(1)}, u32[]{:S(2)}, u32[]{:S(2)}) collective-permute-start(bf16[64,1024]{1,0:T(8,128)(2,1)S(1)} %get-tuple-element.78), channel_id=1, source_target_pairs={{0,3},{1,0},{2,1},{3,2},{4,7},{5,4},{6,5},{7,6},{8,11},{9,8},{10,9... | collective-permute-start | bytes 393224 | tf_op jit(solution)/shard_map/ppermute | solution.py:325
  85.1 20.5 %all-to-all-start.1 = ((bf16[64,16,128]{2,1,0:T(8,128)(2,1)}), bf16[64,16,128]{2,1,0:T(8,128)(2,1)S(1)}, u32[]{:S(2)}, u32[]{:S(2)}) async-start(bf16[64,16,128]{2,1,0:T(8,128)(2,1)} %get-tuple-element.105), calls=%async_computation.1 | async-start | bytes 524288 | tf_op jit(solution)/shard_map/all_to_all | solution.py:373
  91.6 5.9 %collective-permute-start.12 = (bf16[64,1024]{1,0:T(8,128)(2,1)S(1)}, bf16[64,1024]{1,0:T(8,128)(2,1)S(1)}, u32[]{:S(2)}, u32[]{:S(2)}) collective-permute-start(bf16[64,1024]{1,0:T(8,128)(2,1)S(1)} %get-tuple-element.92), channel_id=1, source_target_pairs={{0,1},{1,2},{2,3},{3,0},{4,5},{5,6},{6,7},{7,4},{8,9},{9,10},{10,1... | collective-permute-start | bytes 393224 | tf_op jit(solution)/shard_map/ppermute | solution.py:325
  92.9 8.0 %collective-permute-start.13 = (bf16[64,1024]{1,0:T(8,128)(2,1)S(1)}, bf16[64,1024]{1,0:T(8,128)(2,1)S(1)}, u32[]{:S(2)}, u32[]{:S(2)}) collective-permute-start(bf16[64,1024]{1,0:T(8,128)(2,1)S(1)} %get-tuple-element.93), channel_id=1, source_target_pairs={{0,2},{1,3},{2,0},{3,1},{4,6},{5,7},{6,4},{7,5},{8,10},{9,11},{10,... | collective-permute-start | bytes 393224 | tf_op jit(solution)/shard_map/ppermute | solution.py:325
  95.0 6.0 %collective-permute-start.14 = (bf16[64,1024]{1,0:T(8,128)(2,1)S(1)}, bf16[64,1024]{1,0:T(8,128)(2,1)S(1)}, u32[]{:S(2)}, u32[]{:S(2)}) collective-permute-start(bf16[64,1024]{1,0:T(8,128)(2,1)S(1)} %get-tuple-element.94), channel_id=1, source_target_pairs={{0,3},{1,0},{2,1},{3,2},{4,7},{5,4},{6,5},{7,6},{8,11},{9,8},{10,9... | collective-permute-start | bytes 393224 | tf_op jit(solution)/shard_map/ppermute | solution.py:325
  113.8 66.6 %all-to-all-start.2 = ((bf16[64,136,128]{2,1,0:T(8,128)(2,1)}), bf16[64,136,128]{2,1,0:T(8,128)(2,1)S(1)}, u32[]{:S(2)}, u32[]{:S(2)}) async-start(bf16[64,136,128]{2,1,0:T(8,128)(2,1)} %slice_send.1), calls=%async_computation.2 | async-start | bytes 4456448 | tf_op jit(solution)/shard_map/all_to_all | solution.py:396
  126.6 6.8 %collective-permute-start.18 = (bf16[64,1024]{1,0:T(8,128)(2,1)S(1)}, bf16[64,1024]{1,0:T(8,128)(2,1)S(1)}, u32[]{:S(2)}, u32[]{:S(2)}) collective-permute-start(bf16[64,1024]{1,0:T(8,128)(2,1)S(1)} %copy-done.33), channel_id=1, source_target_pairs={{0,3},{1,0},{2,1},{3,2},{4,7},{5,4},{6,5},{7,6},{8,11},{9,8},{10,9... | collective-permute-start | bytes 393224 | tf_op jit(solution)/shard_map/ppermute | solution.py:325
  128.3 20.0 %collective-permute-start.15 = (f32[64,1024]{1,0:T(8,128)S(1)}, f32[64,1024]{1,0:T(8,128)S(1)}, u32[]{:S(2)}, u32[]{:S(2)}) collective-permute-start(f32[64,1024]{1,0:T(8,128)S(1)} %get-tuple-element.97), channel_id=1, source_target_pairs={{0,1},{1,2},{2,3},{3,0},{4,5},{5,6},{6,7},{7,4},{8,9},{9,10},{10,1... | collective-permute-start | bytes 786440 | tf_op jit(solution)/shard_map/ppermute | solution.py:325
  129.7 18.6 %collective-permute-start.16 = (f32[64,1024]{1,0:T(8,128)S(1)}, f32[64,1024]{1,0:T(8,128)S(1)}, u32[]{:S(2)}, u32[]{:S(2)}) collective-permute-start(f32[64,1024]{1,0:T(8,128)S(1)} %get-tuple-element.98), channel_id=1, source_target_pairs={{0,2},{1,3},{2,0},{3,1},{4,6},{5,7},{6,4},{7,5},{8,10},{9,11},{10,... | collective-permute-start | bytes 786440 | tf_op jit(solution)/shard_map/ppermute | solution.py:325
  130.6 17.7 %collective-permute-start.17 = (f32[64,1024]{1,0:T(8,128)S(1)}, f32[64,1024]{1,0:T(8,128)S(1)}, u32[]{:S(2)}, u32[]{:S(2)}) collective-permute-start(f32[64,1024]{1,0:T(8,128)S(1)} %get-tuple-element.99), channel_id=1, source_target_pairs={{0,3},{1,0},{2,1},{3,2},{4,7},{5,4},{6,5},{7,6},{8,11},{9,8},{10,9... | collective-permute-start | bytes 786440 | tf_op jit(solution)/shard_map/ppermute | solution.py:325
  132.2 12.5 %collective-permute-start.19 = (bf16[64,1024]{1,0:T(8,128)(2,1)S(1)}, bf16[64,1024]{1,0:T(8,128)(2,1)S(1)}, u32[]{:S(2)}, u32[]{:S(2)}) collective-permute-start(bf16[64,1024]{1,0:T(8,128)(2,1)S(1)} %copy-done.32), channel_id=1, source_target_pairs={{0,2},{1,3},{2,0},{3,1},{4,6},{5,7},{6,4},{7,5},{8,10},{9,11},{10,... | collective-permute-start | bytes 393224 | tf_op jit(solution)/shard_map/ppermute | solution.py:325
  133.4 14.8 %collective-permute-start.20 = (bf16[64,1024]{1,0:T(8,128)(2,1)S(1)}, bf16[64,1024]{1,0:T(8,128)(2,1)S(1)}, u32[]{:S(2)}, u32[]{:S(2)}) collective-permute-start(bf16[64,1024]{1,0:T(8,128)(2,1)S(1)} %copy-done.31), channel_id=1, source_target_pairs={{0,1},{1,2},{2,3},{3,0},{4,5},{5,6},{6,7},{7,4},{8,9},{9,10},{10,1... | collective-permute-start | bytes 393224 | tf_op jit(solution)/shard_map/ppermute | solution.py:325
  (37 other events, 419.7 us)

commit v4 on v3

--- a/solution.py
+++ b/solution.py
@@ -159,9 +159,9 @@
 def dense_body(rep_ref, *refs):
     agg, feats, cot, wts = refs[0:4], refs[4:8], refs[8:12], refs[12:16]
     div_ref = refs[16]
-    scaled_out, out_out, grad_hbm, slices_hbm = refs[17:21], refs[21:25], refs[25], refs[26]
-    back_ref, full_feats, full_agg, grad_ref, out_buf, prod_ref, slices_ref = refs[27:34]
-    out_sems, grad_sem, slices_sem = refs[34:37]
+    leaving, out_out, grad_hbm = refs[17:21], refs[21:25], refs[25]
+    back_ref, full_feats, full_agg, grad_ref, out_buf, prod_ref = refs[26:32]
+    out_sems, grad_sem = refs[32:34]
     rep = rep_ref[0]
     reps = 4
     rows, width = agg[0].shape
@@ -183,21 +183,17 @@
     leave(grad_ref, grad_hbm, grad_sem)
     for which, full in ((0, full_feats), (1, full_agg)):
         prod_ref[...] = dot(grad_ref[...], full[...], 1, 1)
-        for group in range(rows // 4):
-            for half in range(2):
-                index = which * 32 + group * 2 + half
-                for k in range(reps):
-                    start = k * rows + group * 4
-                    slices_ref[index, 4 * k : 4 * k + 4, :] = prod_ref[
-                        start : start + 4, half * TILE : (half + 1) * TILE
-                    ].astype(BF16)
-    leave(slices_ref, slices_hbm, slices_sem)
+        full_width = prod_ref.shape[1]
+        for k in range(reps):
+            source = (reps - k) % reps
+            start = width + which * full_width
+            leaving[k][:, start : start + full_width] = prod_ref[source * rows : (source + 1) * rows, :].astype(BF16)
     w_neigh = jnp.concatenate([wts[k][1] for k in range(reps)], axis=0)
     back_ref[...] = dot(w_neigh, grad_ref[...], 0, 0)
     div = div_ref[0:1, lanes(rep, width)]
     for k in range(reps):
         target = lax.rem(rep + k, reps)
-        scaled_out[k][...] = (back_ref[lanes(target, rows), :] / div).astype(BF16)
+        leaving[k][:, :width] = (back_ref[lanes(target, rows), :] / div).astype(BF16)
     for copy in copies:
         copy.wait()
 
@@ -214,15 +210,23 @@
         back_out[k][...] = back_ref[lanes(target, rows), :]
 
 
-def slice_sum_body(got_ref, *outs):
-    total = jnp.sum(got_ref[...].astype(F32), axis=0)
-    for k in range(len(outs)):
-        outs[k][...] = total[4 * k : 4 * k + 4, :]
-
-
-def slice_send_body(*refs):
-    parts, out_ref = refs[:4], refs[-1]
-    total = parts[0][...] + parts[1][...] + parts[2][...] + parts[3][...]
+def slice_body(*refs):
+    pieces, slices_ref = refs[:4], refs[4]
+    rows, wide = pieces[0].shape
+    full = wide // 6
+    first = wide - 2 * full
+    total = pieces[0][:, first:].astype(F32)
+    for piece in pieces[1:]:
+        total = total + piece[:, first:].astype(F32)
+    for which in range(2):
+        for group in range(rows // 4):
+            for half in range(2):
+                start = which * full + half * TILE
+                slices_ref[which * 32 + group * 2 + half] = total[4 * group : 4 * group + 4, start : start + TILE]
+
+
+def slice_send_body(got_ref, rest_ref, out_ref):
+    total = jnp.sum(got_ref[...], axis=0)
     high = total.astype(BF16)
     low = (total - high.astype(F32)).astype(BF16)
     both = jnp.concatenate([high.astype(F32), low.astype(F32)], axis=0).astype(BF16)
@@ -231,10 +235,10 @@
 
 def gather_lanes(ref, pieces, rep):
     reps = len(pieces)
-    width = pieces[0].shape[1]
+    width = ref.shape[1] // reps
     for k in range(reps):
         source = lax.rem(rep + reps - k, reps)
-        ref[:, lanes(source, width)] = pieces[k][...]
+        ref[:, lanes(source, width)] = pieces[k][:, :width]
 
 
 def far_back_body(rep_ref, rows_ref, s0, s1, s2, s3, far_hbm, out_ref, full_ref, buf_ref, far_ref, sems, out_sems):
@@ -270,7 +274,7 @@
     near_ref, acc_ref, output_ref, full_ref = refs[12:16]
     rep = rep_ref[0]
     reps = 4
-    width = scaled[0].shape[1]
+    width = outs[0].shape[1]
     gather_lanes(full_ref, scaled, rep)
     gather_lanes(acc_ref, back, rep)
     for k in range(reps):
@@ -358,18 +362,20 @@
     with jax.named_scope("dense"):
         dense = call(
             dense_body, (rep,), (*agg_in, *feats_in, *cot_in, *weights_in, div),
-            [piece] * reps
+            [shape((chans, width + 2 * full), BF16)] * reps
             + [in_hbm((chans, width), BF16)] * reps
-            + [in_hbm((full, width), BF16), in_hbm((parts, 4 * reps, TILE), BF16)],
+            + [in_hbm((full, width), BF16)],
             [
                 pltpu.VMEM((full, width), F32), pltpu.VMEM((full, width), BF16), pltpu.VMEM((full, width), BF16),
                 pltpu.VMEM((full, width), BF16), pltpu.VMEM((reps, chans, width), BF16), pltpu.VMEM((full, full), F32),
-                pltpu.VMEM((parts, 4 * reps, TILE), BF16), pltpu.SemaphoreType.DMA((reps,)), sem, sem,
+                pltpu.SemaphoreType.DMA((reps,)), sem,
             ],
-            3.0, (), range(reps, 2 * reps + 2),
-        )
-    scaled, out_pieces, grad_pre, slices = dense[:reps], dense[reps : 2 * reps], dense[2 * reps], dense[2 * reps + 1]
+            3.0, (), range(reps, 2 * reps + 1),
+        )
+    scaled, out_pieces, grad_pre = dense[:reps], dense[reps : 2 * reps], dense[2 * reps]
     scaled_in = exchange(scaled)
+    with jax.named_scope("slices"):
+        slices = call(slice_body, (), scaled_in, shape((parts, 4, TILE), F32), (), 0.5)
     slices_in = lax.all_to_all(slices, "dom", split_axis=0, concat_axis=0, tiled=True)
     with jax.named_scope("far_back"):
         far_back = call(
@@ -379,20 +385,16 @@
             ],
             2.0, (reps,), (0,),
         )
-    slices_in, far_back = lax.optimization_barrier((slices_in, far_back))
-    with jax.named_scope("slice_sum"):
-        sums = call(slice_sum_body, (), (slices_in,), [shape((4, TILE), F32)] * reps)
-    sums_in = exchange(sums, -1)
     with jax.named_scope("slice_send"):
         sending = pl.pallas_call(
             slice_send_body,
             grid=(1,),
-            in_specs=[IN_VMEM] * reps + [IN_HBM],
+            in_specs=[IN_VMEM, IN_HBM],
             out_shape=in_hbm(far_back.shape, BF16),
             out_specs=pl.BlockSpec((parts, 8, TILE), lambda i: (0, 2 * chans // 8, 0)),
-            input_output_aliases={reps: 0},
+            input_output_aliases={1: 0},
             compiler_params=pltpu.CompilerParams(vmem_limit_bytes=VMEM_BYTES),
-        )(*sums_in, pinned(far_back))
+        )(slices_in, pinned(far_back))
     returned = lax.all_to_all(sending, "dom", split_axis=0, concat_axis=0, tiled=True)
 
     with jax.named_scope("back"):

time: 184 us -> 179 us (0.973)
  starting transfers between devices: 61.3 us -> 53.5 us
  waiting for transfers between devices: 84.5 us -> 86.6 us
    all_to_all x1, starting transfers between devices: 12.7 us -> 5.01 us  [local(): lax.all_to_all(sending, 'dom', split_axis=0, concat_axis=0, tiled=True)]
    all_to_all x1, waiting for transfers between devices: 0.01 us -> 5.62 us  [local(): lax.all_to_all(slices, 'dom', split_axis=0, concat_axis=0, tiled=True)]
    all_to_all x1, waiting for transfers between devices: 27.9 us -> 25.9 us  [local(): lax.all_to_all(sending, 'dom', split_axis=0, concat_axis=0, tiled=True)]
    ppermute x24 -> x21, starting transfers between devices: 28.8 us -> 27 us  [shift(): lax.ppermute(value, 'rep', [(i, (i + by) % reps) for i in range(reps)])]
    ppermute x24 -> x21, waiting for transfers between devices: 29.1 us -> 27.7 us  [shift(): lax.ppermute(value, 'rep', [(i, (i + by) % reps) for i in range(reps)])]
    unnamed x68 -> x62, local copies, waits for them, and re-layouts: 8.07 us -> 7.94 us
  transfers between devices with their start and end apart: 27 -> 24, of which waited for: 11 -> 10; matrix products, arithmetic and copies ran while one was open for 0% -> 0% of each run, Pallas kernels for 8% -> 9%
where the time goes in v4:
time: 179 us; the launch traced here: 178 us
  waiting for transfers between devices  86.6 us (48%)
  starting transfers between devices  53.5 us (30%)
  Pallas kernels  28.7 us (16%)
  local copies, waits for them, and re-layouts  7.94 us (4%)
    pallas_call x10, Pallas kernels, call(): pl.pallas_call(body, in_specs=[IN_SMEM] * len(scalars) + [IN_HBM if i in...  28 us
    ppermute x21, waiting for transfers between devices, shift(): lax.ppermute(value, 'rep', [(i, (i + by) % reps) for i in range(reps)])  27.7 us
    all_to_all x1, waiting for transfers between devices, local(): lax.all_to_all(outgoing, 'dom', split_axis=0, concat_axis=0, tiled=True)  27.5 us
    ppermute x21, starting transfers between devices, shift(): lax.ppermute(value, 'rep', [(i, (i + by) % reps) for i in range(reps)])  27 us
    all_to_all x1, waiting for transfers between devices, local(): lax.all_to_all(sending, 'dom', split_axis=0, concat_axis=0, tiled=True)  25.9 us
    all_to_all x1, starting transfers between devices, local(): lax.all_to_all(outgoing, 'dom', split_axis=0, concat_axis=0, tiled=True)  13.3 us
    all_to_all x1, starting transfers between devices, local(): lax.all_to_all(slices, 'dom', split_axis=0, concat_axis=0, tiled=True)  8.19 us
    unnamed x62, local copies, waits for them, and re-layouts  7.94 us
  transfers between devices with their start and end apart: 24, of which 10 were waited for; matrix products, arithmetic and copies ran while one was open for 0% of the time, Pallas kernels for 9%

profile of v4, /device:TPU:1, one launch (start us, length us, event | category | flops | bytes accessed | tf_op | source)
XLA Modules:
  0.0 178.0 jit_solution(10122998702313357423)
XLA Ops:
  1.3 3.1 %pick.1 = bf16[64,128,128]{2,1,0:T(8,128)(2,1)} custom-call(s32[2,64]{1,0:T(2,128)S(1)} %bitcast.24, bf16[64,4096]{1,0:T(8,128)(2,1)} %feats_ref.3), custom_call_target="tpu_custom_call" | custom-call | flops 2200000000 | bytes 65536 | tf_op jit(solution)/shard_map/pick/pallas_call | solution.py:27
  4.5 13.3 %all-to-all-start = ((bf16[64,128,128]{2,1,0:T(8,128)(2,1)}), bf16[64,128,128]{2,1,0:T(8,128)(2,1)S(1)}, u32[]{:S(2)}, u32[]{:S(2)}) async-start(bf16[64,128,128]{2,1,0:T(8,128)(2,1)} %pick.1), calls=%async_computation | async-start | bytes 4194304 | tf_op jit(solution)/shard_map/all_to_all | solution.py:339
  29.4 1.9 %collective-permute-start.5 = (bf16[64,1024]{1,0:T(8,128)(2,1)S(1)}, bf16[64,1024]{1,0:T(8,128)(2,1)S(1)}, u32[]{:S(2)}, u32[]{:S(2)}) collective-permute-start(bf16[64,1024]{1,0:T(8,128)(2,1)S(1)} %get-tuple-element.60), channel_id=1, source_target_pairs={{0,3},{1,0},{2,1},{3,2},{4,7},{5,4},{6,5},{7,6},{8,11},{9,8},{10,9... | collective-permute-start | bytes 393224 | tf_op jit(solution)/shard_map/ppermute | solution.py:329
  32.9 7.0 %near.1 = (f32[64,4096]{1,0:T(8,128)S(1)}, f32[8,4096]{1,0:T(8,128)S(1)}, bf16[64,2,128,128]{3,2,1,0:T(8,128)(2,1)}) custom-call(s32[2,32]{1,0:T(2,128)S(1)} %bitcast.22, s32[2,64]{1,0:T(2,128)S(1)} %bitcast.19, bf16[64,4096]{1,0:T(8,128)(2,1)S(1)} %copy-done.4, bf16[32,2,128,128]{3,2,1,0:T(8,128)(2,1)S(1)} %copy-done.1, bf16[64,2,128,128]{3,2,1,0:T(8,128)(2,1)S(1)} %bitcast.18), custom_call_target="tpu_custom_call" | custom-call | flops 8800000000 | bytes 65536 | tf_op jit(solution)/shard_map/near/pallas_call | solution.py:27
  41.6 27.5 %all-to-all-done.got_ref = bf16[64,128,128]{2,1,0:T(8,128)(2,1)S(1)} async-done(((bf16[64,128,128]{2,1,0:T(8,128)(2,1)}), bf16[64,128,128]{2,1,0:T(8,128)(2,1)S(1)}, u32[]{:S(2)}, u32[]{:S(2)}) %all-to-all-start) | async-done | bytes 2097184 | tf_op jit(solution)/shard_map/all_to_all | solution.py:339
  69.0 4.1 %far.1 = (bf16[64,1024]{1,0:T(8,128)(2,1)S(1)}, bf16[64,1024]{1,0:T(8,128)(2,1)S(1)}, bf16[64,1024]{1,0:T(8,128)(2,1)S(1)}, bf16[64,1024]{1,0:T(8,128)(2,1)S(1)}) custom-call(s32[1]{0:T(128)} %bitcast.rep_ref, s32[2,64]{1,0:T(2,128)S(1)} %bitcast.20, bf16[64,128,128]{2,1,0:T(8,128)(2,1)S(1)} %all-to-all-done.got_ref, ...), custom_call_target="tpu_custom_call" | custom-call | flops 6600000000 | bytes 65536 | tf_op jit(solution)/shard_map/far/pallas_call | solution.py:27
  74.4 2.5 %collective-permute-start.10 = (bf16[64,1024]{1,0:T(8,128)(2,1)S(1)}, bf16[64,1024]{1,0:T(8,128)(2,1)S(1)}, u32[]{:S(2)}, u32[]{:S(2)}) collective-permute-start(bf16[64,1024]{1,0:T(8,128)(2,1)S(1)} %get-tuple-element.70), channel_id=1, source_target_pairs={{0,2},{1,3},{2,0},{3,1},{4,6},{5,7},{6,4},{7,5},{8,10},{9,11},{10,... | collective-permute-start | bytes 393224 | tf_op jit(solution)/shard_map/ppermute | solution.py:329
  79.1 3.8 %collective-permute-done.10.refs_2_ = bf16[64,1024]{1,0:T(8,128)(2,1)S(1)} collective-permute-done((bf16[64,1024]{1,0:T(8,128)(2,1)S(1)}, bf16[64,1024]{1,0:T(8,128)(2,1)S(1)}, u32[]{:S(2)}, u32[]{:S(2)}) %collective-permute-start.10) | collective-permute-done | bytes 131104 | tf_op jit(solution)/shard_map/ppermute | solution.py:329
  82.9 2.1 %dense.1 = (bf16[64,1536]{1,0:T(8,128)(2,1)S(1)}, bf16[64,1536]{1,0:T(8,128)(2,1)S(1)}, bf16[64,1536]{1,0:T(8,128)(2,1)S(1)}, bf16[64,1536]{1,0:T(8,128)(2,1)S(1...) custom-call(s32[1]{0:T(128)} %bitcast.rep_ref, ...), custom_call_target="tpu_custom_call" | custom-call | flops 3300000000 | bytes 65536 | tf_op jit(solution)/shard_map/dense/pallas_call | solution.py:27
  86.2 2.2 %collective-permute-start.13 = (bf16[64,1536]{1,0:T(8,128)(2,1)S(1)}, bf16[64,1536]{1,0:T(8,128)(2,1)S(1)}, u32[]{:S(2)}, u32[]{:S(2)}) collective-permute-start(bf16[64,1536]{1,0:T(8,128)(2,1)S(1)} %get-tuple-element.86), channel_id=1, source_target_pairs={{0,2},{1,3},{2,0},{3,1},{4,6},{5,7},{6,4},{7,5},{8,10},{9,11},{10,... | collective-permute-start | bytes 589832 | tf_op jit(solution)/shard_map/ppermute | solution.py:329
  89.2 2.2 %collective-permute-done.12.refs_1_.s1 = bf16[64,1536]{1,0:T(8,128)(2,1)S(1)} collective-permute-done((bf16[64,1536]{1,0:T(8,128)(2,1)S(1)}, bf16[64,1536]{1,0:T(8,128)(2,1)S(1)}, u32[]{:S(2)}, u32[]{:S(2)}) %collective-permute-start.12) | collective-permute-done | bytes 196640 | tf_op jit(solution)/shard_map/ppermute | solution.py:329
  91.5 4.8 %collective-permute-done.13.refs_2_.s2 = bf16[64,1536]{1,0:T(8,128)(2,1)S(1)} collective-permute-done((bf16[64,1536]{1,0:T(8,128)(2,1)S(1)}, bf16[64,1536]{1,0:T(8,128)(2,1)S(1)}, u32[]{:S(2)}, u32[]{:S(2)}) %collective-permute-start.13) | collective-permute-done | bytes 196640 | tf_op jit(solution)/shard_map/ppermute | solution.py:329
  97.0 8.2 %all-to-all-start.1 = ((f32[64,4,128]{2,1,0:T(4,128)}), f32[64,4,128]{2,1,0:T(4,128)S(1)}, u32[]{:S(2)}, u32[]{:S(2)}) async-start(f32[64,4,128]{2,1,0:T(4,128)} %slices.1), calls=%async_computation.1 | async-start | bytes 262144 | tf_op jit(solution)/shard_map/all_to_all | solution.py:379
  105.2 4.7 %far_back.1.rest_ref = bf16[64,136,128]{2,1,0:T(8,128)(2,1)} custom-call(s32[1]{0:T(128)} %bitcast.rep_ref, s32[2,64]{1,0:T(2,128)S(1)} %bitcast.21, bf16[64,1536]{1,0:T(8,128)(2,1)S(1)} %get-tuple-element.84.refs_0_.s0, bf16[64,1536]{1,0:T(8,128)(2,1)S(1)} %collective-permute-done.12.refs_1_.s1, bf16[64,1536]{1,0:T(8,128)(2,1)S(1)} %collective-permute-done.13.refs_2_.s2, ...), custom_call_target="tpu_custom_call" | custom-call | flops 2200000000 | bytes 65536 | tf_op jit(solution)/shard_map/far_back/pallas_call | solution.py:27
  109.9 5.6 %all-to-all-done.1.got_ref = f32[64,4,128]{2,1,0:T(4,128)S(1)} async-done(((f32[64,4,128]{2,1,0:T(4,128)}), f32[64,4,128]{2,1,0:T(4,128)S(1)}, u32[]{:S(2)}, u32[]{:S(2)}) %all-to-all-start.1) | async-done | bytes 131104 | tf_op jit(solution)/shard_map/all_to_all | solution.py:379
  116.3 5.0 %all-to-all-start.2 = ((bf16[64,136,128]{2,1,0:T(8,128)(2,1)}), bf16[64,136,128]{2,1,0:T(8,128)(2,1)S(1)}, u32[]{:S(2)}, u32[]{:S(2)}) async-start(bf16[64,136,128]{2,1,0:T(8,128)(2,1)} %slice_send.1), calls=%async_computation.2 | async-start | bytes 4456448 | tf_op jit(solution)/shard_map/all_to_all | solution.py:398
  121.3 2.4 %collective-permute-start.18 = (bf16[64,1024]{1,0:T(8,128)(2,1)}, bf16[64,1024]{1,0:T(8,128)(2,1)S(1)}, u32[]{:S(2)}, u32[]{:S(2)}) collective-permute-start(bf16[64,1024]{1,0:T(8,128)(2,1)} %get-tuple-element.94), channel_id=1, source_target_pairs={{0,3},{1,0},{2,1},{3,2},{4,7},{5,4},{6,5},{7,6},{8,11},{9,8},{10,9... | collective-permute-start | bytes 393224 | tf_op jit(solution)/shard_map/ppermute | solution.py:329
  125.3 1.8 collective-permute-start.16
  128.2 2.1 %collective-permute-start.19 = (bf16[64,1024]{1,0:T(8,128)(2,1)}, bf16[64,1024]{1,0:T(8,128)(2,1)S(1)}, u32[]{:S(2)}, u32[]{:S(2)}) collective-permute-start(bf16[64,1024]{1,0:T(8,128)(2,1)} %get-tuple-element.95), channel_id=1, source_target_pairs={{0,2},{1,3},{2,0},{3,1},{4,6},{5,7},{6,4},{7,5},{8,10},{9,11},{10,... | collective-permute-start | bytes 393224 | tf_op jit(solution)/shard_map/ppermute | solution.py:329
  130.3 11.1 %collective-permute-done.19.refs_10_ = bf16[64,1024]{1,0:T(8,128)(2,1)S(1)} collective-permute-done((bf16[64,1024]{1,0:T(8,128)(2,1)}, bf16[64,1024]{1,0:T(8,128)(2,1)S(1)}, u32[]{:S(2)}, u32[]{:S(2)}) %collective-permute-start.19) | collective-permute-done | bytes 131104 | tf_op jit(solution)/shard_map/ppermute | solution.py:329
  141.4 3.6 %collective-permute-done.20.refs_11_ = bf16[64,1024]{1,0:T(8,128)(2,1)S(1)} collective-permute-done((bf16[64,1024]{1,0:T(8,128)(2,1)}, bf16[64,1024]{1,0:T(8,128)(2,1)S(1)}, u32[]{:S(2)}, u32[]{:S(2)}) %collective-permute-start.20) | collective-permute-done | bytes 131104 | tf_op jit(solution)/shard_map/ppermute | solution.py:329
  145.1 3.2 %near_back.1 = (f32[64,4096]{1,0:T(8,128)S(1)}, bf16[64,4096]{1,0:T(8,128)(2,1)}) custom-call(s32[1]{0:T(128)} %bitcast.rep_ref, s32[2,32]{1,0:T(2,128)S(1)} %bitcast.23, bf16[64,1536]{1,0:T(8,128)(2,1)S(1)} %copy-done.18, bf16[64,1536]{1,0:T(8,128)(2,1)S(1)} %collective-permute-done.12.refs_1_.s1, bf16[64,1536]{1,0:T(8,128)(2,1)S(1)} %collective-permute-done.13.refs_2_.s2, ...), custom_call_target="tpu_custom_call" | custom-call | flops 2200000000 | bytes 65536 | tf_op jit(solution)/shard_map/near_back/pallas_call | solution.py:27
  149.3 25.9 %all-to-all-done.2.got_ref = bf16[64,136,128]{2,1,0:T(8,128)(2,1)S(1)} async-done(((bf16[64,136,128]{2,1,0:T(8,128)(2,1)}), bf16[64,136,128]{2,1,0:T(8,128)(2,1)S(1)}, u32[]{:S(2)}, u32[]{:S(2)}) %all-to-all-start.2) | async-done | bytes 2228256 | tf_op jit(solution)/shard_map/all_to_all | solution.py:398
  175.1 2.7 %home.1 = (bf16[64,4096]{1,0:T(8,128)(2,1)}, f32[64,256]{1,0:T(8,128)}, f32[64,256]{1,0:T(8,128)}) custom-call(s32[2,64]{1,0:T(2,128)S(1)} %bitcast.25, bf16[64,136,128]{2,1,0:T(8,128)(2,1)S(1)} %all-to-all-done.2.got_ref, f32[64,4096]{1,0:T(8,128)} %copy-done.19), custom_call_target="tpu_custom_call" | custom-call | flops 3300000000 | bytes 65536 | tf_op jit(solution)/shard_map/home/pallas_call | solution.py:27
  (98 shorter events, 26.3 us)
Async XLA Ops:
  4.5 64.6 %all-to-all-start = ((bf16[64,128,128]{2,1,0:T(8,128)(2,1)}), bf16[64,128,128]{2,1,0:T(8,128)(2,1)S(1)}, u32[]{:S(2)}, u32[]{:S(2)}) async-start(bf16[64,128,128]{2,1,0:T(8,128)(2,1)} %pick.1), calls=%async_computation | async-start | bytes 4194304 | tf_op jit(solution)/shard_map/all_to_all | solution.py:339
  18.6 10.8 %collective-permute-start = (bf16[64,1024]{1,0:T(8,128)(2,1)S(1)}, bf16[64,1024]{1,0:T(8,128)(2,1)S(1)}, u32[]{:S(2)}, u32[]{:S(2)}) collective-permute-start(bf16[64,1024]{1,0:T(8,128)(2,1)S(1)} %get-tuple-element.54), channel_id=1, source_target_pairs={{0,1},{1,2},{2,3},{3,0},{4,5},{5,6},{6,7},{7,4},{8,9},{9,10},{10,1... | collective-permute-start | bytes 393224 | tf_op jit(solution)/shard_map/ppermute | solution.py:329
  19.8 5.1 %collective-permute-start.8 = (bf16[2,64,256]{2,1,0:T(8,128)(2,1)S(1)}, bf16[2,64,256]{2,1,0:T(8,128)(2,1)S(1)}, u32[]{:S(2)}, u32[]{:S(2)}) collective-permute-start(bf16[2,64,256]{2,1,0:T(8,128)(2,1)S(1)} %pad_maximum_fusion.refs_12_.refs_0_), channel_id=1, source_target_pairs={{0,3},{1,0},{2,1},{3,2},{4,7},{5,4},{6,5},{7,6},{8,11},{9,8},{10,9... | collective-permute-start | bytes 196616 | tf_op jit(solution)/shard_map/ppermute | solution.py:329
  21.4 5.7 %collective-permute-start.7 = (bf16[2,64,256]{2,1,0:T(8,128)(2,1)S(1)}, bf16[2,64,256]{2,1,0:T(8,128)(2,1)S(1)}, u32[]{:S(2)}, u32[]{:S(2)}) collective-permute-start(bf16[2,64,256]{2,1,0:T(8,128)(2,1)S(1)} %pad_maximum_fusion.refs_12_.refs_0_), channel_id=1, source_target_pairs={{0,2},{1,3},{2,0},{3,1},{4,6},{5,7},{6,4},{7,5},{8,10},{9,11},{10,... | collective-permute-start | bytes 196616 | tf_op jit(solution)/shard_map/ppermute | solution.py:329
  22.9 5.2 %collective-permute-start.6 = (bf16[2,64,256]{2,1,0:T(8,128)(2,1)S(1)}, bf16[2,64,256]{2,1,0:T(8,128)(2,1)S(1)}, u32[]{:S(2)}, u32[]{:S(2)}) collective-permute-start(bf16[2,64,256]{2,1,0:T(8,128)(2,1)S(1)} %pad_maximum_fusion.refs_12_.refs_0_), channel_id=1, source_target_pairs={{0,1},{1,2},{2,3},{3,0},{4,5},{5,6},{6,7},{7,4},{8,9},{9,10},{10,1... | collective-permute-start | bytes 196616 | tf_op jit(solution)/shard_map/ppermute | solution.py:329
  23.2 18.3 %collective-permute-start.1 = (bf16[64,1024]{1,0:T(8,128)(2,1)S(1)}, bf16[64,1024]{1,0:T(8,128)(2,1)S(1)}, u32[]{:S(2)}, u32[]{:S(2)}) collective-permute-start(bf16[64,1024]{1,0:T(8,128)(2,1)S(1)} %get-tuple-element.55), channel_id=1, source_target_pairs={{0,2},{1,3},{2,0},{3,1},{4,6},{5,7},{6,4},{7,5},{8,10},{9,11},{10,... | collective-permute-start | bytes 393224 | tf_op jit(solution)/shard_map/ppermute | solution.py:329
  25.6 16.0 %collective-permute-start.2 = (bf16[64,1024]{1,0:T(8,128)(2,1)S(1)}, bf16[64,1024]{1,0:T(8,128)(2,1)S(1)}, u32[]{:S(2)}, u32[]{:S(2)}) collective-permute-start(bf16[64,1024]{1,0:T(8,128)(2,1)S(1)} %get-tuple-element.56), channel_id=1, source_target_pairs={{0,3},{1,0},{2,1},{3,2},{4,7},{5,4},{6,5},{7,6},{8,11},{9,8},{10,9... | collective-permute-start | bytes 393224 | tf_op jit(solution)/shard_map/ppermute | solution.py:329
  27.0 14.5 %collective-permute-start.3 = (bf16[64,1024]{1,0:T(8,128)(2,1)S(1)}, bf16[64,1024]{1,0:T(8,128)(2,1)S(1)}, u32[]{:S(2)}, u32[]{:S(2)}) collective-permute-start(bf16[64,1024]{1,0:T(8,128)(2,1)S(1)} %get-tuple-element.58), channel_id=1, source_target_pairs={{0,1},{1,2},{2,3},{3,0},{4,5},{5,6},{6,7},{7,4},{8,9},{9,10},{10,1... | collective-permute-start | bytes 393224 | tf_op jit(solution)/shard_map/ppermute | solution.py:329
  28.7 12.8 %collective-permute-start.4 = (bf16[64,1024]{1,0:T(8,128)(2,1)S(1)}, bf16[64,1024]{1,0:T(8,128)(2,1)S(1)}, u32[]{:S(2)}, u32[]{:S(2)}) collective-permute-start(bf16[64,1024]{1,0:T(8,128)(2,1)S(1)} %get-tuple-element.59), channel_id=1, source_target_pairs={{0,2},{1,3},{2,0},{3,1},{4,6},{5,7},{6,4},{7,5},{8,10},{9,11},{10,... | collective-permute-start | bytes 393224 | tf_op jit(solution)/shard_map/ppermute | solution.py:329
  29.4 12.1 %collective-permute-start.5 = (bf16[64,1024]{1,0:T(8,128)(2,1)S(1)}, bf16[64,1024]{1,0:T(8,128)(2,1)S(1)}, u32[]{:S(2)}, u32[]{:S(2)}) collective-permute-start(bf16[64,1024]{1,0:T(8,128)(2,1)S(1)} %get-tuple-element.60), channel_id=1, source_target_pairs={{0,3},{1,0},{2,1},{3,2},{4,7},{5,4},{6,5},{7,6},{8,11},{9,8},{10,9... | collective-permute-start | bytes 393224 | tf_op jit(solution)/shard_map/ppermute | solution.py:329
  73.1 6.0 %collective-permute-start.9 = (bf16[64,1024]{1,0:T(8,128)(2,1)S(1)}, bf16[64,1024]{1,0:T(8,128)(2,1)S(1)}, u32[]{:S(2)}, u32[]{:S(2)}) collective-permute-start(bf16[64,1024]{1,0:T(8,128)(2,1)S(1)} %get-tuple-element.69), channel_id=1, source_target_pairs={{0,1},{1,2},{2,3},{3,0},{4,5},{5,6},{6,7},{7,4},{8,9},{9,10},{10,1... | collective-permute-start | bytes 393224 | tf_op jit(solution)/shard_map/ppermute | solution.py:329
  74.4 8.5 %collective-permute-start.10 = (bf16[64,1024]{1,0:T(8,128)(2,1)S(1)}, bf16[64,1024]{1,0:T(8,128)(2,1)S(1)}, u32[]{:S(2)}, u32[]{:S(2)}) collective-permute-start(bf16[64,1024]{1,0:T(8,128)(2,1)S(1)} %get-tuple-element.70), channel_id=1, source_target_pairs={{0,2},{1,3},{2,0},{3,1},{4,6},{5,7},{6,4},{7,5},{8,10},{9,11},{10,... | collective-permute-start | bytes 393224 | tf_op jit(solution)/shard_map/ppermute | solution.py:329
  76.9 6.0 %collective-permute-start.11 = (bf16[64,1024]{1,0:T(8,128)(2,1)S(1)}, bf16[64,1024]{1,0:T(8,128)(2,1)S(1)}, u32[]{:S(2)}, u32[]{:S(2)}) collective-permute-start(bf16[64,1024]{1,0:T(8,128)(2,1)S(1)} %get-tuple-element.71), channel_id=1, source_target_pairs={{0,3},{1,0},{2,1},{3,2},{4,7},{5,4},{6,5},{7,6},{8,11},{9,8},{10,9... | collective-permute-start | bytes 393224 | tf_op jit(solution)/shard_map/ppermute | solution.py:329
  85.0 6.5 %collective-permute-start.12 = (bf16[64,1536]{1,0:T(8,128)(2,1)S(1)}, bf16[64,1536]{1,0:T(8,128)(2,1)S(1)}, u32[]{:S(2)}, u32[]{:S(2)}) collective-permute-start(bf16[64,1536]{1,0:T(8,128)(2,1)S(1)} %get-tuple-element.85), channel_id=1, source_target_pairs={{0,1},{1,2},{2,3},{3,0},{4,5},{5,6},{6,7},{7,4},{8,9},{9,10},{10,1... | collective-permute-start | bytes 589832 | tf_op jit(solution)/shard_map/ppermute | solution.py:329
  86.2 10.1 %collective-permute-start.13 = (bf16[64,1536]{1,0:T(8,128)(2,1)S(1)}, bf16[64,1536]{1,0:T(8,128)(2,1)S(1)}, u32[]{:S(2)}, u32[]{:S(2)}) collective-permute-start(bf16[64,1536]{1,0:T(8,128)(2,1)S(1)} %get-tuple-element.86), channel_id=1, source_target_pairs={{0,2},{1,3},{2,0},{3,1},{4,6},{5,7},{6,4},{7,5},{8,10},{9,11},{10,... | collective-permute-start | bytes 589832 | tf_op jit(solution)/shard_map/ppermute | solution.py:329
  88.3 8.0 %collective-permute-start.14 = (bf16[64,1536]{1,0:T(8,128)(2,1)S(1)}, bf16[64,1536]{1,0:T(8,128)(2,1)S(1)}, u32[]{:S(2)}, u32[]{:S(2)}) collective-permute-start(bf16[64,1536]{1,0:T(8,128)(2,1)S(1)} %get-tuple-element.87), channel_id=1, source_target_pairs={{0,3},{1,0},{2,1},{3,2},{4,7},{5,4},{6,5},{7,6},{8,11},{9,8},{10,9... | collective-permute-start | bytes 589832 | tf_op jit(solution)/shard_map/ppermute | solution.py:329
  97.0 18.6 %all-to-all-start.1 = ((f32[64,4,128]{2,1,0:T(4,128)}), f32[64,4,128]{2,1,0:T(4,128)S(1)}, u32[]{:S(2)}, u32[]{:S(2)}) async-start(f32[64,4,128]{2,1,0:T(4,128)} %slices.1), calls=%async_computation.1 | async-start | bytes 262144 | tf_op jit(solution)/shard_map/all_to_all | solution.py:379
  116.3 58.9 %all-to-all-start.2 = ((bf16[64,136,128]{2,1,0:T(8,128)(2,1)}), bf16[64,136,128]{2,1,0:T(8,128)(2,1)S(1)}, u32[]{:S(2)}, u32[]{:S(2)}) async-start(bf16[64,136,128]{2,1,0:T(8,128)(2,1)} %slice_send.1), calls=%async_computation.2 | async-start | bytes 4456448 | tf_op jit(solution)/shard_map/all_to_all | solution.py:398
  121.3 9.0 %collective-permute-start.18 = (bf16[64,1024]{1,0:T(8,128)(2,1)}, bf16[64,1024]{1,0:T(8,128)(2,1)S(1)}, u32[]{:S(2)}, u32[]{:S(2)}) collective-permute-start(bf16[64,1024]{1,0:T(8,128)(2,1)} %get-tuple-element.94), channel_id=1, source_target_pairs={{0,3},{1,0},{2,1},{3,2},{4,7},{5,4},{6,5},{7,6},{8,11},{9,8},{10,9... | collective-permute-start | bytes 393224 | tf_op jit(solution)/shard_map/ppermute | solution.py:329
  125.2 19.8 %collective-permute-start.15 = (f32[64,1024]{1,0:T(8,128)S(1)}, f32[64,1024]{1,0:T(8,128)S(1)}, u32[]{:S(2)}, u32[]{:S(2)}) collective-permute-start(f32[64,1024]{1,0:T(8,128)S(1)} %get-tuple-element.90), channel_id=1, source_target_pairs={{0,1},{1,2},{2,3},{3,0},{4,5},{5,6},{6,7},{7,4},{8,9},{9,10},{10,1... | collective-permute-start | bytes 786440 | tf_op jit(solution)/shard_map/ppermute | solution.py:329
  125.3 19.7 %collective-permute-start.16 = (f32[64,1024]{1,0:T(8,128)S(1)}, f32[64,1024]{1,0:T(8,128)S(1)}, u32[]{:S(2)}, u32[]{:S(2)}) collective-permute-start(f32[64,1024]{1,0:T(8,128)S(1)} %get-tuple-element.91), channel_id=1, source_target_pairs={{0,2},{1,3},{2,0},{3,1},{4,6},{5,7},{6,4},{7,5},{8,10},{9,11},{10,... | collective-permute-start | bytes 786440 | tf_op jit(solution)/shard_map/ppermute | solution.py:329
  127.1 18.0 %collective-permute-start.17 = (f32[64,1024]{1,0:T(8,128)S(1)}, f32[64,1024]{1,0:T(8,128)S(1)}, u32[]{:S(2)}, u32[]{:S(2)}) collective-permute-start(f32[64,1024]{1,0:T(8,128)S(1)} %get-tuple-element.92), channel_id=1, source_target_pairs={{0,3},{1,0},{2,1},{3,2},{4,7},{5,4},{6,5},{7,6},{8,11},{9,8},{10,9... | collective-permute-start | bytes 786440 | tf_op jit(solution)/shard_map/ppermute | solution.py:329
  128.2 13.2 %collective-permute-start.19 = (bf16[64,1024]{1,0:T(8,128)(2,1)}, bf16[64,1024]{1,0:T(8,128)(2,1)S(1)}, u32[]{:S(2)}, u32[]{:S(2)}) collective-permute-start(bf16[64,1024]{1,0:T(8,128)(2,1)} %get-tuple-element.95), channel_id=1, source_target_pairs={{0,2},{1,3},{2,0},{3,1},{4,6},{5,7},{6,4},{7,5},{8,10},{9,11},{10,... | collective-permute-start | bytes 393224 | tf_op jit(solution)/shard_map/ppermute | solution.py:329
  130.3 14.7 %collective-permute-start.20 = (bf16[64,1024]{1,0:T(8,128)(2,1)}, bf16[64,1024]{1,0:T(8,128)(2,1)S(1)}, u32[]{:S(2)}, u32[]{:S(2)}) collective-permute-start(bf16[64,1024]{1,0:T(8,128)(2,1)} %get-tuple-element.96), channel_id=1, source_target_pairs={{0,1},{1,2},{2,3},{3,0},{4,5},{5,6},{6,7},{7,4},{8,9},{9,10},{10,1... | collective-permute-start | bytes 393224 | tf_op jit(solution)/shard_map/ppermute | solution.py:329
  (31 other events, 347.6 us)

commit v5 on v3

--- a/solution.py
+++ b/solution.py
@@ -183,14 +183,13 @@
     leave(grad_ref, grad_hbm, grad_sem)
     for which, full in ((0, full_feats), (1, full_agg)):
         prod_ref[...] = dot(grad_ref[...], full[...], 1, 1)
-        for group in range(rows // 4):
-            for half in range(2):
-                index = which * 32 + group * 2 + half
-                for k in range(reps):
-                    start = k * rows + group * 4
-                    slices_ref[index, 4 * k : 4 * k + 4, :] = prod_ref[
-                        start : start + 4, half * TILE : (half + 1) * TILE
-                    ].astype(BF16)
+        wide = prod_ref.shape[1]
+        for part in range(slices_ref.shape[0]):
+            for k in range(reps):
+                start = k * rows + 8 * part
+                slices_ref[part, 8 * k : 8 * k + 8, which * wide : (which + 1) * wide] = prod_ref[
+                    start : start + 8, :
+                ].astype(BF16)
     leave(slices_ref, slices_hbm, slices_sem)
     w_neigh = jnp.concatenate([wts[k][1] for k in range(reps)], axis=0)
     back_ref[...] = dot(w_neigh, grad_ref[...], 0, 0)
@@ -217,16 +216,38 @@
 def slice_sum_body(got_ref, *outs):
     total = jnp.sum(got_ref[...].astype(F32), axis=0)
     for k in range(len(outs)):
-        outs[k][...] = total[4 * k : 4 * k + 4, :]
-
-
-def slice_send_body(*refs):
-    parts, out_ref = refs[:4], refs[-1]
-    total = parts[0][...] + parts[1][...] + parts[2][...] + parts[3][...]
-    high = total.astype(BF16)
-    low = (total - high.astype(F32)).astype(BF16)
-    both = jnp.concatenate([high.astype(F32), low.astype(F32)], axis=0).astype(BF16)
-    out_ref[...] = jnp.broadcast_to(both[None], out_ref.shape)
+        outs[k][...] = total[8 * k : 8 * k + 8, :]
+
+
+def add_body(*refs):
+    total = refs[0][...]
+    for ref in refs[1:-1]:
+        total = total + ref[...]
+    refs[-1][...] = total
+
+
+def stack_body(*refs):
+    rows = refs[0].shape[0]
+    for k, ref in enumerate(refs[:-1]):
+        refs[-1][rows * k : rows * (k + 1), :] = ref[...]
+
+
+def join_body(place_ref, mine_ref, own_ref, other_ref, w_self_ref, w_neigh_ref):
+    full = w_self_ref.shape[1]
+    core = lax.rem(place_ref[1], 2)
+    place = lax.rem(lax.div(place_ref[1], 2), 8)
+    sign = 1 - 2 * core
+
+    def put(place, piece):
+        rows = lanes(place, 8)
+        w_self_ref[rows, :] = piece[:, :full]
+        w_neigh_ref[rows, :] = piece[:, full:]
+
+    put(place, mine_ref[...])
+    for k in range(1, 5):
+        rows = slice(8 * (k - 1), 8 * k)
+        put(lax.rem(place + 8 - sign * k, 8), own_ref[rows, :])
+        put(lax.rem(place + 8 + sign * k, 8), other_ref[rows, :])
 
 
 def gather_lanes(ref, pieces, rep):
@@ -247,7 +268,7 @@
     def copy(step):
         rows = pl.ds(step * STEP, STEP)
         return pltpu.make_async_copy(
-            buf_ref.at[rows], out_ref.at[rows, pl.ds(0, 2 * chans)], out_sems.at[step]
+            buf_ref.at[rows], out_ref.at[rows], out_sems.at[step]
         )
 
     @pl.loop(0, parts // STEP)
@@ -285,7 +306,7 @@
                 acc_ref[:, lanes(cols_ref[link, row], TILE)] += term
 
 
-def home_body(send_ref, got_ref, near_acc_hbm, grad_ref, w_self_ref, w_neigh_ref, acc_ref, near_acc_ref, sem):
+def home_body(send_ref, got_ref, near_acc_hbm, grad_ref, acc_ref, near_acc_ref, sem):
     chans = acc_ref.shape[0]
     parts = got_ref.shape[0]
     load = pltpu.make_async_copy(near_acc_hbm, near_acc_ref, sem)
@@ -295,10 +316,6 @@
         for slot in range(2):
             block = send_ref[slot, item]
             acc_ref[:, lanes(block, TILE)] += got_ref[item, slot * chans : (slot + 1) * chans, :].astype(F32)
-        both = got_ref[item, 2 * chans : 2 * chans + 8, :].astype(F32)
-        weight_ref = (w_self_ref, w_neigh_ref)[item // (parts // 2)]
-        group, half = item % (parts // 2) // 2, item % 2
-        weight_ref[4 * group : 4 * group + 4, half * TILE : (half + 1) * TILE] = both[0:4] + both[4:8]
     load.wait()
     grad_ref[...] = (near_acc_ref[...] + acc_ref[...]).astype(BF16)
 
@@ -313,7 +330,7 @@
     rows = remote_rows[0].T
     sends = send_list[0].T
     cols = local_cols.T
-    rep = lax.axis_index("rep").astype(jnp.int32).reshape(1)
+    rep = jnp.stack([lax.axis_index("rep"), lax.axis_index("dom")]).astype(jnp.int32)
     piece = shape((chans, width), BF16)
     piece32 = shape((chans, width), F32)
     sems = pltpu.SemaphoreType.DMA((parts // STEP,))
@@ -324,6 +341,16 @@
     def shift(value, by):
         return lax.ppermute(value, "rep", [(i, (i + by) % reps) for i in range(reps)])
 
+    def move(value, dy, dz, dc, turn=False):
+        pairs = [
+            ((y * 8 + z) * 2 + c, ((y + dy) % 4 * 8 + (z + (-dz if turn and c else dz)) % 8) * 2 + (c + dc) % 2)
+            for y in range(4)
+            for z in range(8)
+            for c in range(2)
+        ]
+        return lax.ppermute(value, "dom", pairs)
+
+    z_groups = [[(y * 8 + z) * 2 + c for z in range(8)] for y in range(4) for c in range(2)]
     def exchange(pieces, sign=1):
         return [pieces[0]] + [shift(pieces[k], (sign * k) % reps) for k in range(1, reps)]
 
@@ -360,41 +387,34 @@
             dense_body, (rep,), (*agg_in, *feats_in, *cot_in, *weights_in, div),
             [piece] * reps
             + [in_hbm((chans, width), BF16)] * reps
-            + [in_hbm((full, width), BF16), in_hbm((parts, 4 * reps, TILE), BF16)],
+            + [in_hbm((full, width), BF16), in_hbm((8, 8 * reps, 2 * full), BF16)],
             [
                 pltpu.VMEM((full, width), F32), pltpu.VMEM((full, width), BF16), pltpu.VMEM((full, width), BF16),
                 pltpu.VMEM((full, width), BF16), pltpu.VMEM((reps, chans, width), BF16), pltpu.VMEM((full, full), F32),
-                pltpu.VMEM((parts, 4 * reps, TILE), BF16), pltpu.SemaphoreType.DMA((reps,)), sem, sem,
+                pltpu.VMEM((8, 8 * reps, 2 * full), BF16), pltpu.SemaphoreType.DMA((reps,)), sem, sem,
             ],
             3.0, (), range(reps, 2 * reps + 2),
         )
     scaled, out_pieces, grad_pre, slices = dense[:reps], dense[reps : 2 * reps], dense[2 * reps], dense[2 * reps + 1]
     scaled_in = exchange(scaled)
-    slices_in = lax.all_to_all(slices, "dom", split_axis=0, concat_axis=0, tiled=True)
+    slices_in = lax.all_to_all(slices, "dom", 0, 0, axis_index_groups=z_groups, tiled=True)
     with jax.named_scope("far_back"):
         far_back = call(
-            far_back_body, (rep, rows), (*scaled_in, far_tiles), in_hbm((parts, 2 * chans + 8, TILE), BF16),
+            far_back_body, (rep, rows), (*scaled_in, far_tiles), in_hbm((parts, 2 * chans, TILE), BF16),
             [
                 pltpu.VMEM((chans, nodes), BF16), pltpu.VMEM((parts, 2 * chans, TILE), BF16), tile_buf, sems, sems,
             ],
             2.0, (reps,), (0,),
         )
     slices_in, far_back = lax.optimization_barrier((slices_in, far_back))
-    with jax.named_scope("slice_sum"):
-        sums = call(slice_sum_body, (), (slices_in,), [shape((4, TILE), F32)] * reps)
-    sums_in = exchange(sums, -1)
-    with jax.named_scope("slice_send"):
-        sending = pl.pallas_call(
-            slice_send_body,
-            grid=(1,),
-            in_specs=[IN_VMEM] * reps + [IN_HBM],
-            out_shape=in_hbm(far_back.shape, BF16),
-            out_specs=pl.BlockSpec((parts, 8, TILE), lambda i: (0, 2 * chans // 8, 0)),
-            input_output_aliases={reps: 0},
-            compiler_params=pltpu.CompilerParams(vmem_limit_bytes=VMEM_BYTES),
-        )(*sums_in, pinned(far_back))
-    returned = lax.all_to_all(sending, "dom", split_axis=0, concat_axis=0, tiled=True)
-
+    returned = lax.all_to_all(far_back, "dom", split_axis=0, concat_axis=0, tiled=True)
+
+    with jax.named_scope("slice_sums"):
+        slice_shape = shape((8, 2 * full), F32)
+        sums = call(slice_sum_body, (), (slices_in,), [slice_shape] * reps)
+        total = call(add_body, (), exchange(sums, -1), slice_shape)
+        total = call(add_body, (), (total, move(total, 0, 0, 1)), slice_shape)
+        total = call(add_body, (), (total, *[move(total, dy, 0, 0) for dy in range(1, 4)]), slice_shape)
     with jax.named_scope("back"):
         back_self = call(
             back_body, (rep,), (*weights_in, grad_pre), [piece32] * reps, [pltpu.VMEM((full, width), F32)], 1.0
@@ -406,12 +426,19 @@
             near_back_body, (rep, cols), (*scaled_in, *back_in, *out_in, local_tiles),
             [shape((chans, nodes), F32), shape((chans, nodes), BF16)], [pltpu.VMEM((chans, nodes), BF16)], 2.0,
         )
+    total, near_back, output = lax.optimization_barrier((total, near_back, output))
+    with jax.named_scope("spread"):
+        own = call(
+            stack_body, (), [move(total, 0, dz, 0, True) for dz in range(1, 5)], shape((32, 2 * full), F32), (), 0.5
+        )
+        other = move(own, 0, 0, 1)
     with jax.named_scope("home"):
-        grad_feats, wg_self, wg_neigh = call(
-            home_body, (sends,), (returned, near_back),
-            [shape((chans, nodes), BF16), shape((chans, full), F32), shape((chans, full), F32)],
-            [wide32, wide32, sem], 3.0, (1,),
-        )
+        grad_feats = call(
+            home_body, (sends,), (returned, near_back), shape((chans, nodes), BF16), [wide32, wide32, sem], 3.0, (1,)
+        )
+    with jax.named_scope("join"):
+        other, grad_feats = lax.optimization_barrier((other, grad_feats))
+        wg_self, wg_neigh = call(join_body, (rep,), (total, own, other), [shape((chans, full), F32)] * 2)
     return output, grad_feats, wg_self.T, wg_neigh.T
 
 

time: 184 us -> 171 us (0.929)
  waiting for transfers between devices: 84.5 us -> 55.6 us
  starting transfers between devices: 61.3 us -> 77.6 us
  Pallas kernels: 28.2 us -> 30.3 us
  local copies, waits for them, and re-layouts: 8.07 us -> 5.97 us
    all_to_all x2, waiting for transfers between devices: 27.9 us -> 0.01 us  [the longest x1 0.01 us: local(): lax.all_to_all(slices, 'dom', 0, 0, axis_index_groups=z_groups, tiled=True)]
    ppermute x0 -> x9, starting transfers between devices: none -> 19.7 us  [move(): return lax.ppermute(value, 'dom', pairs)]
    ppermute x24, waiting for transfers between devices: 29.1 us -> 19.7 us  [shift(): lax.ppermute(value, 'rep', [(i, (i + by) % reps) for i in range(reps)])]
    ppermute x0 -> x9, waiting for transfers between devices: none -> 9.04 us  [move(): return lax.ppermute(value, 'dom', pairs)]
    all_to_all x2, starting transfers between devices: 19.2 us -> 15.3 us  [the longest x1 11.9 us: local(): lax.all_to_all(far_back, 'dom', split_axis=0, concat_axis=0, tiled=True)]
    pallas_call x10 -> x15, Pallas kernels: 27.5 us -> 30.3 us  [call(): pl.pallas_call(body, in_specs=[IN_SMEM] * len(scalars) + [IN_HBM if i in...]
    unnamed x68, local copies, waits for them, and re-layouts: 8.07 us -> 5.97 us
  transfers between devices with their start and end apart: 27 -> 36, of which waited for: 11 -> 12; matrix products, arithmetic and copies ran while one was open for 0% -> 0% of each run, Pallas kernels for 8% -> 11%
where the time goes in v5:
time: 171 us
  starting transfers between devices  77.6 us (45%)
  waiting for transfers between devices  55.6 us (33%)
  Pallas kernels  30.3 us (18%)
  local copies, waits for them, and re-layouts  5.97 us (3%)
    pallas_call x15, Pallas kernels, call(): pl.pallas_call(body, in_specs=[IN_SMEM] * len(scalars) + [IN_HBM if i in...  30.3 us
    ppermute x24, starting transfers between devices, shift(): lax.ppermute(value, 'rep', [(i, (i + by) % reps) for i in range(reps)])  29.4 us
    all_to_all x1, waiting for transfers between devices, local(): lax.all_to_all(outgoing, 'dom', split_axis=0, concat_axis=0, tiled=True)  26.8 us
    ppermute x24, waiting for transfers between devices, shift(): lax.ppermute(value, 'rep', [(i, (i + by) % reps) for i in range(reps)])  19.7 us
    ppermute x9, starting transfers between devices, move(): return lax.ppermute(value, 'dom', pairs)  19.7 us
    all_to_all x1, starting transfers between devices, local(): lax.all_to_all(outgoing, 'dom', split_axis=0, concat_axis=0, tiled=True)  13.3 us
    all_to_all x1, starting transfers between devices, local(): lax.all_to_all(far_back, 'dom', split_axis=0, concat_axis=0, tiled=True)  11.9 us
    ppermute x9, waiting for transfers between devices, move(): return lax.ppermute(value, 'dom', pairs)  9.04 us
  transfers between devices with their start and end apart: 36, of which 12 were waited for; matrix products, arithmetic and copies ran while one was open for 0% of the time, Pallas kernels for 11%

profile of v5, /device:TPU:1, one launch (start us, length us, event | category | flops | bytes accessed | tf_op | source)
XLA Modules:
  0.0 170.7 jit_solution(9039470696359288215)
XLA Ops:
  1.3 3.1 %pick.1 = bf16[64,128,128]{2,1,0:T(8,128)(2,1)} custom-call(s32[2,64]{1,0:T(2,128)S(1)} %bitcast.25, bf16[64,4096]{1,0:T(8,128)(2,1)} %feats_ref.3), custom_call_target="tpu_custom_call" | custom-call | flops 2200000000 | bytes 65536 | tf_op jit(solution)/shard_map/pick/pallas_call | solution.py:27
  4.4 13.3 %all-to-all-start = ((bf16[64,128,128]{2,1,0:T(8,128)(2,1)}), bf16[64,128,128]{2,1,0:T(8,128)(2,1)S(1)}, u32[]{:S(2)}, u32[]{:S(2)}) async-start(bf16[64,128,128]{2,1,0:T(8,128)(2,1)} %pick.1), calls=%async_computation | async-start | bytes 4194304 | tf_op jit(solution)/shard_map/all_to_all | solution.py:362
  33.4 7.0 %near.1 = (f32[64,4096]{1,0:T(8,128)S(1)}, f32[8,4096]{1,0:T(8,128)S(1)}, bf16[64,2,128,128]{3,2,1,0:T(8,128)(2,1)}) custom-call(s32[2,32]{1,0:T(2,128)S(1)} %bitcast.23, s32[2,64]{1,0:T(2,128)S(1)} %bitcast.20, bf16[64,4096]{1,0:T(8,128)(2,1)S(1)} %copy-done.4, bf16[32,2,128,128]{3,2,1,0:T(8,128)(2,1)S(1)} %copy-done.1, bf16[64,2,128,128]{3,2,1,0:T(8,128)(2,1)S(1)} %bitcast.19), custom_call_target="tpu_custom_call" | custom-call | flops 8800000000 | bytes 65536 | tf_op jit(solution)/shard_map/near/pallas_call | solution.py:27
  42.2 26.8 %all-to-all-done.got_ref = bf16[64,128,128]{2,1,0:T(8,128)(2,1)S(1)} async-done(((bf16[64,128,128]{2,1,0:T(8,128)(2,1)}), bf16[64,128,128]{2,1,0:T(8,128)(2,1)S(1)}, u32[]{:S(2)}, u32[]{:S(2)}) %all-to-all-start) | async-done | bytes 2097184 | tf_op jit(solution)/shard_map/all_to_all | solution.py:362
  69.0 4.1 %far.1 = (bf16[64,1024]{1,0:T(8,128)(2,1)S(1)}, bf16[64,1024]{1,0:T(8,128)(2,1)S(1)}, bf16[64,1024]{1,0:T(8,128)(2,1)S(1)}, bf16[64,1024]{1,0:T(8,128)(2,1)S(1)}) custom-call(s32[2]{0:T(128)S(1)} %pad_add_fusion.rep_ref.place_ref, s32[2,64]{1,0:T(2,128)S(1)} %bitcast.21, bf16[64,128,128]{2,1,0:T(8,128)(2,1)S(1)} %all-to-all-done.got_ref, ...), custom_call_target="tpu_custom_call" | custom-call | flops 6600000000 | bytes 65536 | tf_op jit(solution)/shard_map/far/pallas_call | solution.py:27
  74.5 2.5 %collective-permute-start.10 = (bf16[64,1024]{1,0:T(8,128)(2,1)S(1)}, bf16[64,1024]{1,0:T(8,128)(2,1)S(1)}, u32[]{:S(2)}, u32[]{:S(2)}) collective-permute-start(bf16[64,1024]{1,0:T(8,128)(2,1)S(1)} %get-tuple-element.81), channel_id=1, source_target_pairs={{0,2},{1,3},{2,0},{3,1},{4,6},{5,7},{6,4},{7,5},{8,10},{9,11},{10,... | collective-permute-start | bytes 393224 | tf_op jit(solution)/shard_map/ppermute | solution.py:342
  79.1 3.8 %collective-permute-done.10.refs_2_ = bf16[64,1024]{1,0:T(8,128)(2,1)S(1)} collective-permute-done((bf16[64,1024]{1,0:T(8,128)(2,1)S(1)}, bf16[64,1024]{1,0:T(8,128)(2,1)S(1)}, u32[]{:S(2)}, u32[]{:S(2)}) %collective-permute-start.10) | collective-permute-done | bytes 131104 | tf_op jit(solution)/shard_map/ppermute | solution.py:342
  83.0 2.7 %dense.1 = (bf16[64,1024]{1,0:T(8,128)(2,1)S(1)}, bf16[64,1024]{1,0:T(8,128)(2,1)S(1)}, bf16[64,1024]{1,0:T(8,128)(2,1)S(1)}, bf16[64,1024]{1,0:T(8,128)(2,1)S(1...) custom-call(s32[2]{0:T(128)S(1)} %pad_add_fusion.rep_ref.place_ref, ...), custom_call_target="tpu_custom_call" | custom-call | flops 3300000000 | bytes 65536 | tf_op jit(solution)/shard_map/dense/pallas_call | solution.py:27
  85.7 3.4 %all-to-all-start.1 = ((bf16[8,32,512]{2,1,0:T(8,128)(2,1)}), bf16[8,32,512]{2,1,0:T(8,128)(2,1)S(1)}, u32[]{:S(2)}, u32[]{:S(2)}) async-start(bf16[8,32,512]{2,1,0:T(8,128)(2,1)} %get-tuple-element.95), calls=%async_computation.1 | async-start | bytes 524288 | tf_op jit(solution)/shard_map/all_to_all | solution.py:400
  90.3 2.2 %collective-permute-start.13 = (bf16[64,1024]{1,0:T(8,128)(2,1)S(1)}, bf16[64,1024]{1,0:T(8,128)(2,1)S(1)}, u32[]{:S(2)}, u32[]{:S(2)}) collective-permute-start(bf16[64,1024]{1,0:T(8,128)(2,1)S(1)} %get-tuple-element.98), channel_id=1, source_target_pairs={{0,2},{1,3},{2,0},{3,1},{4,6},{5,7},{6,4},{7,5},{8,10},{9,11},{10,... | collective-permute-start | bytes 393224 | tf_op jit(solution)/shard_map/ppermute | solution.py:342
  94.2 3.0 %collective-permute-done.13.s2.refs_2_ = bf16[64,1024]{1,0:T(8,128)(2,1)S(1)} collective-permute-done((bf16[64,1024]{1,0:T(8,128)(2,1)S(1)}, bf16[64,1024]{1,0:T(8,128)(2,1)S(1)}, u32[]{:S(2)}, u32[]{:S(2)}) %collective-permute-start.13) | collective-permute-done | bytes 131104 | tf_op jit(solution)/shard_map/ppermute | solution.py:342
  97.3 4.7 %far_back.1 = bf16[64,128,128]{2,1,0:T(8,128)(2,1)} custom-call(s32[2]{0:T(128)S(1)} %pad_add_fusion.rep_ref.place_ref, s32[2,64]{1,0:T(2,128)S(1)} %bitcast.22, bf16[64,1024]{1,0:T(8,128)(2,1)S(1)} %get-tuple-element.96.s0.refs_0_, bf16[64,1024]{1,0:T(8,128)(2,1)S(1)} %collective-permute-done.12.s1.refs_1_, ...), custom_call_target="tpu_custom_call" | custom-call | flops 2200000000 | bytes 65536 | tf_op jit(solution)/shard_map/far_back/pallas_call | solution.py:27
  102.0 11.9 %all-to-all-start.2 = ((bf16[64,128,128]{2,1,0:T(8,128)(2,1)}), bf16[64,128,128]{2,1,0:T(8,128)(2,1)S(1)}, u32[]{:S(2)}, u32[]{:S(2)}) async-start(bf16[64,128,128]{2,1,0:T(8,128)(2,1)} %far_back.1), calls=%async_computation.2 | async-start | bytes 4194304 | tf_op jit(solution)/shard_map/all_to_all | solution.py:410
  113.9 2.5 %collective-permute-start.25 = (bf16[64,1024]{1,0:T(8,128)(2,1)S(1)}, bf16[64,1024]{1,0:T(8,128)(2,1)S(1)}, u32[]{:S(2)}, u32[]{:S(2)}) collective-permute-start(bf16[64,1024]{1,0:T(8,128)(2,1)S(1)} %copy-done.33), channel_id=1, source_target_pairs={{0,3},{1,0},{2,1},{3,2},{4,7},{5,4},{6,5},{7,6},{8,11},{9,8},{10,9... | collective-permute-start | bytes 393224 | tf_op jit(solution)/shard_map/ppermute | solution.py:342
  120.5 2.2 %collective-permute-start.23 = (f32[64,1024]{1,0:T(8,128)S(1)}, f32[64,1024]{1,0:T(8,128)S(1)}, u32[]{:S(2)}, u32[]{:S(2)}) collective-permute-start(f32[64,1024]{1,0:T(8,128)S(1)} %get-tuple-element.108), channel_id=1, source_target_pairs={{0,2},{1,3},{2,0},{3,1},{4,6},{5,7},{6,4},{7,5},{8,10},{9,11},{10,... | collective-permute-start | bytes 786440 | tf_op jit(solution)/shard_map/ppermute | solution.py:342
  124.8 2.5 %collective-permute-start.18 = (f32[8,512]{1,0:T(8,128)S(1)}, f32[8,512]{1,0:T(8,128)S(1)}, u32[]{:S(2)}, u32[]{:S(2)}) collective-permute-start(f32[8,512]{1,0:T(8,128)S(1)} %slice_sums.5.refs_0_), channel_id=1, source_target_pairs={{0,4},{4,0},{8,12},{12,8},{16,20},{20,16},{24,28},{28,24},{32,36},... | collective-permute-start | bytes 49160 | tf_op jit(solution)/shard_map/slice_sums/ppermute | solution.py:351
  128.1 8.4 %collective-permute-done.26.refs_10_ = bf16[64,1024]{1,0:T(8,128)(2,1)S(1)} collective-permute-done((bf16[64,1024]{1,0:T(8,128)(2,1)S(1)}, bf16[64,1024]{1,0:T(8,128)(2,1)S(1)}, u32[]{:S(2)}, u32[]{:S(2)}) %collective-permute-start.26) | collective-permute-done | bytes 131104 | tf_op jit(solution)/shard_map/ppermute | solution.py:342
  136.5 2.9 %collective-permute-start.21 = (f32[8,512]{1,0:T(8,128)S(1)}, f32[8,512]{1,0:T(8,128)S(1)}, u32[]{:S(2)}, u32[]{:S(2)}) collective-permute-start(f32[8,512]{1,0:T(8,128)S(1)} %slice_sums.6.refs_0_), channel_id=1, source_target_pairs={{0,192},{4,196},{8,200},{12,204},{16,208},{20,212},{24,216},{28,22... | collective-permute-start | bytes 49160 | tf_op jit(solution)/shard_map/slice_sums/ppermute | solution.py:351
  140.9 3.0 %collective-permute-start.20 = (f32[8,512]{1,0:T(8,128)S(1)}, f32[8,512]{1,0:T(8,128)S(1)}, u32[]{:S(2)}, u32[]{:S(2)}) collective-permute-start(f32[8,512]{1,0:T(8,128)S(1)} %slice_sums.6.refs_0_), channel_id=1, source_target_pairs={{0,128},{4,132},{8,136},{12,140},{16,144},{20,148},{24,152},{28,15... | collective-permute-start | bytes 49160 | tf_op jit(solution)/shard_map/slice_sums/ppermute | solution.py:351
  144.3 3.2 %near_back.1 = (f32[64,4096]{1,0:T(8,128)S(1)}, bf16[64,4096]{1,0:T(8,128)(2,1)}) custom-call(s32[2]{0:T(128)S(1)} %pad_add_fusion.rep_ref.place_ref, s32[2,32]{1,0:T(2,128)S(1)} %bitcast.24, bf16[64,1024]{1,0:T(8,128)(2,1)S(1)} %copy-done.18, bf16[64,1024]{1,0:T(8,128)(2,1)S(1)} %collective-permute-done.12.s1.refs_1_, ...), custom_call_target="tpu_custom_call" | custom-call | flops 2200000000 | bytes 65536 | tf_op jit(solution)/shard_map/near_back/pallas_call | solution.py:27
  148.2 5.3 %collective-permute-start.31 = (f32[8,512]{1,0:T(8,128)S(1)}, f32[8,512]{1,0:T(8,128)S(1)}, u32[]{:S(2)}, u32[]{:S(2)}) collective-permute-start(f32[8,512]{1,0:T(8,128)S(1)} %slice_sums.7.mine_ref), channel_id=1, source_target_pairs={{0,32},{4,36},{8,40},{12,44},{16,48},{20,52},{24,56},{28,60},{32,0... | collective-permute-start | bytes 49160 | tf_op jit(solution)/shard_map/spread/ppermute | solution.py:351
  153.8 2.6 %collective-permute-start.29 = (f32[8,512]{1,0:T(8,128)S(1)}, f32[8,512]{1,0:T(8,128)S(1)}, u32[]{:S(2)}, u32[]{:S(2)}) collective-permute-start(f32[8,512]{1,0:T(8,128)S(1)} %slice_sums.7.mine_ref), channel_id=1, source_target_pairs={{0,16},{4,52},{8,24},{12,60},{16,32},{20,4},{24,40},{28,12},{32,48... | collective-permute-start | bytes 49160 | tf_op jit(solution)/shard_map/spread/ppermute | solution.py:351
  157.8 7.6 %collective-permute-done.31.refs_3_ = f32[8,512]{1,0:T(8,128)S(1)} collective-permute-done((f32[8,512]{1,0:T(8,128)S(1)}, f32[8,512]{1,0:T(8,128)S(1)}, u32[]{:S(2)}, u32[]{:S(2)}) %collective-permute-start.31) | collective-permute-done | bytes 16416 | tf_op jit(solution)/shard_map/spread/ppermute | solution.py:351
  166.8 2.7 %home.1 = bf16[64,4096]{1,0:T(8,128)(2,1)} custom-call(s32[2,64]{1,0:T(2,128)S(1)} %bitcast.26, bf16[64,128,128]{2,1,0:T(8,128)(2,1)S(1)} %all-to-all-done.2.got_ref, f32[64,4096]{1,0:T(8,128)} %copy-done.19), custom_call_target="tpu_custom_call" | custom-call | flops 3300000000 | bytes 65536 | tf_op jit(solution)/shard_map/home/pallas_call | solution.py:27
  (133 shorter events, 38.1 us)
Async XLA Ops:
  4.4 64.6 %all-to-all-start = ((bf16[64,128,128]{2,1,0:T(8,128)(2,1)}), bf16[64,128,128]{2,1,0:T(8,128)(2,1)S(1)}, u32[]{:S(2)}, u32[]{:S(2)}) async-start(bf16[64,128,128]{2,1,0:T(8,128)(2,1)} %pick.1), calls=%async_computation | async-start | bytes 4194304 | tf_op jit(solution)/shard_map/all_to_all | solution.py:362
  19.1 11.5 %collective-permute-start = (bf16[64,1024]{1,0:T(8,128)(2,1)S(1)}, bf16[64,1024]{1,0:T(8,128)(2,1)S(1)}, u32[]{:S(2)}, u32[]{:S(2)}) collective-permute-start(bf16[64,1024]{1,0:T(8,128)(2,1)S(1)} %get-tuple-element.65), channel_id=1, source_target_pairs={{0,1},{1,2},{2,3},{3,0},{4,5},{5,6},{6,7},{7,4},{8,9},{9,10},{10,1... | collective-permute-start | bytes 393224 | tf_op jit(solution)/shard_map/ppermute | solution.py:342
  23.8 18.4 %collective-permute-start.1 = (bf16[64,1024]{1,0:T(8,128)(2,1)S(1)}, bf16[64,1024]{1,0:T(8,128)(2,1)S(1)}, u32[]{:S(2)}, u32[]{:S(2)}) collective-permute-start(bf16[64,1024]{1,0:T(8,128)(2,1)S(1)} %get-tuple-element.66), channel_id=1, source_target_pairs={{0,2},{1,3},{2,0},{3,1},{4,6},{5,7},{6,4},{7,5},{8,10},{9,11},{10,... | collective-permute-start | bytes 393224 | tf_op jit(solution)/shard_map/ppermute | solution.py:342
  25.5 16.6 %collective-permute-start.2 = (bf16[64,1024]{1,0:T(8,128)(2,1)S(1)}, bf16[64,1024]{1,0:T(8,128)(2,1)S(1)}, u32[]{:S(2)}, u32[]{:S(2)}) collective-permute-start(bf16[64,1024]{1,0:T(8,128)(2,1)S(1)} %get-tuple-element.67), channel_id=1, source_target_pairs={{0,3},{1,0},{2,1},{3,2},{4,7},{5,4},{6,5},{7,6},{8,11},{9,8},{10,9... | collective-permute-start | bytes 393224 | tf_op jit(solution)/shard_map/ppermute | solution.py:342
  28.2 14.0 %collective-permute-start.3 = (bf16[64,1024]{1,0:T(8,128)(2,1)S(1)}, bf16[64,1024]{1,0:T(8,128)(2,1)S(1)}, u32[]{:S(2)}, u32[]{:S(2)}) collective-permute-start(bf16[64,1024]{1,0:T(8,128)(2,1)S(1)} %get-tuple-element.69), channel_id=1, source_target_pairs={{0,1},{1,2},{2,3},{3,0},{4,5},{5,6},{6,7},{7,4},{8,9},{9,10},{10,1... | collective-permute-start | bytes 393224 | tf_op jit(solution)/shard_map/ppermute | solution.py:342
  29.3 12.9 %collective-permute-start.4 = (bf16[64,1024]{1,0:T(8,128)(2,1)S(1)}, bf16[64,1024]{1,0:T(8,128)(2,1)S(1)}, u32[]{:S(2)}, u32[]{:S(2)}) collective-permute-start(bf16[64,1024]{1,0:T(8,128)(2,1)S(1)} %get-tuple-element.70), channel_id=1, source_target_pairs={{0,2},{1,3},{2,0},{3,1},{4,6},{5,7},{6,4},{7,5},{8,10},{9,11},{10,... | collective-permute-start | bytes 393224 | tf_op jit(solution)/shard_map/ppermute | solution.py:342
  30.6 11.6 %collective-permute-start.5 = (bf16[64,1024]{1,0:T(8,128)(2,1)S(1)}, bf16[64,1024]{1,0:T(8,128)(2,1)S(1)}, u32[]{:S(2)}, u32[]{:S(2)}) collective-permute-start(bf16[64,1024]{1,0:T(8,128)(2,1)S(1)} %get-tuple-element.71), channel_id=1, source_target_pairs={{0,3},{1,0},{2,1},{3,2},{4,7},{5,4},{6,5},{7,6},{8,11},{9,8},{10,9... | collective-permute-start | bytes 393224 | tf_op jit(solution)/shard_map/ppermute | solution.py:342
  74.5 8.5 %collective-permute-start.10 = (bf16[64,1024]{1,0:T(8,128)(2,1)S(1)}, bf16[64,1024]{1,0:T(8,128)(2,1)S(1)}, u32[]{:S(2)}, u32[]{:S(2)}) collective-permute-start(bf16[64,1024]{1,0:T(8,128)(2,1)S(1)} %get-tuple-element.81), channel_id=1, source_target_pairs={{0,2},{1,3},{2,0},{3,1},{4,6},{5,7},{6,4},{7,5},{8,10},{9,11},{10,... | collective-permute-start | bytes 393224 | tf_op jit(solution)/shard_map/ppermute | solution.py:342
  85.7 16.3 %all-to-all-start.1 = ((bf16[8,32,512]{2,1,0:T(8,128)(2,1)}), bf16[8,32,512]{2,1,0:T(8,128)(2,1)S(1)}, u32[]{:S(2)}, u32[]{:S(2)}) async-start(bf16[8,32,512]{2,1,0:T(8,128)(2,1)} %get-tuple-element.95), calls=%async_computation.1 | async-start | bytes 524288 | tf_op jit(solution)/shard_map/all_to_all | solution.py:400
  90.3 7.0 %collective-permute-start.13 = (bf16[64,1024]{1,0:T(8,128)(2,1)S(1)}, bf16[64,1024]{1,0:T(8,128)(2,1)S(1)}, u32[]{:S(2)}, u32[]{:S(2)}) collective-permute-start(bf16[64,1024]{1,0:T(8,128)(2,1)S(1)} %get-tuple-element.98), channel_id=1, source_target_pairs={{0,2},{1,3},{2,0},{3,1},{4,6},{5,7},{6,4},{7,5},{8,10},{9,11},{10,... | collective-permute-start | bytes 393224 | tf_op jit(solution)/shard_map/ppermute | solution.py:342
  102.0 64.8 %all-to-all-start.2 = ((bf16[64,128,128]{2,1,0:T(8,128)(2,1)}), bf16[64,128,128]{2,1,0:T(8,128)(2,1)S(1)}, u32[]{:S(2)}, u32[]{:S(2)}) async-start(bf16[64,128,128]{2,1,0:T(8,128)(2,1)} %far_back.1), calls=%async_computation.2 | async-start | bytes 4194304 | tf_op jit(solution)/shard_map/all_to_all | solution.py:410
  113.9 13.4 %collective-permute-start.25 = (bf16[64,1024]{1,0:T(8,128)(2,1)S(1)}, bf16[64,1024]{1,0:T(8,128)(2,1)S(1)}, u32[]{:S(2)}, u32[]{:S(2)}) collective-permute-start(bf16[64,1024]{1,0:T(8,128)(2,1)S(1)} %copy-done.33), channel_id=1, source_target_pairs={{0,3},{1,0},{2,1},{3,2},{4,7},{5,4},{6,5},{7,6},{8,11},{9,8},{10,9... | collective-permute-start | bytes 393224 | tf_op jit(solution)/shard_map/ppermute | solution.py:342
  117.4 7.3 %collective-permute-start.17 = (f32[8,512]{1,0:T(8,128)S(1)}, f32[8,512]{1,0:T(8,128)S(1)}, u32[]{:S(2)}, u32[]{:S(2)}) collective-permute-start(f32[8,512]{1,0:T(8,128)S(1)} %get-tuple-element.104), channel_id=1, source_target_pairs={{0,1},{1,2},{2,3},{3,0},{4,5},{5,6},{6,7},{7,4},{8,9},{9,10},{10,1... | collective-permute-start | bytes 49160 | tf_op jit(solution)/shard_map/slice_sums/ppermute | solution.py:342
  119.2 24.7 %collective-permute-start.22 = (f32[64,1024]{1,0:T(8,128)S(1)}, f32[64,1024]{1,0:T(8,128)S(1)}, u32[]{:S(2)}, u32[]{:S(2)}) collective-permute-start(f32[64,1024]{1,0:T(8,128)S(1)} %get-tuple-element.107), channel_id=1, source_target_pairs={{0,1},{1,2},{2,3},{3,0},{4,5},{5,6},{6,7},{7,4},{8,9},{9,10},{10,1... | collective-permute-start | bytes 786440 | tf_op jit(solution)/shard_map/ppermute | solution.py:342
  120.5 23.7 %collective-permute-start.23 = (f32[64,1024]{1,0:T(8,128)S(1)}, f32[64,1024]{1,0:T(8,128)S(1)}, u32[]{:S(2)}, u32[]{:S(2)}) collective-permute-start(f32[64,1024]{1,0:T(8,128)S(1)} %get-tuple-element.108), channel_id=1, source_target_pairs={{0,2},{1,3},{2,0},{3,1},{4,6},{5,7},{6,4},{7,5},{8,10},{9,11},{10,... | collective-permute-start | bytes 786440 | tf_op jit(solution)/shard_map/ppermute | solution.py:342
  122.8 21.5 %collective-permute-start.24 = (f32[64,1024]{1,0:T(8,128)S(1)}, f32[64,1024]{1,0:T(8,128)S(1)}, u32[]{:S(2)}, u32[]{:S(2)}) collective-permute-start(f32[64,1024]{1,0:T(8,128)S(1)} %get-tuple-element.109), channel_id=1, source_target_pairs={{0,3},{1,0},{2,1},{3,2},{4,7},{5,4},{6,5},{7,6},{8,11},{9,8},{10,9... | collective-permute-start | bytes 786440 | tf_op jit(solution)/shard_map/ppermute | solution.py:342
  127.3 9.2 %collective-permute-start.26 = (bf16[64,1024]{1,0:T(8,128)(2,1)S(1)}, bf16[64,1024]{1,0:T(8,128)(2,1)S(1)}, u32[]{:S(2)}, u32[]{:S(2)}) collective-permute-start(bf16[64,1024]{1,0:T(8,128)(2,1)S(1)} %copy-done.32), channel_id=1, source_target_pairs={{0,2},{1,3},{2,0},{3,1},{4,6},{5,7},{6,4},{7,5},{8,10},{9,11},{10,... | collective-permute-start | bytes 393224 | tf_op jit(solution)/shard_map/ppermute | solution.py:342
  128.1 12.7 %collective-permute-start.27 = (bf16[64,1024]{1,0:T(8,128)(2,1)S(1)}, bf16[64,1024]{1,0:T(8,128)(2,1)S(1)}, u32[]{:S(2)}, u32[]{:S(2)}) collective-permute-start(bf16[64,1024]{1,0:T(8,128)(2,1)S(1)} %copy-done.31), channel_id=1, source_target_pairs={{0,1},{1,2},{2,3},{3,0},{4,5},{5,6},{6,7},{7,4},{8,9},{9,10},{10,1... | collective-permute-start | bytes 393224 | tf_op jit(solution)/shard_map/ppermute | solution.py:342
  136.5 11.0 %collective-permute-start.21 = (f32[8,512]{1,0:T(8,128)S(1)}, f32[8,512]{1,0:T(8,128)S(1)}, u32[]{:S(2)}, u32[]{:S(2)}) collective-permute-start(f32[8,512]{1,0:T(8,128)S(1)} %slice_sums.6.refs_0_), channel_id=1, source_target_pairs={{0,192},{4,196},{8,200},{12,204},{16,208},{20,212},{24,216},{28,22... | collective-permute-start | bytes 49160 | tf_op jit(solution)/shard_map/slice_sums/ppermute | solution.py:351
  140.9 6.6 %collective-permute-start.20 = (f32[8,512]{1,0:T(8,128)S(1)}, f32[8,512]{1,0:T(8,128)S(1)}, u32[]{:S(2)}, u32[]{:S(2)}) collective-permute-start(f32[8,512]{1,0:T(8,128)S(1)} %slice_sums.6.refs_0_), channel_id=1, source_target_pairs={{0,128},{4,132},{8,136},{12,140},{16,144},{20,148},{24,152},{28,15... | collective-permute-start | bytes 49160 | tf_op jit(solution)/shard_map/slice_sums/ppermute | solution.py:351
  148.2 17.2 %collective-permute-start.31 = (f32[8,512]{1,0:T(8,128)S(1)}, f32[8,512]{1,0:T(8,128)S(1)}, u32[]{:S(2)}, u32[]{:S(2)}) collective-permute-start(f32[8,512]{1,0:T(8,128)S(1)} %slice_sums.7.mine_ref), channel_id=1, source_target_pairs={{0,32},{4,36},{8,40},{12,44},{16,48},{20,52},{24,56},{28,60},{32,0... | collective-permute-start | bytes 49160 | tf_op jit(solution)/shard_map/spread/ppermute | solution.py:351
  153.5 11.9 %collective-permute-start.30 = (f32[8,512]{1,0:T(8,128)S(1)}, f32[8,512]{1,0:T(8,128)S(1)}, u32[]{:S(2)}, u32[]{:S(2)}) collective-permute-start(f32[8,512]{1,0:T(8,128)S(1)} %slice_sums.7.mine_ref), channel_id=1, source_target_pairs={{0,24},{4,44},{8,32},{12,52},{16,40},{20,60},{24,48},{28,4},{32,56... | collective-permute-start | bytes 49160 | tf_op jit(solution)/shard_map/spread/ppermute | solution.py:351
  153.8 11.6 %collective-permute-start.29 = (f32[8,512]{1,0:T(8,128)S(1)}, f32[8,512]{1,0:T(8,128)S(1)}, u32[]{:S(2)}, u32[]{:S(2)}) collective-permute-start(f32[8,512]{1,0:T(8,128)S(1)} %slice_sums.7.mine_ref), channel_id=1, source_target_pairs={{0,16},{4,52},{8,24},{12,60},{16,32},{20,4},{24,40},{28,12},{32,48... | collective-permute-start | bytes 49160 | tf_op jit(solution)/shard_map/spread/ppermute | solution.py:351
  156.4 9.0 %collective-permute-start.28 = (f32[8,512]{1,0:T(8,128)S(1)}, f32[8,512]{1,0:T(8,128)S(1)}, u32[]{:S(2)}, u32[]{:S(2)}) collective-permute-start(f32[8,512]{1,0:T(8,128)S(1)} %slice_sums.7.mine_ref), channel_id=1, source_target_pairs={{0,8},{4,60},{8,16},{12,4},{16,24},{20,12},{24,32},{28,20},{32,40}... | collective-permute-start | bytes 49160 | tf_op jit(solution)/shard_map/spread/ppermute | solution.py:351
  (46 other events, 418.1 us)

commit v6 on v5

--- a/solution.py
+++ b/solution.py
@@ -159,9 +159,10 @@
 def dense_body(rep_ref, *refs):
     agg, feats, cot, wts = refs[0:4], refs[4:8], refs[8:12], refs[12:16]
     div_ref = refs[16]
-    scaled_out, out_out, grad_hbm, slices_hbm = refs[17:21], refs[21:25], refs[25], refs[26]
-    back_ref, full_feats, full_agg, grad_ref, out_buf, prod_ref, slices_ref = refs[27:34]
-    out_sems, grad_sem, slices_sem = refs[34:37]
+    scaled_out, out_out, grad_hbm, slices_out = refs[17:21], refs[21:25], refs[25], refs[26:30]
+    back_ref, full_feats, full_agg, grad_ref, out_buf, prod_ref, kept_ref = refs[30:37]
+    out_sems, grad_sem, kept_sem = refs[37:40]
+    low = lax.rem(lax.div(rep_ref[1], 2), 4)
     rep = rep_ref[0]
     reps = 4
     rows, width = agg[0].shape
@@ -184,13 +185,15 @@
     for which, full in ((0, full_feats), (1, full_agg)):
         prod_ref[...] = dot(grad_ref[...], full[...], 1, 1)
         wide = prod_ref.shape[1]
-        for part in range(slices_ref.shape[0]):
+        for part in range(4):
+            target = lax.rem(low + part, 4)
+            slice_ref = slices_out[part] if part else kept_ref
             for k in range(reps):
-                start = k * rows + 8 * part
-                slices_ref[part, 8 * k : 8 * k + 8, which * wide : (which + 1) * wide] = prod_ref[
-                    start : start + 8, :
+                start = pl.multiple_of(k * rows + 16 * target, 16)
+                slice_ref[16 * k : 16 * k + 16, which * wide : (which + 1) * wide] = prod_ref[
+                    pl.ds(start, 16), :
                 ].astype(BF16)
-    leave(slices_ref, slices_hbm, slices_sem)
+    leave(kept_ref, slices_out[0], kept_sem)
     w_neigh = jnp.concatenate([wts[k][1] for k in range(reps)], axis=0)
     back_ref[...] = dot(w_neigh, grad_ref[...], 0, 0)
     div = div_ref[0:1, lanes(rep, width)]
@@ -213,17 +216,20 @@
         back_out[k][...] = back_ref[lanes(target, rows), :]
 
 
-def slice_sum_body(got_ref, *outs):
-    total = jnp.sum(got_ref[...].astype(F32), axis=0)
+def slice_sum_body(*refs):
+    pieces, outs = refs[:4], refs[4:]
+    total = pieces[0][...].astype(F32)
+    for piece in pieces[1:]:
+        total = total + piece[...].astype(F32)
     for k in range(len(outs)):
-        outs[k][...] = total[8 * k : 8 * k + 8, :]
+        outs[k][...] = total[16 * k : 16 * k + 16, :]
 
 
 def add_body(*refs):
     total = refs[0][...]
     for ref in refs[1:-1]:
         total = total + ref[...]
-    refs[-1][...] = total
+    refs[-1][...] = total.astype(refs[-1].dtype)
 
 
 def stack_body(*refs):
@@ -232,22 +238,20 @@
         refs[-1][rows * k : rows * (k + 1), :] = ref[...]
 
 
-def join_body(place_ref, mine_ref, own_ref, other_ref, w_self_ref, w_neigh_ref):
+def join_body(place_ref, mine_ref, own_ref, other_ref, w_self_ref, w_neigh_ref, parts_ref):
     full = w_self_ref.shape[1]
     core = lax.rem(place_ref[1], 2)
     place = lax.rem(lax.div(place_ref[1], 2), 8)
     sign = 1 - 2 * core
-
-    def put(place, piece):
-        rows = lanes(place, 8)
-        w_self_ref[rows, :] = piece[:, :full]
-        w_neigh_ref[rows, :] = piece[:, full:]
-
-    put(place, mine_ref[...])
+    parts_ref[place] = mine_ref[...].astype(F32)
     for k in range(1, 5):
-        rows = slice(8 * (k - 1), 8 * k)
-        put(lax.rem(place + 8 - sign * k, 8), own_ref[rows, :])
-        put(lax.rem(place + 8 + sign * k, 8), other_ref[rows, :])
+        rows = slice(16 * (k - 1), 16 * k)
+        parts_ref[lax.rem(place + 8 - sign * k, 8)] = own_ref[rows, :].astype(F32)
+        parts_ref[lax.rem(place + 8 + sign * k, 8)] = other_ref[rows, :].astype(F32)
+    for low in range(4):
+        total = parts_ref[low] + parts_ref[low + 4]
+        w_self_ref[16 * low : 16 * low + 16, :] = total[:, :full]
+        w_neigh_ref[16 * low : 16 * low + 16, :] = total[:, full:]
 
 
 def gather_lanes(ref, pieces, rep):
@@ -328,7 +332,7 @@
     parts = remote_tiles.shape[1]
     far_tiles = remote_tiles[0]
     rows = remote_rows[0].T
-    sends = send_list[0].T
+    sends = pinned(send_list[0].T)
     cols = local_cols.T
     rep = jnp.stack([lax.axis_index("rep"), lax.axis_index("dom")]).astype(jnp.int32)
     piece = shape((chans, width), BF16)
@@ -350,7 +354,15 @@
         ]
         return lax.ppermute(value, "dom", pairs)
 
-    z_groups = [[(y * 8 + z) * 2 + c for z in range(8)] for y in range(4) for c in range(2)]
+    def move_low(value, k):
+        pairs = [
+            ((y * 8 + z) * 2 + c, (y * 8 + z // 4 * 4 + (z + k) % 4) * 2 + c)
+            for y in range(4)
+            for z in range(8)
+            for c in range(2)
+        ]
+        return lax.ppermute(value, "dom", pairs)
+
     def exchange(pieces, sign=1):
         return [pieces[0]] + [shift(pieces[k], (sign * k) % reps) for k in range(1, reps)]
 
@@ -387,34 +399,36 @@
             dense_body, (rep,), (*agg_in, *feats_in, *cot_in, *weights_in, div),
             [piece] * reps
             + [in_hbm((chans, width), BF16)] * reps
-            + [in_hbm((full, width), BF16), in_hbm((8, 8 * reps, 2 * full), BF16)],
+            + [in_hbm((full, width), BF16), in_hbm((16 * reps, 2 * full), BF16)]
+            + [shape((16 * reps, 2 * full), BF16)] * 3,
             [
                 pltpu.VMEM((full, width), F32), pltpu.VMEM((full, width), BF16), pltpu.VMEM((full, width), BF16),
                 pltpu.VMEM((full, width), BF16), pltpu.VMEM((reps, chans, width), BF16), pltpu.VMEM((full, full), F32),
-                pltpu.VMEM((8, 8 * reps, 2 * full), BF16), pltpu.SemaphoreType.DMA((reps,)), sem, sem,
+                pltpu.VMEM((16 * reps, 2 * full), BF16), pltpu.SemaphoreType.DMA((reps,)), sem, sem,
             ],
             3.0, (), range(reps, 2 * reps + 2),
         )
-    scaled, out_pieces, grad_pre, slices = dense[:reps], dense[reps : 2 * reps], dense[2 * reps], dense[2 * reps + 1]
+    scaled, out_pieces, grad_pre, slices = dense[:reps], dense[reps : 2 * reps], dense[2 * reps], dense[2 * reps + 1 :]
     scaled_in = exchange(scaled)
-    slices_in = lax.all_to_all(slices, "dom", 0, 0, axis_index_groups=z_groups, tiled=True)
+    slices_in = [slices[0]] + [move_low(slices[k], k) for k in range(1, 4)]
     with jax.named_scope("far_back"):
         far_back = call(
             far_back_body, (rep, rows), (*scaled_in, far_tiles), in_hbm((parts, 2 * chans, TILE), BF16),
             [
                 pltpu.VMEM((chans, nodes), BF16), pltpu.VMEM((parts, 2 * chans, TILE), BF16), tile_buf, sems, sems,
             ],
-            2.0, (reps,), (0,),
+            5.0, (reps,), (0,),
         )
     slices_in, far_back = lax.optimization_barrier((slices_in, far_back))
     returned = lax.all_to_all(far_back, "dom", split_axis=0, concat_axis=0, tiled=True)
 
     with jax.named_scope("slice_sums"):
-        slice_shape = shape((8, 2 * full), F32)
-        sums = call(slice_sum_body, (), (slices_in,), [slice_shape] * reps)
+        slice_shape = shape((16, 2 * full), F32)
+        sums = call(slice_sum_body, (), slices_in, [slice_shape] * reps)
         total = call(add_body, (), exchange(sums, -1), slice_shape)
         total = call(add_body, (), (total, move(total, 0, 0, 1)), slice_shape)
-        total = call(add_body, (), (total, *[move(total, dy, 0, 0) for dy in range(1, 4)]), slice_shape)
+        others = [move(total, dy, 0, 0) for dy in range(1, 4)]
+        total = call(add_body, (), (total, *others), shape((16, 2 * full), BF16))
     with jax.named_scope("back"):
         back_self = call(
             back_body, (rep,), (*weights_in, grad_pre), [piece32] * reps, [pltpu.VMEM((full, width), F32)], 1.0
@@ -429,7 +443,7 @@
     total, near_back, output = lax.optimization_barrier((total, near_back, output))
     with jax.named_scope("spread"):
         own = call(
-            stack_body, (), [move(total, 0, dz, 0, True) for dz in range(1, 5)], shape((32, 2 * full), F32), (), 0.5
+            stack_body, (), [move(total, 0, dz, 0, True) for dz in range(1, 5)], shape((64, 2 * full), BF16), (), 0.5
         )
         other = move(own, 0, 0, 1)
     with jax.named_scope("home"):
@@ -438,7 +452,9 @@
         )
     with jax.named_scope("join"):
         other, grad_feats = lax.optimization_barrier((other, grad_feats))
-        wg_self, wg_neigh = call(join_body, (rep,), (total, own, other), [shape((chans, full), F32)] * 2)
+        wg_self, wg_neigh = call(
+            join_body, (rep,), (total, own, other), [shape((chans, full), F32)] * 2, [pltpu.VMEM((8, 16, 2 * full), F32)]
+        )
     return output, grad_feats, wg_self.T, wg_neigh.T
 
 

time: 171 us -> 165 us (0.965)
  starting transfers between devices: 77.6 us -> 71.7 us
    ppermute x24, waiting for transfers between devices: 19.7 us -> 15.4 us  [shift(): lax.ppermute(value, 'rep', [(i, (i + by) % reps) for i in range(reps)])]
    ppermute x9, waiting for transfers between devices: 9.04 us -> 12.9 us  [move(): return lax.ppermute(value, 'dom', pairs)]
    ppermute x9, starting transfers between devices: 19.7 us -> 16.1 us  [move(): return lax.ppermute(value, 'dom', pairs)]
    all_to_all x1 -> x0, starting transfers between devices: 3.42 us -> none  [local(): lax.all_to_all(slices, 'dom', 0, 0, axis_index_groups=z_groups, tiled=True)]
    ppermute x0 -> x3, starting transfers between devices: none -> 3.27 us  [move_low(): return lax.ppermute(value, 'dom', pairs)]
    all_to_all x1, starting transfers between devices: 11.9 us -> 8.97 us  [local(): lax.all_to_all(far_back, 'dom', split_axis=0, concat_axis=0, tiled=True)]
    unnamed x68 -> x62, local copies, waits for them, and re-layouts: 5.97 us -> 5.27 us
  transfers between devices with their start and end apart: 36 -> 38, of which waited for: 12 -> 13; matrix products, arithmetic and copies ran while one was open for 0% -> 0% of each run, Pallas kernels for 11% -> 12%
where the time goes in v6:
time: 165 us; the launch traced here: 164 us
  starting transfers between devices  71.7 us (43%)
  waiting for transfers between devices  55.2 us (33%)
  Pallas kernels  30.8 us (19%)
  local copies, waits for them, and re-layouts  5.27 us (3%)
    pallas_call x15, Pallas kernels, call(): pl.pallas_call(body, in_specs=[IN_SMEM] * len(scalars) + [IN_HBM if i in...  30.8 us
    ppermute x24, starting transfers between devices, shift(): lax.ppermute(value, 'rep', [(i, (i + by) % reps) for i in range(reps)])  30 us
    all_to_all x1, waiting for transfers between devices, local(): lax.all_to_all(outgoing, 'dom', split_axis=0, concat_axis=0, tiled=True)  26.9 us
    ppermute x9, starting transfers between devices, move(): return lax.ppermute(value, 'dom', pairs)  16.1 us
    ppermute x24, waiting for transfers between devices, shift(): lax.ppermute(value, 'rep', [(i, (i + by) % reps) for i in range(reps)])  15.4 us
    all_to_all x1, starting transfers between devices, local(): lax.all_to_all(outgoing, 'dom', split_axis=0, concat_axis=0, tiled=True)  13.3 us
    ppermute x9, waiting for transfers between devices, move(): return lax.ppermute(value, 'dom', pairs)  12.9 us
    all_to_all x1, starting transfers between devices, local(): lax.all_to_all(far_back, 'dom', split_axis=0, concat_axis=0, tiled=True)  8.97 us
  transfers between devices with their start and end apart: 38, of which 13 were waited for; matrix products, arithmetic and copies ran while one was open for 0% of the time, Pallas kernels for 12%

profile of v6, /device:TPU:1, one launch (start us, length us, event | category | flops | bytes accessed | tf_op | source)
XLA Modules:
  0.0 164.1 jit_solution(9647787413101617384)
XLA Ops:
  0.6 3.2 %pick.1 = bf16[64,128,128]{2,1,0:T(8,128)(2,1)} custom-call(s32[2,64]{1,0:T(2,128)} %bitcast.27, bf16[64,4096]{1,0:T(8,128)(2,1)} %feats_ref.3), custom_call_target="tpu_custom_call" | custom-call | flops 2200000000 | bytes 65536 | tf_op jit(solution)/shard_map/pick/pallas_call | solution.py:27
  3.9 13.3 %all-to-all-start = ((bf16[64,128,128]{2,1,0:T(8,128)(2,1)}), bf16[64,128,128]{2,1,0:T(8,128)(2,1)S(1)}, u32[]{:S(2)}, u32[]{:S(2)}) async-start(bf16[64,128,128]{2,1,0:T(8,128)(2,1)} %pick.1), calls=%async_computation | async-start | bytes 4194304 | tf_op jit(solution)/shard_map/all_to_all | solution.py:374
  32.9 7.0 %near.1 = (f32[64,4096]{1,0:T(8,128)S(1)}, f32[8,4096]{1,0:T(8,128)S(1)}, bf16[64,2,128,128]{3,2,1,0:T(8,128)(2,1)}) custom-call(s32[2,32]{1,0:T(2,128)S(1)} %bitcast.23, s32[2,64]{1,0:T(2,128)S(1)} %bitcast.20, bf16[64,4096]{1,0:T(8,128)(2,1)S(1)} %copy-done.4, bf16[32,2,128,128]{3,2,1,0:T(8,128)(2,1)S(1)} %copy-done.1, bf16[64,2,128,128]{3,2,1,0:T(8,128)(2,1)S(1)} %bitcast.19), custom_call_target="tpu_custom_call" | custom-call | flops 8800000000 | bytes 65536 | tf_op jit(solution)/shard_map/near/pallas_call | solution.py:27
  41.6 26.9 %all-to-all-done.got_ref = bf16[64,128,128]{2,1,0:T(8,128)(2,1)S(1)} async-done(((bf16[64,128,128]{2,1,0:T(8,128)(2,1)}), bf16[64,128,128]{2,1,0:T(8,128)(2,1)S(1)}, u32[]{:S(2)}, u32[]{:S(2)}) %all-to-all-start) | async-done | bytes 2097184 | tf_op jit(solution)/shard_map/all_to_all | solution.py:374
  68.5 4.1 %far.1 = (bf16[64,1024]{1,0:T(8,128)(2,1)S(1)}, bf16[64,1024]{1,0:T(8,128)(2,1)S(1)}, bf16[64,1024]{1,0:T(8,128)(2,1)S(1)}, bf16[64,1024]{1,0:T(8,128)(2,1)S(1)}) custom-call(s32[2]{0:T(128)S(1)} %pad_add_fusion.rep_ref.place_ref, s32[2,64]{1,0:T(2,128)S(1)} %bitcast.21, bf16[64,128,128]{2,1,0:T(8,128)(2,1)S(1)} %all-to-all-done.got_ref, ...), custom_call_target="tpu_custom_call" | custom-call | flops 6600000000 | bytes 65536 | tf_op jit(solution)/shard_map/far/pallas_call | solution.py:27
  73.9 2.4 %collective-permute-start.10 = (bf16[64,1024]{1,0:T(8,128)(2,1)S(1)}, bf16[64,1024]{1,0:T(8,128)(2,1)S(1)}, u32[]{:S(2)}, u32[]{:S(2)}) collective-permute-start(bf16[64,1024]{1,0:T(8,128)(2,1)S(1)} %get-tuple-element.87), channel_id=1, source_target_pairs={{0,2},{1,3},{2,0},{3,1},{4,6},{5,7},{6,4},{7,5},{8,10},{9,11},{10,... | collective-permute-start | bytes 393224 | tf_op jit(solution)/shard_map/ppermute | solution.py:346
  78.6 3.8 %collective-permute-done.10.refs_2_ = bf16[64,1024]{1,0:T(8,128)(2,1)S(1)} collective-permute-done((bf16[64,1024]{1,0:T(8,128)(2,1)S(1)}, bf16[64,1024]{1,0:T(8,128)(2,1)S(1)}, u32[]{:S(2)}, u32[]{:S(2)}) %collective-permute-start.10) | collective-permute-done | bytes 131104 | tf_op jit(solution)/shard_map/ppermute | solution.py:346
  82.4 2.9 %dense.1 = (bf16[64,1024]{1,0:T(8,128)(2,1)S(1)}, bf16[64,1024]{1,0:T(8,128)(2,1)S(1)}, bf16[64,1024]{1,0:T(8,128)(2,1)S(1)}, bf16[64,1024]{1,0:T(8,128)(2,1)S(1...) custom-call(s32[2]{0:T(128)S(1)} %pad_add_fusion.rep_ref.place_ref, ...), custom_call_target="tpu_custom_call" | custom-call | flops 3300000000 | bytes 65536 | tf_op jit(solution)/shard_map/dense/pallas_call | solution.py:27
  86.5 2.2 %collective-permute-start.16 = (bf16[64,1024]{1,0:T(8,128)(2,1)S(1)}, bf16[64,1024]{1,0:T(8,128)(2,1)S(1)}, u32[]{:S(2)}, u32[]{:S(2)}) collective-permute-start(bf16[64,1024]{1,0:T(8,128)(2,1)S(1)} %get-tuple-element.107), channel_id=1, source_target_pairs={{0,2},{1,3},{2,0},{3,1},{4,6},{5,7},{6,4},{7,5},{8,10},{9,11},{10,... | collective-permute-start | bytes 393224 | tf_op jit(solution)/shard_map/ppermute | solution.py:346
  93.7 4.7 %far_back.1 = bf16[64,128,128]{2,1,0:T(8,128)(2,1)} custom-call(s32[2]{0:T(128)S(1)} %pad_add_fusion.rep_ref.place_ref, s32[2,64]{1,0:T(2,128)S(1)} %bitcast.22, bf16[64,1024]{1,0:T(8,128)(2,1)S(1)} %get-tuple-element.105.s0.refs_0_, bf16[64,1024]{1,0:T(8,128)(2,1)S(1)} %collective-permute-done.15.s1.refs_1_, ...), custom_call_target="tpu_custom_call" | custom-call | flops 5500000256 | bytes 65536 | tf_op jit(solution)/shard_map/far_back/pallas_call | solution.py:27
  98.4 9.0 %all-to-all-start.1 = ((bf16[64,128,128]{2,1,0:T(8,128)(2,1)}), bf16[64,128,128]{2,1,0:T(8,128)(2,1)S(1)}, u32[]{:S(2)}, u32[]{:S(2)}) async-start(bf16[64,128,128]{2,1,0:T(8,128)(2,1)} %far_back.1), calls=%async_computation.1 | async-start | bytes 4194304 | tf_op jit(solution)/shard_map/all_to_all | solution.py:423
  107.5 2.0 %collective-permute-start.18 = (f32[16,512]{1,0:T(8,128)S(1)}, f32[16,512]{1,0:T(8,128)S(1)}, u32[]{:S(2)}, u32[]{:S(2)}) collective-permute-start(f32[16,512]{1,0:T(8,128)S(1)} %get-tuple-element.114), channel_id=1, source_target_pairs={{0,3},{1,0},{2,1},{3,2},{4,7},{5,4},{6,5},{7,6},{8,11},{9,8},{10,9... | collective-permute-start | bytes 98312 | tf_op jit(solution)/shard_map/slice_sums/ppermute | solution.py:346
  110.4 2.6 %collective-permute-start.28 = (bf16[64,1024]{1,0:T(8,128)(2,1)S(1)}, bf16[64,1024]{1,0:T(8,128)(2,1)S(1)}, u32[]{:S(2)}, u32[]{:S(2)}) collective-permute-start(bf16[64,1024]{1,0:T(8,128)(2,1)S(1)} %copy-done.30), channel_id=1, source_target_pairs={{0,3},{1,0},{2,1},{3,2},{4,7},{5,4},{6,5},{7,6},{8,11},{9,8},{10,9... | collective-permute-start | bytes 393224 | tf_op jit(solution)/shard_map/ppermute | solution.py:346
  114.6 2.0 %collective-permute-start.21 = (f32[16,512]{1,0:T(8,128)S(1)}, f32[16,512]{1,0:T(8,128)S(1)}, u32[]{:S(2)}, u32[]{:S(2)}) collective-permute-start(f32[16,512]{1,0:T(8,128)S(1)} %slice_sums.5.refs_0_), channel_id=1, source_target_pairs={{0,4},{4,0},{8,12},{12,8},{16,20},{20,16},{24,28},{28,24},{32,36},... | collective-permute-start | bytes 98312 | tf_op jit(solution)/shard_map/slice_sums/ppermute | solution.py:355
  118.7 1.9 %collective-permute-start.27 = (f32[64,1024]{1,0:T(8,128)S(1)}, f32[64,1024]{1,0:T(8,128)S(1)}, u32[]{:S(2)}, u32[]{:S(2)}) collective-permute-start(f32[64,1024]{1,0:T(8,128)S(1)} %get-tuple-element.121), channel_id=1, source_target_pairs={{0,3},{1,0},{2,1},{3,2},{4,7},{5,4},{6,5},{7,6},{8,11},{9,8},{10,9... | collective-permute-start | bytes 786440 | tf_op jit(solution)/shard_map/ppermute | solution.py:346
  120.6 2.8 %collective-permute-start.24 = (f32[16,512]{1,0:T(8,128)S(1)}, f32[16,512]{1,0:T(8,128)S(1)}, u32[]{:S(2)}, u32[]{:S(2)}) collective-permute-start(f32[16,512]{1,0:T(8,128)S(1)} %slice_sums.6.refs_0_), channel_id=1, source_target_pairs={{0,192},{4,196},{8,200},{12,204},{16,208},{20,212},{24,216},{28,22... | collective-permute-start | bytes 98312 | tf_op jit(solution)/shard_map/slice_sums/ppermute | solution.py:355
  125.2 3.5 %collective-permute-done.23.refs_2_ = f32[16,512]{1,0:T(8,128)S(1)} collective-permute-done((f32[16,512]{1,0:T(8,128)S(1)}, f32[16,512]{1,0:T(8,128)S(1)}, u32[]{:S(2)}, u32[]{:S(2)}) %collective-permute-start.23) | collective-permute-done | bytes 32800 | tf_op jit(solution)/shard_map/slice_sums/ppermute | solution.py:355
  128.7 2.0 %collective-permute-start.29 = (bf16[64,1024]{1,0:T(8,128)(2,1)S(1)}, bf16[64,1024]{1,0:T(8,128)(2,1)S(1)}, u32[]{:S(2)}, u32[]{:S(2)}) collective-permute-start(bf16[64,1024]{1,0:T(8,128)(2,1)S(1)} %copy-done.29), channel_id=1, source_target_pairs={{0,2},{1,3},{2,0},{3,1},{4,6},{5,7},{6,4},{7,5},{8,10},{9,11},{10,... | collective-permute-start | bytes 393224 | tf_op jit(solution)/shard_map/ppermute | solution.py:346
  130.7 3.6 %collective-permute-done.29.refs_10_ = bf16[64,1024]{1,0:T(8,128)(2,1)S(1)} collective-permute-done((bf16[64,1024]{1,0:T(8,128)(2,1)S(1)}, bf16[64,1024]{1,0:T(8,128)(2,1)S(1)}, u32[]{:S(2)}, u32[]{:S(2)}) %collective-permute-start.29) | collective-permute-done | bytes 131104 | tf_op jit(solution)/shard_map/ppermute | solution.py:346
  134.3 3.4 %collective-permute-done.30.refs_11_ = bf16[64,1024]{1,0:T(8,128)(2,1)S(1)} collective-permute-done((bf16[64,1024]{1,0:T(8,128)(2,1)S(1)}, bf16[64,1024]{1,0:T(8,128)(2,1)S(1)}, u32[]{:S(2)}, u32[]{:S(2)}) %collective-permute-start.30) | collective-permute-done | bytes 131104 | tf_op jit(solution)/shard_map/ppermute | solution.py:346
  137.7 3.2 %near_back.1 = (f32[64,4096]{1,0:T(8,128)S(1)}, bf16[64,4096]{1,0:T(8,128)(2,1)}) custom-call(s32[2]{0:T(128)S(1)} %pad_add_fusion.rep_ref.place_ref, s32[2,32]{1,0:T(2,128)S(1)} %bitcast.24, bf16[64,1024]{1,0:T(8,128)(2,1)S(1)} %get-tuple-element.105.s0.refs_0_, bf16[64,1024]{1,0:T(8,128)(2,1)S(1)} %collective-permute-done.15.s1.refs_1_, ...), custom_call_target="tpu_custom_call" | custom-call | flops 2200000000 | bytes 65536 | tf_op jit(solution)/shard_map/near_back/pallas_call | solution.py:27
  140.9 5.0 %collective-permute-start.34 = (bf16[16,512]{1,0:T(8,128)(2,1)S(1)}, bf16[16,512]{1,0:T(8,128)(2,1)S(1)}, u32[]{:S(2)}, u32[]{:S(2)}) collective-permute-start(bf16[16,512]{1,0:T(8,128)(2,1)S(1)} %slice_sums.7.mine_ref), channel_id=1, source_target_pairs={{0,32},{4,36},{8,40},{12,44},{16,48},{20,52},{24,56},{28,60},{32,0... | collective-permute-start | bytes 49160 | tf_op jit(solution)/shard_map/spread/ppermute | solution.py:355
  150.2 8.8 %collective-permute-done.34.refs_3_ = bf16[16,512]{1,0:T(8,128)(2,1)S(1)} collective-permute-done((bf16[16,512]{1,0:T(8,128)(2,1)S(1)}, bf16[16,512]{1,0:T(8,128)(2,1)S(1)}, u32[]{:S(2)}, u32[]{:S(2)}) %collective-permute-start.34) | collective-permute-done | bytes 16416 | tf_op jit(solution)/shard_map/spread/ppermute | solution.py:355
  160.0 2.8 %home.1 = bf16[64,4096]{1,0:T(8,128)(2,1)} custom-call(s32[2,64]{1,0:T(2,128)} %bitcast.28, bf16[64,128,128]{2,1,0:T(8,128)(2,1)S(1)} %all-to-all-done.1.got_ref, f32[64,4096]{1,0:T(8,128)} %copy-done.15), custom_call_target="tpu_custom_call" | custom-call | flops 3300000000 | bytes 65536 | tf_op jit(solution)/shard_map/home/pallas_call | solution.py:27
  (131 shorter events, 40.1 us)
Async XLA Ops:
  3.9 64.6 %all-to-all-start = ((bf16[64,128,128]{2,1,0:T(8,128)(2,1)}), bf16[64,128,128]{2,1,0:T(8,128)(2,1)S(1)}, u32[]{:S(2)}, u32[]{:S(2)}) async-start(bf16[64,128,128]{2,1,0:T(8,128)(2,1)} %pick.1), calls=%async_computation | async-start | bytes 4194304 | tf_op jit(solution)/shard_map/all_to_all | solution.py:374
  18.6 10.8 %collective-permute-start = (bf16[64,1024]{1,0:T(8,128)(2,1)S(1)}, bf16[64,1024]{1,0:T(8,128)(2,1)S(1)}, u32[]{:S(2)}, u32[]{:S(2)}) collective-permute-start(bf16[64,1024]{1,0:T(8,128)(2,1)S(1)} %get-tuple-element.71), channel_id=1, source_target_pairs={{0,1},{1,2},{2,3},{3,0},{4,5},{5,6},{6,7},{7,4},{8,9},{9,10},{10,1... | collective-permute-start | bytes 393224 | tf_op jit(solution)/shard_map/ppermute | solution.py:346
  23.2 18.3 %collective-permute-start.1 = (bf16[64,1024]{1,0:T(8,128)(2,1)S(1)}, bf16[64,1024]{1,0:T(8,128)(2,1)S(1)}, u32[]{:S(2)}, u32[]{:S(2)}) collective-permute-start(bf16[64,1024]{1,0:T(8,128)(2,1)S(1)} %get-tuple-element.72), channel_id=1, source_target_pairs={{0,2},{1,3},{2,0},{3,1},{4,6},{5,7},{6,4},{7,5},{8,10},{9,11},{10,... | collective-permute-start | bytes 393224 | tf_op jit(solution)/shard_map/ppermute | solution.py:346
  25.6 16.0 %collective-permute-start.2 = (bf16[64,1024]{1,0:T(8,128)(2,1)S(1)}, bf16[64,1024]{1,0:T(8,128)(2,1)S(1)}, u32[]{:S(2)}, u32[]{:S(2)}) collective-permute-start(bf16[64,1024]{1,0:T(8,128)(2,1)S(1)} %get-tuple-element.73), channel_id=1, source_target_pairs={{0,3},{1,0},{2,1},{3,2},{4,7},{5,4},{6,5},{7,6},{8,11},{9,8},{10,9... | collective-permute-start | bytes 393224 | tf_op jit(solution)/shard_map/ppermute | solution.py:346
  27.1 14.5 %collective-permute-start.3 = (bf16[64,1024]{1,0:T(8,128)(2,1)S(1)}, bf16[64,1024]{1,0:T(8,128)(2,1)S(1)}, u32[]{:S(2)}, u32[]{:S(2)}) collective-permute-start(bf16[64,1024]{1,0:T(8,128)(2,1)S(1)} %get-tuple-element.75), channel_id=1, source_target_pairs={{0,1},{1,2},{2,3},{3,0},{4,5},{5,6},{6,7},{7,4},{8,9},{9,10},{10,1... | collective-permute-start | bytes 393224 | tf_op jit(solution)/shard_map/ppermute | solution.py:346
  28.8 12.8 %collective-permute-start.4 = (bf16[64,1024]{1,0:T(8,128)(2,1)S(1)}, bf16[64,1024]{1,0:T(8,128)(2,1)S(1)}, u32[]{:S(2)}, u32[]{:S(2)}) collective-permute-start(bf16[64,1024]{1,0:T(8,128)(2,1)S(1)} %get-tuple-element.76), channel_id=1, source_target_pairs={{0,2},{1,3},{2,0},{3,1},{4,6},{5,7},{6,4},{7,5},{8,10},{9,11},{10,... | collective-permute-start | bytes 393224 | tf_op jit(solution)/shard_map/ppermute | solution.py:346
  29.5 12.1 %collective-permute-start.5 = (bf16[64,1024]{1,0:T(8,128)(2,1)S(1)}, bf16[64,1024]{1,0:T(8,128)(2,1)S(1)}, u32[]{:S(2)}, u32[]{:S(2)}) collective-permute-start(bf16[64,1024]{1,0:T(8,128)(2,1)S(1)} %get-tuple-element.77), channel_id=1, source_target_pairs={{0,3},{1,0},{2,1},{3,2},{4,7},{5,4},{6,5},{7,6},{8,11},{9,8},{10,9... | collective-permute-start | bytes 393224 | tf_op jit(solution)/shard_map/ppermute | solution.py:346
  73.9 8.5 %collective-permute-start.10 = (bf16[64,1024]{1,0:T(8,128)(2,1)S(1)}, bf16[64,1024]{1,0:T(8,128)(2,1)S(1)}, u32[]{:S(2)}, u32[]{:S(2)}) collective-permute-start(bf16[64,1024]{1,0:T(8,128)(2,1)S(1)} %get-tuple-element.87), channel_id=1, source_target_pairs={{0,2},{1,3},{2,0},{3,1},{4,6},{5,7},{6,4},{7,5},{8,10},{9,11},{10,... | collective-permute-start | bytes 393224 | tf_op jit(solution)/shard_map/ppermute | solution.py:346
  76.3 6.0 %collective-permute-start.11 = (bf16[64,1024]{1,0:T(8,128)(2,1)S(1)}, bf16[64,1024]{1,0:T(8,128)(2,1)S(1)}, u32[]{:S(2)}, u32[]{:S(2)}) collective-permute-start(bf16[64,1024]{1,0:T(8,128)(2,1)S(1)} %get-tuple-element.88), channel_id=1, source_target_pairs={{0,3},{1,0},{2,1},{3,2},{4,7},{5,4},{6,5},{7,6},{8,11},{9,8},{10,9... | collective-permute-start | bytes 393224 | tf_op jit(solution)/shard_map/ppermute | solution.py:346
  86.5 7.0 %collective-permute-start.16 = (bf16[64,1024]{1,0:T(8,128)(2,1)S(1)}, bf16[64,1024]{1,0:T(8,128)(2,1)S(1)}, u32[]{:S(2)}, u32[]{:S(2)}) collective-permute-start(bf16[64,1024]{1,0:T(8,128)(2,1)S(1)} %get-tuple-element.107), channel_id=1, source_target_pairs={{0,2},{1,3},{2,0},{3,1},{4,6},{5,7},{6,4},{7,5},{8,10},{9,11},{10,... | collective-permute-start | bytes 393224 | tf_op jit(solution)/shard_map/ppermute | solution.py:346
  89.6 8.8 %collective-permute-start.12 = (bf16[64,512]{1,0:T(8,128)(2,1)S(1)}, bf16[64,512]{1,0:T(8,128)(2,1)S(1)}, u32[]{:S(2)}, u32[]{:S(2)}) collective-permute-start(bf16[64,512]{1,0:T(8,128)(2,1)S(1)} %get-tuple-element.102), channel_id=1, source_target_pairs={{0,8},{4,12},{8,16},{12,20},{16,24},{20,28},{24,0},{28,4},{32,40},... | collective-permute-start | bytes 196616 | tf_op jit(solution)/shard_map/ppermute | solution.py:364
  89.8 8.6 %collective-permute-start.13 = (bf16[64,512]{1,0:T(8,128)(2,1)S(1)}, bf16[64,512]{1,0:T(8,128)(2,1)S(1)}, u32[]{:S(2)}, u32[]{:S(2)}) collective-permute-start(bf16[64,512]{1,0:T(8,128)(2,1)S(1)} %get-tuple-element.103), channel_id=1, source_target_pairs={{0,16},{4,20},{8,24},{12,28},{16,0},{20,4},{24,8},{28,12},{32,48},... | collective-permute-start | bytes 196616 | tf_op jit(solution)/shard_map/ppermute | solution.py:364
  91.3 7.1 %collective-permute-start.14 = (bf16[64,512]{1,0:T(8,128)(2,1)S(1)}, bf16[64,512]{1,0:T(8,128)(2,1)S(1)}, u32[]{:S(2)}, u32[]{:S(2)}) collective-permute-start(bf16[64,512]{1,0:T(8,128)(2,1)S(1)} %get-tuple-element.104), channel_id=1, source_target_pairs={{0,24},{4,28},{8,0},{12,4},{16,8},{20,12},{24,16},{28,20},{32,56},... | collective-permute-start | bytes 196616 | tf_op jit(solution)/shard_map/ppermute | solution.py:364
  98.4 61.6 %all-to-all-start.1 = ((bf16[64,128,128]{2,1,0:T(8,128)(2,1)}), bf16[64,128,128]{2,1,0:T(8,128)(2,1)S(1)}, u32[]{:S(2)}, u32[]{:S(2)}) async-start(bf16[64,128,128]{2,1,0:T(8,128)(2,1)} %far_back.1), calls=%async_computation.1 | async-start | bytes 4194304 | tf_op jit(solution)/shard_map/all_to_all | solution.py:423
  110.4 13.0 %collective-permute-start.28 = (bf16[64,1024]{1,0:T(8,128)(2,1)S(1)}, bf16[64,1024]{1,0:T(8,128)(2,1)S(1)}, u32[]{:S(2)}, u32[]{:S(2)}) collective-permute-start(bf16[64,1024]{1,0:T(8,128)(2,1)S(1)} %copy-done.30), channel_id=1, source_target_pairs={{0,3},{1,0},{2,1},{3,2},{4,7},{5,4},{6,5},{7,6},{8,11},{9,8},{10,9... | collective-permute-start | bytes 393224 | tf_op jit(solution)/shard_map/ppermute | solution.py:346
  117.6 20.1 %collective-permute-start.25 = (f32[64,1024]{1,0:T(8,128)S(1)}, f32[64,1024]{1,0:T(8,128)S(1)}, u32[]{:S(2)}, u32[]{:S(2)}) collective-permute-start(f32[64,1024]{1,0:T(8,128)S(1)} %get-tuple-element.119), channel_id=1, source_target_pairs={{0,1},{1,2},{2,3},{3,0},{4,5},{5,6},{6,7},{7,4},{8,9},{9,10},{10,1... | collective-permute-start | bytes 786440 | tf_op jit(solution)/shard_map/ppermute | solution.py:346
  117.6 20.1 %collective-permute-start.26 = (f32[64,1024]{1,0:T(8,128)S(1)}, f32[64,1024]{1,0:T(8,128)S(1)}, u32[]{:S(2)}, u32[]{:S(2)}) collective-permute-start(f32[64,1024]{1,0:T(8,128)S(1)} %get-tuple-element.120), channel_id=1, source_target_pairs={{0,2},{1,3},{2,0},{3,1},{4,6},{5,7},{6,4},{7,5},{8,10},{9,11},{10,... | collective-permute-start | bytes 786440 | tf_op jit(solution)/shard_map/ppermute | solution.py:346
  118.7 19.0 %collective-permute-start.27 = (f32[64,1024]{1,0:T(8,128)S(1)}, f32[64,1024]{1,0:T(8,128)S(1)}, u32[]{:S(2)}, u32[]{:S(2)}) collective-permute-start(f32[64,1024]{1,0:T(8,128)S(1)} %get-tuple-element.121), channel_id=1, source_target_pairs={{0,3},{1,0},{2,1},{3,2},{4,7},{5,4},{6,5},{7,6},{8,11},{9,8},{10,9... | collective-permute-start | bytes 786440 | tf_op jit(solution)/shard_map/ppermute | solution.py:346
  124.4 6.2 %collective-permute-start.22 = (f32[16,512]{1,0:T(8,128)S(1)}, f32[16,512]{1,0:T(8,128)S(1)}, u32[]{:S(2)}, u32[]{:S(2)}) collective-permute-start(f32[16,512]{1,0:T(8,128)S(1)} %slice_sums.6.refs_0_), channel_id=1, source_target_pairs={{0,64},{4,68},{8,72},{12,76},{16,80},{20,84},{24,88},{28,92},{32,9... | collective-permute-start | bytes 98312 | tf_op jit(solution)/shard_map/slice_sums/ppermute | solution.py:355
  130.7 7.0 %collective-permute-start.30 = (bf16[64,1024]{1,0:T(8,128)(2,1)S(1)}, bf16[64,1024]{1,0:T(8,128)(2,1)S(1)}, u32[]{:S(2)}, u32[]{:S(2)}) collective-permute-start(bf16[64,1024]{1,0:T(8,128)(2,1)S(1)} %copy-done.28), channel_id=1, source_target_pairs={{0,1},{1,2},{2,3},{3,0},{4,5},{5,6},{6,7},{7,4},{8,9},{9,10},{10,1... | collective-permute-start | bytes 393224 | tf_op jit(solution)/shard_map/ppermute | solution.py:346
  140.9 18.0 %collective-permute-start.34 = (bf16[16,512]{1,0:T(8,128)(2,1)S(1)}, bf16[16,512]{1,0:T(8,128)(2,1)S(1)}, u32[]{:S(2)}, u32[]{:S(2)}) collective-permute-start(bf16[16,512]{1,0:T(8,128)(2,1)S(1)} %slice_sums.7.mine_ref), channel_id=1, source_target_pairs={{0,32},{4,36},{8,40},{12,44},{16,48},{20,52},{24,56},{28,60},{32,0... | collective-permute-start | bytes 49160 | tf_op jit(solution)/shard_map/spread/ppermute | solution.py:355
  145.9 13.0 %collective-permute-start.33 = (bf16[16,512]{1,0:T(8,128)(2,1)S(1)}, bf16[16,512]{1,0:T(8,128)(2,1)S(1)}, u32[]{:S(2)}, u32[]{:S(2)}) collective-permute-start(bf16[16,512]{1,0:T(8,128)(2,1)S(1)} %slice_sums.7.mine_ref), channel_id=1, source_target_pairs={{0,24},{4,44},{8,32},{12,52},{16,40},{20,60},{24,48},{28,4},{32,56... | collective-permute-start | bytes 49160 | tf_op jit(solution)/shard_map/spread/ppermute | solution.py:355
  147.0 11.9 %collective-permute-start.32 = (bf16[16,512]{1,0:T(8,128)(2,1)S(1)}, bf16[16,512]{1,0:T(8,128)(2,1)S(1)}, u32[]{:S(2)}, u32[]{:S(2)}) collective-permute-start(bf16[16,512]{1,0:T(8,128)(2,1)S(1)} %slice_sums.7.mine_ref), channel_id=1, source_target_pairs={{0,16},{4,52},{8,24},{12,60},{16,32},{20,4},{24,40},{28,12},{32,48... | collective-permute-start | bytes 49160 | tf_op jit(solution)/shard_map/spread/ppermute | solution.py:355
  148.5 10.5 %collective-permute-start.31 = (bf16[16,512]{1,0:T(8,128)(2,1)S(1)}, bf16[16,512]{1,0:T(8,128)(2,1)S(1)}, u32[]{:S(2)}, u32[]{:S(2)}) collective-permute-start(bf16[16,512]{1,0:T(8,128)(2,1)S(1)} %slice_sums.7.mine_ref), channel_id=1, source_target_pairs={{0,8},{4,60},{8,16},{12,4},{16,24},{20,12},{24,32},{28,20},{32,40}... | collective-permute-start | bytes 49160 | tf_op jit(solution)/shard_map/spread/ppermute | solution.py:355
  (45 other events, 388.7 us)

commit v7 on v6

--- a/solution.py
+++ b/solution.py
@@ -159,10 +159,8 @@
 def dense_body(rep_ref, *refs):
     agg, feats, cot, wts = refs[0:4], refs[4:8], refs[8:12], refs[12:16]
     div_ref = refs[16]
-    scaled_out, out_out, grad_hbm, slices_out = refs[17:21], refs[21:25], refs[25], refs[26:30]
-    back_ref, full_feats, full_agg, grad_ref, out_buf, prod_ref, kept_ref = refs[30:37]
-    out_sems, grad_sem, kept_sem = refs[37:40]
-    low = lax.rem(lax.div(rep_ref[1], 2), 4)
+    scaled_out, out_out, grad_out = refs[17:21], refs[21:25], refs[25]
+    back_ref, full_feats, full_agg, grad_ref, out_buf, out_sems = refs[26:32]
     rep = rep_ref[0]
     reps = 4
     rows, width = agg[0].shape
@@ -181,10 +179,31 @@
         grad_ref[k * rows : (k + 1) * rows, :] = (cot[k][...].astype(F32) * slope).astype(BF16)
         out_buf[k] = (preact * gate).astype(BF16)
         leave(out_buf.at[k], out_out[k], out_sems.at[k])
-    leave(grad_ref, grad_hbm, grad_sem)
-    for which, full in ((0, full_feats), (1, full_agg)):
+    grad_out[...] = grad_ref[...]
+    w_neigh = jnp.concatenate([wts[k][1] for k in range(reps)], axis=0)
+    back_ref[...] = dot(w_neigh, grad_ref[...], 0, 0)
+    div = div_ref[0:1, lanes(rep, width)]
+    for k in range(reps):
+        target = lax.rem(rep + k, reps)
+        scaled_out[k][...] = (back_ref[lanes(target, rows), :] / div).astype(BF16)
+    for copy in copies:
+        copy.wait()
+
+
+def weight_body(rep_ref, *refs):
+    agg, feats, grad_ref = refs[0:4], refs[4:8], refs[8]
+    grad_hbm, slices_out = refs[9], refs[10:14]
+    full, prod_ref, kept_ref, grad_sem, kept_sem = refs[14:19]
+    rep = rep_ref[0]
+    low = lax.rem(lax.div(rep_ref[1], 2), 4)
+    reps = 4
+    rows = agg[0].shape[0]
+    wide = prod_ref.shape[1]
+    save = pltpu.make_async_copy(grad_ref, grad_hbm, grad_sem)
+    save.start()
+    for which, pieces in ((0, feats), (1, agg)):
+        gather_rows(full, pieces, rep)
         prod_ref[...] = dot(grad_ref[...], full[...], 1, 1)
-        wide = prod_ref.shape[1]
         for part in range(4):
             target = lax.rem(low + part, 4)
             slice_ref = slices_out[part] if part else kept_ref
@@ -193,15 +212,10 @@
                 slice_ref[16 * k : 16 * k + 16, which * wide : (which + 1) * wide] = prod_ref[
                     pl.ds(start, 16), :
                 ].astype(BF16)
-    leave(kept_ref, slices_out[0], kept_sem)
-    w_neigh = jnp.concatenate([wts[k][1] for k in range(reps)], axis=0)
-    back_ref[...] = dot(w_neigh, grad_ref[...], 0, 0)
-    div = div_ref[0:1, lanes(rep, width)]
-    for k in range(reps):
-        target = lax.rem(rep + k, reps)
-        scaled_out[k][...] = (back_ref[lanes(target, rows), :] / div).astype(BF16)
-    for copy in copies:
-        copy.wait()
+    keep = pltpu.make_async_copy(kept_ref, slices_out[0], kept_sem)
+    keep.start()
+    save.wait()
+    keep.wait()
 
 
 def back_body(rep_ref, *refs):
@@ -399,17 +413,26 @@
             dense_body, (rep,), (*agg_in, *feats_in, *cot_in, *weights_in, div),
             [piece] * reps
             + [in_hbm((chans, width), BF16)] * reps
-            + [in_hbm((full, width), BF16), in_hbm((16 * reps, 2 * full), BF16)]
+            + [shape((full, width), BF16)],
+            [
+                pltpu.VMEM((full, width), F32), pltpu.VMEM((full, width), BF16), pltpu.VMEM((full, width), BF16),
+                pltpu.VMEM((full, width), BF16), pltpu.VMEM((reps, chans, width), BF16), pltpu.SemaphoreType.DMA((reps,)),
+            ],
+            2.0, (), range(reps, 2 * reps),
+        )
+    scaled, out_pieces, grad = dense[:reps], dense[reps : 2 * reps], dense[2 * reps]
+    scaled_in = exchange(scaled)
+    with jax.named_scope("weights"):
+        grad_pre, *slices = call(
+            weight_body, (rep,), (*agg_in, *feats_in, grad),
+            [in_hbm((full, width), BF16), in_hbm((16 * reps, 2 * full), BF16)]
             + [shape((16 * reps, 2 * full), BF16)] * 3,
             [
-                pltpu.VMEM((full, width), F32), pltpu.VMEM((full, width), BF16), pltpu.VMEM((full, width), BF16),
-                pltpu.VMEM((full, width), BF16), pltpu.VMEM((reps, chans, width), BF16), pltpu.VMEM((full, full), F32),
-                pltpu.VMEM((16 * reps, 2 * full), BF16), pltpu.SemaphoreType.DMA((reps,)), sem, sem,
+                pltpu.VMEM((full, width), BF16), pltpu.VMEM((full, full), F32), pltpu.VMEM((16 * reps, 2 * full), BF16),
+                sem, sem,
             ],
-            3.0, (), range(reps, 2 * reps + 2),
-        )
-    scaled, out_pieces, grad_pre, slices = dense[:reps], dense[reps : 2 * reps], dense[2 * reps], dense[2 * reps + 1 :]
-    scaled_in = exchange(scaled)
+            2.0, (), (0, 1),
+        )
     slices_in = [slices[0]] + [move_low(slices[k], k) for k in range(1, 4)]
     with jax.named_scope("far_back"):
         far_back = call(

time: 165 us -> 166 us (level)
  waiting for transfers between devices: 55.2 us -> 52.4 us
  starting transfers between devices: 71.7 us -> 73.9 us
    ppermute x24, waiting for transfers between devices: 15.4 us -> 13 us  [shift(): lax.ppermute(value, 'rep', [(i, (i + by) % reps) for i in range(reps)])]
    pallas_call x15 -> x16, Pallas kernels: 30.8 us -> 32.1 us  [call(): pl.pallas_call(body, in_specs=[IN_SMEM] * len(scalars) + [IN_HBM if i in...]
  transfers between devices with their start and end apart: 38 -> 38, of which waited for: 13 -> 10; matrix products, arithmetic and copies ran while one was open for 0% -> 0% of each run, Pallas kernels for 12% -> 13%
where the time goes in v7:
time: 166 us; the launch traced here: 165 us
  starting transfers between devices  73.9 us (45%)
  waiting for transfers between devices  52.4 us (32%)
  Pallas kernels  32.1 us (19%)
  local copies, waits for them, and re-layouts  5.88 us (4%)
    pallas_call x16, Pallas kernels, call(): pl.pallas_call(body, in_specs=[IN_SMEM] * len(scalars) + [IN_HBM if i in...  32.1 us
    ppermute x24, starting transfers between devices, shift(): lax.ppermute(value, 'rep', [(i, (i + by) % reps) for i in range(reps)])  30.2 us
    all_to_all x1, waiting for transfers between devices, local(): lax.all_to_all(outgoing, 'dom', split_axis=0, concat_axis=0, tiled=True)  26.2 us
    ppermute x9, starting transfers between devices, move(): return lax.ppermute(value, 'dom', pairs)  17.3 us
    all_to_all x1, starting transfers between devices, local(): lax.all_to_all(outgoing, 'dom', split_axis=0, concat_axis=0, tiled=True)  13.3 us
    ppermute x9, waiting for transfers between devices, move(): return lax.ppermute(value, 'dom', pairs)  13.1 us
    ppermute x24, waiting for transfers between devices, shift(): lax.ppermute(value, 'rep', [(i, (i + by) % reps) for i in range(reps)])  13 us
    all_to_all x1, starting transfers between devices, local(): lax.all_to_all(far_back, 'dom', split_axis=0, concat_axis=0, tiled=True)  9.76 us
  transfers between devices with their start and end apart: 38, of which 10 were waited for; matrix products, arithmetic and copies ran while one was open for 0% of the time, Pallas kernels for 13%

profile of v7, /device:TPU:1, one launch (start us, length us, event | category | flops | bytes accessed | tf_op | source)
XLA Modules:
  0.0 165.5 jit_solution(3521411999725015492)
XLA Ops:
  0.6 3.2 %pick.1 = bf16[64,128,128]{2,1,0:T(8,128)(2,1)} custom-call(s32[2,64]{1,0:T(2,128)} %bitcast.27, bf16[64,4096]{1,0:T(8,128)(2,1)} %feats_ref.3), custom_call_target="tpu_custom_call" | custom-call | flops 2200000000 | bytes 65536 | tf_op jit(solution)/shard_map/pick/pallas_call | solution.py:27
  3.9 13.3 %all-to-all-start = ((bf16[64,128,128]{2,1,0:T(8,128)(2,1)}), bf16[64,128,128]{2,1,0:T(8,128)(2,1)S(1)}, u32[]{:S(2)}, u32[]{:S(2)}) async-start(bf16[64,128,128]{2,1,0:T(8,128)(2,1)} %pick.1), calls=%async_computation | async-start | bytes 4194304 | tf_op jit(solution)/shard_map/all_to_all | solution.py:388
  33.5 7.0 %near.1 = (f32[64,4096]{1,0:T(8,128)S(1)}, f32[8,4096]{1,0:T(8,128)S(1)}, bf16[64,2,128,128]{3,2,1,0:T(8,128)(2,1)}) custom-call(s32[2,32]{1,0:T(2,128)S(1)} %bitcast.23, s32[2,64]{1,0:T(2,128)S(1)} %bitcast.20, bf16[64,4096]{1,0:T(8,128)(2,1)S(1)} %copy-done.4, bf16[32,2,128,128]{3,2,1,0:T(8,128)(2,1)S(1)} %copy-done.1, bf16[64,2,128,128]{3,2,1,0:T(8,128)(2,1)S(1)} %bitcast.19), custom_call_target="tpu_custom_call" | custom-call | flops 8800000000 | bytes 65536 | tf_op jit(solution)/shard_map/near/pallas_call | solution.py:27
  42.2 26.2 %all-to-all-done.got_ref = bf16[64,128,128]{2,1,0:T(8,128)(2,1)S(1)} async-done(((bf16[64,128,128]{2,1,0:T(8,128)(2,1)}), bf16[64,128,128]{2,1,0:T(8,128)(2,1)S(1)}, u32[]{:S(2)}, u32[]{:S(2)}) %all-to-all-start) | async-done | bytes 2097184 | tf_op jit(solution)/shard_map/all_to_all | solution.py:388
  68.5 4.1 %far.1 = (bf16[64,1024]{1,0:T(8,128)(2,1)S(1)}, bf16[64,1024]{1,0:T(8,128)(2,1)S(1)}, bf16[64,1024]{1,0:T(8,128)(2,1)S(1)}, bf16[64,1024]{1,0:T(8,128)(2,1)S(1)}) custom-call(s32[2]{0:T(128)S(1)} %pad_add_fusion.rep_ref.place_ref, s32[2,64]{1,0:T(2,128)S(1)} %bitcast.21, bf16[64,128,128]{2,1,0:T(8,128)(2,1)S(1)} %all-to-all-done.got_ref, ...), custom_call_target="tpu_custom_call" | custom-call | flops 6600000000 | bytes 65536 | tf_op jit(solution)/shard_map/far/pallas_call | solution.py:27
  73.9 2.4 %collective-permute-start.10 = (bf16[64,1024]{1,0:T(8,128)(2,1)S(1)}, bf16[64,1024]{1,0:T(8,128)(2,1)S(1)}, u32[]{:S(2)}, u32[]{:S(2)}) collective-permute-start(bf16[64,1024]{1,0:T(8,128)(2,1)S(1)} %get-tuple-element.88), channel_id=1, source_target_pairs={{0,2},{1,3},{2,0},{3,1},{4,6},{5,7},{6,4},{7,5},{8,10},{9,11},{10,... | collective-permute-start | bytes 393224 | tf_op jit(solution)/shard_map/ppermute | solution.py:360
  78.5 3.8 %collective-permute-done.10.refs_2_ = bf16[64,1024]{1,0:T(8,128)(2,1)S(1)} collective-permute-done((bf16[64,1024]{1,0:T(8,128)(2,1)S(1)}, bf16[64,1024]{1,0:T(8,128)(2,1)S(1)}, u32[]{:S(2)}, u32[]{:S(2)}) %collective-permute-start.10) | collective-permute-done | bytes 131104 | tf_op jit(solution)/shard_map/ppermute | solution.py:360
  82.4 2.3 %dense.1 = (bf16[64,1024]{1,0:T(8,128)(2,1)S(1)}, bf16[64,1024]{1,0:T(8,128)(2,1)S(1)}, bf16[64,1024]{1,0:T(8,128)(2,1)S(1)}, bf16[64,1024]{1,0:T(8,128)(2,1)S(1...) custom-call(s32[2]{0:T(128)S(1)} %pad_add_fusion.rep_ref.place_ref, ...), custom_call_target="tpu_custom_call" | custom-call | flops 2200000000 | bytes 65536 | tf_op jit(solution)/shard_map/dense/pallas_call | solution.py:27
  85.9 2.2 %collective-permute-start.16 = (bf16[64,1024]{1,0:T(8,128)(2,1)S(1)}, bf16[64,1024]{1,0:T(8,128)(2,1)S(1)}, u32[]{:S(2)}, u32[]{:S(2)}) collective-permute-start(bf16[64,1024]{1,0:T(8,128)(2,1)S(1)} %get-tuple-element.109), channel_id=1, source_target_pairs={{0,2},{1,3},{2,0},{3,1},{4,6},{5,7},{6,4},{7,5},{8,10},{9,11},{10,... | collective-permute-start | bytes 393224 | tf_op jit(solution)/shard_map/ppermute | solution.py:360
  94.3 4.7 %far_back.1 = bf16[64,128,128]{2,1,0:T(8,128)(2,1)} custom-call(s32[2]{0:T(128)S(1)} %pad_add_fusion.rep_ref.place_ref, s32[2,64]{1,0:T(2,128)S(1)} %bitcast.22, bf16[64,1024]{1,0:T(8,128)(2,1)S(1)} %get-tuple-element.107.s0.refs_0_, bf16[64,1024]{1,0:T(8,128)(2,1)S(1)} %collective-permute-done.15.s1.refs_1_, ...), custom_call_target="tpu_custom_call" | custom-call | flops 5500000256 | bytes 65536 | tf_op jit(solution)/shard_map/far_back/pallas_call | solution.py:27
  99.0 9.8 %all-to-all-start.1 = ((bf16[64,128,128]{2,1,0:T(8,128)(2,1)}), bf16[64,128,128]{2,1,0:T(8,128)(2,1)S(1)}, u32[]{:S(2)}, u32[]{:S(2)}) async-start(bf16[64,128,128]{2,1,0:T(8,128)(2,1)} %far_back.1), calls=%async_computation.1 | async-start | bytes 4194304 | tf_op jit(solution)/shard_map/all_to_all | solution.py:446
  109.0 2.0 %collective-permute-start.19 = (f32[16,512]{1,0:T(8,128)S(1)}, f32[16,512]{1,0:T(8,128)S(1)}, u32[]{:S(2)}, u32[]{:S(2)}) collective-permute-start(f32[16,512]{1,0:T(8,128)S(1)} %get-tuple-element.117), channel_id=1, source_target_pairs={{0,2},{1,3},{2,0},{3,1},{4,6},{5,7},{6,4},{7,5},{8,10},{9,11},{10,... | collective-permute-start | bytes 98312 | tf_op jit(solution)/shard_map/slice_sums/ppermute | solution.py:360
  111.0 2.7 %collective-permute-start.28 = (bf16[64,1024]{1,0:T(8,128)(2,1)S(1)}, bf16[64,1024]{1,0:T(8,128)(2,1)S(1)}, u32[]{:S(2)}, u32[]{:S(2)}) collective-permute-start(bf16[64,1024]{1,0:T(8,128)(2,1)S(1)} %copy-done.30), channel_id=1, source_target_pairs={{0,3},{1,0},{2,1},{3,2},{4,7},{5,4},{6,5},{7,6},{8,11},{9,8},{10,9... | collective-permute-start | bytes 393224 | tf_op jit(solution)/shard_map/ppermute | solution.py:360
  115.0 2.3 %collective-permute-start.21 = (f32[16,512]{1,0:T(8,128)S(1)}, f32[16,512]{1,0:T(8,128)S(1)}, u32[]{:S(2)}, u32[]{:S(2)}) collective-permute-start(f32[16,512]{1,0:T(8,128)S(1)} %slice_sums.5.refs_0_), channel_id=1, source_target_pairs={{0,4},{4,0},{8,12},{12,8},{16,20},{20,16},{24,28},{28,24},{32,36},... | collective-permute-start | bytes 98312 | tf_op jit(solution)/shard_map/slice_sums/ppermute | solution.py:369
  121.0 2.8 %collective-permute-start.24 = (f32[16,512]{1,0:T(8,128)S(1)}, f32[16,512]{1,0:T(8,128)S(1)}, u32[]{:S(2)}, u32[]{:S(2)}) collective-permute-start(f32[16,512]{1,0:T(8,128)S(1)} %slice_sums.6.refs_0_), channel_id=1, source_target_pairs={{0,192},{4,196},{8,200},{12,204},{16,208},{20,212},{24,216},{28,22... | collective-permute-start | bytes 98312 | tf_op jit(solution)/shard_map/slice_sums/ppermute | solution.py:369
  125.9 2.5 %collective-permute-done.23.refs_2_ = f32[16,512]{1,0:T(8,128)S(1)} collective-permute-done((f32[16,512]{1,0:T(8,128)S(1)}, f32[16,512]{1,0:T(8,128)S(1)}, u32[]{:S(2)}, u32[]{:S(2)}) %collective-permute-start.23) | collective-permute-done | bytes 32800 | tf_op jit(solution)/shard_map/slice_sums/ppermute | solution.py:369
  128.4 2.1 %collective-permute-start.29 = (bf16[64,1024]{1,0:T(8,128)(2,1)S(1)}, bf16[64,1024]{1,0:T(8,128)(2,1)S(1)}, u32[]{:S(2)}, u32[]{:S(2)}) collective-permute-start(bf16[64,1024]{1,0:T(8,128)(2,1)S(1)} %copy-done.29), channel_id=1, source_target_pairs={{0,2},{1,3},{2,0},{3,1},{4,6},{5,7},{6,4},{7,5},{8,10},{9,11},{10,... | collective-permute-start | bytes 393224 | tf_op jit(solution)/shard_map/ppermute | solution.py:360
  131.0 3.0 %collective-permute-done.29.refs_10_ = bf16[64,1024]{1,0:T(8,128)(2,1)S(1)} collective-permute-done((bf16[64,1024]{1,0:T(8,128)(2,1)S(1)}, bf16[64,1024]{1,0:T(8,128)(2,1)S(1)}, u32[]{:S(2)}, u32[]{:S(2)}) %collective-permute-start.29) | collective-permute-done | bytes 131104 | tf_op jit(solution)/shard_map/ppermute | solution.py:360
  134.0 3.3 %collective-permute-done.30.refs_11_ = bf16[64,1024]{1,0:T(8,128)(2,1)S(1)} collective-permute-done((bf16[64,1024]{1,0:T(8,128)(2,1)S(1)}, bf16[64,1024]{1,0:T(8,128)(2,1)S(1)}, u32[]{:S(2)}, u32[]{:S(2)}) %collective-permute-start.30) | collective-permute-done | bytes 131104 | tf_op jit(solution)/shard_map/ppermute | solution.py:360
  137.4 3.2 %near_back.1 = (f32[64,4096]{1,0:T(8,128)S(1)}, bf16[64,4096]{1,0:T(8,128)(2,1)}) custom-call(s32[2]{0:T(128)S(1)} %pad_add_fusion.rep_ref.place_ref, s32[2,32]{1,0:T(2,128)S(1)} %bitcast.24, bf16[64,1024]{1,0:T(8,128)(2,1)S(1)} %get-tuple-element.107.s0.refs_0_, bf16[64,1024]{1,0:T(8,128)(2,1)S(1)} %collective-permute-done.15.s1.refs_1_, ...), custom_call_target="tpu_custom_call" | custom-call | flops 2200000000 | bytes 65536 | tf_op jit(solution)/shard_map/near_back/pallas_call | solution.py:27
  140.6 5.5 %collective-permute-start.34 = (bf16[16,512]{1,0:T(8,128)(2,1)S(1)}, bf16[16,512]{1,0:T(8,128)(2,1)S(1)}, u32[]{:S(2)}, u32[]{:S(2)}) collective-permute-start(bf16[16,512]{1,0:T(8,128)(2,1)S(1)} %slice_sums.7.mine_ref), channel_id=1, source_target_pairs={{0,32},{4,36},{8,40},{12,44},{16,48},{20,52},{24,56},{28,60},{32,0... | collective-permute-start | bytes 49160 | tf_op jit(solution)/shard_map/spread/ppermute | solution.py:369
  146.6 2.2 %collective-permute-start.32 = (bf16[16,512]{1,0:T(8,128)(2,1)S(1)}, bf16[16,512]{1,0:T(8,128)(2,1)S(1)}, u32[]{:S(2)}, u32[]{:S(2)}) collective-permute-start(bf16[16,512]{1,0:T(8,128)(2,1)S(1)} %slice_sums.7.mine_ref), channel_id=1, source_target_pairs={{0,16},{4,52},{8,24},{12,60},{16,32},{20,4},{24,40},{28,12},{32,48... | collective-permute-start | bytes 49160 | tf_op jit(solution)/shard_map/spread/ppermute | solution.py:369
  150.4 9.9 %collective-permute-done.34.refs_3_ = bf16[16,512]{1,0:T(8,128)(2,1)S(1)} collective-permute-done((bf16[16,512]{1,0:T(8,128)(2,1)S(1)}, bf16[16,512]{1,0:T(8,128)(2,1)S(1)}, u32[]{:S(2)}, u32[]{:S(2)}) %collective-permute-start.34) | collective-permute-done | bytes 16416 | tf_op jit(solution)/shard_map/spread/ppermute | solution.py:369
  161.4 2.8 %home.1 = bf16[64,4096]{1,0:T(8,128)(2,1)} custom-call(s32[2,64]{1,0:T(2,128)} %bitcast.28, bf16[64,128,128]{2,1,0:T(8,128)(2,1)S(1)} %all-to-all-done.1.got_ref, f32[64,4096]{1,0:T(8,128)} %copy-done.15), custom_call_target="tpu_custom_call" | custom-call | flops 3300000000 | bytes 65536 | tf_op jit(solution)/shard_map/home/pallas_call | solution.py:27
  (132 shorter events, 41.0 us)
Async XLA Ops:
  3.9 64.6 %all-to-all-start = ((bf16[64,128,128]{2,1,0:T(8,128)(2,1)}), bf16[64,128,128]{2,1,0:T(8,128)(2,1)S(1)}, u32[]{:S(2)}, u32[]{:S(2)}) async-start(bf16[64,128,128]{2,1,0:T(8,128)(2,1)} %pick.1), calls=%async_computation | async-start | bytes 4194304 | tf_op jit(solution)/shard_map/all_to_all | solution.py:388
  18.6 11.5 %collective-permute-start = (bf16[64,1024]{1,0:T(8,128)(2,1)S(1)}, bf16[64,1024]{1,0:T(8,128)(2,1)S(1)}, u32[]{:S(2)}, u32[]{:S(2)}) collective-permute-start(bf16[64,1024]{1,0:T(8,128)(2,1)S(1)} %get-tuple-element.72), channel_id=1, source_target_pairs={{0,1},{1,2},{2,3},{3,0},{4,5},{5,6},{6,7},{7,4},{8,9},{9,10},{10,1... | collective-permute-start | bytes 393224 | tf_op jit(solution)/shard_map/ppermute | solution.py:360
  23.2 18.9 %collective-permute-start.1 = (bf16[64,1024]{1,0:T(8,128)(2,1)S(1)}, bf16[64,1024]{1,0:T(8,128)(2,1)S(1)}, u32[]{:S(2)}, u32[]{:S(2)}) collective-permute-start(bf16[64,1024]{1,0:T(8,128)(2,1)S(1)} %get-tuple-element.73), channel_id=1, source_target_pairs={{0,2},{1,3},{2,0},{3,1},{4,6},{5,7},{6,4},{7,5},{8,10},{9,11},{10,... | collective-permute-start | bytes 393224 | tf_op jit(solution)/shard_map/ppermute | solution.py:360
  25.6 16.6 %collective-permute-start.2 = (bf16[64,1024]{1,0:T(8,128)(2,1)S(1)}, bf16[64,1024]{1,0:T(8,128)(2,1)S(1)}, u32[]{:S(2)}, u32[]{:S(2)}) collective-permute-start(bf16[64,1024]{1,0:T(8,128)(2,1)S(1)} %get-tuple-element.74), channel_id=1, source_target_pairs={{0,3},{1,0},{2,1},{3,2},{4,7},{5,4},{6,5},{7,6},{8,11},{9,8},{10,9... | collective-permute-start | bytes 393224 | tf_op jit(solution)/shard_map/ppermute | solution.py:360
  27.7 14.5 %collective-permute-start.3 = (bf16[64,1024]{1,0:T(8,128)(2,1)S(1)}, bf16[64,1024]{1,0:T(8,128)(2,1)S(1)}, u32[]{:S(2)}, u32[]{:S(2)}) collective-permute-start(bf16[64,1024]{1,0:T(8,128)(2,1)S(1)} %get-tuple-element.76), channel_id=1, source_target_pairs={{0,1},{1,2},{2,3},{3,0},{4,5},{5,6},{6,7},{7,4},{8,9},{9,10},{10,1... | collective-permute-start | bytes 393224 | tf_op jit(solution)/shard_map/ppermute | solution.py:360
  28.7 13.4 %collective-permute-start.4 = (bf16[64,1024]{1,0:T(8,128)(2,1)S(1)}, bf16[64,1024]{1,0:T(8,128)(2,1)S(1)}, u32[]{:S(2)}, u32[]{:S(2)}) collective-permute-start(bf16[64,1024]{1,0:T(8,128)(2,1)S(1)} %get-tuple-element.77), channel_id=1, source_target_pairs={{0,2},{1,3},{2,0},{3,1},{4,6},{5,7},{6,4},{7,5},{8,10},{9,11},{10,... | collective-permute-start | bytes 393224 | tf_op jit(solution)/shard_map/ppermute | solution.py:360
  30.1 12.1 %collective-permute-start.5 = (bf16[64,1024]{1,0:T(8,128)(2,1)S(1)}, bf16[64,1024]{1,0:T(8,128)(2,1)S(1)}, u32[]{:S(2)}, u32[]{:S(2)}) collective-permute-start(bf16[64,1024]{1,0:T(8,128)(2,1)S(1)} %get-tuple-element.78), channel_id=1, source_target_pairs={{0,3},{1,0},{2,1},{3,2},{4,7},{5,4},{6,5},{7,6},{8,11},{9,8},{10,9... | collective-permute-start | bytes 393224 | tf_op jit(solution)/shard_map/ppermute | solution.py:360
  73.9 8.5 %collective-permute-start.10 = (bf16[64,1024]{1,0:T(8,128)(2,1)S(1)}, bf16[64,1024]{1,0:T(8,128)(2,1)S(1)}, u32[]{:S(2)}, u32[]{:S(2)}) collective-permute-start(bf16[64,1024]{1,0:T(8,128)(2,1)S(1)} %get-tuple-element.88), channel_id=1, source_target_pairs={{0,2},{1,3},{2,0},{3,1},{4,6},{5,7},{6,4},{7,5},{8,10},{9,11},{10,... | collective-permute-start | bytes 393224 | tf_op jit(solution)/shard_map/ppermute | solution.py:360
  84.7 7.9 %collective-permute-start.15 = (bf16[64,1024]{1,0:T(8,128)(2,1)S(1)}, bf16[64,1024]{1,0:T(8,128)(2,1)S(1)}, u32[]{:S(2)}, u32[]{:S(2)}) collective-permute-start(bf16[64,1024]{1,0:T(8,128)(2,1)S(1)} %get-tuple-element.108), channel_id=1, source_target_pairs={{0,1},{1,2},{2,3},{3,0},{4,5},{5,6},{6,7},{7,4},{8,9},{9,10},{10,1... | collective-permute-start | bytes 393224 | tf_op jit(solution)/shard_map/ppermute | solution.py:360
  85.9 8.4 %collective-permute-start.16 = (bf16[64,1024]{1,0:T(8,128)(2,1)S(1)}, bf16[64,1024]{1,0:T(8,128)(2,1)S(1)}, u32[]{:S(2)}, u32[]{:S(2)}) collective-permute-start(bf16[64,1024]{1,0:T(8,128)(2,1)S(1)} %get-tuple-element.109), channel_id=1, source_target_pairs={{0,2},{1,3},{2,0},{3,1},{4,6},{5,7},{6,4},{7,5},{8,10},{9,11},{10,... | collective-permute-start | bytes 393224 | tf_op jit(solution)/shard_map/ppermute | solution.py:360
  88.0 6.2 %collective-permute-start.17 = (bf16[64,1024]{1,0:T(8,128)(2,1)S(1)}, bf16[64,1024]{1,0:T(8,128)(2,1)S(1)}, u32[]{:S(2)}, u32[]{:S(2)}) collective-permute-start(bf16[64,1024]{1,0:T(8,128)(2,1)S(1)} %get-tuple-element.110), channel_id=1, source_target_pairs={{0,3},{1,0},{2,1},{3,2},{4,7},{5,4},{6,5},{7,6},{8,11},{9,8},{10,9... | collective-permute-start | bytes 393224 | tf_op jit(solution)/shard_map/ppermute | solution.py:360
  90.9 8.1 %collective-permute-start.12 = (bf16[64,512]{1,0:T(8,128)(2,1)S(1)}, bf16[64,512]{1,0:T(8,128)(2,1)S(1)}, u32[]{:S(2)}, u32[]{:S(2)}) collective-permute-start(bf16[64,512]{1,0:T(8,128)(2,1)S(1)} %get-tuple-element.104), channel_id=1, source_target_pairs={{0,8},{4,12},{8,16},{12,20},{16,24},{20,28},{24,0},{28,4},{32,40},... | collective-permute-start | bytes 196616 | tf_op jit(solution)/shard_map/ppermute | solution.py:378
  91.2 7.8 %collective-permute-start.13 = (bf16[64,512]{1,0:T(8,128)(2,1)S(1)}, bf16[64,512]{1,0:T(8,128)(2,1)S(1)}, u32[]{:S(2)}, u32[]{:S(2)}) collective-permute-start(bf16[64,512]{1,0:T(8,128)(2,1)S(1)} %get-tuple-element.105), channel_id=1, source_target_pairs={{0,16},{4,20},{8,24},{12,28},{16,0},{20,4},{24,8},{28,12},{32,48},... | collective-permute-start | bytes 196616 | tf_op jit(solution)/shard_map/ppermute | solution.py:378
  92.7 6.3 %collective-permute-start.14 = (bf16[64,512]{1,0:T(8,128)(2,1)S(1)}, bf16[64,512]{1,0:T(8,128)(2,1)S(1)}, u32[]{:S(2)}, u32[]{:S(2)}) collective-permute-start(bf16[64,512]{1,0:T(8,128)(2,1)S(1)} %get-tuple-element.106), channel_id=1, source_target_pairs={{0,24},{4,28},{8,0},{12,4},{16,8},{20,12},{24,16},{28,20},{32,56},... | collective-permute-start | bytes 196616 | tf_op jit(solution)/shard_map/ppermute | solution.py:378
  99.0 62.4 %all-to-all-start.1 = ((bf16[64,128,128]{2,1,0:T(8,128)(2,1)}), bf16[64,128,128]{2,1,0:T(8,128)(2,1)S(1)}, u32[]{:S(2)}, u32[]{:S(2)}) async-start(bf16[64,128,128]{2,1,0:T(8,128)(2,1)} %far_back.1), calls=%async_computation.1 | async-start | bytes 4194304 | tf_op jit(solution)/shard_map/all_to_all | solution.py:446
  111.0 12.8 %collective-permute-start.28 = (bf16[64,1024]{1,0:T(8,128)(2,1)S(1)}, bf16[64,1024]{1,0:T(8,128)(2,1)S(1)}, u32[]{:S(2)}, u32[]{:S(2)}) collective-permute-start(bf16[64,1024]{1,0:T(8,128)(2,1)S(1)} %copy-done.30), channel_id=1, source_target_pairs={{0,3},{1,0},{2,1},{3,2},{4,7},{5,4},{6,5},{7,6},{8,11},{9,8},{10,9... | collective-permute-start | bytes 393224 | tf_op jit(solution)/shard_map/ppermute | solution.py:360
  118.2 19.1 %collective-permute-start.25 = (f32[64,1024]{1,0:T(8,128)S(1)}, f32[64,1024]{1,0:T(8,128)S(1)}, u32[]{:S(2)}, u32[]{:S(2)}) collective-permute-start(f32[64,1024]{1,0:T(8,128)S(1)} %get-tuple-element.121), channel_id=1, source_target_pairs={{0,1},{1,2},{2,3},{3,0},{4,5},{5,6},{6,7},{7,4},{8,9},{9,10},{10,1... | collective-permute-start | bytes 786440 | tf_op jit(solution)/shard_map/ppermute | solution.py:360
  118.3 19.0 %collective-permute-start.26 = (f32[64,1024]{1,0:T(8,128)S(1)}, f32[64,1024]{1,0:T(8,128)S(1)}, u32[]{:S(2)}, u32[]{:S(2)}) collective-permute-start(f32[64,1024]{1,0:T(8,128)S(1)} %get-tuple-element.122), channel_id=1, source_target_pairs={{0,2},{1,3},{2,0},{3,1},{4,6},{5,7},{6,4},{7,5},{8,10},{9,11},{10,... | collective-permute-start | bytes 786440 | tf_op jit(solution)/shard_map/ppermute | solution.py:360
  120.1 17.3 %collective-permute-start.27 = (f32[64,1024]{1,0:T(8,128)S(1)}, f32[64,1024]{1,0:T(8,128)S(1)}, u32[]{:S(2)}, u32[]{:S(2)}) collective-permute-start(f32[64,1024]{1,0:T(8,128)S(1)} %get-tuple-element.123), channel_id=1, source_target_pairs={{0,3},{1,0},{2,1},{3,2},{4,7},{5,4},{6,5},{7,6},{8,11},{9,8},{10,9... | collective-permute-start | bytes 786440 | tf_op jit(solution)/shard_map/ppermute | solution.py:360
  130.5 6.8 %collective-permute-start.30 = (bf16[64,1024]{1,0:T(8,128)(2,1)S(1)}, bf16[64,1024]{1,0:T(8,128)(2,1)S(1)}, u32[]{:S(2)}, u32[]{:S(2)}) collective-permute-start(bf16[64,1024]{1,0:T(8,128)(2,1)S(1)} %copy-done.28), channel_id=1, source_target_pairs={{0,1},{1,2},{2,3},{3,0},{4,5},{5,6},{6,7},{7,4},{8,9},{9,10},{10,1... | collective-permute-start | bytes 393224 | tf_op jit(solution)/shard_map/ppermute | solution.py:360
  140.6 19.7 %collective-permute-start.34 = (bf16[16,512]{1,0:T(8,128)(2,1)S(1)}, bf16[16,512]{1,0:T(8,128)(2,1)S(1)}, u32[]{:S(2)}, u32[]{:S(2)}) collective-permute-start(bf16[16,512]{1,0:T(8,128)(2,1)S(1)} %slice_sums.7.mine_ref), channel_id=1, source_target_pairs={{0,32},{4,36},{8,40},{12,44},{16,48},{20,52},{24,56},{28,60},{32,0... | collective-permute-start | bytes 49160 | tf_op jit(solution)/shard_map/spread/ppermute | solution.py:369
  146.1 14.2 %collective-permute-start.33 = (bf16[16,512]{1,0:T(8,128)(2,1)S(1)}, bf16[16,512]{1,0:T(8,128)(2,1)S(1)}, u32[]{:S(2)}, u32[]{:S(2)}) collective-permute-start(bf16[16,512]{1,0:T(8,128)(2,1)S(1)} %slice_sums.7.mine_ref), channel_id=1, source_target_pairs={{0,24},{4,44},{8,32},{12,52},{16,40},{20,60},{24,48},{28,4},{32,56... | collective-permute-start | bytes 49160 | tf_op jit(solution)/shard_map/spread/ppermute | solution.py:369
  146.6 13.7 %collective-permute-start.32 = (bf16[16,512]{1,0:T(8,128)(2,1)S(1)}, bf16[16,512]{1,0:T(8,128)(2,1)S(1)}, u32[]{:S(2)}, u32[]{:S(2)}) collective-permute-start(bf16[16,512]{1,0:T(8,128)(2,1)S(1)} %slice_sums.7.mine_ref), channel_id=1, source_target_pairs={{0,16},{4,52},{8,24},{12,60},{16,32},{20,4},{24,40},{28,12},{32,48... | collective-permute-start | bytes 49160 | tf_op jit(solution)/shard_map/spread/ppermute | solution.py:369
  148.8 11.5 %collective-permute-start.31 = (bf16[16,512]{1,0:T(8,128)(2,1)S(1)}, bf16[16,512]{1,0:T(8,128)(2,1)S(1)}, u32[]{:S(2)}, u32[]{:S(2)}) collective-permute-start(bf16[16,512]{1,0:T(8,128)(2,1)S(1)} %slice_sums.7.mine_ref), channel_id=1, source_target_pairs={{0,8},{4,60},{8,16},{12,4},{16,24},{20,12},{24,32},{28,20},{32,40}... | collective-permute-start | bytes 49160 | tf_op jit(solution)/shard_map/spread/ppermute | solution.py:369
  (45 other events, 375.0 us)

commit v8 on v6

--- a/solution.py
+++ b/solution.py
@@ -6,7 +6,7 @@
 from jax.sharding import PartitionSpec as P
 
 TILE = 128
-STEP = 8
+STEP = 4
 VMEM_BYTES = 12 * 1024 * 1024
 F32 = jnp.float32
 BF16 = jnp.bfloat16
@@ -310,7 +310,7 @@
                 acc_ref[:, lanes(cols_ref[link, row], TILE)] += term
 
 
-def home_body(send_ref, got_ref, near_acc_hbm, grad_ref, acc_ref, near_acc_ref, sem):
+def home_body(send_ref, got_ref, near_acc_hbm, grad_hbm, acc_ref, near_acc_ref, grad_ref, sem, sems):
     chans = acc_ref.shape[0]
     parts = got_ref.shape[0]
     load = pltpu.make_async_copy(near_acc_hbm, near_acc_ref, sem)
@@ -321,7 +321,15 @@
             block = send_ref[slot, item]
             acc_ref[:, lanes(block, TILE)] += got_ref[item, slot * chans : (slot + 1) * chans, :].astype(F32)
     load.wait()
-    grad_ref[...] = (near_acc_ref[...] + acc_ref[...]).astype(BF16)
+    rows = chans // 4
+    copies = []
+    for piece in range(4):
+        where = slice(piece * rows, (piece + 1) * rows)
+        grad_ref[where, :] = (near_acc_ref[where, :] + acc_ref[where, :]).astype(BF16)
+        copies.append(pltpu.make_async_copy(grad_ref.at[where], grad_hbm.at[where], sems.at[piece]))
+        copies[-1].start()
+    for copy in copies:
+        copy.wait()
 
 
 def local(feats, w_self, w_neigh, local_cols, local_tiles, send_list, remote_rows, remote_tiles, cotangent):
@@ -448,7 +456,8 @@
         other = move(own, 0, 0, 1)
     with jax.named_scope("home"):
         grad_feats = call(
-            home_body, (sends,), (returned, near_back), shape((chans, nodes), BF16), [wide32, wide32, sem], 3.0, (1,)
+            home_body, (sends,), (returned, near_back), in_hbm((chans, nodes), BF16),
+            [wide32, wide32, pltpu.VMEM((chans, nodes), BF16), sem, pltpu.SemaphoreType.DMA((4,))], 3.0, (1,), (0,),
         )
     with jax.named_scope("join"):
         other, grad_feats = lax.optimization_barrier((other, grad_feats))

time: 165 us -> 167 us (1.012)
  Pallas kernels: 30.8 us -> 34.3 us
    pallas_call x15, Pallas kernels: 30.8 us -> 34.3 us  [call(): pl.pallas_call(body, in_specs=[IN_SMEM] * len(scalars) + [IN_HBM if i in...]
  transfers between devices with their start and end apart: 38 -> 38, of which waited for: 13 -> 13; matrix products, arithmetic and copies ran while one was open for 0% -> 0% of each run, Pallas kernels for 12% -> 13%
where the time goes in v8:
time: 167 us; the launch traced here: 166 us
  starting transfers between devices  71.7 us (43%)
  waiting for transfers between devices  53.8 us (32%)
  Pallas kernels  34.3 us (21%)
  local copies, waits for them, and re-layouts  5.27 us (3%)
    pallas_call x15, Pallas kernels, call(): pl.pallas_call(body, in_specs=[IN_SMEM] * len(scalars) + [IN_HBM if i in...  34.3 us
    ppermute x24, starting transfers between devices, shift(): lax.ppermute(value, 'rep', [(i, (i + by) % reps) for i in range(reps)])  30 us
    all_to_all x1, waiting for transfers between devices, local(): lax.all_to_all(outgoing, 'dom', split_axis=0, concat_axis=0, tiled=True)  25.5 us
    ppermute x9, starting transfers between devices, move(): return lax.ppermute(value, 'dom', pairs)  16.2 us
    ppermute x24, waiting for transfers between devices, shift(): lax.ppermute(value, 'rep', [(i, (i + by) % reps) for i in range(reps)])  15.4 us
    all_to_all x1, starting transfers between devices, local(): lax.all_to_all(outgoing, 'dom', split_axis=0, concat_axis=0, tiled=True)  13.3 us
    ppermute x9, waiting for transfers between devices, move(): return lax.ppermute(value, 'dom', pairs)  13 us
    all_to_all x1, starting transfers between devices, local(): lax.all_to_all(far_back, 'dom', split_axis=0, concat_axis=0, tiled=True)  9 us
  transfers between devices with their start and end apart: 38, of which 13 were waited for; matrix products, arithmetic and copies ran while one was open for 0% of the time, Pallas kernels for 13%

profile of v8, /device:TPU:1, one launch (start us, length us, event | category | flops | bytes accessed | tf_op | source)
XLA Modules:
  0.0 166.4 jit_solution(2002296203913903987)
XLA Ops:
  0.6 3.3 %pick.1 = bf16[64,128,128]{2,1,0:T(8,128)(2,1)} custom-call(s32[2,64]{1,0:T(2,128)} %bitcast.27, bf16[64,4096]{1,0:T(8,128)(2,1)} %feats_ref.3), custom_call_target="tpu_custom_call" | custom-call | flops 2200000000 | bytes 65536 | tf_op jit(solution)/shard_map/pick/pallas_call | solution.py:27
  4.0 13.3 %all-to-all-start = ((bf16[64,128,128]{2,1,0:T(8,128)(2,1)}), bf16[64,128,128]{2,1,0:T(8,128)(2,1)S(1)}, u32[]{:S(2)}, u32[]{:S(2)}) async-start(bf16[64,128,128]{2,1,0:T(8,128)(2,1)} %pick.1), calls=%async_computation | async-start | bytes 4194304 | tf_op jit(solution)/shard_map/all_to_all | solution.py:382
  29.5 1.9 %collective-permute-start.5 = (bf16[64,1024]{1,0:T(8,128)(2,1)S(1)}, bf16[64,1024]{1,0:T(8,128)(2,1)S(1)}, u32[]{:S(2)}, u32[]{:S(2)}) collective-permute-start(bf16[64,1024]{1,0:T(8,128)(2,1)S(1)} %get-tuple-element.77), channel_id=1, source_target_pairs={{0,3},{1,0},{2,1},{3,2},{4,7},{5,4},{6,5},{7,6},{8,11},{9,8},{10,9... | collective-permute-start | bytes 393224 | tf_op jit(solution)/shard_map/ppermute | solution.py:354
  33.0 8.3 %near.1 = (f32[64,4096]{1,0:T(8,128)S(1)}, f32[8,4096]{1,0:T(8,128)S(1)}, bf16[64,2,128,128]{3,2,1,0:T(8,128)(2,1)}) custom-call(s32[2,32]{1,0:T(2,128)S(1)} %bitcast.23, s32[2,64]{1,0:T(2,128)S(1)} %bitcast.20, bf16[64,4096]{1,0:T(8,128)(2,1)S(1)} %copy-done.4, bf16[32,2,128,128]{3,2,1,0:T(8,128)(2,1)S(1)} %copy-done.1, bf16[64,2,128,128]{3,2,1,0:T(8,128)(2,1)S(1)} %bitcast.19), custom_call_target="tpu_custom_call" | custom-call | flops 8800000000 | bytes 65536 | tf_op jit(solution)/shard_map/near/pallas_call | solution.py:27
  43.0 25.5 %all-to-all-done.got_ref = bf16[64,128,128]{2,1,0:T(8,128)(2,1)S(1)} async-done(((bf16[64,128,128]{2,1,0:T(8,128)(2,1)}), bf16[64,128,128]{2,1,0:T(8,128)(2,1)S(1)}, u32[]{:S(2)}, u32[]{:S(2)}) %all-to-all-start) | async-done | bytes 2097184 | tf_op jit(solution)/shard_map/all_to_all | solution.py:382
  68.5 5.2 %far.1 = (bf16[64,1024]{1,0:T(8,128)(2,1)S(1)}, bf16[64,1024]{1,0:T(8,128)(2,1)S(1)}, bf16[64,1024]{1,0:T(8,128)(2,1)S(1)}, bf16[64,1024]{1,0:T(8,128)(2,1)S(1)}) custom-call(s32[2]{0:T(128)S(1)} %pad_add_fusion.rep_ref.place_ref, s32[2,64]{1,0:T(2,128)S(1)} %bitcast.21, bf16[64,128,128]{2,1,0:T(8,128)(2,1)S(1)} %all-to-all-done.got_ref, ...), custom_call_target="tpu_custom_call" | custom-call | flops 6600000000 | bytes 65536 | tf_op jit(solution)/shard_map/far/pallas_call | solution.py:27
  75.1 2.4 %collective-permute-start.10 = (bf16[64,1024]{1,0:T(8,128)(2,1)S(1)}, bf16[64,1024]{1,0:T(8,128)(2,1)S(1)}, u32[]{:S(2)}, u32[]{:S(2)}) collective-permute-start(bf16[64,1024]{1,0:T(8,128)(2,1)S(1)} %get-tuple-element.87), channel_id=1, source_target_pairs={{0,2},{1,3},{2,0},{3,1},{4,6},{5,7},{6,4},{7,5},{8,10},{9,11},{10,... | collective-permute-start | bytes 393224 | tf_op jit(solution)/shard_map/ppermute | solution.py:354
  79.7 3.8 %collective-permute-done.10.refs_2_ = bf16[64,1024]{1,0:T(8,128)(2,1)S(1)} collective-permute-done((bf16[64,1024]{1,0:T(8,128)(2,1)S(1)}, bf16[64,1024]{1,0:T(8,128)(2,1)S(1)}, u32[]{:S(2)}, u32[]{:S(2)}) %collective-permute-start.10) | collective-permute-done | bytes 131104 | tf_op jit(solution)/shard_map/ppermute | solution.py:354
  83.6 2.9 %dense.1 = (bf16[64,1024]{1,0:T(8,128)(2,1)S(1)}, bf16[64,1024]{1,0:T(8,128)(2,1)S(1)}, bf16[64,1024]{1,0:T(8,128)(2,1)S(1)}, bf16[64,1024]{1,0:T(8,128)(2,1)S(1...) custom-call(s32[2]{0:T(128)S(1)} %pad_add_fusion.rep_ref.place_ref, ...), custom_call_target="tpu_custom_call" | custom-call | flops 3300000000 | bytes 65536 | tf_op jit(solution)/shard_map/dense/pallas_call | solution.py:27
  87.7 2.2 %collective-permute-start.16 = (bf16[64,1024]{1,0:T(8,128)(2,1)S(1)}, bf16[64,1024]{1,0:T(8,128)(2,1)S(1)}, u32[]{:S(2)}, u32[]{:S(2)}) collective-permute-start(bf16[64,1024]{1,0:T(8,128)(2,1)S(1)} %get-tuple-element.107), channel_id=1, source_target_pairs={{0,2},{1,3},{2,0},{3,1},{4,6},{5,7},{6,4},{7,5},{8,10},{9,11},{10,... | collective-permute-start | bytes 393224 | tf_op jit(solution)/shard_map/ppermute | solution.py:354
  94.9 5.8 %far_back.1 = bf16[64,128,128]{2,1,0:T(8,128)(2,1)} custom-call(s32[2]{0:T(128)S(1)} %pad_add_fusion.rep_ref.place_ref, s32[2,64]{1,0:T(2,128)S(1)} %bitcast.22, bf16[64,1024]{1,0:T(8,128)(2,1)S(1)} %get-tuple-element.105.s0.refs_0_, bf16[64,1024]{1,0:T(8,128)(2,1)S(1)} %collective-permute-done.15.s1.refs_1_, ...), custom_call_target="tpu_custom_call" | custom-call | flops 5500000256 | bytes 65536 | tf_op jit(solution)/shard_map/far_back/pallas_call | solution.py:27
  100.7 9.0 %all-to-all-start.1 = ((bf16[64,128,128]{2,1,0:T(8,128)(2,1)}), bf16[64,128,128]{2,1,0:T(8,128)(2,1)S(1)}, u32[]{:S(2)}, u32[]{:S(2)}) async-start(bf16[64,128,128]{2,1,0:T(8,128)(2,1)} %far_back.1), calls=%async_computation.1 | async-start | bytes 4194304 | tf_op jit(solution)/shard_map/all_to_all | solution.py:431
  109.8 1.9 %collective-permute-start.18 = (f32[16,512]{1,0:T(8,128)S(1)}, f32[16,512]{1,0:T(8,128)S(1)}, u32[]{:S(2)}, u32[]{:S(2)}) collective-permute-start(f32[16,512]{1,0:T(8,128)S(1)} %get-tuple-element.114), channel_id=1, source_target_pairs={{0,3},{1,0},{2,1},{3,2},{4,7},{5,4},{6,5},{7,6},{8,11},{9,8},{10,9... | collective-permute-start | bytes 98312 | tf_op jit(solution)/shard_map/slice_sums/ppermute | solution.py:354
  112.7 2.6 %collective-permute-start.28 = (bf16[64,1024]{1,0:T(8,128)(2,1)S(1)}, bf16[64,1024]{1,0:T(8,128)(2,1)S(1)}, u32[]{:S(2)}, u32[]{:S(2)}) collective-permute-start(bf16[64,1024]{1,0:T(8,128)(2,1)S(1)} %copy-done.30), channel_id=1, source_target_pairs={{0,3},{1,0},{2,1},{3,2},{4,7},{5,4},{6,5},{7,6},{8,11},{9,8},{10,9... | collective-permute-start | bytes 393224 | tf_op jit(solution)/shard_map/ppermute | solution.py:354
  116.9 2.0 %collective-permute-start.21 = (f32[16,512]{1,0:T(8,128)S(1)}, f32[16,512]{1,0:T(8,128)S(1)}, u32[]{:S(2)}, u32[]{:S(2)}) collective-permute-start(f32[16,512]{1,0:T(8,128)S(1)} %slice_sums.5.refs_0_), channel_id=1, source_target_pairs={{0,4},{4,0},{8,12},{12,8},{16,20},{20,16},{24,28},{28,24},{32,36},... | collective-permute-start | bytes 98312 | tf_op jit(solution)/shard_map/slice_sums/ppermute | solution.py:363
  122.9 2.8 %collective-permute-start.24 = (f32[16,512]{1,0:T(8,128)S(1)}, f32[16,512]{1,0:T(8,128)S(1)}, u32[]{:S(2)}, u32[]{:S(2)}) collective-permute-start(f32[16,512]{1,0:T(8,128)S(1)} %slice_sums.6.refs_0_), channel_id=1, source_target_pairs={{0,192},{4,196},{8,200},{12,204},{16,208},{20,212},{24,216},{28,22... | collective-permute-start | bytes 98312 | tf_op jit(solution)/shard_map/slice_sums/ppermute | solution.py:363
  127.4 3.5 %collective-permute-done.23.refs_2_ = f32[16,512]{1,0:T(8,128)S(1)} collective-permute-done((f32[16,512]{1,0:T(8,128)S(1)}, f32[16,512]{1,0:T(8,128)S(1)}, u32[]{:S(2)}, u32[]{:S(2)}) %collective-permute-start.23) | collective-permute-done | bytes 32800 | tf_op jit(solution)/shard_map/slice_sums/ppermute | solution.py:363
  131.0 2.0 %collective-permute-start.29 = (bf16[64,1024]{1,0:T(8,128)(2,1)S(1)}, bf16[64,1024]{1,0:T(8,128)(2,1)S(1)}, u32[]{:S(2)}, u32[]{:S(2)}) collective-permute-start(bf16[64,1024]{1,0:T(8,128)(2,1)S(1)} %copy-done.29), channel_id=1, source_target_pairs={{0,2},{1,3},{2,0},{3,1},{4,6},{5,7},{6,4},{7,5},{8,10},{9,11},{10,... | collective-permute-start | bytes 393224 | tf_op jit(solution)/shard_map/ppermute | solution.py:354
  133.0 3.6 %collective-permute-done.29.refs_10_ = bf16[64,1024]{1,0:T(8,128)(2,1)S(1)} collective-permute-done((bf16[64,1024]{1,0:T(8,128)(2,1)S(1)}, bf16[64,1024]{1,0:T(8,128)(2,1)S(1)}, u32[]{:S(2)}, u32[]{:S(2)}) %collective-permute-start.29) | collective-permute-done | bytes 131104 | tf_op jit(solution)/shard_map/ppermute | solution.py:354
  136.6 3.4 %collective-permute-done.30.refs_11_ = bf16[64,1024]{1,0:T(8,128)(2,1)S(1)} collective-permute-done((bf16[64,1024]{1,0:T(8,128)(2,1)S(1)}, bf16[64,1024]{1,0:T(8,128)(2,1)S(1)}, u32[]{:S(2)}, u32[]{:S(2)}) %collective-permute-start.30) | collective-permute-done | bytes 131104 | tf_op jit(solution)/shard_map/ppermute | solution.py:354
  140.0 3.2 %near_back.1 = (f32[64,4096]{1,0:T(8,128)S(1)}, bf16[64,4096]{1,0:T(8,128)(2,1)}) custom-call(s32[2]{0:T(128)S(1)} %pad_add_fusion.rep_ref.place_ref, s32[2,32]{1,0:T(2,128)S(1)} %bitcast.24, bf16[64,1024]{1,0:T(8,128)(2,1)S(1)} %get-tuple-element.105.s0.refs_0_, bf16[64,1024]{1,0:T(8,128)(2,1)S(1)} %collective-permute-done.15.s1.refs_1_, ...), custom_call_target="tpu_custom_call" | custom-call | flops 2200000000 | bytes 65536 | tf_op jit(solution)/shard_map/near_back/pallas_call | solution.py:27
  143.2 5.0 %collective-permute-start.34 = (bf16[16,512]{1,0:T(8,128)(2,1)S(1)}, bf16[16,512]{1,0:T(8,128)(2,1)S(1)}, u32[]{:S(2)}, u32[]{:S(2)}) collective-permute-start(bf16[16,512]{1,0:T(8,128)(2,1)S(1)} %slice_sums.7.mine_ref), channel_id=1, source_target_pairs={{0,32},{4,36},{8,40},{12,44},{16,48},{20,52},{24,56},{28,60},{32,0... | collective-permute-start | bytes 49160 | tf_op jit(solution)/shard_map/spread/ppermute | solution.py:363
  152.5 8.8 %collective-permute-done.34.refs_3_ = bf16[16,512]{1,0:T(8,128)(2,1)S(1)} collective-permute-done((bf16[16,512]{1,0:T(8,128)(2,1)S(1)}, bf16[16,512]{1,0:T(8,128)(2,1)S(1)}, u32[]{:S(2)}, u32[]{:S(2)}) %collective-permute-start.34) | collective-permute-done | bytes 16416 | tf_op jit(solution)/shard_map/spread/ppermute | solution.py:363
  162.3 2.8 %home.1 = bf16[64,4096]{1,0:T(8,128)(2,1)} custom-call(s32[2,64]{1,0:T(2,128)} %bitcast.28, bf16[64,128,128]{2,1,0:T(8,128)(2,1)S(1)} %all-to-all-done.1.got_ref, f32[64,4096]{1,0:T(8,128)} %copy-done.15), custom_call_target="tpu_custom_call" | custom-call | flops 3300000000 | bytes 65536 | tf_op jit(solution)/shard_map/home/pallas_call | solution.py:27
  (131 shorter events, 40.2 us)
Async XLA Ops:
  4.0 64.6 %all-to-all-start = ((bf16[64,128,128]{2,1,0:T(8,128)(2,1)}), bf16[64,128,128]{2,1,0:T(8,128)(2,1)S(1)}, u32[]{:S(2)}, u32[]{:S(2)}) async-start(bf16[64,128,128]{2,1,0:T(8,128)(2,1)} %pick.1), calls=%async_computation | async-start | bytes 4194304 | tf_op jit(solution)/shard_map/all_to_all | solution.py:382
  18.7 10.8 %collective-permute-start = (bf16[64,1024]{1,0:T(8,128)(2,1)S(1)}, bf16[64,1024]{1,0:T(8,128)(2,1)S(1)}, u32[]{:S(2)}, u32[]{:S(2)}) collective-permute-start(bf16[64,1024]{1,0:T(8,128)(2,1)S(1)} %get-tuple-element.71), channel_id=1, source_target_pairs={{0,1},{1,2},{2,3},{3,0},{4,5},{5,6},{6,7},{7,4},{8,9},{9,10},{10,1... | collective-permute-start | bytes 393224 | tf_op jit(solution)/shard_map/ppermute | solution.py:354
  23.3 19.7 %collective-permute-start.1 = (bf16[64,1024]{1,0:T(8,128)(2,1)S(1)}, bf16[64,1024]{1,0:T(8,128)(2,1)S(1)}, u32[]{:S(2)}, u32[]{:S(2)}) collective-permute-start(bf16[64,1024]{1,0:T(8,128)(2,1)S(1)} %get-tuple-element.72), channel_id=1, source_target_pairs={{0,2},{1,3},{2,0},{3,1},{4,6},{5,7},{6,4},{7,5},{8,10},{9,11},{10,... | collective-permute-start | bytes 393224 | tf_op jit(solution)/shard_map/ppermute | solution.py:354
  25.6 17.3 %collective-permute-start.2 = (bf16[64,1024]{1,0:T(8,128)(2,1)S(1)}, bf16[64,1024]{1,0:T(8,128)(2,1)S(1)}, u32[]{:S(2)}, u32[]{:S(2)}) collective-permute-start(bf16[64,1024]{1,0:T(8,128)(2,1)S(1)} %get-tuple-element.73), channel_id=1, source_target_pairs={{0,3},{1,0},{2,1},{3,2},{4,7},{5,4},{6,5},{7,6},{8,11},{9,8},{10,9... | collective-permute-start | bytes 393224 | tf_op jit(solution)/shard_map/ppermute | solution.py:354
  27.1 15.8 %collective-permute-start.3 = (bf16[64,1024]{1,0:T(8,128)(2,1)S(1)}, bf16[64,1024]{1,0:T(8,128)(2,1)S(1)}, u32[]{:S(2)}, u32[]{:S(2)}) collective-permute-start(bf16[64,1024]{1,0:T(8,128)(2,1)S(1)} %get-tuple-element.75), channel_id=1, source_target_pairs={{0,1},{1,2},{2,3},{3,0},{4,5},{5,6},{6,7},{7,4},{8,9},{9,10},{10,1... | collective-permute-start | bytes 393224 | tf_op jit(solution)/shard_map/ppermute | solution.py:354
  28.8 14.2 %collective-permute-start.4 = (bf16[64,1024]{1,0:T(8,128)(2,1)S(1)}, bf16[64,1024]{1,0:T(8,128)(2,1)S(1)}, u32[]{:S(2)}, u32[]{:S(2)}) collective-permute-start(bf16[64,1024]{1,0:T(8,128)(2,1)S(1)} %get-tuple-element.76), channel_id=1, source_target_pairs={{0,2},{1,3},{2,0},{3,1},{4,6},{5,7},{6,4},{7,5},{8,10},{9,11},{10,... | collective-permute-start | bytes 393224 | tf_op jit(solution)/shard_map/ppermute | solution.py:354
  29.5 13.5 %collective-permute-start.5 = (bf16[64,1024]{1,0:T(8,128)(2,1)S(1)}, bf16[64,1024]{1,0:T(8,128)(2,1)S(1)}, u32[]{:S(2)}, u32[]{:S(2)}) collective-permute-start(bf16[64,1024]{1,0:T(8,128)(2,1)S(1)} %get-tuple-element.77), channel_id=1, source_target_pairs={{0,3},{1,0},{2,1},{3,2},{4,7},{5,4},{6,5},{7,6},{8,11},{9,8},{10,9... | collective-permute-start | bytes 393224 | tf_op jit(solution)/shard_map/ppermute | solution.py:354
  75.1 8.5 %collective-permute-start.10 = (bf16[64,1024]{1,0:T(8,128)(2,1)S(1)}, bf16[64,1024]{1,0:T(8,128)(2,1)S(1)}, u32[]{:S(2)}, u32[]{:S(2)}) collective-permute-start(bf16[64,1024]{1,0:T(8,128)(2,1)S(1)} %get-tuple-element.87), channel_id=1, source_target_pairs={{0,2},{1,3},{2,0},{3,1},{4,6},{5,7},{6,4},{7,5},{8,10},{9,11},{10,... | collective-permute-start | bytes 393224 | tf_op jit(solution)/shard_map/ppermute | solution.py:354
  77.5 6.0 %collective-permute-start.11 = (bf16[64,1024]{1,0:T(8,128)(2,1)S(1)}, bf16[64,1024]{1,0:T(8,128)(2,1)S(1)}, u32[]{:S(2)}, u32[]{:S(2)}) collective-permute-start(bf16[64,1024]{1,0:T(8,128)(2,1)S(1)} %get-tuple-element.88), channel_id=1, source_target_pairs={{0,3},{1,0},{2,1},{3,2},{4,7},{5,4},{6,5},{7,6},{8,11},{9,8},{10,9... | collective-permute-start | bytes 393224 | tf_op jit(solution)/shard_map/ppermute | solution.py:354
  87.7 7.0 %collective-permute-start.16 = (bf16[64,1024]{1,0:T(8,128)(2,1)S(1)}, bf16[64,1024]{1,0:T(8,128)(2,1)S(1)}, u32[]{:S(2)}, u32[]{:S(2)}) collective-permute-start(bf16[64,1024]{1,0:T(8,128)(2,1)S(1)} %get-tuple-element.107), channel_id=1, source_target_pairs={{0,2},{1,3},{2,0},{3,1},{4,6},{5,7},{6,4},{7,5},{8,10},{9,11},{10,... | collective-permute-start | bytes 393224 | tf_op jit(solution)/shard_map/ppermute | solution.py:354
  90.8 9.9 %collective-permute-start.12 = (bf16[64,512]{1,0:T(8,128)(2,1)S(1)}, bf16[64,512]{1,0:T(8,128)(2,1)S(1)}, u32[]{:S(2)}, u32[]{:S(2)}) collective-permute-start(bf16[64,512]{1,0:T(8,128)(2,1)S(1)} %get-tuple-element.102), channel_id=1, source_target_pairs={{0,8},{4,12},{8,16},{12,20},{16,24},{20,28},{24,0},{28,4},{32,40},... | collective-permute-start | bytes 196616 | tf_op jit(solution)/shard_map/ppermute | solution.py:372
  91.0 9.7 %collective-permute-start.13 = (bf16[64,512]{1,0:T(8,128)(2,1)S(1)}, bf16[64,512]{1,0:T(8,128)(2,1)S(1)}, u32[]{:S(2)}, u32[]{:S(2)}) collective-permute-start(bf16[64,512]{1,0:T(8,128)(2,1)S(1)} %get-tuple-element.103), channel_id=1, source_target_pairs={{0,16},{4,20},{8,24},{12,28},{16,0},{20,4},{24,8},{28,12},{32,48},... | collective-permute-start | bytes 196616 | tf_op jit(solution)/shard_map/ppermute | solution.py:372
  92.5 8.2 %collective-permute-start.14 = (bf16[64,512]{1,0:T(8,128)(2,1)S(1)}, bf16[64,512]{1,0:T(8,128)(2,1)S(1)}, u32[]{:S(2)}, u32[]{:S(2)}) collective-permute-start(bf16[64,512]{1,0:T(8,128)(2,1)S(1)} %get-tuple-element.104), channel_id=1, source_target_pairs={{0,24},{4,28},{8,0},{12,4},{16,8},{20,12},{24,16},{28,20},{32,56},... | collective-permute-start | bytes 196616 | tf_op jit(solution)/shard_map/ppermute | solution.py:372
  100.7 61.6 %all-to-all-start.1 = ((bf16[64,128,128]{2,1,0:T(8,128)(2,1)}), bf16[64,128,128]{2,1,0:T(8,128)(2,1)S(1)}, u32[]{:S(2)}, u32[]{:S(2)}) async-start(bf16[64,128,128]{2,1,0:T(8,128)(2,1)} %far_back.1), calls=%async_computation.1 | async-start | bytes 4194304 | tf_op jit(solution)/shard_map/all_to_all | solution.py:431
  112.7 13.0 %collective-permute-start.28 = (bf16[64,1024]{1,0:T(8,128)(2,1)S(1)}, bf16[64,1024]{1,0:T(8,128)(2,1)S(1)}, u32[]{:S(2)}, u32[]{:S(2)}) collective-permute-start(bf16[64,1024]{1,0:T(8,128)(2,1)S(1)} %copy-done.30), channel_id=1, source_target_pairs={{0,3},{1,0},{2,1},{3,2},{4,7},{5,4},{6,5},{7,6},{8,11},{9,8},{10,9... | collective-permute-start | bytes 393224 | tf_op jit(solution)/shard_map/ppermute | solution.py:354
  119.8 20.2 %collective-permute-start.25 = (f32[64,1024]{1,0:T(8,128)S(1)}, f32[64,1024]{1,0:T(8,128)S(1)}, u32[]{:S(2)}, u32[]{:S(2)}) collective-permute-start(f32[64,1024]{1,0:T(8,128)S(1)} %get-tuple-element.119), channel_id=1, source_target_pairs={{0,1},{1,2},{2,3},{3,0},{4,5},{5,6},{6,7},{7,4},{8,9},{9,10},{10,1... | collective-permute-start | bytes 786440 | tf_op jit(solution)/shard_map/ppermute | solution.py:354
  119.9 20.1 %collective-permute-start.26 = (f32[64,1024]{1,0:T(8,128)S(1)}, f32[64,1024]{1,0:T(8,128)S(1)}, u32[]{:S(2)}, u32[]{:S(2)}) collective-permute-start(f32[64,1024]{1,0:T(8,128)S(1)} %get-tuple-element.120), channel_id=1, source_target_pairs={{0,2},{1,3},{2,0},{3,1},{4,6},{5,7},{6,4},{7,5},{8,10},{9,11},{10,... | collective-permute-start | bytes 786440 | tf_op jit(solution)/shard_map/ppermute | solution.py:354
  121.0 19.0 %collective-permute-start.27 = (f32[64,1024]{1,0:T(8,128)S(1)}, f32[64,1024]{1,0:T(8,128)S(1)}, u32[]{:S(2)}, u32[]{:S(2)}) collective-permute-start(f32[64,1024]{1,0:T(8,128)S(1)} %get-tuple-element.121), channel_id=1, source_target_pairs={{0,3},{1,0},{2,1},{3,2},{4,7},{5,4},{6,5},{7,6},{8,11},{9,8},{10,9... | collective-permute-start | bytes 786440 | tf_op jit(solution)/shard_map/ppermute | solution.py:354
  126.7 6.2 %collective-permute-start.22 = (f32[16,512]{1,0:T(8,128)S(1)}, f32[16,512]{1,0:T(8,128)S(1)}, u32[]{:S(2)}, u32[]{:S(2)}) collective-permute-start(f32[16,512]{1,0:T(8,128)S(1)} %slice_sums.6.refs_0_), channel_id=1, source_target_pairs={{0,64},{4,68},{8,72},{12,76},{16,80},{20,84},{24,88},{28,92},{32,9... | collective-permute-start | bytes 98312 | tf_op jit(solution)/shard_map/slice_sums/ppermute | solution.py:363
  132.9 7.0 %collective-permute-start.30 = (bf16[64,1024]{1,0:T(8,128)(2,1)S(1)}, bf16[64,1024]{1,0:T(8,128)(2,1)S(1)}, u32[]{:S(2)}, u32[]{:S(2)}) collective-permute-start(bf16[64,1024]{1,0:T(8,128)(2,1)S(1)} %copy-done.28), channel_id=1, source_target_pairs={{0,1},{1,2},{2,3},{3,0},{4,5},{5,6},{6,7},{7,4},{8,9},{9,10},{10,1... | collective-permute-start | bytes 393224 | tf_op jit(solution)/shard_map/ppermute | solution.py:354
  143.2 18.0 %collective-permute-start.34 = (bf16[16,512]{1,0:T(8,128)(2,1)S(1)}, bf16[16,512]{1,0:T(8,128)(2,1)S(1)}, u32[]{:S(2)}, u32[]{:S(2)}) collective-permute-start(bf16[16,512]{1,0:T(8,128)(2,1)S(1)} %slice_sums.7.mine_ref), channel_id=1, source_target_pairs={{0,32},{4,36},{8,40},{12,44},{16,48},{20,52},{24,56},{28,60},{32,0... | collective-permute-start | bytes 49160 | tf_op jit(solution)/shard_map/spread/ppermute | solution.py:363
  148.2 13.0 %collective-permute-start.33 = (bf16[16,512]{1,0:T(8,128)(2,1)S(1)}, bf16[16,512]{1,0:T(8,128)(2,1)S(1)}, u32[]{:S(2)}, u32[]{:S(2)}) collective-permute-start(bf16[16,512]{1,0:T(8,128)(2,1)S(1)} %slice_sums.7.mine_ref), channel_id=1, source_target_pairs={{0,24},{4,44},{8,32},{12,52},{16,40},{20,60},{24,48},{28,4},{32,56... | collective-permute-start | bytes 49160 | tf_op jit(solution)/shard_map/spread/ppermute | solution.py:363
  149.0 12.2 %collective-permute-start.32 = (bf16[16,512]{1,0:T(8,128)(2,1)S(1)}, bf16[16,512]{1,0:T(8,128)(2,1)S(1)}, u32[]{:S(2)}, u32[]{:S(2)}) collective-permute-start(bf16[16,512]{1,0:T(8,128)(2,1)S(1)} %slice_sums.7.mine_ref), channel_id=1, source_target_pairs={{0,16},{4,52},{8,24},{12,60},{16,32},{20,4},{24,40},{28,12},{32,48... | collective-permute-start | bytes 49160 | tf_op jit(solution)/shard_map/spread/ppermute | solution.py:363
  150.7 10.5 %collective-permute-start.31 = (bf16[16,512]{1,0:T(8,128)(2,1)S(1)}, bf16[16,512]{1,0:T(8,128)(2,1)S(1)}, u32[]{:S(2)}, u32[]{:S(2)}) collective-permute-start(bf16[16,512]{1,0:T(8,128)(2,1)S(1)} %slice_sums.7.mine_ref), channel_id=1, source_target_pairs={{0,8},{4,60},{8,16},{12,4},{16,24},{20,12},{24,32},{28,20},{32,40}... | collective-permute-start | bytes 49160 | tf_op jit(solution)/shard_map/spread/ppermute | solution.py:363
  (45 other events, 396.9 us)

commit v9 on v6

--- a/solution.py
+++ b/solution.py
@@ -74,6 +74,15 @@
     return pltpu.make_async_copy(far_hbm.at[rows], far_ref.at[rows], sems.at[step])
 
 
+def runs(parts):
+    return [(0, parts // 8), (parts // 8, parts // 8), (parts // 4, parts // 4), (parts // 2, parts // 2)]
+
+
+def run_copy(far_hbm, far_ref, sems, index):
+    rows = pl.ds(*runs(far_ref.shape[0])[index])
+    return pltpu.make_async_copy(far_hbm.at[rows], far_ref.at[rows], sems.at[index])
+
+
 def chunk_body(rep_ref, feats_ref, cot_ref, *outs):
     reps = len(outs) // 2
     width = outs[0].shape[1]
@@ -125,18 +134,16 @@
     width = outs[0].shape[1]
     load_acc = pltpu.make_async_copy(near_acc_hbm, near_acc_ref, acc_sem)
     load_div = pltpu.make_async_copy(div_hbm, div_ref, div_sem)
-    for step in range(far_ref.shape[0] // STEP):
-        tile_copy(far_hbm, far_ref, sems, step).start()
+    for index in range(4):
+        run_copy(far_hbm, far_ref, sems, index).start()
     load_acc.start()
     load_div.start()
     acc_ref[...] = jnp.zeros_like(acc_ref)
 
-    @pl.loop(0, far_ref.shape[0] // STEP)
-    def _(step):
-        tile_copy(far_hbm, far_ref, sems, step).wait()
-        for item in range(STEP):
+    for index, (first, count) in enumerate(runs(far_ref.shape[0])):
+        run_copy(far_hbm, far_ref, sems, index).wait()
+        for part in range(first, first + count):
             for slot in range(2):
-                part = step * STEP + item
                 row = rows_ref[slot, part]
                 block = got_ref[part, slot * chans : (slot + 1) * chans, :]
                 acc_ref[:, lanes(row, TILE)] += dot(block, far_ref[part, slot], 1, 0)
@@ -265,28 +272,26 @@
 def far_back_body(rep_ref, rows_ref, s0, s1, s2, s3, far_hbm, out_ref, full_ref, buf_ref, far_ref, sems, out_sems):
     chans = full_ref.shape[0]
     parts = far_ref.shape[0]
-    for step in range(parts // STEP):
-        tile_copy(far_hbm, far_ref, sems, step).start()
+    for index in range(4):
+        run_copy(far_hbm, far_ref, sems, index).start()
     gather_lanes(full_ref, (s0, s1, s2, s3), rep_ref[0])
 
+    each = parts // 4
+
     def copy(step):
-        rows = pl.ds(step * STEP, STEP)
-        return pltpu.make_async_copy(
-            buf_ref.at[rows], out_ref.at[rows], out_sems.at[step]
-        )
-
-    @pl.loop(0, parts // STEP)
-    def _(step):
-        tile_copy(far_hbm, far_ref, sems, step).wait()
-        for item in range(STEP):
+        rows = pl.ds(step * each, each)
+        return pltpu.make_async_copy(buf_ref.at[rows], out_ref.at[rows], out_sems.at[step])
+
+    for index, (first, count) in enumerate(runs(parts)):
+        run_copy(far_hbm, far_ref, sems, index).wait()
+        for part in range(first, first + count):
             for slot in range(2):
-                part = step * STEP + item
                 row = rows_ref[slot, part]
                 term = dot(full_ref[:, lanes(row, TILE)], far_ref[part, slot], 1, 0)
                 buf_ref[part, slot * chans : (slot + 1) * chans, :] = term.astype(BF16)
-        copy(step).start()
-
-    for step in range(parts // STEP):
+            if (part + 1) % each == 0:
+                copy(part // each).start()
+    for step in range(4):
         copy(step).wait()
 
 

time: 165 us -> 164 us (level)
    ppermute x9, waiting for transfers between devices: 12.9 us -> 14.6 us  [move(): return lax.ppermute(value, 'dom', pairs)]
  transfers between devices with their start and end apart: 38 -> 38, of which waited for: 13 -> 14; matrix products, arithmetic and copies ran while one was open for 0% -> 0% of each run, Pallas kernels for 12% -> 12%
where the time goes in v9:
time: 164 us; the launch traced here: 163 us
  starting transfers between devices  70.5 us (43%)
  waiting for transfers between devices  56.3 us (34%)
  Pallas kernels  30.2 us (18%)
  local copies, waits for them, and re-layouts  5.27 us (3%)
    pallas_call x15, Pallas kernels, call(): pl.pallas_call(body, in_specs=[IN_SMEM] * len(scalars) + [IN_HBM if i in...  30.2 us
    ppermute x24, starting transfers between devices, shift(): lax.ppermute(value, 'rep', [(i, (i + by) % reps) for i in range(reps)])  30 us
    all_to_all x1, waiting for transfers between devices, local(): lax.all_to_all(outgoing, 'dom', split_axis=0, concat_axis=0, tiled=True)  26.9 us
    ppermute x9, starting transfers between devices, move(): return lax.ppermute(value, 'dom', pairs)  15.1 us
    ppermute x24, waiting for transfers between devices, shift(): lax.ppermute(value, 'rep', [(i, (i + by) % reps) for i in range(reps)])  14.8 us
    ppermute x9, waiting for transfers between devices, move(): return lax.ppermute(value, 'dom', pairs)  14.6 us
    all_to_all x1, starting transfers between devices, local(): lax.all_to_all(outgoing, 'dom', split_axis=0, concat_axis=0, tiled=True)  13.3 us
    all_to_all x1, starting transfers between devices, local(): lax.all_to_all(far_back, 'dom', split_axis=0, concat_axis=0, tiled=True)  8.94 us
  transfers between devices with their start and end apart: 38, of which 14 were waited for; matrix products, arithmetic and copies ran while one was open for 0% of the time, Pallas kernels for 12%

profile of v9, /device:TPU:1, one launch (start us, length us, event | category | flops | bytes accessed | tf_op | source)
XLA Modules:
  0.0 163.5 jit_solution(1792110710383327389)
XLA Ops:
  0.6 3.2 %pick.1 = bf16[64,128,128]{2,1,0:T(8,128)(2,1)} custom-call(s32[2,64]{1,0:T(2,128)} %bitcast.27, bf16[64,4096]{1,0:T(8,128)(2,1)} %feats_ref.3), custom_call_target="tpu_custom_call" | custom-call | flops 2200000000 | bytes 65536 | tf_op jit(solution)/shard_map/pick/pallas_call | solution.py:27
  3.9 13.3 %all-to-all-start = ((bf16[64,128,128]{2,1,0:T(8,128)(2,1)}), bf16[64,128,128]{2,1,0:T(8,128)(2,1)S(1)}, u32[]{:S(2)}, u32[]{:S(2)}) async-start(bf16[64,128,128]{2,1,0:T(8,128)(2,1)} %pick.1), calls=%async_computation | async-start | bytes 4194304 | tf_op jit(solution)/shard_map/all_to_all | solution.py:379
  32.9 7.0 %near.1 = (f32[64,4096]{1,0:T(8,128)S(1)}, f32[8,4096]{1,0:T(8,128)S(1)}, bf16[64,2,128,128]{3,2,1,0:T(8,128)(2,1)}) custom-call(s32[2,32]{1,0:T(2,128)S(1)} %bitcast.23, s32[2,64]{1,0:T(2,128)S(1)} %bitcast.20, bf16[64,4096]{1,0:T(8,128)(2,1)S(1)} %copy-done.4, bf16[32,2,128,128]{3,2,1,0:T(8,128)(2,1)S(1)} %copy-done.1, bf16[64,2,128,128]{3,2,1,0:T(8,128)(2,1)S(1)} %bitcast.19), custom_call_target="tpu_custom_call" | custom-call | flops 8800000000 | bytes 65536 | tf_op jit(solution)/shard_map/near/pallas_call | solution.py:27
  41.6 26.9 %all-to-all-done.got_ref = bf16[64,128,128]{2,1,0:T(8,128)(2,1)S(1)} async-done(((bf16[64,128,128]{2,1,0:T(8,128)(2,1)}), bf16[64,128,128]{2,1,0:T(8,128)(2,1)S(1)}, u32[]{:S(2)}, u32[]{:S(2)}) %all-to-all-start) | async-done | bytes 2097184 | tf_op jit(solution)/shard_map/all_to_all | solution.py:379
  68.5 3.8 %far.1 = (bf16[64,1024]{1,0:T(8,128)(2,1)S(1)}, bf16[64,1024]{1,0:T(8,128)(2,1)S(1)}, bf16[64,1024]{1,0:T(8,128)(2,1)S(1)}, bf16[64,1024]{1,0:T(8,128)(2,1)S(1)}) custom-call(s32[2]{0:T(128)S(1)} %pad_add_fusion.rep_ref.place_ref, s32[2,64]{1,0:T(2,128)S(1)} %bitcast.21, bf16[64,128,128]{2,1,0:T(8,128)(2,1)S(1)} %all-to-all-done.got_ref, ...), custom_call_target="tpu_custom_call" | custom-call | flops 6600000000 | bytes 65536 | tf_op jit(solution)/shard_map/far/pallas_call | solution.py:27
  73.6 2.5 %collective-permute-start.10 = (bf16[64,1024]{1,0:T(8,128)(2,1)S(1)}, bf16[64,1024]{1,0:T(8,128)(2,1)S(1)}, u32[]{:S(2)}, u32[]{:S(2)}) collective-permute-start(bf16[64,1024]{1,0:T(8,128)(2,1)S(1)} %get-tuple-element.87), channel_id=1, source_target_pairs={{0,2},{1,3},{2,0},{3,1},{4,6},{5,7},{6,4},{7,5},{8,10},{9,11},{10,... | collective-permute-start | bytes 393224 | tf_op jit(solution)/shard_map/ppermute | solution.py:351
  78.2 3.8 %collective-permute-done.10.refs_2_ = bf16[64,1024]{1,0:T(8,128)(2,1)S(1)} collective-permute-done((bf16[64,1024]{1,0:T(8,128)(2,1)S(1)}, bf16[64,1024]{1,0:T(8,128)(2,1)S(1)}, u32[]{:S(2)}, u32[]{:S(2)}) %collective-permute-start.10) | collective-permute-done | bytes 131104 | tf_op jit(solution)/shard_map/ppermute | solution.py:351
  82.1 2.9 %dense.1 = (bf16[64,1024]{1,0:T(8,128)(2,1)S(1)}, bf16[64,1024]{1,0:T(8,128)(2,1)S(1)}, bf16[64,1024]{1,0:T(8,128)(2,1)S(1)}, bf16[64,1024]{1,0:T(8,128)(2,1)S(1...) custom-call(s32[2]{0:T(128)S(1)} %pad_add_fusion.rep_ref.place_ref, ...), custom_call_target="tpu_custom_call" | custom-call | flops 3300000000 | bytes 65536 | tf_op jit(solution)/shard_map/dense/pallas_call | solution.py:27
  86.2 2.2 %collective-permute-start.16 = (bf16[64,1024]{1,0:T(8,128)(2,1)S(1)}, bf16[64,1024]{1,0:T(8,128)(2,1)S(1)}, u32[]{:S(2)}, u32[]{:S(2)}) collective-permute-start(bf16[64,1024]{1,0:T(8,128)(2,1)S(1)} %get-tuple-element.107), channel_id=1, source_target_pairs={{0,2},{1,3},{2,0},{3,1},{4,6},{5,7},{6,4},{7,5},{8,10},{9,11},{10,... | collective-permute-start | bytes 393224 | tf_op jit(solution)/shard_map/ppermute | solution.py:351
  93.4 4.4 %far_back.1 = bf16[64,128,128]{2,1,0:T(8,128)(2,1)} custom-call(s32[2]{0:T(128)S(1)} %pad_add_fusion.rep_ref.place_ref, s32[2,64]{1,0:T(2,128)S(1)} %bitcast.22, bf16[64,1024]{1,0:T(8,128)(2,1)S(1)} %get-tuple-element.105.s0.refs_0_, bf16[64,1024]{1,0:T(8,128)(2,1)S(1)} %collective-permute-done.15.s1.refs_1_, ...), custom_call_target="tpu_custom_call" | custom-call | flops 5500000256 | bytes 65536 | tf_op jit(solution)/shard_map/far_back/pallas_call | solution.py:27
  97.9 8.9 %all-to-all-start.1 = ((bf16[64,128,128]{2,1,0:T(8,128)(2,1)}), bf16[64,128,128]{2,1,0:T(8,128)(2,1)S(1)}, u32[]{:S(2)}, u32[]{:S(2)}) async-start(bf16[64,128,128]{2,1,0:T(8,128)(2,1)} %far_back.1), calls=%async_computation.1 | async-start | bytes 4194304 | tf_op jit(solution)/shard_map/all_to_all | solution.py:428
  106.9 2.0 %collective-permute-start.18 = (f32[16,512]{1,0:T(8,128)S(1)}, f32[16,512]{1,0:T(8,128)S(1)}, u32[]{:S(2)}, u32[]{:S(2)}) collective-permute-start(f32[16,512]{1,0:T(8,128)S(1)} %get-tuple-element.114), channel_id=1, source_target_pairs={{0,3},{1,0},{2,1},{3,2},{4,7},{5,4},{6,5},{7,6},{8,11},{9,8},{10,9... | collective-permute-start | bytes 98312 | tf_op jit(solution)/shard_map/slice_sums/ppermute | solution.py:351
  109.8 2.6 %collective-permute-start.28 = (bf16[64,1024]{1,0:T(8,128)(2,1)S(1)}, bf16[64,1024]{1,0:T(8,128)(2,1)S(1)}, u32[]{:S(2)}, u32[]{:S(2)}) collective-permute-start(bf16[64,1024]{1,0:T(8,128)(2,1)S(1)} %copy-done.30), channel_id=1, source_target_pairs={{0,3},{1,0},{2,1},{3,2},{4,7},{5,4},{6,5},{7,6},{8,11},{9,8},{10,9... | collective-permute-start | bytes 393224 | tf_op jit(solution)/shard_map/ppermute | solution.py:351
  114.0 2.2 %collective-permute-start.21 = (f32[16,512]{1,0:T(8,128)S(1)}, f32[16,512]{1,0:T(8,128)S(1)}, u32[]{:S(2)}, u32[]{:S(2)}) collective-permute-start(f32[16,512]{1,0:T(8,128)S(1)} %slice_sums.5.refs_0_), channel_id=1, source_target_pairs={{0,4},{4,0},{8,12},{12,8},{16,20},{20,16},{24,28},{28,24},{32,36},... | collective-permute-start | bytes 98312 | tf_op jit(solution)/shard_map/slice_sums/ppermute | solution.py:360
  118.3 1.9 %collective-permute-start.27 = (f32[64,1024]{1,0:T(8,128)S(1)}, f32[64,1024]{1,0:T(8,128)S(1)}, u32[]{:S(2)}, u32[]{:S(2)}) collective-permute-start(f32[64,1024]{1,0:T(8,128)S(1)} %get-tuple-element.121), channel_id=1, source_target_pairs={{0,3},{1,0},{2,1},{3,2},{4,7},{5,4},{6,5},{7,6},{8,11},{9,8},{10,9... | collective-permute-start | bytes 786440 | tf_op jit(solution)/shard_map/ppermute | solution.py:351
  120.2 2.8 %collective-permute-start.24 = (f32[16,512]{1,0:T(8,128)S(1)}, f32[16,512]{1,0:T(8,128)S(1)}, u32[]{:S(2)}, u32[]{:S(2)}) collective-permute-start(f32[16,512]{1,0:T(8,128)S(1)} %slice_sums.6.refs_0_), channel_id=1, source_target_pairs={{0,192},{4,196},{8,200},{12,204},{16,208},{20,212},{24,216},{28,22... | collective-permute-start | bytes 98312 | tf_op jit(solution)/shard_map/slice_sums/ppermute | solution.py:360
  124.8 3.3 %collective-permute-done.23.refs_2_ = f32[16,512]{1,0:T(8,128)S(1)} collective-permute-done((f32[16,512]{1,0:T(8,128)S(1)}, f32[16,512]{1,0:T(8,128)S(1)}, u32[]{:S(2)}, u32[]{:S(2)}) %collective-permute-start.23) | collective-permute-done | bytes 32800 | tf_op jit(solution)/shard_map/slice_sums/ppermute | solution.py:360
  128.1 1.9 %collective-permute-start.29 = (bf16[64,1024]{1,0:T(8,128)(2,1)S(1)}, bf16[64,1024]{1,0:T(8,128)(2,1)S(1)}, u32[]{:S(2)}, u32[]{:S(2)}) collective-permute-start(bf16[64,1024]{1,0:T(8,128)(2,1)S(1)} %copy-done.29), channel_id=1, source_target_pairs={{0,2},{1,3},{2,0},{3,1},{4,6},{5,7},{6,4},{7,5},{8,10},{9,11},{10,... | collective-permute-start | bytes 393224 | tf_op jit(solution)/shard_map/ppermute | solution.py:351
  133.7 4.5 %collective-permute-done.30.refs_11_ = bf16[64,1024]{1,0:T(8,128)(2,1)S(1)} collective-permute-done((bf16[64,1024]{1,0:T(8,128)(2,1)S(1)}, bf16[64,1024]{1,0:T(8,128)(2,1)S(1)}, u32[]{:S(2)}, u32[]{:S(2)}) %collective-permute-start.30) | collective-permute-done | bytes 131104 | tf_op jit(solution)/shard_map/ppermute | solution.py:351
  138.3 3.2 %near_back.1 = (f32[64,4096]{1,0:T(8,128)S(1)}, bf16[64,4096]{1,0:T(8,128)(2,1)}) custom-call(s32[2]{0:T(128)S(1)} %pad_add_fusion.rep_ref.place_ref, s32[2,32]{1,0:T(2,128)S(1)} %bitcast.24, bf16[64,1024]{1,0:T(8,128)(2,1)S(1)} %get-tuple-element.105.s0.refs_0_, bf16[64,1024]{1,0:T(8,128)(2,1)S(1)} %collective-permute-done.15.s1.refs_1_, ...), custom_call_target="tpu_custom_call" | custom-call | flops 2200000000 | bytes 65536 | tf_op jit(solution)/shard_map/near_back/pallas_call | solution.py:27
  141.5 3.7 %collective-permute-start.34 = (bf16[16,512]{1,0:T(8,128)(2,1)S(1)}, bf16[16,512]{1,0:T(8,128)(2,1)S(1)}, u32[]{:S(2)}, u32[]{:S(2)}) collective-permute-start(bf16[16,512]{1,0:T(8,128)(2,1)S(1)} %slice_sums.7.mine_ref), channel_id=1, source_target_pairs={{0,32},{4,36},{8,40},{12,44},{16,48},{20,52},{24,56},{28,60},{32,0... | collective-permute-start | bytes 49160 | tf_op jit(solution)/shard_map/spread/ppermute | solution.py:360
  145.8 2.1 %collective-permute-start.32 = (bf16[16,512]{1,0:T(8,128)(2,1)S(1)}, bf16[16,512]{1,0:T(8,128)(2,1)S(1)}, u32[]{:S(2)}, u32[]{:S(2)}) collective-permute-start(bf16[16,512]{1,0:T(8,128)(2,1)S(1)} %slice_sums.7.mine_ref), channel_id=1, source_target_pairs={{0,16},{4,52},{8,24},{12,60},{16,32},{20,4},{24,40},{28,12},{32,48... | collective-permute-start | bytes 49160 | tf_op jit(solution)/shard_map/spread/ppermute | solution.py:360
  149.4 8.9 %collective-permute-done.34.refs_3_ = bf16[16,512]{1,0:T(8,128)(2,1)S(1)} collective-permute-done((bf16[16,512]{1,0:T(8,128)(2,1)S(1)}, bf16[16,512]{1,0:T(8,128)(2,1)S(1)}, u32[]{:S(2)}, u32[]{:S(2)}) %collective-permute-start.34) | collective-permute-done | bytes 16416 | tf_op jit(solution)/shard_map/spread/ppermute | solution.py:360
  159.4 2.8 %home.1 = bf16[64,4096]{1,0:T(8,128)(2,1)} custom-call(s32[2,64]{1,0:T(2,128)} %bitcast.28, bf16[64,128,128]{2,1,0:T(8,128)(2,1)S(1)} %all-to-all-done.1.got_ref, f32[64,4096]{1,0:T(8,128)} %copy-done.15), custom_call_target="tpu_custom_call" | custom-call | flops 3300000000 | bytes 65536 | tf_op jit(solution)/shard_map/home/pallas_call | solution.py:27
  (131 shorter events, 41.6 us)
Async XLA Ops:
  3.9 64.6 %all-to-all-start = ((bf16[64,128,128]{2,1,0:T(8,128)(2,1)}), bf16[64,128,128]{2,1,0:T(8,128)(2,1)S(1)}, u32[]{:S(2)}, u32[]{:S(2)}) async-start(bf16[64,128,128]{2,1,0:T(8,128)(2,1)} %pick.1), calls=%async_computation | async-start | bytes 4194304 | tf_op jit(solution)/shard_map/all_to_all | solution.py:379
  18.6 10.8 %collective-permute-start = (bf16[64,1024]{1,0:T(8,128)(2,1)S(1)}, bf16[64,1024]{1,0:T(8,128)(2,1)S(1)}, u32[]{:S(2)}, u32[]{:S(2)}) collective-permute-start(bf16[64,1024]{1,0:T(8,128)(2,1)S(1)} %get-tuple-element.71), channel_id=1, source_target_pairs={{0,1},{1,2},{2,3},{3,0},{4,5},{5,6},{6,7},{7,4},{8,9},{9,10},{10,1... | collective-permute-start | bytes 393224 | tf_op jit(solution)/shard_map/ppermute | solution.py:351
  23.2 18.3 %collective-permute-start.1 = (bf16[64,1024]{1,0:T(8,128)(2,1)S(1)}, bf16[64,1024]{1,0:T(8,128)(2,1)S(1)}, u32[]{:S(2)}, u32[]{:S(2)}) collective-permute-start(bf16[64,1024]{1,0:T(8,128)(2,1)S(1)} %get-tuple-element.72), channel_id=1, source_target_pairs={{0,2},{1,3},{2,0},{3,1},{4,6},{5,7},{6,4},{7,5},{8,10},{9,11},{10,... | collective-permute-start | bytes 393224 | tf_op jit(solution)/shard_map/ppermute | solution.py:351
  25.6 16.0 %collective-permute-start.2 = (bf16[64,1024]{1,0:T(8,128)(2,1)S(1)}, bf16[64,1024]{1,0:T(8,128)(2,1)S(1)}, u32[]{:S(2)}, u32[]{:S(2)}) collective-permute-start(bf16[64,1024]{1,0:T(8,128)(2,1)S(1)} %get-tuple-element.73), channel_id=1, source_target_pairs={{0,3},{1,0},{2,1},{3,2},{4,7},{5,4},{6,5},{7,6},{8,11},{9,8},{10,9... | collective-permute-start | bytes 393224 | tf_op jit(solution)/shard_map/ppermute | solution.py:351
  27.1 14.5 %collective-permute-start.3 = (bf16[64,1024]{1,0:T(8,128)(2,1)S(1)}, bf16[64,1024]{1,0:T(8,128)(2,1)S(1)}, u32[]{:S(2)}, u32[]{:S(2)}) collective-permute-start(bf16[64,1024]{1,0:T(8,128)(2,1)S(1)} %get-tuple-element.75), channel_id=1, source_target_pairs={{0,1},{1,2},{2,3},{3,0},{4,5},{5,6},{6,7},{7,4},{8,9},{9,10},{10,1... | collective-permute-start | bytes 393224 | tf_op jit(solution)/shard_map/ppermute | solution.py:351
  28.8 12.8 %collective-permute-start.4 = (bf16[64,1024]{1,0:T(8,128)(2,1)S(1)}, bf16[64,1024]{1,0:T(8,128)(2,1)S(1)}, u32[]{:S(2)}, u32[]{:S(2)}) collective-permute-start(bf16[64,1024]{1,0:T(8,128)(2,1)S(1)} %get-tuple-element.76), channel_id=1, source_target_pairs={{0,2},{1,3},{2,0},{3,1},{4,6},{5,7},{6,4},{7,5},{8,10},{9,11},{10,... | collective-permute-start | bytes 393224 | tf_op jit(solution)/shard_map/ppermute | solution.py:351
  29.5 12.1 %collective-permute-start.5 = (bf16[64,1024]{1,0:T(8,128)(2,1)S(1)}, bf16[64,1024]{1,0:T(8,128)(2,1)S(1)}, u32[]{:S(2)}, u32[]{:S(2)}) collective-permute-start(bf16[64,1024]{1,0:T(8,128)(2,1)S(1)} %get-tuple-element.77), channel_id=1, source_target_pairs={{0,3},{1,0},{2,1},{3,2},{4,7},{5,4},{6,5},{7,6},{8,11},{9,8},{10,9... | collective-permute-start | bytes 393224 | tf_op jit(solution)/shard_map/ppermute | solution.py:351
  73.6 8.5 %collective-permute-start.10 = (bf16[64,1024]{1,0:T(8,128)(2,1)S(1)}, bf16[64,1024]{1,0:T(8,128)(2,1)S(1)}, u32[]{:S(2)}, u32[]{:S(2)}) collective-permute-start(bf16[64,1024]{1,0:T(8,128)(2,1)S(1)} %get-tuple-element.87), channel_id=1, source_target_pairs={{0,2},{1,3},{2,0},{3,1},{4,6},{5,7},{6,4},{7,5},{8,10},{9,11},{10,... | collective-permute-start | bytes 393224 | tf_op jit(solution)/shard_map/ppermute | solution.py:351
  86.2 7.0 %collective-permute-start.16 = (bf16[64,1024]{1,0:T(8,128)(2,1)S(1)}, bf16[64,1024]{1,0:T(8,128)(2,1)S(1)}, u32[]{:S(2)}, u32[]{:S(2)}) collective-permute-start(bf16[64,1024]{1,0:T(8,128)(2,1)S(1)} %get-tuple-element.107), channel_id=1, source_target_pairs={{0,2},{1,3},{2,0},{3,1},{4,6},{5,7},{6,4},{7,5},{8,10},{9,11},{10,... | collective-permute-start | bytes 393224 | tf_op jit(solution)/shard_map/ppermute | solution.py:351
  89.3 8.5 %collective-permute-start.12 = (bf16[64,512]{1,0:T(8,128)(2,1)S(1)}, bf16[64,512]{1,0:T(8,128)(2,1)S(1)}, u32[]{:S(2)}, u32[]{:S(2)}) collective-permute-start(bf16[64,512]{1,0:T(8,128)(2,1)S(1)} %get-tuple-element.102), channel_id=1, source_target_pairs={{0,8},{4,12},{8,16},{12,20},{16,24},{20,28},{24,0},{28,4},{32,40},... | collective-permute-start | bytes 196616 | tf_op jit(solution)/shard_map/ppermute | solution.py:369
  89.5 8.4 %collective-permute-start.13 = (bf16[64,512]{1,0:T(8,128)(2,1)S(1)}, bf16[64,512]{1,0:T(8,128)(2,1)S(1)}, u32[]{:S(2)}, u32[]{:S(2)}) collective-permute-start(bf16[64,512]{1,0:T(8,128)(2,1)S(1)} %get-tuple-element.103), channel_id=1, source_target_pairs={{0,16},{4,20},{8,24},{12,28},{16,0},{20,4},{24,8},{28,12},{32,48},... | collective-permute-start | bytes 196616 | tf_op jit(solution)/shard_map/ppermute | solution.py:369
  91.0 6.9 %collective-permute-start.14 = (bf16[64,512]{1,0:T(8,128)(2,1)S(1)}, bf16[64,512]{1,0:T(8,128)(2,1)S(1)}, u32[]{:S(2)}, u32[]{:S(2)}) collective-permute-start(bf16[64,512]{1,0:T(8,128)(2,1)S(1)} %get-tuple-element.104), channel_id=1, source_target_pairs={{0,24},{4,28},{8,0},{12,4},{16,8},{20,12},{24,16},{28,20},{32,56},... | collective-permute-start | bytes 196616 | tf_op jit(solution)/shard_map/ppermute | solution.py:369
  97.9 61.6 %all-to-all-start.1 = ((bf16[64,128,128]{2,1,0:T(8,128)(2,1)}), bf16[64,128,128]{2,1,0:T(8,128)(2,1)S(1)}, u32[]{:S(2)}, u32[]{:S(2)}) async-start(bf16[64,128,128]{2,1,0:T(8,128)(2,1)} %far_back.1), calls=%async_computation.1 | async-start | bytes 4194304 | tf_op jit(solution)/shard_map/all_to_all | solution.py:428
  109.8 13.3 %collective-permute-start.28 = (bf16[64,1024]{1,0:T(8,128)(2,1)S(1)}, bf16[64,1024]{1,0:T(8,128)(2,1)S(1)}, u32[]{:S(2)}, u32[]{:S(2)}) collective-permute-start(bf16[64,1024]{1,0:T(8,128)(2,1)S(1)} %copy-done.30), channel_id=1, source_target_pairs={{0,3},{1,0},{2,1},{3,2},{4,7},{5,4},{6,5},{7,6},{8,11},{9,8},{10,9... | collective-permute-start | bytes 393224 | tf_op jit(solution)/shard_map/ppermute | solution.py:351
  114.0 6.2 %collective-permute-start.21 = (f32[16,512]{1,0:T(8,128)S(1)}, f32[16,512]{1,0:T(8,128)S(1)}, u32[]{:S(2)}, u32[]{:S(2)}) collective-permute-start(f32[16,512]{1,0:T(8,128)S(1)} %slice_sums.5.refs_0_), channel_id=1, source_target_pairs={{0,4},{4,0},{8,12},{12,8},{16,20},{20,16},{24,28},{28,24},{32,36},... | collective-permute-start | bytes 98312 | tf_op jit(solution)/shard_map/slice_sums/ppermute | solution.py:360
  117.2 21.1 %collective-permute-start.25 = (f32[64,1024]{1,0:T(8,128)S(1)}, f32[64,1024]{1,0:T(8,128)S(1)}, u32[]{:S(2)}, u32[]{:S(2)}) collective-permute-start(f32[64,1024]{1,0:T(8,128)S(1)} %get-tuple-element.119), channel_id=1, source_target_pairs={{0,1},{1,2},{2,3},{3,0},{4,5},{5,6},{6,7},{7,4},{8,9},{9,10},{10,1... | collective-permute-start | bytes 786440 | tf_op jit(solution)/shard_map/ppermute | solution.py:351
  117.3 21.0 %collective-permute-start.26 = (f32[64,1024]{1,0:T(8,128)S(1)}, f32[64,1024]{1,0:T(8,128)S(1)}, u32[]{:S(2)}, u32[]{:S(2)}) collective-permute-start(f32[64,1024]{1,0:T(8,128)S(1)} %get-tuple-element.120), channel_id=1, source_target_pairs={{0,2},{1,3},{2,0},{3,1},{4,6},{5,7},{6,4},{7,5},{8,10},{9,11},{10,... | collective-permute-start | bytes 786440 | tf_op jit(solution)/shard_map/ppermute | solution.py:351
  118.3 20.0 %collective-permute-start.27 = (f32[64,1024]{1,0:T(8,128)S(1)}, f32[64,1024]{1,0:T(8,128)S(1)}, u32[]{:S(2)}, u32[]{:S(2)}) collective-permute-start(f32[64,1024]{1,0:T(8,128)S(1)} %get-tuple-element.121), channel_id=1, source_target_pairs={{0,3},{1,0},{2,1},{3,2},{4,7},{5,4},{6,5},{7,6},{8,11},{9,8},{10,9... | collective-permute-start | bytes 786440 | tf_op jit(solution)/shard_map/ppermute | solution.py:351
  124.1 7.8 %collective-permute-start.22 = (f32[16,512]{1,0:T(8,128)S(1)}, f32[16,512]{1,0:T(8,128)S(1)}, u32[]{:S(2)}, u32[]{:S(2)}) collective-permute-start(f32[16,512]{1,0:T(8,128)S(1)} %slice_sums.6.refs_0_), channel_id=1, source_target_pairs={{0,64},{4,68},{8,72},{12,76},{16,80},{20,84},{24,88},{28,92},{32,9... | collective-permute-start | bytes 98312 | tf_op jit(solution)/shard_map/slice_sums/ppermute | solution.py:360
  131.8 6.4 %collective-permute-start.30 = (bf16[64,1024]{1,0:T(8,128)(2,1)S(1)}, bf16[64,1024]{1,0:T(8,128)(2,1)S(1)}, u32[]{:S(2)}, u32[]{:S(2)}) collective-permute-start(bf16[64,1024]{1,0:T(8,128)(2,1)S(1)} %copy-done.28), channel_id=1, source_target_pairs={{0,1},{1,2},{2,3},{3,0},{4,5},{5,6},{6,7},{7,4},{8,9},{9,10},{10,1... | collective-permute-start | bytes 393224 | tf_op jit(solution)/shard_map/ppermute | solution.py:351
  141.5 16.8 %collective-permute-start.34 = (bf16[16,512]{1,0:T(8,128)(2,1)S(1)}, bf16[16,512]{1,0:T(8,128)(2,1)S(1)}, u32[]{:S(2)}, u32[]{:S(2)}) collective-permute-start(bf16[16,512]{1,0:T(8,128)(2,1)S(1)} %slice_sums.7.mine_ref), channel_id=1, source_target_pairs={{0,32},{4,36},{8,40},{12,44},{16,48},{20,52},{24,56},{28,60},{32,0... | collective-permute-start | bytes 49160 | tf_op jit(solution)/shard_map/spread/ppermute | solution.py:360
  145.2 13.1 %collective-permute-start.33 = (bf16[16,512]{1,0:T(8,128)(2,1)S(1)}, bf16[16,512]{1,0:T(8,128)(2,1)S(1)}, u32[]{:S(2)}, u32[]{:S(2)}) collective-permute-start(bf16[16,512]{1,0:T(8,128)(2,1)S(1)} %slice_sums.7.mine_ref), channel_id=1, source_target_pairs={{0,24},{4,44},{8,32},{12,52},{16,40},{20,60},{24,48},{28,4},{32,56... | collective-permute-start | bytes 49160 | tf_op jit(solution)/shard_map/spread/ppermute | solution.py:360
  145.8 12.5 %collective-permute-start.32 = (bf16[16,512]{1,0:T(8,128)(2,1)S(1)}, bf16[16,512]{1,0:T(8,128)(2,1)S(1)}, u32[]{:S(2)}, u32[]{:S(2)}) collective-permute-start(bf16[16,512]{1,0:T(8,128)(2,1)S(1)} %slice_sums.7.mine_ref), channel_id=1, source_target_pairs={{0,16},{4,52},{8,24},{12,60},{16,32},{20,4},{24,40},{28,12},{32,48... | collective-permute-start | bytes 49160 | tf_op jit(solution)/shard_map/spread/ppermute | solution.py:360
  148.0 10.4 %collective-permute-start.31 = (bf16[16,512]{1,0:T(8,128)(2,1)S(1)}, bf16[16,512]{1,0:T(8,128)(2,1)S(1)}, u32[]{:S(2)}, u32[]{:S(2)}) collective-permute-start(bf16[16,512]{1,0:T(8,128)(2,1)S(1)} %slice_sums.7.mine_ref), channel_id=1, source_target_pairs={{0,8},{4,60},{8,16},{12,4},{16,24},{20,12},{24,32},{28,20},{32,40}... | collective-permute-start | bytes 49160 | tf_op jit(solution)/shard_map/spread/ppermute | solution.py:360
  (45 other events, 389.5 us)

commit v10 on v9

--- a/solution.py
+++ b/solution.py
@@ -128,7 +128,7 @@
 
 def far_body(rep_ref, rows_ref, got_ref, far_hbm, near_acc_hbm, div_hbm, *rest):
     outs = rest[:4]
-    acc_ref, near_acc_ref, far_ref, div_ref, sems, acc_sem, div_sem = rest[4:]
+    acc_ref, second_ref, near_acc_ref, far_ref, div_ref, sems, acc_sem, div_sem = rest[4:]
     reps = len(outs)
     chans = acc_ref.shape[0]
     width = outs[0].shape[1]
@@ -139,6 +139,7 @@
     load_acc.start()
     load_div.start()
     acc_ref[...] = jnp.zeros_like(acc_ref)
+    second_ref[...] = jnp.zeros_like(second_ref)
 
     for index, (first, count) in enumerate(runs(far_ref.shape[0])):
         run_copy(far_hbm, far_ref, sems, index).wait()
@@ -146,13 +147,14 @@
             for slot in range(2):
                 row = rows_ref[slot, part]
                 block = got_ref[part, slot * chans : (slot + 1) * chans, :]
-                acc_ref[:, lanes(row, TILE)] += dot(block, far_ref[part, slot], 1, 0)
+                (acc_ref, second_ref)[slot][:, lanes(row, TILE)] += dot(block, far_ref[part, slot], 1, 0)
 
     load_acc.wait()
     load_div.wait()
     for k in range(reps):
         where = lanes(lax.rem(rep_ref[0] + k, reps), width)
-        outs[k][...] = ((near_acc_ref[:, where] + acc_ref[:, where]) / div_ref[0:1, where]).astype(BF16)
+        total = near_acc_ref[:, where] + (acc_ref[:, where] + second_ref[:, where])
+        outs[k][...] = (total / div_ref[0:1, where]).astype(BF16)
 
 
 def gather_rows(ref, pieces, rep):
@@ -315,18 +317,20 @@
                 acc_ref[:, lanes(cols_ref[link, row], TILE)] += term
 
 
-def home_body(send_ref, got_ref, near_acc_hbm, grad_ref, acc_ref, near_acc_ref, sem):
+def home_body(send_ref, got_ref, near_acc_hbm, grad_ref, acc_ref, second_ref, near_acc_ref, sem):
     chans = acc_ref.shape[0]
     parts = got_ref.shape[0]
     load = pltpu.make_async_copy(near_acc_hbm, near_acc_ref, sem)
     load.start()
     acc_ref[...] = jnp.zeros_like(acc_ref)
+    second_ref[...] = jnp.zeros_like(second_ref)
     for item in range(parts):
         for slot in range(2):
             block = send_ref[slot, item]
-            acc_ref[:, lanes(block, TILE)] += got_ref[item, slot * chans : (slot + 1) * chans, :].astype(F32)
+            target = (acc_ref, second_ref)[slot]
+            target[:, lanes(block, TILE)] += got_ref[item, slot * chans : (slot + 1) * chans, :].astype(F32)
     load.wait()
-    grad_ref[...] = (near_acc_ref[...] + acc_ref[...]).astype(BF16)
+    grad_ref[...] = (near_acc_ref[...] + (acc_ref[...] + second_ref[...])).astype(BF16)
 
 
 def local(feats, w_self, w_neigh, local_cols, local_tiles, send_list, remote_rows, remote_tiles, cotangent):
@@ -395,7 +399,7 @@
     with jax.named_scope("far"):
         agg = call(
             far_body, (rep, rows), (incoming, turned, near_acc, div), [piece] * reps,
-            [wide32, wide32, tile_buf, pltpu.VMEM((8, nodes), F32), sems, sem, sem], 6.0, (1, 2, 3),
+            [wide32, wide32, wide32, tile_buf, pltpu.VMEM((8, nodes), F32), sems, sem, sem], 6.0, (1, 2, 3),
         )
     agg_in = exchange(agg)
 
@@ -453,7 +457,7 @@
         other = move(own, 0, 0, 1)
     with jax.named_scope("home"):
         grad_feats = call(
-            home_body, (sends,), (returned, near_back), shape((chans, nodes), BF16), [wide32, wide32, sem], 3.0, (1,)
+            home_body, (sends,), (returned, near_back), shape((chans, nodes), BF16), [wide32, wide32, wide32, sem], 3.0, (1,)
         )
     with jax.named_scope("join"):
         other, grad_feats = lax.optimization_barrier((other, grad_feats))

time: 164 us -> 164 us (level)
  no operation moved by 1% of the time
where the time goes in v10:
time: 164 us
  starting transfers between devices  70.6 us (43%)
  waiting for transfers between devices  56.3 us (34%)
  Pallas kernels  30.2 us (18%)
  local copies, waits for them, and re-layouts  5.27 us (3%)
    pallas_call x15, Pallas kernels, call(): pl.pallas_call(body, in_specs=[IN_SMEM] * len(scalars) + [IN_HBM if i in...  30.2 us
    ppermute x24, starting transfers between devices, shift(): lax.ppermute(value, 'rep', [(i, (i + by) % reps) for i in range(reps)])  30 us
    all_to_all x1, waiting for transfers between devices, local(): lax.all_to_all(outgoing, 'dom', split_axis=0, concat_axis=0, tiled=True)  26.9 us
    ppermute x9, starting transfers between devices, move(): return lax.ppermute(value, 'dom', pairs)  15.1 us
    ppermute x24, waiting for transfers between devices, shift(): lax.ppermute(value, 'rep', [(i, (i + by) % reps) for i in range(reps)])  14.8 us
    ppermute x9, waiting for transfers between devices, move(): return lax.ppermute(value, 'dom', pairs)  14.6 us
    all_to_all x1, starting transfers between devices, local(): lax.all_to_all(outgoing, 'dom', split_axis=0, concat_axis=0, tiled=True)  13.3 us
    all_to_all x1, starting transfers between devices, local(): lax.all_to_all(far_back, 'dom', split_axis=0, concat_axis=0, tiled=True)  8.96 us
  transfers between devices with their start and end apart: 38, of which 14 were waited for; matrix products, arithmetic and copies ran while one was open for 0% of the time, Pallas kernels for 12%

profile of v10, /device:TPU:1, one launch (start us, length us, event | category | flops | bytes accessed | tf_op | source)
XLA Modules:
  0.0 163.5 jit_solution(14483765060351565733)
XLA Ops:
  0.6 3.2 %pick.1 = bf16[64,128,128]{2,1,0:T(8,128)(2,1)} custom-call(s32[2,64]{1,0:T(2,128)} %bitcast.27, bf16[64,4096]{1,0:T(8,128)(2,1)} %feats_ref.3), custom_call_target="tpu_custom_call" | custom-call | flops 2200000000 | bytes 65536 | tf_op jit(solution)/shard_map/pick/pallas_call | solution.py:27
  3.9 13.3 %all-to-all-start = ((bf16[64,128,128]{2,1,0:T(8,128)(2,1)}), bf16[64,128,128]{2,1,0:T(8,128)(2,1)S(1)}, u32[]{:S(2)}, u32[]{:S(2)}) async-start(bf16[64,128,128]{2,1,0:T(8,128)(2,1)} %pick.1), calls=%async_computation | async-start | bytes 4194304 | tf_op jit(solution)/shard_map/all_to_all | solution.py:383
  32.9 7.0 %near.1 = (f32[64,4096]{1,0:T(8,128)S(1)}, f32[8,4096]{1,0:T(8,128)S(1)}, bf16[64,2,128,128]{3,2,1,0:T(8,128)(2,1)}) custom-call(s32[2,32]{1,0:T(2,128)S(1)} %bitcast.23, s32[2,64]{1,0:T(2,128)S(1)} %bitcast.20, bf16[64,4096]{1,0:T(8,128)(2,1)S(1)} %copy-done.4, bf16[32,2,128,128]{3,2,1,0:T(8,128)(2,1)S(1)} %copy-done.1, bf16[64,2,128,128]{3,2,1,0:T(8,128)(2,1)S(1)} %bitcast.19), custom_call_target="tpu_custom_call" | custom-call | flops 8800000000 | bytes 65536 | tf_op jit(solution)/shard_map/near/pallas_call | solution.py:27
  41.6 26.9 %all-to-all-done.got_ref = bf16[64,128,128]{2,1,0:T(8,128)(2,1)S(1)} async-done(((bf16[64,128,128]{2,1,0:T(8,128)(2,1)}), bf16[64,128,128]{2,1,0:T(8,128)(2,1)S(1)}, u32[]{:S(2)}, u32[]{:S(2)}) %all-to-all-start) | async-done | bytes 2097184 | tf_op jit(solution)/shard_map/all_to_all | solution.py:383
  68.5 3.8 %far.1 = (bf16[64,1024]{1,0:T(8,128)(2,1)S(1)}, bf16[64,1024]{1,0:T(8,128)(2,1)S(1)}, bf16[64,1024]{1,0:T(8,128)(2,1)S(1)}, bf16[64,1024]{1,0:T(8,128)(2,1)S(1)}) custom-call(s32[2]{0:T(128)S(1)} %pad_add_fusion.rep_ref.place_ref, s32[2,64]{1,0:T(2,128)S(1)} %bitcast.21, bf16[64,128,128]{2,1,0:T(8,128)(2,1)S(1)} %all-to-all-done.got_ref, ...), custom_call_target="tpu_custom_call" | custom-call | flops 6600000000 | bytes 65536 | tf_op jit(solution)/shard_map/far/pallas_call | solution.py:27
  73.6 2.5 %collective-permute-start.10 = (bf16[64,1024]{1,0:T(8,128)(2,1)S(1)}, bf16[64,1024]{1,0:T(8,128)(2,1)S(1)}, u32[]{:S(2)}, u32[]{:S(2)}) collective-permute-start(bf16[64,1024]{1,0:T(8,128)(2,1)S(1)} %get-tuple-element.87), channel_id=1, source_target_pairs={{0,2},{1,3},{2,0},{3,1},{4,6},{5,7},{6,4},{7,5},{8,10},{9,11},{10,... | collective-permute-start | bytes 393224 | tf_op jit(solution)/shard_map/ppermute | solution.py:355
  78.3 3.8 %collective-permute-done.10.refs_2_ = bf16[64,1024]{1,0:T(8,128)(2,1)S(1)} collective-permute-done((bf16[64,1024]{1,0:T(8,128)(2,1)S(1)}, bf16[64,1024]{1,0:T(8,128)(2,1)S(1)}, u32[]{:S(2)}, u32[]{:S(2)}) %collective-permute-start.10) | collective-permute-done | bytes 131104 | tf_op jit(solution)/shard_map/ppermute | solution.py:355
  82.1 2.9 %dense.1 = (bf16[64,1024]{1,0:T(8,128)(2,1)S(1)}, bf16[64,1024]{1,0:T(8,128)(2,1)S(1)}, bf16[64,1024]{1,0:T(8,128)(2,1)S(1)}, bf16[64,1024]{1,0:T(8,128)(2,1)S(1...) custom-call(s32[2]{0:T(128)S(1)} %pad_add_fusion.rep_ref.place_ref, ...), custom_call_target="tpu_custom_call" | custom-call | flops 3300000000 | bytes 65536 | tf_op jit(solution)/shard_map/dense/pallas_call | solution.py:27
  86.2 2.2 %collective-permute-start.16 = (bf16[64,1024]{1,0:T(8,128)(2,1)S(1)}, bf16[64,1024]{1,0:T(8,128)(2,1)S(1)}, u32[]{:S(2)}, u32[]{:S(2)}) collective-permute-start(bf16[64,1024]{1,0:T(8,128)(2,1)S(1)} %get-tuple-element.107), channel_id=1, source_target_pairs={{0,2},{1,3},{2,0},{3,1},{4,6},{5,7},{6,4},{7,5},{8,10},{9,11},{10,... | collective-permute-start | bytes 393224 | tf_op jit(solution)/shard_map/ppermute | solution.py:355
  93.4 4.4 %far_back.1 = bf16[64,128,128]{2,1,0:T(8,128)(2,1)} custom-call(s32[2]{0:T(128)S(1)} %pad_add_fusion.rep_ref.place_ref, s32[2,64]{1,0:T(2,128)S(1)} %bitcast.22, bf16[64,1024]{1,0:T(8,128)(2,1)S(1)} %get-tuple-element.105.s0.refs_0_, bf16[64,1024]{1,0:T(8,128)(2,1)S(1)} %collective-permute-done.15.s1.refs_1_, ...), custom_call_target="tpu_custom_call" | custom-call | flops 5500000256 | bytes 65536 | tf_op jit(solution)/shard_map/far_back/pallas_call | solution.py:27
  97.8 9.0 %all-to-all-start.1 = ((bf16[64,128,128]{2,1,0:T(8,128)(2,1)}), bf16[64,128,128]{2,1,0:T(8,128)(2,1)S(1)}, u32[]{:S(2)}, u32[]{:S(2)}) async-start(bf16[64,128,128]{2,1,0:T(8,128)(2,1)} %far_back.1), calls=%async_computation.1 | async-start | bytes 4194304 | tf_op jit(solution)/shard_map/all_to_all | solution.py:432
  106.9 2.0 %collective-permute-start.18 = (f32[16,512]{1,0:T(8,128)S(1)}, f32[16,512]{1,0:T(8,128)S(1)}, u32[]{:S(2)}, u32[]{:S(2)}) collective-permute-start(f32[16,512]{1,0:T(8,128)S(1)} %get-tuple-element.114), channel_id=1, source_target_pairs={{0,3},{1,0},{2,1},{3,2},{4,7},{5,4},{6,5},{7,6},{8,11},{9,8},{10,9... | collective-permute-start | bytes 98312 | tf_op jit(solution)/shard_map/slice_sums/ppermute | solution.py:355
  109.8 2.6 %collective-permute-start.28 = (bf16[64,1024]{1,0:T(8,128)(2,1)S(1)}, bf16[64,1024]{1,0:T(8,128)(2,1)S(1)}, u32[]{:S(2)}, u32[]{:S(2)}) collective-permute-start(bf16[64,1024]{1,0:T(8,128)(2,1)S(1)} %copy-done.30), channel_id=1, source_target_pairs={{0,3},{1,0},{2,1},{3,2},{4,7},{5,4},{6,5},{7,6},{8,11},{9,8},{10,9... | collective-permute-start | bytes 393224 | tf_op jit(solution)/shard_map/ppermute | solution.py:355
  114.0 2.2 %collective-permute-start.21 = (f32[16,512]{1,0:T(8,128)S(1)}, f32[16,512]{1,0:T(8,128)S(1)}, u32[]{:S(2)}, u32[]{:S(2)}) collective-permute-start(f32[16,512]{1,0:T(8,128)S(1)} %slice_sums.5.refs_0_), channel_id=1, source_target_pairs={{0,4},{4,0},{8,12},{12,8},{16,20},{20,16},{24,28},{28,24},{32,36},... | collective-permute-start | bytes 98312 | tf_op jit(solution)/shard_map/slice_sums/ppermute | solution.py:364
  118.3 1.9 %collective-permute-start.27 = (f32[64,1024]{1,0:T(8,128)S(1)}, f32[64,1024]{1,0:T(8,128)S(1)}, u32[]{:S(2)}, u32[]{:S(2)}) collective-permute-start(f32[64,1024]{1,0:T(8,128)S(1)} %get-tuple-element.121), channel_id=1, source_target_pairs={{0,3},{1,0},{2,1},{3,2},{4,7},{5,4},{6,5},{7,6},{8,11},{9,8},{10,9... | collective-permute-start | bytes 786440 | tf_op jit(solution)/shard_map/ppermute | solution.py:355
  120.3 2.8 %collective-permute-start.24 = (f32[16,512]{1,0:T(8,128)S(1)}, f32[16,512]{1,0:T(8,128)S(1)}, u32[]{:S(2)}, u32[]{:S(2)}) collective-permute-start(f32[16,512]{1,0:T(8,128)S(1)} %slice_sums.6.refs_0_), channel_id=1, source_target_pairs={{0,192},{4,196},{8,200},{12,204},{16,208},{20,212},{24,216},{28,22... | collective-permute-start | bytes 98312 | tf_op jit(solution)/shard_map/slice_sums/ppermute | solution.py:364
  124.8 3.3 %collective-permute-done.23.refs_2_ = f32[16,512]{1,0:T(8,128)S(1)} collective-permute-done((f32[16,512]{1,0:T(8,128)S(1)}, f32[16,512]{1,0:T(8,128)S(1)}, u32[]{:S(2)}, u32[]{:S(2)}) %collective-permute-start.23) | collective-permute-done | bytes 32800 | tf_op jit(solution)/shard_map/slice_sums/ppermute | solution.py:364
  128.1 1.9 %collective-permute-start.29 = (bf16[64,1024]{1,0:T(8,128)(2,1)S(1)}, bf16[64,1024]{1,0:T(8,128)(2,1)S(1)}, u32[]{:S(2)}, u32[]{:S(2)}) collective-permute-start(bf16[64,1024]{1,0:T(8,128)(2,1)S(1)} %copy-done.29), channel_id=1, source_target_pairs={{0,2},{1,3},{2,0},{3,1},{4,6},{5,7},{6,4},{7,5},{8,10},{9,11},{10,... | collective-permute-start | bytes 393224 | tf_op jit(solution)/shard_map/ppermute | solution.py:355
  133.7 4.5 %collective-permute-done.30.refs_11_ = bf16[64,1024]{1,0:T(8,128)(2,1)S(1)} collective-permute-done((bf16[64,1024]{1,0:T(8,128)(2,1)S(1)}, bf16[64,1024]{1,0:T(8,128)(2,1)S(1)}, u32[]{:S(2)}, u32[]{:S(2)}) %collective-permute-start.30) | collective-permute-done | bytes 131104 | tf_op jit(solution)/shard_map/ppermute | solution.py:355
  138.3 3.2 %near_back.1 = (f32[64,4096]{1,0:T(8,128)S(1)}, bf16[64,4096]{1,0:T(8,128)(2,1)}) custom-call(s32[2]{0:T(128)S(1)} %pad_add_fusion.rep_ref.place_ref, s32[2,32]{1,0:T(2,128)S(1)} %bitcast.24, bf16[64,1024]{1,0:T(8,128)(2,1)S(1)} %get-tuple-element.105.s0.refs_0_, bf16[64,1024]{1,0:T(8,128)(2,1)S(1)} %collective-permute-done.15.s1.refs_1_, ...), custom_call_target="tpu_custom_call" | custom-call | flops 2200000000 | bytes 65536 | tf_op jit(solution)/shard_map/near_back/pallas_call | solution.py:27
  141.5 3.7 %collective-permute-start.34 = (bf16[16,512]{1,0:T(8,128)(2,1)S(1)}, bf16[16,512]{1,0:T(8,128)(2,1)S(1)}, u32[]{:S(2)}, u32[]{:S(2)}) collective-permute-start(bf16[16,512]{1,0:T(8,128)(2,1)S(1)} %slice_sums.7.mine_ref), channel_id=1, source_target_pairs={{0,32},{4,36},{8,40},{12,44},{16,48},{20,52},{24,56},{28,60},{32,0... | collective-permute-start | bytes 49160 | tf_op jit(solution)/shard_map/spread/ppermute | solution.py:364
  145.8 2.1 %collective-permute-start.32 = (bf16[16,512]{1,0:T(8,128)(2,1)S(1)}, bf16[16,512]{1,0:T(8,128)(2,1)S(1)}, u32[]{:S(2)}, u32[]{:S(2)}) collective-permute-start(bf16[16,512]{1,0:T(8,128)(2,1)S(1)} %slice_sums.7.mine_ref), channel_id=1, source_target_pairs={{0,16},{4,52},{8,24},{12,60},{16,32},{20,4},{24,40},{28,12},{32,48... | collective-permute-start | bytes 49160 | tf_op jit(solution)/shard_map/spread/ppermute | solution.py:364
  149.5 8.9 %collective-permute-done.34.refs_3_ = bf16[16,512]{1,0:T(8,128)(2,1)S(1)} collective-permute-done((bf16[16,512]{1,0:T(8,128)(2,1)S(1)}, bf16[16,512]{1,0:T(8,128)(2,1)S(1)}, u32[]{:S(2)}, u32[]{:S(2)}) %collective-permute-start.34) | collective-permute-done | bytes 16416 | tf_op jit(solution)/shard_map/spread/ppermute | solution.py:364
  159.4 2.9 %home.1 = bf16[64,4096]{1,0:T(8,128)(2,1)} custom-call(s32[2,64]{1,0:T(2,128)} %bitcast.28, bf16[64,128,128]{2,1,0:T(8,128)(2,1)S(1)} %all-to-all-done.1.got_ref, f32[64,4096]{1,0:T(8,128)} %copy-done.15), custom_call_target="tpu_custom_call" | custom-call | flops 3300000000 | bytes 65536 | tf_op jit(solution)/shard_map/home/pallas_call | solution.py:27
  (131 shorter events, 41.6 us)
Async XLA Ops:
  3.9 64.6 %all-to-all-start = ((bf16[64,128,128]{2,1,0:T(8,128)(2,1)}), bf16[64,128,128]{2,1,0:T(8,128)(2,1)S(1)}, u32[]{:S(2)}, u32[]{:S(2)}) async-start(bf16[64,128,128]{2,1,0:T(8,128)(2,1)} %pick.1), calls=%async_computation | async-start | bytes 4194304 | tf_op jit(solution)/shard_map/all_to_all | solution.py:383
  18.6 10.8 %collective-permute-start = (bf16[64,1024]{1,0:T(8,128)(2,1)S(1)}, bf16[64,1024]{1,0:T(8,128)(2,1)S(1)}, u32[]{:S(2)}, u32[]{:S(2)}) collective-permute-start(bf16[64,1024]{1,0:T(8,128)(2,1)S(1)} %get-tuple-element.71), channel_id=1, source_target_pairs={{0,1},{1,2},{2,3},{3,0},{4,5},{5,6},{6,7},{7,4},{8,9},{9,10},{10,1... | collective-permute-start | bytes 393224 | tf_op jit(solution)/shard_map/ppermute | solution.py:355
  23.2 18.3 %collective-permute-start.1 = (bf16[64,1024]{1,0:T(8,128)(2,1)S(1)}, bf16[64,1024]{1,0:T(8,128)(2,1)S(1)}, u32[]{:S(2)}, u32[]{:S(2)}) collective-permute-start(bf16[64,1024]{1,0:T(8,128)(2,1)S(1)} %get-tuple-element.72), channel_id=1, source_target_pairs={{0,2},{1,3},{2,0},{3,1},{4,6},{5,7},{6,4},{7,5},{8,10},{9,11},{10,... | collective-permute-start | bytes 393224 | tf_op jit(solution)/shard_map/ppermute | solution.py:355
  25.6 16.0 %collective-permute-start.2 = (bf16[64,1024]{1,0:T(8,128)(2,1)S(1)}, bf16[64,1024]{1,0:T(8,128)(2,1)S(1)}, u32[]{:S(2)}, u32[]{:S(2)}) collective-permute-start(bf16[64,1024]{1,0:T(8,128)(2,1)S(1)} %get-tuple-element.73), channel_id=1, source_target_pairs={{0,3},{1,0},{2,1},{3,2},{4,7},{5,4},{6,5},{7,6},{8,11},{9,8},{10,9... | collective-permute-start | bytes 393224 | tf_op jit(solution)/shard_map/ppermute | solution.py:355
  27.1 14.5 %collective-permute-start.3 = (bf16[64,1024]{1,0:T(8,128)(2,1)S(1)}, bf16[64,1024]{1,0:T(8,128)(2,1)S(1)}, u32[]{:S(2)}, u32[]{:S(2)}) collective-permute-start(bf16[64,1024]{1,0:T(8,128)(2,1)S(1)} %get-tuple-element.75), channel_id=1, source_target_pairs={{0,1},{1,2},{2,3},{3,0},{4,5},{5,6},{6,7},{7,4},{8,9},{9,10},{10,1... | collective-permute-start | bytes 393224 | tf_op jit(solution)/shard_map/ppermute | solution.py:355
  28.8 12.8 %collective-permute-start.4 = (bf16[64,1024]{1,0:T(8,128)(2,1)S(1)}, bf16[64,1024]{1,0:T(8,128)(2,1)S(1)}, u32[]{:S(2)}, u32[]{:S(2)}) collective-permute-start(bf16[64,1024]{1,0:T(8,128)(2,1)S(1)} %get-tuple-element.76), channel_id=1, source_target_pairs={{0,2},{1,3},{2,0},{3,1},{4,6},{5,7},{6,4},{7,5},{8,10},{9,11},{10,... | collective-permute-start | bytes 393224 | tf_op jit(solution)/shard_map/ppermute | solution.py:355
  29.5 12.1 %collective-permute-start.5 = (bf16[64,1024]{1,0:T(8,128)(2,1)S(1)}, bf16[64,1024]{1,0:T(8,128)(2,1)S(1)}, u32[]{:S(2)}, u32[]{:S(2)}) collective-permute-start(bf16[64,1024]{1,0:T(8,128)(2,1)S(1)} %get-tuple-element.77), channel_id=1, source_target_pairs={{0,3},{1,0},{2,1},{3,2},{4,7},{5,4},{6,5},{7,6},{8,11},{9,8},{10,9... | collective-permute-start | bytes 393224 | tf_op jit(solution)/shard_map/ppermute | solution.py:355
  73.6 8.5 %collective-permute-start.10 = (bf16[64,1024]{1,0:T(8,128)(2,1)S(1)}, bf16[64,1024]{1,0:T(8,128)(2,1)S(1)}, u32[]{:S(2)}, u32[]{:S(2)}) collective-permute-start(bf16[64,1024]{1,0:T(8,128)(2,1)S(1)} %get-tuple-element.87), channel_id=1, source_target_pairs={{0,2},{1,3},{2,0},{3,1},{4,6},{5,7},{6,4},{7,5},{8,10},{9,11},{10,... | collective-permute-start | bytes 393224 | tf_op jit(solution)/shard_map/ppermute | solution.py:355
  86.2 7.0 %collective-permute-start.16 = (bf16[64,1024]{1,0:T(8,128)(2,1)S(1)}, bf16[64,1024]{1,0:T(8,128)(2,1)S(1)}, u32[]{:S(2)}, u32[]{:S(2)}) collective-permute-start(bf16[64,1024]{1,0:T(8,128)(2,1)S(1)} %get-tuple-element.107), channel_id=1, source_target_pairs={{0,2},{1,3},{2,0},{3,1},{4,6},{5,7},{6,4},{7,5},{8,10},{9,11},{10,... | collective-permute-start | bytes 393224 | tf_op jit(solution)/shard_map/ppermute | solution.py:355
  89.3 8.5 %collective-permute-start.12 = (bf16[64,512]{1,0:T(8,128)(2,1)S(1)}, bf16[64,512]{1,0:T(8,128)(2,1)S(1)}, u32[]{:S(2)}, u32[]{:S(2)}) collective-permute-start(bf16[64,512]{1,0:T(8,128)(2,1)S(1)} %get-tuple-element.102), channel_id=1, source_target_pairs={{0,8},{4,12},{8,16},{12,20},{16,24},{20,28},{24,0},{28,4},{32,40},... | collective-permute-start | bytes 196616 | tf_op jit(solution)/shard_map/ppermute | solution.py:373
  89.5 8.3 %collective-permute-start.13 = (bf16[64,512]{1,0:T(8,128)(2,1)S(1)}, bf16[64,512]{1,0:T(8,128)(2,1)S(1)}, u32[]{:S(2)}, u32[]{:S(2)}) collective-permute-start(bf16[64,512]{1,0:T(8,128)(2,1)S(1)} %get-tuple-element.103), channel_id=1, source_target_pairs={{0,16},{4,20},{8,24},{12,28},{16,0},{20,4},{24,8},{28,12},{32,48},... | collective-permute-start | bytes 196616 | tf_op jit(solution)/shard_map/ppermute | solution.py:373
  91.0 6.8 %collective-permute-start.14 = (bf16[64,512]{1,0:T(8,128)(2,1)S(1)}, bf16[64,512]{1,0:T(8,128)(2,1)S(1)}, u32[]{:S(2)}, u32[]{:S(2)}) collective-permute-start(bf16[64,512]{1,0:T(8,128)(2,1)S(1)} %get-tuple-element.104), channel_id=1, source_target_pairs={{0,24},{4,28},{8,0},{12,4},{16,8},{20,12},{24,16},{28,20},{32,56},... | collective-permute-start | bytes 196616 | tf_op jit(solution)/shard_map/ppermute | solution.py:373
  97.8 61.6 %all-to-all-start.1 = ((bf16[64,128,128]{2,1,0:T(8,128)(2,1)}), bf16[64,128,128]{2,1,0:T(8,128)(2,1)S(1)}, u32[]{:S(2)}, u32[]{:S(2)}) async-start(bf16[64,128,128]{2,1,0:T(8,128)(2,1)} %far_back.1), calls=%async_computation.1 | async-start | bytes 4194304 | tf_op jit(solution)/shard_map/all_to_all | solution.py:432
  109.8 13.3 %collective-permute-start.28 = (bf16[64,1024]{1,0:T(8,128)(2,1)S(1)}, bf16[64,1024]{1,0:T(8,128)(2,1)S(1)}, u32[]{:S(2)}, u32[]{:S(2)}) collective-permute-start(bf16[64,1024]{1,0:T(8,128)(2,1)S(1)} %copy-done.30), channel_id=1, source_target_pairs={{0,3},{1,0},{2,1},{3,2},{4,7},{5,4},{6,5},{7,6},{8,11},{9,8},{10,9... | collective-permute-start | bytes 393224 | tf_op jit(solution)/shard_map/ppermute | solution.py:355
  114.0 6.2 %collective-permute-start.21 = (f32[16,512]{1,0:T(8,128)S(1)}, f32[16,512]{1,0:T(8,128)S(1)}, u32[]{:S(2)}, u32[]{:S(2)}) collective-permute-start(f32[16,512]{1,0:T(8,128)S(1)} %slice_sums.5.refs_0_), channel_id=1, source_target_pairs={{0,4},{4,0},{8,12},{12,8},{16,20},{20,16},{24,28},{28,24},{32,36},... | collective-permute-start | bytes 98312 | tf_op jit(solution)/shard_map/slice_sums/ppermute | solution.py:364
  117.2 21.1 %collective-permute-start.25 = (f32[64,1024]{1,0:T(8,128)S(1)}, f32[64,1024]{1,0:T(8,128)S(1)}, u32[]{:S(2)}, u32[]{:S(2)}) collective-permute-start(f32[64,1024]{1,0:T(8,128)S(1)} %get-tuple-element.119), channel_id=1, source_target_pairs={{0,1},{1,2},{2,3},{3,0},{4,5},{5,6},{6,7},{7,4},{8,9},{9,10},{10,1... | collective-permute-start | bytes 786440 | tf_op jit(solution)/shard_map/ppermute | solution.py:355
  117.3 21.0 %collective-permute-start.26 = (f32[64,1024]{1,0:T(8,128)S(1)}, f32[64,1024]{1,0:T(8,128)S(1)}, u32[]{:S(2)}, u32[]{:S(2)}) collective-permute-start(f32[64,1024]{1,0:T(8,128)S(1)} %get-tuple-element.120), channel_id=1, source_target_pairs={{0,2},{1,3},{2,0},{3,1},{4,6},{5,7},{6,4},{7,5},{8,10},{9,11},{10,... | collective-permute-start | bytes 786440 | tf_op jit(solution)/shard_map/ppermute | solution.py:355
  118.3 20.0 %collective-permute-start.27 = (f32[64,1024]{1,0:T(8,128)S(1)}, f32[64,1024]{1,0:T(8,128)S(1)}, u32[]{:S(2)}, u32[]{:S(2)}) collective-permute-start(f32[64,1024]{1,0:T(8,128)S(1)} %get-tuple-element.121), channel_id=1, source_target_pairs={{0,3},{1,0},{2,1},{3,2},{4,7},{5,4},{6,5},{7,6},{8,11},{9,8},{10,9... | collective-permute-start | bytes 786440 | tf_op jit(solution)/shard_map/ppermute | solution.py:355
  124.1 7.8 %collective-permute-start.22 = (f32[16,512]{1,0:T(8,128)S(1)}, f32[16,512]{1,0:T(8,128)S(1)}, u32[]{:S(2)}, u32[]{:S(2)}) collective-permute-start(f32[16,512]{1,0:T(8,128)S(1)} %slice_sums.6.refs_0_), channel_id=1, source_target_pairs={{0,64},{4,68},{8,72},{12,76},{16,80},{20,84},{24,88},{28,92},{32,9... | collective-permute-start | bytes 98312 | tf_op jit(solution)/shard_map/slice_sums/ppermute | solution.py:364
  131.8 6.5 %collective-permute-start.30 = (bf16[64,1024]{1,0:T(8,128)(2,1)S(1)}, bf16[64,1024]{1,0:T(8,128)(2,1)S(1)}, u32[]{:S(2)}, u32[]{:S(2)}) collective-permute-start(bf16[64,1024]{1,0:T(8,128)(2,1)S(1)} %copy-done.28), channel_id=1, source_target_pairs={{0,1},{1,2},{2,3},{3,0},{4,5},{5,6},{6,7},{7,4},{8,9},{9,10},{10,1... | collective-permute-start | bytes 393224 | tf_op jit(solution)/shard_map/ppermute | solution.py:355
  141.5 16.8 %collective-permute-start.34 = (bf16[16,512]{1,0:T(8,128)(2,1)S(1)}, bf16[16,512]{1,0:T(8,128)(2,1)S(1)}, u32[]{:S(2)}, u32[]{:S(2)}) collective-permute-start(bf16[16,512]{1,0:T(8,128)(2,1)S(1)} %slice_sums.7.mine_ref), channel_id=1, source_target_pairs={{0,32},{4,36},{8,40},{12,44},{16,48},{20,52},{24,56},{28,60},{32,0... | collective-permute-start | bytes 49160 | tf_op jit(solution)/shard_map/spread/ppermute | solution.py:364
  145.2 13.1 %collective-permute-start.33 = (bf16[16,512]{1,0:T(8,128)(2,1)S(1)}, bf16[16,512]{1,0:T(8,128)(2,1)S(1)}, u32[]{:S(2)}, u32[]{:S(2)}) collective-permute-start(bf16[16,512]{1,0:T(8,128)(2,1)S(1)} %slice_sums.7.mine_ref), channel_id=1, source_target_pairs={{0,24},{4,44},{8,32},{12,52},{16,40},{20,60},{24,48},{28,4},{32,56... | collective-permute-start | bytes 49160 | tf_op jit(solution)/shard_map/spread/ppermute | solution.py:364
  145.8 12.5 %collective-permute-start.32 = (bf16[16,512]{1,0:T(8,128)(2,1)S(1)}, bf16[16,512]{1,0:T(8,128)(2,1)S(1)}, u32[]{:S(2)}, u32[]{:S(2)}) collective-permute-start(bf16[16,512]{1,0:T(8,128)(2,1)S(1)} %slice_sums.7.mine_ref), channel_id=1, source_target_pairs={{0,16},{4,52},{8,24},{12,60},{16,32},{20,4},{24,40},{28,12},{32,48... | collective-permute-start | bytes 49160 | tf_op jit(solution)/shard_map/spread/ppermute | solution.py:364
  148.0 10.4 %collective-permute-start.31 = (bf16[16,512]{1,0:T(8,128)(2,1)S(1)}, bf16[16,512]{1,0:T(8,128)(2,1)S(1)}, u32[]{:S(2)}, u32[]{:S(2)}) collective-permute-start(bf16[16,512]{1,0:T(8,128)(2,1)S(1)} %slice_sums.7.mine_ref), channel_id=1, source_target_pairs={{0,8},{4,60},{8,16},{12,4},{16,24},{20,12},{24,32},{28,20},{32,40}... | collective-permute-start | bytes 49160 | tf_op jit(solution)/shard_map/spread/ppermute | solution.py:364
  (45 other events, 389.9 us)

commit v11 on v9

--- a/solution.py
+++ b/solution.py
@@ -75,7 +75,7 @@
 
 
 def runs(parts):
-    return [(0, parts // 8), (parts // 8, parts // 8), (parts // 4, parts // 4), (parts // 2, parts // 2)]
+    return [(0, parts // 8), (parts // 8, 3 * parts // 8), (parts // 2, parts // 2)]
 
 
 def run_copy(far_hbm, far_ref, sems, index):
@@ -134,7 +134,7 @@
     width = outs[0].shape[1]
     load_acc = pltpu.make_async_copy(near_acc_hbm, near_acc_ref, acc_sem)
     load_div = pltpu.make_async_copy(div_hbm, div_ref, div_sem)
-    for index in range(4):
+    for index in range(3):
         run_copy(far_hbm, far_ref, sems, index).start()
     load_acc.start()
     load_div.start()
@@ -272,7 +272,7 @@
 def far_back_body(rep_ref, rows_ref, s0, s1, s2, s3, far_hbm, out_ref, full_ref, buf_ref, far_ref, sems, out_sems):
     chans = full_ref.shape[0]
     parts = far_ref.shape[0]
-    for index in range(4):
+    for index in range(3):
         run_copy(far_hbm, far_ref, sems, index).start()
     gather_lanes(full_ref, (s0, s1, s2, s3), rep_ref[0])
 

time: 164 us -> 164 us (level)
  no operation moved by 1% of the time
where the time goes in v11:
time: 164 us
  starting transfers between devices  70.7 us (43%)
  waiting for transfers between devices  56.2 us (34%)
  Pallas kernels  30.2 us (18%)
  local copies, waits for them, and re-layouts  5.27 us (3%)
    pallas_call x15, Pallas kernels, call(): pl.pallas_call(body, in_specs=[IN_SMEM] * len(scalars) + [IN_HBM if i in...  30.2 us
    ppermute x24, starting transfers between devices, shift(): lax.ppermute(value, 'rep', [(i, (i + by) % reps) for i in range(reps)])  30.2 us
    all_to_all x1, waiting for transfers between devices, local(): lax.all_to_all(outgoing, 'dom', split_axis=0, concat_axis=0, tiled=True)  26.9 us
    ppermute x9, starting transfers between devices, move(): return lax.ppermute(value, 'dom', pairs)  15 us
    ppermute x9, waiting for transfers between devices, move(): return lax.ppermute(value, 'dom', pairs)  14.7 us
    ppermute x24, waiting for transfers between devices, shift(): lax.ppermute(value, 'rep', [(i, (i + by) % reps) for i in range(reps)])  14.6 us
    all_to_all x1, starting transfers between devices, local(): lax.all_to_all(outgoing, 'dom', split_axis=0, concat_axis=0, tiled=True)  13.3 us
    all_to_all x1, starting transfers between devices, local(): lax.all_to_all(far_back, 'dom', split_axis=0, concat_axis=0, tiled=True)  9.01 us
  transfers between devices with their start and end apart: 38, of which 14 were waited for; matrix products, arithmetic and copies ran while one was open for 0% of the time, Pallas kernels for 12%

profile of v11, /device:TPU:1, one launch (start us, length us, event | category | flops | bytes accessed | tf_op | source)
XLA Modules:
  0.0 163.5 jit_solution(14897118418054436614)
XLA Ops:
  0.6 3.2 %pick.1 = bf16[64,128,128]{2,1,0:T(8,128)(2,1)} custom-call(s32[2,64]{1,0:T(2,128)} %bitcast.27, bf16[64,4096]{1,0:T(8,128)(2,1)} %feats_ref.3), custom_call_target="tpu_custom_call" | custom-call | flops 2200000000 | bytes 65536 | tf_op jit(solution)/shard_map/pick/pallas_call | solution.py:27
  3.9 13.3 %all-to-all-start = ((bf16[64,128,128]{2,1,0:T(8,128)(2,1)}), bf16[64,128,128]{2,1,0:T(8,128)(2,1)S(1)}, u32[]{:S(2)}, u32[]{:S(2)}) async-start(bf16[64,128,128]{2,1,0:T(8,128)(2,1)} %pick.1), calls=%async_computation | async-start | bytes 4194304 | tf_op jit(solution)/shard_map/all_to_all | solution.py:379
  29.5 1.9 %collective-permute-start.5 = (bf16[64,1024]{1,0:T(8,128)(2,1)S(1)}, bf16[64,1024]{1,0:T(8,128)(2,1)S(1)}, u32[]{:S(2)}, u32[]{:S(2)}) collective-permute-start(bf16[64,1024]{1,0:T(8,128)(2,1)S(1)} %get-tuple-element.77), channel_id=1, source_target_pairs={{0,3},{1,0},{2,1},{3,2},{4,7},{5,4},{6,5},{7,6},{8,11},{9,8},{10,9... | collective-permute-start | bytes 393224 | tf_op jit(solution)/shard_map/ppermute | solution.py:351
  32.9 7.0 %near.1 = (f32[64,4096]{1,0:T(8,128)S(1)}, f32[8,4096]{1,0:T(8,128)S(1)}, bf16[64,2,128,128]{3,2,1,0:T(8,128)(2,1)}) custom-call(s32[2,32]{1,0:T(2,128)S(1)} %bitcast.23, s32[2,64]{1,0:T(2,128)S(1)} %bitcast.20, bf16[64,4096]{1,0:T(8,128)(2,1)S(1)} %copy-done.4, bf16[32,2,128,128]{3,2,1,0:T(8,128)(2,1)S(1)} %copy-done.1, bf16[64,2,128,128]{3,2,1,0:T(8,128)(2,1)S(1)} %bitcast.19), custom_call_target="tpu_custom_call" | custom-call | flops 8800000000 | bytes 65536 | tf_op jit(solution)/shard_map/near/pallas_call | solution.py:27
  41.6 26.9 %all-to-all-done.got_ref = bf16[64,128,128]{2,1,0:T(8,128)(2,1)S(1)} async-done(((bf16[64,128,128]{2,1,0:T(8,128)(2,1)}), bf16[64,128,128]{2,1,0:T(8,128)(2,1)S(1)}, u32[]{:S(2)}, u32[]{:S(2)}) %all-to-all-start) | async-done | bytes 2097184 | tf_op jit(solution)/shard_map/all_to_all | solution.py:379
  68.5 3.7 %far.1 = (bf16[64,1024]{1,0:T(8,128)(2,1)S(1)}, bf16[64,1024]{1,0:T(8,128)(2,1)S(1)}, bf16[64,1024]{1,0:T(8,128)(2,1)S(1)}, bf16[64,1024]{1,0:T(8,128)(2,1)S(1)}) custom-call(s32[2]{0:T(128)S(1)} %pad_add_fusion.rep_ref.place_ref, s32[2,64]{1,0:T(2,128)S(1)} %bitcast.21, bf16[64,128,128]{2,1,0:T(8,128)(2,1)S(1)} %all-to-all-done.got_ref, ...), custom_call_target="tpu_custom_call" | custom-call | flops 6600000000 | bytes 65536 | tf_op jit(solution)/shard_map/far/pallas_call | solution.py:27
  73.5 2.5 %collective-permute-start.10 = (bf16[64,1024]{1,0:T(8,128)(2,1)S(1)}, bf16[64,1024]{1,0:T(8,128)(2,1)S(1)}, u32[]{:S(2)}, u32[]{:S(2)}) collective-permute-start(bf16[64,1024]{1,0:T(8,128)(2,1)S(1)} %get-tuple-element.87), channel_id=1, source_target_pairs={{0,2},{1,3},{2,0},{3,1},{4,6},{5,7},{6,4},{7,5},{8,10},{9,11},{10,... | collective-permute-start | bytes 393224 | tf_op jit(solution)/shard_map/ppermute | solution.py:351
  78.2 3.8 %collective-permute-done.10.refs_2_ = bf16[64,1024]{1,0:T(8,128)(2,1)S(1)} collective-permute-done((bf16[64,1024]{1,0:T(8,128)(2,1)S(1)}, bf16[64,1024]{1,0:T(8,128)(2,1)S(1)}, u32[]{:S(2)}, u32[]{:S(2)}) %collective-permute-start.10) | collective-permute-done | bytes 131104 | tf_op jit(solution)/shard_map/ppermute | solution.py:351
  82.1 2.9 %dense.1 = (bf16[64,1024]{1,0:T(8,128)(2,1)S(1)}, bf16[64,1024]{1,0:T(8,128)(2,1)S(1)}, bf16[64,1024]{1,0:T(8,128)(2,1)S(1)}, bf16[64,1024]{1,0:T(8,128)(2,1)S(1...) custom-call(s32[2]{0:T(128)S(1)} %pad_add_fusion.rep_ref.place_ref, ...), custom_call_target="tpu_custom_call" | custom-call | flops 3300000000 | bytes 65536 | tf_op jit(solution)/shard_map/dense/pallas_call | solution.py:27
  86.1 2.2 %collective-permute-start.16 = (bf16[64,1024]{1,0:T(8,128)(2,1)S(1)}, bf16[64,1024]{1,0:T(8,128)(2,1)S(1)}, u32[]{:S(2)}, u32[]{:S(2)}) collective-permute-start(bf16[64,1024]{1,0:T(8,128)(2,1)S(1)} %get-tuple-element.107), channel_id=1, source_target_pairs={{0,2},{1,3},{2,0},{3,1},{4,6},{5,7},{6,4},{7,5},{8,10},{9,11},{10,... | collective-permute-start | bytes 393224 | tf_op jit(solution)/shard_map/ppermute | solution.py:351
  93.3 4.4 %far_back.1 = bf16[64,128,128]{2,1,0:T(8,128)(2,1)} custom-call(s32[2]{0:T(128)S(1)} %pad_add_fusion.rep_ref.place_ref, s32[2,64]{1,0:T(2,128)S(1)} %bitcast.22, bf16[64,1024]{1,0:T(8,128)(2,1)S(1)} %get-tuple-element.105.s0.refs_0_, bf16[64,1024]{1,0:T(8,128)(2,1)S(1)} %collective-permute-done.15.s1.refs_1_, ...), custom_call_target="tpu_custom_call" | custom-call | flops 5500000256 | bytes 65536 | tf_op jit(solution)/shard_map/far_back/pallas_call | solution.py:27
  97.8 9.0 %all-to-all-start.1 = ((bf16[64,128,128]{2,1,0:T(8,128)(2,1)}), bf16[64,128,128]{2,1,0:T(8,128)(2,1)S(1)}, u32[]{:S(2)}, u32[]{:S(2)}) async-start(bf16[64,128,128]{2,1,0:T(8,128)(2,1)} %far_back.1), calls=%async_computation.1 | async-start | bytes 4194304 | tf_op jit(solution)/shard_map/all_to_all | solution.py:428
  106.9 1.9 %collective-permute-start.18 = (f32[16,512]{1,0:T(8,128)S(1)}, f32[16,512]{1,0:T(8,128)S(1)}, u32[]{:S(2)}, u32[]{:S(2)}) collective-permute-start(f32[16,512]{1,0:T(8,128)S(1)} %get-tuple-element.114), channel_id=1, source_target_pairs={{0,3},{1,0},{2,1},{3,2},{4,7},{5,4},{6,5},{7,6},{8,11},{9,8},{10,9... | collective-permute-start | bytes 98312 | tf_op jit(solution)/shard_map/slice_sums/ppermute | solution.py:351
  109.8 2.6 %collective-permute-start.28 = (bf16[64,1024]{1,0:T(8,128)(2,1)S(1)}, bf16[64,1024]{1,0:T(8,128)(2,1)S(1)}, u32[]{:S(2)}, u32[]{:S(2)}) collective-permute-start(bf16[64,1024]{1,0:T(8,128)(2,1)S(1)} %copy-done.30), channel_id=1, source_target_pairs={{0,3},{1,0},{2,1},{3,2},{4,7},{5,4},{6,5},{7,6},{8,11},{9,8},{10,9... | collective-permute-start | bytes 393224 | tf_op jit(solution)/shard_map/ppermute | solution.py:351
  114.0 2.0 %collective-permute-start.21 = (f32[16,512]{1,0:T(8,128)S(1)}, f32[16,512]{1,0:T(8,128)S(1)}, u32[]{:S(2)}, u32[]{:S(2)}) collective-permute-start(f32[16,512]{1,0:T(8,128)S(1)} %slice_sums.5.refs_0_), channel_id=1, source_target_pairs={{0,4},{4,0},{8,12},{12,8},{16,20},{20,16},{24,28},{28,24},{32,36},... | collective-permute-start | bytes 98312 | tf_op jit(solution)/shard_map/slice_sums/ppermute | solution.py:360
  118.4 1.8 %collective-permute-start.27 = (f32[64,1024]{1,0:T(8,128)S(1)}, f32[64,1024]{1,0:T(8,128)S(1)}, u32[]{:S(2)}, u32[]{:S(2)}) collective-permute-start(f32[64,1024]{1,0:T(8,128)S(1)} %get-tuple-element.121), channel_id=1, source_target_pairs={{0,3},{1,0},{2,1},{3,2},{4,7},{5,4},{6,5},{7,6},{8,11},{9,8},{10,9... | collective-permute-start | bytes 786440 | tf_op jit(solution)/shard_map/ppermute | solution.py:351
  120.2 2.8 %collective-permute-start.24 = (f32[16,512]{1,0:T(8,128)S(1)}, f32[16,512]{1,0:T(8,128)S(1)}, u32[]{:S(2)}, u32[]{:S(2)}) collective-permute-start(f32[16,512]{1,0:T(8,128)S(1)} %slice_sums.6.refs_0_), channel_id=1, source_target_pairs={{0,192},{4,196},{8,200},{12,204},{16,208},{20,212},{24,216},{28,22... | collective-permute-start | bytes 98312 | tf_op jit(solution)/shard_map/slice_sums/ppermute | solution.py:360
  124.8 3.3 %collective-permute-done.23.refs_2_ = f32[16,512]{1,0:T(8,128)S(1)} collective-permute-done((f32[16,512]{1,0:T(8,128)S(1)}, f32[16,512]{1,0:T(8,128)S(1)}, u32[]{:S(2)}, u32[]{:S(2)}) %collective-permute-start.23) | collective-permute-done | bytes 32800 | tf_op jit(solution)/shard_map/slice_sums/ppermute | solution.py:360
  128.1 1.9 %collective-permute-start.29 = (bf16[64,1024]{1,0:T(8,128)(2,1)S(1)}, bf16[64,1024]{1,0:T(8,128)(2,1)S(1)}, u32[]{:S(2)}, u32[]{:S(2)}) collective-permute-start(bf16[64,1024]{1,0:T(8,128)(2,1)S(1)} %copy-done.29), channel_id=1, source_target_pairs={{0,2},{1,3},{2,0},{3,1},{4,6},{5,7},{6,4},{7,5},{8,10},{9,11},{10,... | collective-permute-start | bytes 393224 | tf_op jit(solution)/shard_map/ppermute | solution.py:351
  133.7 4.4 %collective-permute-done.30.refs_11_ = bf16[64,1024]{1,0:T(8,128)(2,1)S(1)} collective-permute-done((bf16[64,1024]{1,0:T(8,128)(2,1)S(1)}, bf16[64,1024]{1,0:T(8,128)(2,1)S(1)}, u32[]{:S(2)}, u32[]{:S(2)}) %collective-permute-start.30) | collective-permute-done | bytes 131104 | tf_op jit(solution)/shard_map/ppermute | solution.py:351
  138.2 3.2 %near_back.1 = (f32[64,4096]{1,0:T(8,128)S(1)}, bf16[64,4096]{1,0:T(8,128)(2,1)}) custom-call(s32[2]{0:T(128)S(1)} %pad_add_fusion.rep_ref.place_ref, s32[2,32]{1,0:T(2,128)S(1)} %bitcast.24, bf16[64,1024]{1,0:T(8,128)(2,1)S(1)} %get-tuple-element.105.s0.refs_0_, bf16[64,1024]{1,0:T(8,128)(2,1)S(1)} %collective-permute-done.15.s1.refs_1_, ...), custom_call_target="tpu_custom_call" | custom-call | flops 2200000000 | bytes 65536 | tf_op jit(solution)/shard_map/near_back/pallas_call | solution.py:27
  141.4 3.8 %collective-permute-start.34 = (bf16[16,512]{1,0:T(8,128)(2,1)S(1)}, bf16[16,512]{1,0:T(8,128)(2,1)S(1)}, u32[]{:S(2)}, u32[]{:S(2)}) collective-permute-start(bf16[16,512]{1,0:T(8,128)(2,1)S(1)} %slice_sums.7.mine_ref), channel_id=1, source_target_pairs={{0,32},{4,36},{8,40},{12,44},{16,48},{20,52},{24,56},{28,60},{32,0... | collective-permute-start | bytes 49160 | tf_op jit(solution)/shard_map/spread/ppermute | solution.py:360
  149.5 8.9 %collective-permute-done.34.refs_3_ = bf16[16,512]{1,0:T(8,128)(2,1)S(1)} collective-permute-done((bf16[16,512]{1,0:T(8,128)(2,1)S(1)}, bf16[16,512]{1,0:T(8,128)(2,1)S(1)}, u32[]{:S(2)}, u32[]{:S(2)}) %collective-permute-start.34) | collective-permute-done | bytes 16416 | tf_op jit(solution)/shard_map/spread/ppermute | solution.py:360
  159.5 2.8 %home.1 = bf16[64,4096]{1,0:T(8,128)(2,1)} custom-call(s32[2,64]{1,0:T(2,128)} %bitcast.28, bf16[64,128,128]{2,1,0:T(8,128)(2,1)S(1)} %all-to-all-done.1.got_ref, f32[64,4096]{1,0:T(8,128)} %copy-done.15), custom_call_target="tpu_custom_call" | custom-call | flops 3300000000 | bytes 65536 | tf_op jit(solution)/shard_map/home/pallas_call | solution.py:27
  (131 shorter events, 42.2 us)
Async XLA Ops:
  3.9 64.6 %all-to-all-start = ((bf16[64,128,128]{2,1,0:T(8,128)(2,1)}), bf16[64,128,128]{2,1,0:T(8,128)(2,1)S(1)}, u32[]{:S(2)}, u32[]{:S(2)}) async-start(bf16[64,128,128]{2,1,0:T(8,128)(2,1)} %pick.1), calls=%async_computation | async-start | bytes 4194304 | tf_op jit(solution)/shard_map/all_to_all | solution.py:379
  18.6 10.8 %collective-permute-start = (bf16[64,1024]{1,0:T(8,128)(2,1)S(1)}, bf16[64,1024]{1,0:T(8,128)(2,1)S(1)}, u32[]{:S(2)}, u32[]{:S(2)}) collective-permute-start(bf16[64,1024]{1,0:T(8,128)(2,1)S(1)} %get-tuple-element.71), channel_id=1, source_target_pairs={{0,1},{1,2},{2,3},{3,0},{4,5},{5,6},{6,7},{7,4},{8,9},{9,10},{10,1... | collective-permute-start | bytes 393224 | tf_op jit(solution)/shard_map/ppermute | solution.py:351
  23.2 18.3 %collective-permute-start.1 = (bf16[64,1024]{1,0:T(8,128)(2,1)S(1)}, bf16[64,1024]{1,0:T(8,128)(2,1)S(1)}, u32[]{:S(2)}, u32[]{:S(2)}) collective-permute-start(bf16[64,1024]{1,0:T(8,128)(2,1)S(1)} %get-tuple-element.72), channel_id=1, source_target_pairs={{0,2},{1,3},{2,0},{3,1},{4,6},{5,7},{6,4},{7,5},{8,10},{9,11},{10,... | collective-permute-start | bytes 393224 | tf_op jit(solution)/shard_map/ppermute | solution.py:351
  25.6 16.0 %collective-permute-start.2 = (bf16[64,1024]{1,0:T(8,128)(2,1)S(1)}, bf16[64,1024]{1,0:T(8,128)(2,1)S(1)}, u32[]{:S(2)}, u32[]{:S(2)}) collective-permute-start(bf16[64,1024]{1,0:T(8,128)(2,1)S(1)} %get-tuple-element.73), channel_id=1, source_target_pairs={{0,3},{1,0},{2,1},{3,2},{4,7},{5,4},{6,5},{7,6},{8,11},{9,8},{10,9... | collective-permute-start | bytes 393224 | tf_op jit(solution)/shard_map/ppermute | solution.py:351
  27.1 14.5 %collective-permute-start.3 = (bf16[64,1024]{1,0:T(8,128)(2,1)S(1)}, bf16[64,1024]{1,0:T(8,128)(2,1)S(1)}, u32[]{:S(2)}, u32[]{:S(2)}) collective-permute-start(bf16[64,1024]{1,0:T(8,128)(2,1)S(1)} %get-tuple-element.75), channel_id=1, source_target_pairs={{0,1},{1,2},{2,3},{3,0},{4,5},{5,6},{6,7},{7,4},{8,9},{9,10},{10,1... | collective-permute-start | bytes 393224 | tf_op jit(solution)/shard_map/ppermute | solution.py:351
  28.8 12.8 %collective-permute-start.4 = (bf16[64,1024]{1,0:T(8,128)(2,1)S(1)}, bf16[64,1024]{1,0:T(8,128)(2,1)S(1)}, u32[]{:S(2)}, u32[]{:S(2)}) collective-permute-start(bf16[64,1024]{1,0:T(8,128)(2,1)S(1)} %get-tuple-element.76), channel_id=1, source_target_pairs={{0,2},{1,3},{2,0},{3,1},{4,6},{5,7},{6,4},{7,5},{8,10},{9,11},{10,... | collective-permute-start | bytes 393224 | tf_op jit(solution)/shard_map/ppermute | solution.py:351
  29.5 12.1 %collective-permute-start.5 = (bf16[64,1024]{1,0:T(8,128)(2,1)S(1)}, bf16[64,1024]{1,0:T(8,128)(2,1)S(1)}, u32[]{:S(2)}, u32[]{:S(2)}) collective-permute-start(bf16[64,1024]{1,0:T(8,128)(2,1)S(1)} %get-tuple-element.77), channel_id=1, source_target_pairs={{0,3},{1,0},{2,1},{3,2},{4,7},{5,4},{6,5},{7,6},{8,11},{9,8},{10,9... | collective-permute-start | bytes 393224 | tf_op jit(solution)/shard_map/ppermute | solution.py:351
  73.5 8.5 %collective-permute-start.10 = (bf16[64,1024]{1,0:T(8,128)(2,1)S(1)}, bf16[64,1024]{1,0:T(8,128)(2,1)S(1)}, u32[]{:S(2)}, u32[]{:S(2)}) collective-permute-start(bf16[64,1024]{1,0:T(8,128)(2,1)S(1)} %get-tuple-element.87), channel_id=1, source_target_pairs={{0,2},{1,3},{2,0},{3,1},{4,6},{5,7},{6,4},{7,5},{8,10},{9,11},{10,... | collective-permute-start | bytes 393224 | tf_op jit(solution)/shard_map/ppermute | solution.py:351
  86.1 7.0 %collective-permute-start.16 = (bf16[64,1024]{1,0:T(8,128)(2,1)S(1)}, bf16[64,1024]{1,0:T(8,128)(2,1)S(1)}, u32[]{:S(2)}, u32[]{:S(2)}) collective-permute-start(bf16[64,1024]{1,0:T(8,128)(2,1)S(1)} %get-tuple-element.107), channel_id=1, source_target_pairs={{0,2},{1,3},{2,0},{3,1},{4,6},{5,7},{6,4},{7,5},{8,10},{9,11},{10,... | collective-permute-start | bytes 393224 | tf_op jit(solution)/shard_map/ppermute | solution.py:351
  89.3 8.5 %collective-permute-start.12 = (bf16[64,512]{1,0:T(8,128)(2,1)S(1)}, bf16[64,512]{1,0:T(8,128)(2,1)S(1)}, u32[]{:S(2)}, u32[]{:S(2)}) collective-permute-start(bf16[64,512]{1,0:T(8,128)(2,1)S(1)} %get-tuple-element.102), channel_id=1, source_target_pairs={{0,8},{4,12},{8,16},{12,20},{16,24},{20,28},{24,0},{28,4},{32,40},... | collective-permute-start | bytes 196616 | tf_op jit(solution)/shard_map/ppermute | solution.py:369
  89.5 8.3 %collective-permute-start.13 = (bf16[64,512]{1,0:T(8,128)(2,1)S(1)}, bf16[64,512]{1,0:T(8,128)(2,1)S(1)}, u32[]{:S(2)}, u32[]{:S(2)}) collective-permute-start(bf16[64,512]{1,0:T(8,128)(2,1)S(1)} %get-tuple-element.103), channel_id=1, source_target_pairs={{0,16},{4,20},{8,24},{12,28},{16,0},{20,4},{24,8},{28,12},{32,48},... | collective-permute-start | bytes 196616 | tf_op jit(solution)/shard_map/ppermute | solution.py:369
  91.0 6.8 %collective-permute-start.14 = (bf16[64,512]{1,0:T(8,128)(2,1)S(1)}, bf16[64,512]{1,0:T(8,128)(2,1)S(1)}, u32[]{:S(2)}, u32[]{:S(2)}) collective-permute-start(bf16[64,512]{1,0:T(8,128)(2,1)S(1)} %get-tuple-element.104), channel_id=1, source_target_pairs={{0,24},{4,28},{8,0},{12,4},{16,8},{20,12},{24,16},{28,20},{32,56},... | collective-permute-start | bytes 196616 | tf_op jit(solution)/shard_map/ppermute | solution.py:369
  97.8 61.6 %all-to-all-start.1 = ((bf16[64,128,128]{2,1,0:T(8,128)(2,1)}), bf16[64,128,128]{2,1,0:T(8,128)(2,1)S(1)}, u32[]{:S(2)}, u32[]{:S(2)}) async-start(bf16[64,128,128]{2,1,0:T(8,128)(2,1)} %far_back.1), calls=%async_computation.1 | async-start | bytes 4194304 | tf_op jit(solution)/shard_map/all_to_all | solution.py:428
  109.8 13.2 %collective-permute-start.28 = (bf16[64,1024]{1,0:T(8,128)(2,1)S(1)}, bf16[64,1024]{1,0:T(8,128)(2,1)S(1)}, u32[]{:S(2)}, u32[]{:S(2)}) collective-permute-start(bf16[64,1024]{1,0:T(8,128)(2,1)S(1)} %copy-done.30), channel_id=1, source_target_pairs={{0,3},{1,0},{2,1},{3,2},{4,7},{5,4},{6,5},{7,6},{8,11},{9,8},{10,9... | collective-permute-start | bytes 393224 | tf_op jit(solution)/shard_map/ppermute | solution.py:351
  114.0 6.2 %collective-permute-start.21 = (f32[16,512]{1,0:T(8,128)S(1)}, f32[16,512]{1,0:T(8,128)S(1)}, u32[]{:S(2)}, u32[]{:S(2)}) collective-permute-start(f32[16,512]{1,0:T(8,128)S(1)} %slice_sums.5.refs_0_), channel_id=1, source_target_pairs={{0,4},{4,0},{8,12},{12,8},{16,20},{20,16},{24,28},{28,24},{32,36},... | collective-permute-start | bytes 98312 | tf_op jit(solution)/shard_map/slice_sums/ppermute | solution.py:360
  116.9 21.2 %collective-permute-start.25 = (f32[64,1024]{1,0:T(8,128)S(1)}, f32[64,1024]{1,0:T(8,128)S(1)}, u32[]{:S(2)}, u32[]{:S(2)}) collective-permute-start(f32[64,1024]{1,0:T(8,128)S(1)} %get-tuple-element.119), channel_id=1, source_target_pairs={{0,1},{1,2},{2,3},{3,0},{4,5},{5,6},{6,7},{7,4},{8,9},{9,10},{10,1... | collective-permute-start | bytes 786440 | tf_op jit(solution)/shard_map/ppermute | solution.py:351
  117.2 20.9 %collective-permute-start.26 = (f32[64,1024]{1,0:T(8,128)S(1)}, f32[64,1024]{1,0:T(8,128)S(1)}, u32[]{:S(2)}, u32[]{:S(2)}) collective-permute-start(f32[64,1024]{1,0:T(8,128)S(1)} %get-tuple-element.120), channel_id=1, source_target_pairs={{0,2},{1,3},{2,0},{3,1},{4,6},{5,7},{6,4},{7,5},{8,10},{9,11},{10,... | collective-permute-start | bytes 786440 | tf_op jit(solution)/shard_map/ppermute | solution.py:351
  118.4 19.8 %collective-permute-start.27 = (f32[64,1024]{1,0:T(8,128)S(1)}, f32[64,1024]{1,0:T(8,128)S(1)}, u32[]{:S(2)}, u32[]{:S(2)}) collective-permute-start(f32[64,1024]{1,0:T(8,128)S(1)} %get-tuple-element.121), channel_id=1, source_target_pairs={{0,3},{1,0},{2,1},{3,2},{4,7},{5,4},{6,5},{7,6},{8,11},{9,8},{10,9... | collective-permute-start | bytes 786440 | tf_op jit(solution)/shard_map/ppermute | solution.py:351
  124.1 7.8 %collective-permute-start.22 = (f32[16,512]{1,0:T(8,128)S(1)}, f32[16,512]{1,0:T(8,128)S(1)}, u32[]{:S(2)}, u32[]{:S(2)}) collective-permute-start(f32[16,512]{1,0:T(8,128)S(1)} %slice_sums.6.refs_0_), channel_id=1, source_target_pairs={{0,64},{4,68},{8,72},{12,76},{16,80},{20,84},{24,88},{28,92},{32,9... | collective-permute-start | bytes 98312 | tf_op jit(solution)/shard_map/slice_sums/ppermute | solution.py:360
  131.9 6.3 %collective-permute-start.30 = (bf16[64,1024]{1,0:T(8,128)(2,1)S(1)}, bf16[64,1024]{1,0:T(8,128)(2,1)S(1)}, u32[]{:S(2)}, u32[]{:S(2)}) collective-permute-start(bf16[64,1024]{1,0:T(8,128)(2,1)S(1)} %copy-done.28), channel_id=1, source_target_pairs={{0,1},{1,2},{2,3},{3,0},{4,5},{5,6},{6,7},{7,4},{8,9},{9,10},{10,1... | collective-permute-start | bytes 393224 | tf_op jit(solution)/shard_map/ppermute | solution.py:351
  141.4 16.9 %collective-permute-start.34 = (bf16[16,512]{1,0:T(8,128)(2,1)S(1)}, bf16[16,512]{1,0:T(8,128)(2,1)S(1)}, u32[]{:S(2)}, u32[]{:S(2)}) collective-permute-start(bf16[16,512]{1,0:T(8,128)(2,1)S(1)} %slice_sums.7.mine_ref), channel_id=1, source_target_pairs={{0,32},{4,36},{8,40},{12,44},{16,48},{20,52},{24,56},{28,60},{32,0... | collective-permute-start | bytes 49160 | tf_op jit(solution)/shard_map/spread/ppermute | solution.py:360
  145.3 13.1 %collective-permute-start.33 = (bf16[16,512]{1,0:T(8,128)(2,1)S(1)}, bf16[16,512]{1,0:T(8,128)(2,1)S(1)}, u32[]{:S(2)}, u32[]{:S(2)}) collective-permute-start(bf16[16,512]{1,0:T(8,128)(2,1)S(1)} %slice_sums.7.mine_ref), channel_id=1, source_target_pairs={{0,24},{4,44},{8,32},{12,52},{16,40},{20,60},{24,48},{28,4},{32,56... | collective-permute-start | bytes 49160 | tf_op jit(solution)/shard_map/spread/ppermute | solution.py:360
  146.3 12.1 %collective-permute-start.32 = (bf16[16,512]{1,0:T(8,128)(2,1)S(1)}, bf16[16,512]{1,0:T(8,128)(2,1)S(1)}, u32[]{:S(2)}, u32[]{:S(2)}) collective-permute-start(bf16[16,512]{1,0:T(8,128)(2,1)S(1)} %slice_sums.7.mine_ref), channel_id=1, source_target_pairs={{0,16},{4,52},{8,24},{12,60},{16,32},{20,4},{24,40},{28,12},{32,48... | collective-permute-start | bytes 49160 | tf_op jit(solution)/shard_map/spread/ppermute | solution.py:360
  148.0 10.4 %collective-permute-start.31 = (bf16[16,512]{1,0:T(8,128)(2,1)S(1)}, bf16[16,512]{1,0:T(8,128)(2,1)S(1)}, u32[]{:S(2)}, u32[]{:S(2)}) collective-permute-start(bf16[16,512]{1,0:T(8,128)(2,1)S(1)} %slice_sums.7.mine_ref), channel_id=1, source_target_pairs={{0,8},{4,60},{8,16},{12,4},{16,24},{20,12},{24,32},{28,20},{32,40}... | collective-permute-start | bytes 49160 | tf_op jit(solution)/shard_map/spread/ppermute | solution.py:360
  (45 other events, 389.1 us)
